TPU v7x, 32 devices: a whole 2x2x4 slice. The times are simulated.
32 devices in a mesh: row: 4 (over y, x), col: 8 (over z, core).
Axes of the slice: x: 2, y: 2, z: 4, core: 2. Of those that a mesh axis runs over, the one named last changes fastest.
Arguments:
- coupling: float32 [4, 4608, 18432], P(None, 'col', 'row'), may hold values from -0.046875 to 0.046875
- energies: float32 [18432], P(('row', 'col')), may hold values from 0.7 to 14.2
- block: float32 [18432, 16], P(('row', 'col')), may hold values from -6 to 6
Outputs:
- basis: float32 [18432, 16], P(('row', 'col'))
- projections: float32 [2, 16, 16], replicated
- factors: float32 [2, 16, 16], replicated
All inputs are finite; a program needn't handle non-finite values.
Results may differ from a plain program's by a relative error of at most 0.0003.
Values sent between devices are 32-bit elements; how exact they have to be, the bound alone decides.
No kernel may reach another device: no remote copies, remote signals or barrier semaphores. Data moves between devices by JAX's collectives and lax.ppermute only.
A program may use at most 128 MiB of HBM per device.

v0:
```python
import jax
import jax.numpy as jnp
from jax import lax
from jax.sharding import PartitionSpec as P

N = 18432
ITERS = 2


precise = lax.Precision.HIGHEST


def combined(moments_local):
    return lax.psum(moments_local, "row")


def on_device(coupling, energies, block):
    segment = block.shape[0]
    width = block.shape[1]
    column = lax.axis_index("col")
    current, energy_rows = (
        lax.all_gather(block, "col", axis=0, tiled=True),
        lax.all_gather(energies, "col", axis=0, tiled=True),
    )
    prior = jnp.zeros_like(current)
    projection_list = []
    factor_list = []
    for section in range(ITERS):
        own_rows = lax.dynamic_slice_in_dim(current, column * segment, segment, 0)
        column_block = current
        spread = lax.all_gather(own_rows, "row", axis=0, tiled=True)
        spread = spread.reshape(coupling.shape[0], segment, width)
        direct = lax.psum_scatter(
            jnp.einsum("aig,gk->aik", coupling, column_block, precision=precise),
            "row",
            scatter_dimension=0,
            tiled=True,
        ).reshape(segment, width)
        partial_value = jnp.einsum("aig,aik->gk", coupling, spread, precision=precise)
        transposed = lax.psum(partial_value, "col")
        direct_rows = lax.all_gather(direct, "col", axis=0, tiled=True)
        product = energy_rows[:, None] * current + direct_rows + transposed
        stacked = jnp.concatenate([current, prior, product], axis=1)
        moments = combined(jnp.einsum("nk,nl->kl", stacked, stacked, precision=precise)) / N
        projection = moments[:width, 2 * width :]
        cross = moments[width : 2 * width, 2 * width :]
        weights = jnp.concatenate([-projection, -cross, jnp.eye(width, dtype=jnp.float32)], axis=0)
        gram_matrix = jnp.dot(
            weights.T, jnp.dot(moments, weights, precision=precise), precision=precise
        )
        factor = jnp.linalg.cholesky(gram_matrix)
        residual = (
            product
            - jnp.dot(current, projection, precision=precise)
            - jnp.dot(prior, cross, precision=precise)
        )
        prior = current
        current = jax.scipy.linalg.solve_triangular(factor, residual.T, lower=True).T
        projection_list.append(projection)
        factor_list.append(factor)
    basis = lax.dynamic_slice_in_dim(current, column * segment, segment, 0)
    return (basis, jnp.stack(projection_list), jnp.stack(factor_list))


def solution(mesh):
    placed = (P(None, "col", "row"), P(("row", "col")), P(("row", "col"), None))
    return jax.shard_map(
        on_device,
        mesh=mesh,
        in_specs=placed,
        out_specs=(P(("row", "col"), None), P(), P()),
        check_vma=False,
    )
```

profile of v0, /device:TPU:0, one launch (start us, length us, event | category | flops | bytes accessed | tf_op | source)
XLA Modules:
  0.0 340.6 jit_solution(8555709565530399333)
XLA Ops:
  8.0 0.0 reduce-scatter.7.cloned.1.call-start
  8.0 16.3 %all-gather.2 = f32[8,576,16]{1,2,0:T(8,128)S(1)} all-gather(f32[1,576,16]{1,2,0:T(8,128)} %bitcast.93), channel_id=1, replica_groups=mesh['row'=4,'col'=8] {'col'}, dimensions={0}, use_global_device_ids=true | all-gather | bytes 331776 | tf_op jit(solution)/shard_map/all_gather | solution.py:22
  24.3 0.1 copy.9
  24.4 0.1 reshape.46
  24.6 40.0 %fusion.44 = f32[4,576,16]{1,2,0:T(8,128)} fusion(f32[4,576,4608]{2,1,0:T(8,128)} %param.6, f32[4608,16,1]{0,1,2:T(8,128)S(1)} %reshape.46), kind=kOutput, calls=%fused_computation.77 | convolution fusion | flops 2038431744 | bytes 42909696 | tf_op jit(solution)/shard_map/aig,gk->aik/dot_general | solution.py:34
  64.6 0.0 all-reduce.6.cloned.1.call-start
  64.7 0.1 reshape.37
  64.8 0.1 dynamic-slice_bitcast_fusion.2
  64.9 8.8 %all-gather.3 = f32[4,576,16]{1,2,0:T(8,128)S(1)} all-gather(f32[1,576,16]{1,2,0:T(8,128)S(1)} %dynamic-slice_bitcast_fusion.2), channel_id=1, replica_groups=mesh['row'=4,'col'=8] {'row'}, dimensions={0}, use_global_device_ids=true | all-gather | bytes 184320 | tf_op jit(solution)/shard_map/all_gather | solution.py:31
  73.6 24.6 %convolution_bitcast_fusion.3 = f32[4608,16]{0,1:T(8,128)} fusion(f32[4,576,16]{1,2,0:T(8,128)S(1)} %all-gather.3, f32[4,576,4608]{2,1,0:T(8,128)} %param.6), kind=kOutput, calls=%fused_computation.9 | convolution fusion | flops 2038431744 | bytes 42909696 | tf_op jit(solution)/shard_map/aig,aik->gk/dot_general | solution.py:39
  98.3 0.0 reduce-scatter.9.cloned.1.call-start
  98.3 0.6 dynamic-slice.8
  99.6 0.1 pad.14.clone
  99.7 0.3 dynamic-update-slice.2
  99.9 27.3 %all-reduce = f32[4608]{0:T(1024)S(1)} all-reduce(f32[4608]{0:T(1024)S(1)} %dynamic-update-slice.2), channel_id=1, replica_groups=mesh['row'=4,'col'=8] {'col'}, use_global_device_ids=true, to_apply=%add | all-reduce | flops 4608 | bytes 36864
  127.2 0.9 copy.10
  128.2 24.6 %all-gather = f32[1,4608,16]{2,0,1:T(1,128)S(1)} all-gather(f32[1,576,16]{2,0,1:T(1,128)S(1)} %copy.10), channel_id=2, replica_groups=mesh['row'=4,'col'=8] {'col'}, dimensions={1}, use_global_device_ids=true | all-gather | bytes 331776 | tf_op jit(solution)/shard_map/all_gather | solution.py:41
  152.7 2.2 copy.11
  154.9 0.0 all-reduce.6.cloned.1.call-done
  154.9 1.0 fusion.19
  156.0 0.9 fusion.5
  156.9 15.3 %psum.29 = f32[48,48]{1,0:T(8,128)S(1)} all-reduce(f32[48,48]{1,0:T(8,128)S(1)} %fusion.5), channel_id=1, replica_groups=mesh['row'=4,'col'=8] {'row'}, use_global_device_ids=true, to_apply=%region_2.0 | all-reduce | flops 2304 | bytes 18432 | tf_op jit(solution)/shard_map/psum | solution.py:14
  172.3 0.7 slice_bitcast_fusion.1
  172.9 0.1 copy.12
  173.0 0.1 copy.13
  173.1 0.2 fusion.40
  173.3 0.2 fusion.43
  173.5 0.1 copy.14
  173.6 1.5 cholesky.44
  175.1 0.6 compare_reduce_fusion.1
  175.7 0.6 fusion.37
  176.4 1.2 custom-call.6
  177.6 0.5 fusion.4
  178.2 0.4 fusion.23
  178.6 39.3 %convolution_bitcast_fusion.4 = f32[4,576,16]{1,2,0:T(8,128)} fusion(f32[4,576,4608]{2,1,0:T(8,128)} %param.6, f32[16,4608]{1,0:T(8,128)S(1)} %fusion.23), kind=kOutput, calls=%fused_computation.10 | convolution fusion | flops 2038431744 | bytes 42909696 | tf_op jit(solution)/shard_map/aig,gk->aik/dot_general | solution.py:34
  217.9 0.1 dynamic-slice_bitcast_fusion.1
  218.0 0.0 reduce-scatter.9.cloned.1.call-update
  218.0 0.0 all-reduce.8.cloned.1.call-start
  218.1 8.7 %all-gather.4 = f32[4,576,16]{1,2,0:T(8,128)S(1)} all-gather(f32[1,576,16]{1,2,0:T(8,128)S(1)} %dynamic-slice_bitcast_fusion.1), channel_id=1, replica_groups=mesh['row'=4,'col'=8] {'row'}, dimensions={0}, use_global_device_ids=true | all-gather | bytes 184320 | tf_op jit(solution)/shard_map/all_gather | solution.py:31
  226.8 24.6 %convolution_bitcast_fusion.2 = f32[4608,16]{0,1:T(8,128)} fusion(f32[4,576,16]{1,2,0:T(8,128)S(1)} %all-gather.4, f32[4,576,4608]{2,1,0:T(8,128)} %param.6), kind=kOutput, calls=%fused_computation.8 | convolution fusion | flops 2038431744 | bytes 42909696 | tf_op jit(solution)/shard_map/aig,aik->gk/dot_general | solution.py:39
  251.4 0.0 all-reduce.8.cloned.1.call-update
  251.4 0.0 reduce-scatter.9.cloned.1.call-done
  251.4 0.9 copy.15
  252.4 28.0 %all-gather.1 = f32[1,4608,16]{2,0,1:T(1,128)S(1)} all-gather(f32[1,576,16]{2,0,1:T(1,128)S(1)} %copy.15), channel_id=3, replica_groups=mesh['row'=4,'col'=8] {'col'}, dimensions={1}, use_global_device_ids=true | all-gather | bytes 331776 | tf_op jit(solution)/shard_map/all_gather | solution.py:41
  280.4 2.2 copy.16
  282.6 24.1 %all-reduce.8.cloned.1.call-done = f32[4608,16]{0,1:T(8,128)} async-done(((f32[4608,16]{0,1:T(8,128)}), f32[4608,16]{0,1:T(8,128)}) %all-reduce.8.cloned.1.call-update) | async-done | bytes 294928 | tf_op jit(solution)/shard_map/psum | solution.py:40
  306.7 1.1 fusion.17
  307.7 0.8 fusion.10
  308.6 16.3 %psum.31 = f32[48,48]{1,0:T(8,128)S(1)} all-reduce(f32[48,48]{1,0:T(8,128)S(1)} %fusion.10), channel_id=1, replica_groups=mesh['row'=4,'col'=8] {'row'}, use_global_device_ids=true, to_apply=%region_8.11 | all-reduce | flops 2304 | bytes 18432 | tf_op jit(solution)/shard_map/psum | solution.py:14
  324.9 0.1 slice_bitcast_fusion
  324.9 0.5 convolution_bitcast_fusion
  325.5 0.1 copy.17
  325.5 0.1 copy.18
  325.6 0.2 fusion.41
  325.8 0.2 fusion.42
  326.0 0.1 copy.19
  326.1 1.5 cholesky.55
  327.6 0.6 compare_reduce_fusion
  328.3 0.6 fusion.36
  328.9 1.2 custom-call.7
  330.1 0.5 fusion.1
  330.7 0.4 fusion.20
  331.1 0.7 dynamic-slice_bitcast_fusion
  331.8 1.3 pad_maximum_fusion
  (18 shorter events, 0.2 us)
Async XLA Ops:
  8.0 119.2 %reduce-scatter.7.cloned.1.call-start = ((), (), s32[]{:S(2)}) async-start(), calls=%async_computation.4 | async-start | bytes 204800
  24.5 73.8 %copy-start.2 = (u32[32]{0:T(128)S(1)}, u32[32]{0:T(128)}, u32[]{:S(2)}) copy-start(u32[32]{0:T(128)} %constant.50) | copy-start | bytes 388
  24.5 75.1 %copy-start.1 = (f32[576]{0:T(1024)S(1)}, f32[576]{0:T(1024)}, u32[]{:S(2)}) copy-start(f32[576]{0:T(1024)} %param.7) | copy-start | bytes 6916
  64.6 90.3 %all-reduce.6.cloned.1.call-start = ((), (), s32[]{:S(2)}) async-start(), calls=%async_computation.2 | async-start | bytes 589824 | tf_op jit(solution)/shard_map/psum | solution.py:40
  98.3 153.2 %reduce-scatter.9.cloned.1.call-start = ((), (), s32[]{:S(2)}) async-start(), calls=%async_computation.5 | async-start | bytes 204800
  127.2 124.2 %copy-start = (f32[4608]{0:T(1024)}, f32[4608]{0:T(1024)S(1)}, u32[]{:S(2)}) copy-start(f32[4608]{0:T(1024)S(1)} %all-reduce) | copy-start | bytes 55300
  218.0 88.7 %all-reduce.8.cloned.1.call-start = ((), (), s32[]{:S(2)}) async-start(), calls=%async_computation.3 | async-start | bytes 589824 | tf_op jit(solution)/shard_map/psum | solution.py:40
Sparse Core Ops, SparseCore 0:
  64.7 25.2 reduce-scatter.6
  218.1 24.4 reduce-scatter.8
Sparse Core Ops, SparseCore 1:
  98.3 55.3 all-reduce.5
  251.5 55.1 all-reduce.7
where the time goes:
time: 341 us
  blocking collectives  145 us (43%)
  matrix products  134 us (39%)
  waiting for transfers between devices  24.2 us (7%)
  between operations  16.4 us (5%)
  other arithmetic  12.2 us (4%)
  local copies, waits for them, and re-layouts  8.71 us (3%)
    dot_general x2, matrix products, on_device(): jnp.einsum('aig,gk->aik', coupling, column_block, precision=precise)  79.3 us
    all_gather x2, blocking collectives, on_device(): direct_rows = lax.all_gather(direct, 'col', axis=0, tiled=True)  52.6 us
    dot_general x2, matrix products, on_device(): jnp.einsum('aig,aik->gk', coupling, spread, precision=precise)  49.2 us
    psum x2, blocking collectives, combined(): return lax.psum(moments_local, 'row')  31.6 us
    unnamed x1, blocking collectives  27.3 us
    psum x2, waiting for transfers between devices, on_device(): transposed = lax.psum(partial_value, 'col')  24.1 us
    all_gather x2, blocking collectives, on_device(): spread = lax.all_gather(own_rows, 'row', axis=0, tiled=True)  17.5 us
    all_gather x1, blocking collectives, on_device(): lax.all_gather(block, 'col', axis=0, tiled=True)  16.3 us
  transfers between devices with their start and end apart: 4, of which 1 were waited for; matrix products, arithmetic and copies ran while one was open for 17% of the time, Pallas kernels for 0%

commit v1 on v0

v1 whole, which is shorter than its diff:
```python
import functools

import jax
import jax.numpy as jnp
from jax import lax
from jax.experimental import pallas as pl
from jax.experimental.pallas import tpu as pltpu
from jax.sharding import PartitionSpec as P

ITERS = 2
F32 = jnp.float32
BF16 = jnp.bfloat16

precise = lax.Precision.HIGHEST

NN = (((1,), (0,)), ((), ()))
NT = (((1,), (1,)), ((), ()))
TN = (((0,), (0,)), ((), ()))

VMEM_SPEC = pl.BlockSpec(memory_space=pltpu.VMEM)


def generic(coupling, energies, block):
    order = block.shape[0] * lax.axis_size("row") * lax.axis_size("col")
    segment = block.shape[0]
    width = block.shape[1]
    column = lax.axis_index("col")
    current, energy_rows = (
        lax.all_gather(block, "col", axis=0, tiled=True),
        lax.all_gather(energies, "col", axis=0, tiled=True),
    )
    prior = jnp.zeros_like(current)
    projection_list = []
    factor_list = []
    for section in range(ITERS):
        own_rows = lax.dynamic_slice_in_dim(current, column * segment, segment, 0)
        spread = lax.all_gather(own_rows, "row", axis=0, tiled=True)
        spread = spread.reshape(coupling.shape[0], segment, width)
        direct = lax.psum_scatter(
            jnp.einsum("aig,gk->aik", coupling, current, precision=precise),
            "row",
            scatter_dimension=0,
            tiled=True,
        ).reshape(segment, width)
        partial_value = jnp.einsum("aig,aik->gk", coupling, spread, precision=precise)
        transposed = lax.psum(partial_value, "col")
        direct_rows = lax.all_gather(direct, "col", axis=0, tiled=True)
        product = energy_rows[:, None] * current + direct_rows + transposed
        stacked = jnp.concatenate([current, prior, product], axis=1)
        moments = lax.psum(jnp.einsum("nk,nl->kl", stacked, stacked, precision=precise), "row") / order
        projection = moments[:width, 2 * width :]
        cross = moments[width : 2 * width, 2 * width :]
        weights = jnp.concatenate([-projection, -cross, jnp.eye(width, dtype=F32)], axis=0)
        gram_matrix = jnp.dot(weights.T, jnp.dot(moments, weights, precision=precise), precision=precise)
        factor = jnp.linalg.cholesky(gram_matrix)
        residual = (
            product
            - jnp.dot(current, projection, precision=precise)
            - jnp.dot(prior, cross, precision=precise)
        )
        prior = current
        current = jax.scipy.linalg.solve_triangular(factor, residual.T, lower=True).T
        projection_list.append(projection)
        factor_list.append(factor)
    basis = lax.dynamic_slice_in_dim(current, column * segment, segment, 0)
    return (basis, jnp.stack(projection_list), jnp.stack(factor_list))


def place():
    column = lax.axis_index("col")
    return lax.rem(column, 2), lax.div(column, 2), lax.axis_index("row")


def split(value):
    high = value.astype(BF16)
    return high, (value - high.astype(F32)).astype(BF16)


def dot(left, right, dims):
    return lax.dot_general(left, right, dims, preferred_element_type=F32)


def dot32(left, right, dims):
    return lax.dot_general(left, right, dims, preferred_element_type=F32, precision=precise)


def product_kernel(k, n, group, tile, a_ref, pair_ref, *refs):
    mine = refs[: group - 1]
    theirs = refs[group - 1 : 2 * (group - 1)]
    send_ref, keep_ref, xg, xr, rows, u_acc, v_acc = refs[2 * (group - 1) :]
    parity, z, r = place()
    even = parity == 0

    def put(slab, at, first, second):
        high, low = split(jnp.concatenate([first, second], axis=1))
        cols = pl.ds(pl.multiple_of(at * (2 * n), 2 * n), 2 * n)
        slab[:k, cols] = high
        slab[k:, cols] = low

    pair = pair_ref[: 2 * k, :]
    put(xg, z, pair[:k], pair[k:])
    rows[pl.ds(r, 1)] = jnp.where(even, pair[:k], pair[k:])[None]
    for s in range(1, group):
        y, w = mine[s - 1][: 2 * k, :], theirs[s - 1][: 2 * k, :]
        along_z = jnp.where(even, y, w)
        along_row = jnp.where(even, w, y)
        put(xg, lax.bitwise_xor(z, s), along_z[:k], along_z[k:])
        rows[pl.ds(lax.bitwise_xor(r, s), 1)] = jnp.where(even, along_row[:k], along_row[k:])[None]
    for a in range(0, group, 2):
        put(xr, a // 2, rows[a], rows[a + 1])

    v_acc[...] = jnp.zeros_like(v_acc)

    def step(t, carry):
        at = pl.ds(pl.multiple_of(t * tile, tile), tile)
        high, low = split(a_ref[at, :])
        p = dot(xr[:, at], high, NN)
        q = dot(xr[:k, at], low, NN)
        v_acc[...] += p[:k] + p[k:] + q
        p = dot(xg[...], high, NT)
        q = dot(xg[:k, :], low, NT)
        u_acc[:, at] = p[:k] + p[k:] + q
        return carry

    lax.fori_loop(0, a_ref.shape[0] // tile, step, 0)

    def by_z(out):
        for g in range(group):
            both = v_acc[:, 2 * n * g : 2 * n * (g + 1)]
            out[g, :k, :] = both[:, :n]
            out[g, k:, :] = both[:, n:]

    def by_row(out, first):
        for a in range(0, group, 2):
            both = u_acc[:, n * a : n * (a + 2)]
            at = slice(0, k) if first else slice(k, 2 * k)
            rest = slice(k, 2 * k) if first else slice(0, k)
            out[a, at, :] = both[:, :n]
            out[a + 1, at, :] = both[:, n:]
            out[a, rest, :] = jnp.zeros((k, n), F32)
            out[a + 1, rest, :] = jnp.zeros((k, n), F32)

    @pl.when(even)
    def _():
        by_z(keep_ref)
        by_row(send_ref, True)

    @pl.when(jnp.logical_not(even))
    def _():
        by_z(send_ref)
        by_row(keep_ref, False)


def combine_kernel(k, n, group, extra, keep_ref, got_ref, pair_ref, energy_ref, *refs):
    theirs = refs[: group - 1] if extra else ()
    outs = refs[len(theirs) :]
    parity, z, r = place()
    even = parity == 0
    at = jnp.where(even, z, r)
    for s in range(group):
        i = lax.bitwise_xor(at, s)
        total = keep_ref[pl.ds(i, 1)][0] + got_ref[pl.ds(i, 1)][0]
        if s == 0:
            own = energy_ref[...] * pair_ref[: 2 * k, :]
            row = lax.broadcasted_iota(jnp.int32, own.shape, 0)
            total = total + jnp.where((row < k) == even, own, 0.0)
        outs[s][: 2 * k, :] = total
    if extra:
        part = pair_ref[2 * k :, :]
        for w in theirs:
            part = part + w[2 * k :, :]
        part = jnp.where(even, part, jnp.zeros_like(part))
        for s in range(group):
            outs[s][2 * k :, :] = part


def pair_kernel(k, n, first_ref, mine_ref, got_ref, out_ref):
    value = mine_ref[...] + got_ref[...]
    out_ref[: 2 * k, :] = value
    moments = jnp.zeros((2 * k, 2 * k), F32)
    for p in range(2):
        s = jnp.concatenate([first_ref[p * k : (p + 1) * k, :], value[p * k : (p + 1) * k]], axis=0)
        moments = moments + dot32(s, s, NT)
    out_ref[2 * k :, :] = jnp.zeros((8, n), F32)
    for j in range(2 * k // 8):
        out_ref[2 * k : 2 * k + 8, 2 * k * j : 2 * k * (j + 1)] = moments[8 * j : 8 * (j + 1), :]


def factor_of(gram):
    k = gram.shape[0]
    rows = lax.broadcasted_iota(jnp.int32, (k, 2 * k), 0)
    cols = lax.broadcasted_iota(jnp.int32, (k, 2 * k), 1)
    row = lax.broadcasted_iota(jnp.int32, (k, 1), 0)
    both = jnp.concatenate([gram, jnp.where(rows == cols, 1.0, 0.0)[:, :k]], axis=1)
    lower = jnp.zeros((k, k), F32)
    for j in range(k):
        scale = 1.0 / jnp.sqrt(both[j : j + 1, j : j + 1])
        column = jnp.where(row >= j, both[:, j : j + 1] * scale, 0.0)
        lower = jnp.where(cols[:, :k] == j, column, lower)
        lead = both[j : j + 1, :] * scale
        below = jnp.where(row > j, column, 0.0)
        both = jnp.where(rows == j, lead, both - below * lead)
    return lower, both[:, k:]


def gram_of(moments, coefficients):
    k = moments.shape[0]
    w = coefficients.shape[1]
    parts = jnp.concatenate([-coefficients, eye(w)], axis=0)
    return dot32(parts, dot32(moments, parts, NN), TN)


def eye(k):
    return jnp.where(
        lax.broadcasted_iota(jnp.int32, (k, k), 0) == lax.broadcasted_iota(jnp.int32, (k, k), 1), 1.0, 0.0
    ).astype(F32)


def second_kernel(k, n, order, first_ref, pair_ref, mine_ref, got_ref, q_ref, prod_ref, mom_ref, proj_ref, fact_ref):
    packed = mine_ref[2 * k :, :] + got_ref[2 * k :, :]
    moments = jnp.concatenate(
        [packed[:, 2 * k * j : 2 * k * (j + 1)] for j in range(2 * k // 8)], axis=0
    ) * (1.0 / order)
    projection = moments[:k, k:]
    lower, inverse = factor_of(gram_of(moments, projection))
    proj_ref[...] = projection
    fact_ref[...] = lower
    total = jnp.zeros((3 * k, 3 * k), F32)
    for p in range(2):
        at = slice(p * k, (p + 1) * k)
        x, y = first_ref[at, :], pair_ref[at, :]
        w = mine_ref[at, :] + got_ref[at, :]
        q = dot32(inverse, y - dot32(projection, x, TN), NN)
        prod = dot32(inverse, w - dot32(projection, y, TN), NN)
        q_ref[at, :] = q
        prod_ref[at, :] = prod
        s = jnp.concatenate([q, x, prod], axis=0)
        total = total + dot32(s, s, NT)
    mom_ref[...] = total


def last_kernel(k, n, order, group, first_ref, q_ref, prod_ref, proj0_ref, fact0_ref, *refs):
    basis_ref, proj_ref, fact_ref = refs[group:]
    total = refs[0][...]
    for m in refs[1:group]:
        total = total + m[...]
    moments = total * (1.0 / order)
    coefficients = moments[: 2 * k, 2 * k :]
    lower, inverse = factor_of(gram_of(moments, coefficients))
    proj_ref[0] = proj0_ref[...]
    proj_ref[1] = coefficients[:k]
    fact_ref[0] = fact0_ref[...]
    fact_ref[1] = lower
    even = place()[0] == 0
    q = jnp.where(even, q_ref[:k, :], q_ref[k:, :])
    x = jnp.where(even, first_ref[:k, :], first_ref[k:, :])
    prod = jnp.where(even, prod_ref[:k, :], prod_ref[k:, :])
    rest = prod - dot32(coefficients[:k], q, TN) - dot32(coefficients[k:], x, TN)
    basis_ref[...] = dot32(inverse, rest, NN)


def call(kernel, out_shape, n_in, scratch=(), limit=8 << 20, name=None):
    many = isinstance(out_shape, (tuple, list))
    return pl.pallas_call(
        kernel,
        out_shape=out_shape,
        in_specs=[VMEM_SPEC] * n_in,
        out_specs=tuple([VMEM_SPEC] * len(out_shape)) if many else VMEM_SPEC,
        scratch_shapes=list(scratch),
        compiler_params=pltpu.CompilerParams(vmem_limit_bytes=limit),
        name=name,
    )


def shape(*dims):
    return jax.ShapeDtypeStruct(dims, F32)


def on_device(n_row, n_col, coupling, energies, block):
    n, k = block.shape
    group = n_row
    order = n * n_row * n_col
    rows = coupling.shape[0] * n
    width = coupling.shape[2]
    axes = ("row", "col")
    flat = [(r, c) for r in range(n_row) for c in range(n_col)]

    def send(value, to):
        return lax.ppermute(value, axes, [(r * n_col + c, to(r, c)) for r, c in flat])

    def swap(value):
        return send(value, lambda r, c: r * n_col + (c ^ 1))

    def spread(s):
        return lambda r, c: (r ^ s) * n_col + c if c % 2 else r * n_col + (c ^ (2 * s))

    steps = range(1, group)
    tile = 256 if rows % 256 == 0 else rows
    a = pltpu.with_memory_space_constraint(coupling.reshape(rows, width), pltpu.VMEM)
    energy = energies.reshape(1, n)
    own = block.T
    other = swap(own)
    even = lax.rem(lax.axis_index("col"), 2) == 0
    first = jnp.concatenate([jnp.where(even, own, other), jnp.where(even, other, own)], axis=0)

    def products(pair, name):
        mine = [send(pair, spread(s)) for s in steps]
        theirs = [swap(y) for y in mine]
        kept, gone = pltpu.VMEM, BF16
        keep_send = call(
            functools.partial(product_kernel, k, n, group, tile),
            (shape(group, 2 * k, n), shape(group, 2 * k, n)),
            2 + 2 * (group - 1),
            scratch=[
                pltpu.VMEM((2 * k, width), BF16),
                pltpu.VMEM((2 * k, rows), BF16),
                pltpu.VMEM((group, k, n), F32),
                pltpu.VMEM((k, rows), F32),
                pltpu.VMEM((k, width), F32),
            ],
            limit=14 << 20,
            name=name,
        )(a, pair, *mine, *theirs)
        out, keep = keep_send
        got = swap(out)
        extra = pair.shape[0] > 2 * k
        parts = call(
            functools.partial(combine_kernel, k, n, group, extra),
            tuple([shape(pair.shape[0], n)] * group),
            4 + (group - 1 if extra else 0),
            name=name + "_combine",
        )(keep, got, pair, energy, *(theirs if extra else ()))
        total = parts[0]
        for s in steps:
            total = total + send(parts[s], spread(s))
        return total, swap(total)

    mine, got = products(first, "first")
    pair = call(functools.partial(pair_kernel, k, n), shape(2 * k + 8, n), 3, name="pair")(first, mine, got)
    mine, got = products(pair, "second")
    q, prod, moments, proj0, fact0 = call(
        functools.partial(second_kernel, k, n, order),
        (shape(2 * k, n), shape(2 * k, n), shape(3 * k, 3 * k), shape(k, k), shape(k, k)),
        4,
        name="middle",
    )(first, pair, mine, got)
    for s in [None]:
        moments = sum([send(moments, lambda r, c, s=s: (r ^ s) * n_col + c) for s in steps], moments)
    parts = [moments] + [send(moments, lambda r, c, s=s: r * n_col + (c ^ (2 * s))) for s in steps]
    basis, proj, fact = call(
        functools.partial(last_kernel, k, n, order, group),
        (shape(k, n), shape(2, k, k), shape(2, k, k)),
        5 + group,
        name="last",
    )(first, q, prod, proj0, fact0, *parts)
    return basis.T, proj, fact


def solution(mesh):
    n_row, n_col = mesh.shape["row"], mesh.shape["col"]

    def body(coupling, energies, block):
        n, k = block.shape
        paired = n_col == 2 * n_row and n_row & (n_row - 1) == 0 and n_row > 1
        whole = n % 64 == 0 and k % 8 == 0 and 8 * k == 128
        small = coupling.size * 4 <= 44 << 20
        if paired and whole and small:
            return on_device(n_row, n_col, coupling, energies, block)
        return generic(coupling, energies, block)

    placed = (P(None, "col", "row"), P(("row", "col")), P(("row", "col"), None))
    return jax.shard_map(
        body,
        mesh=mesh,
        in_specs=placed,
        out_specs=(P(("row", "col"), None), P(), P()),
        check_vma=False,
    )
```

time: 341 us -> 136 us (0.40)
  blocking collectives: 145 us -> 0 us
  matrix products: 134 us -> 0 us
  Pallas kernels: 0 us -> 48.9 us
  starting transfers between devices: 0.17 us -> 29.1 us
  between operations: 16.4 us -> 0.79 us
  local copies, waits for them, and re-layouts: 8.71 us -> 23 us
  other arithmetic: 12.2 us -> 0.87 us
  waiting for transfers between devices: 24.2 us -> 32.2 us
    dot_general x13 -> x0, matrix products: 133 us -> none  [the longest x2 79.3 us: on_device(): jnp.einsum('aig,gk->aik', coupling, column_block, precision=precise)]
    all_gather x5 -> x0, blocking collectives: 86.4 us -> none  [the longest x2 52.6 us: on_device(): direct_rows = lax.all_gather(direct, 'col', axis=0, tiled=True)]
    pallas_call x0 -> x7, Pallas kernels: none -> 48.9 us  [the longest x2 42.4 us: products(): call(functools.partial(product_kernel, k, n, group, tile), (shape(group,...]
    ppermute x0 -> x29, waiting for transfers between devices: none -> 32.2 us  [send(): lax.ppermute(value, axes, [(r * n_col + c, to(r, c)) for r, c in flat])]
    psum x2 -> x0, blocking collectives: 31.6 us -> none  [combined(): return lax.psum(moments_local, 'row')]
    ppermute x0 -> x29, starting transfers between devices: none -> 29.1 us  [send(): lax.ppermute(value, axes, [(r * n_col + c, to(r, c)) for r, c in flat])]
    unnamed x1 -> x0, blocking collectives: 27.3 us -> none
    psum x2 -> x0, waiting for transfers between devices: 24.1 us -> none  [on_device(): transposed = lax.psum(partial_value, 'col')]
  transfers between devices with their start and end apart: 4 -> 29, of which waited for: 1 -> 23; matrix products, arithmetic and copies ran while one was open for 17% -> 0% of each run, Pallas kernels for 0% -> 0%
where the time goes in v1:
time: 136 us; the launch traced here: 135 us
  Pallas kernels  48.9 us (36%)
  waiting for transfers between devices  32.2 us (24%)
  starting transfers between devices  29.1 us (21%)
  local copies, waits for them, and re-layouts  23 us (17%)
    pallas_call x2, Pallas kernels, products(): call(functools.partial(product_kernel, k, n, group, tile), (shape(group,...  42.4 us
    ppermute x29, waiting for transfers between devices, send(): lax.ppermute(value, axes, [(r * n_col + c, to(r, c)) for r, c in flat])  32.2 us
    ppermute x29, starting transfers between devices, send(): lax.ppermute(value, axes, [(r * n_col + c, to(r, c)) for r, c in flat])  29.1 us
    unnamed x52, local copies, waits for them, and re-layouts  23 us
    pallas_call x1, Pallas kernels, on_device(): call(functools.partial(second_kernel, k, n, order), (shape(2 * k, n), sha...  3.18 us
    pallas_call x1, Pallas kernels, on_device(): call(functools.partial(last_kernel, k, n, order, group), (shape(k, n), sh...  2.82 us
  transfers between devices with their start and end apart: 29, of which 23 were waited for; matrix products, arithmetic and copies ran while one was open for 0% of the time, Pallas kernels for 0%

profile of v1, /device:TPU:0, one launch (start us, length us, event | category | flops | bytes accessed | tf_op | source)
XLA Modules:
  0.0 134.9 jit_solution(18223048473505364490)
XLA Ops:
  0.6 0.6 collective-permute-start
  1.2 1.1 collective-permute-done
  2.3 0.8 broadcast_select_fusion.1
  3.1 5.0 %collective-permute-start.3 = (f32[32,576]{1,0:T(8,128)S(1)}, f32[32,576]{1,0:T(8,128)S(1)}, u32[]{:S(2)}, u32[]{:S(2)}) collective-permute-start(f32[32,576]{1,0:T(8,128)S(1)} %pad_maximum_fusion.pair_ref.first_ref), channel_id=1, source_target_pairs={{0,6},{1,25},{2,4},{3,27},{4,2},{5,29},{6,0},{7,31},{8,14},{9,17},... | collective-permute-start | bytes 221192 | tf_op jit(solution)/shard_map/ppermute | solution.py:289
  8.1 0.6 collective-permute-start.1
  8.7 1.9 %collective-permute-done.3.refs_2_ = f32[32,576]{1,0:T(8,128)S(1)} collective-permute-done((f32[32,576]{1,0:T(8,128)S(1)}, f32[32,576]{1,0:T(8,128)S(1)}, u32[]{:S(2)}, u32[]{:S(2)}) %collective-permute-start.3) | collective-permute-done | bytes 73760 | tf_op jit(solution)/shard_map/ppermute | solution.py:289
  10.6 2.8 %collective-permute-done.2.refs_1_ = f32[32,576]{1,0:T(8,128)S(1)} collective-permute-done((f32[32,576]{1,0:T(8,128)S(1)}, f32[32,576]{1,0:T(8,128)S(1)}, u32[]{:S(2)}, u32[]{:S(2)}) %collective-permute-start.2) | collective-permute-done | bytes 73760 | tf_op jit(solution)/shard_map/ppermute | solution.py:289
  13.4 0.5 collective-permute-start.4
  14.0 0.8 collective-permute-done.5.refs_4_
  14.7 0.2 collective-permute-done.4.refs_3_
  14.9 0.4 copy-done.23
  15.3 0.2 copy-done.24
  15.5 13.1 %copy-done = f32[4,576,4608]{2,1,0:T(8,128)S(1)} copy-done((f32[4,576,4608]{2,1,0:T(8,128)S(1)}, f32[4,576,4608]{2,1,0:T(8,128)}, u32[]{:S(2)}) %copy-start) | copy-done | bytes 42467352
  28.6 21.2 %first.1 = (f32[4,32,576]{2,1,0:T(8,128)}, f32[4,32,576]{2,1,0:T(8,128)}) custom-call(f32[2304,4608]{1,0:T(8,128)S(1)} %bitcast.5, f32[32,576]{1,0:T(8,128)} %copy-done.1, f32[32,576]{1,0:T(8,128)} %copy-done.21, f32[32,576]{1,0:T(8,128)} %copy-done.20, f32[32,576]{1,0:T(8,128)} %copy-done.19, f32[32,576]{1,0:T(8,128)} %copy-done.24, f32[32,576]{1,0:T(8,128)} %copy-done.23, ...), custom_call_target="tpu_custom_call" | custom-call | tf_op jit(solution)/shard_map/first/pallas_call | solution.py:310
  49.8 0.4 collective-permute-start.7
  50.1 1.5 %collective-permute-done.7.got_ref = f32[4,32,576]{2,1,0:T(8,128)S(1)} collective-permute-done((f32[4,32,576]{2,1,0:T(8,128)}, f32[4,32,576]{2,1,0:T(8,128)S(1)}, u32[]{:S(2)}, u32[]{:S(2)}) %collective-permute-start.7) | collective-permute-done | bytes 294944 | tf_op jit(solution)/shard_map/ppermute | solution.py:289
  51.6 0.9 copy-done.2
  52.5 1.0 copy-done.14
  53.5 0.8 collective-permute-start.8
  54.3 1.5 %collective-permute-start.9 = (f32[32,576]{1,0:T(8,128)S(1)}, f32[32,576]{1,0:T(8,128)S(1)}, u32[]{:S(2)}, u32[]{:S(2)}) collective-permute-start(f32[32,576]{1,0:T(8,128)S(1)} %get-tuple-element.27), channel_id=1, source_target_pairs={{0,4},{1,17},{2,6},{3,19},{4,0},{5,21},{6,2},{7,23},{8,12},{9,25},... | collective-permute-start | bytes 221192 | tf_op jit(solution)/shard_map/ppermute | solution.py:289
  55.8 2.2 %collective-permute-start.10 = (f32[32,576]{1,0:T(8,128)S(1)}, f32[32,576]{1,0:T(8,128)S(1)}, u32[]{:S(2)}, u32[]{:S(2)}) collective-permute-start(f32[32,576]{1,0:T(8,128)S(1)} %get-tuple-element.28), channel_id=1, source_target_pairs={{0,6},{1,25},{2,4},{3,27},{4,2},{5,29},{6,0},{7,31},{8,14},{9,17},... | collective-permute-start | bytes 221192 | tf_op jit(solution)/shard_map/ppermute | solution.py:289
  58.0 2.5 %collective-permute-done.9 = f32[32,576]{1,0:T(8,128)S(1)} collective-permute-done((f32[32,576]{1,0:T(8,128)S(1)}, f32[32,576]{1,0:T(8,128)S(1)}, u32[]{:S(2)}, u32[]{:S(2)}) %collective-permute-start.9) | collective-permute-done | bytes 73760 | tf_op jit(solution)/shard_map/ppermute | solution.py:289
  60.5 1.7 %collective-permute-done.10 = f32[32,576]{1,0:T(8,128)S(1)} collective-permute-done((f32[32,576]{1,0:T(8,128)S(1)}, f32[32,576]{1,0:T(8,128)S(1)}, u32[]{:S(2)}, u32[]{:S(2)}) %collective-permute-start.10) | collective-permute-done | bytes 73760 | tf_op jit(solution)/shard_map/ppermute | solution.py:289
  62.2 0.1 collective-permute-start.11
  62.3 1.3 collective-permute-done.11.got_ref
  63.5 0.9 copy-done.3
  64.4 0.4 pair.1.pair_ref
  64.8 2.2 %collective-permute-start.14 = (f32[40,576]{1,0:T(8,128)S(1)}, f32[40,576]{1,0:T(8,128)S(1)}, u32[]{:S(2)}, u32[]{:S(2)}) collective-permute-start(f32[40,576]{1,0:T(8,128)S(1)} %pair.1.pair_ref), channel_id=1, source_target_pairs={{0,6},{1,25},{2,4},{3,27},{4,2},{5,29},{6,0},{7,31},{8,14},{9,17},... | collective-permute-start | bytes 276488 | tf_op jit(solution)/shard_map/ppermute | solution.py:289
  66.9 2.2 %collective-permute-start.12 = (f32[40,576]{1,0:T(8,128)S(1)}, f32[40,576]{1,0:T(8,128)S(1)}, u32[]{:S(2)}, u32[]{:S(2)}) collective-permute-start(f32[40,576]{1,0:T(8,128)S(1)} %pair.1.pair_ref), channel_id=1, source_target_pairs={{0,2},{1,9},{2,0},{3,11},{4,6},{5,13},{6,4},{7,15},{8,10},{9,1},{1... | collective-permute-start | bytes 276488 | tf_op jit(solution)/shard_map/ppermute | solution.py:289
  69.2 2.1 %collective-permute-done.14.refs_2_ = f32[40,576]{1,0:T(8,128)S(1)} collective-permute-done((f32[40,576]{1,0:T(8,128)S(1)}, f32[40,576]{1,0:T(8,128)S(1)}, u32[]{:S(2)}, u32[]{:S(2)}) %collective-permute-start.14) | collective-permute-done | bytes 92192 | tf_op jit(solution)/shard_map/ppermute | solution.py:289
  71.3 2.1 %collective-permute-done.13.refs_1_ = f32[40,576]{1,0:T(8,128)S(1)} collective-permute-done((f32[40,576]{1,0:T(8,128)S(1)}, f32[40,576]{1,0:T(8,128)S(1)}, u32[]{:S(2)}, u32[]{:S(2)}) %collective-permute-start.13) | collective-permute-done | bytes 92192 | tf_op jit(solution)/shard_map/ppermute | solution.py:289
  73.5 0.5 collective-permute-start.15
  74.0 0.8 collective-permute-done.16.refs_4_.refs_1_
  74.8 0.2 collective-permute-done.15.refs_3_.refs_0_
  74.9 0.5 copy-done.10
  75.4 0.6 copy-done.12
  76.0 21.3 %second.1 = (f32[4,32,576]{2,1,0:T(8,128)}, f32[4,32,576]{2,1,0:T(8,128)}) custom-call(f32[2304,4608]{1,0:T(8,128)S(1)} %bitcast.6, f32[40,576]{1,0:T(8,128)} %copy-done.5, f32[40,576]{1,0:T(8,128)} %copy-done.18, f32[40,576]{1,0:T(8,128)} %copy-done.17, f32[40,576]{1,0:T(8,128)} %copy-done.16, f32[40,576]{1,0:T(8,128)} %copy-done.12, f32[40,576]{1,0:T(8,128)} %copy-done.10, ...), custom_call_target="tpu_custom_call" | custom-call | tf_op jit(solution)/shard_map/second/pallas_call | solution.py:310
  97.3 0.1 collective-permute-start.18
  97.5 1.7 %collective-permute-done.18.got_ref = f32[4,32,576]{2,1,0:T(8,128)S(1)} collective-permute-done((f32[4,32,576]{2,1,0:T(8,128)}, f32[4,32,576]{2,1,0:T(8,128)S(1)}, u32[]{:S(2)}, u32[]{:S(2)}) %collective-permute-start.18) | collective-permute-done | bytes 294944 | tf_op jit(solution)/shard_map/ppermute | solution.py:289
  99.2 0.9 copy-done.6
  100.1 0.9 copy-done.9
  101.0 0.9 copy-done.11
  101.9 0.9 copy-done.13
  102.7 1.0 copy-done.15
  103.8 0.1 collective-permute-start.19
  103.9 2.7 %collective-permute-start.20 = (f32[40,576]{1,0:T(8,128)S(1)}, f32[40,576]{1,0:T(8,128)S(1)}, u32[]{:S(2)}, u32[]{:S(2)}) collective-permute-start(f32[40,576]{1,0:T(8,128)S(1)} %get-tuple-element.33), channel_id=1, source_target_pairs={{0,4},{1,17},{2,6},{3,19},{4,0},{5,21},{6,2},{7,23},{8,12},{9,25},... | collective-permute-start | bytes 276488 | tf_op jit(solution)/shard_map/ppermute | solution.py:289
  106.6 1.7 %collective-permute-start.21 = (f32[40,576]{1,0:T(8,128)S(1)}, f32[40,576]{1,0:T(8,128)S(1)}, u32[]{:S(2)}, u32[]{:S(2)}) collective-permute-start(f32[40,576]{1,0:T(8,128)S(1)} %get-tuple-element.34), channel_id=1, source_target_pairs={{0,6},{1,25},{2,4},{3,27},{4,2},{5,29},{6,0},{7,31},{8,14},{9,17},... | collective-permute-start | bytes 276488 | tf_op jit(solution)/shard_map/ppermute | solution.py:289
  108.2 1.4 %collective-permute-done.19 = f32[40,576]{1,0:T(8,128)S(1)} collective-permute-done((f32[40,576]{1,0:T(8,128)S(1)}, f32[40,576]{1,0:T(8,128)S(1)}, u32[]{:S(2)}, u32[]{:S(2)}) %collective-permute-start.19) | collective-permute-done | bytes 92192 | tf_op jit(solution)/shard_map/ppermute | solution.py:289
  109.6 3.4 %collective-permute-done.21 = f32[40,576]{1,0:T(8,128)S(1)} collective-permute-done((f32[40,576]{1,0:T(8,128)S(1)}, f32[40,576]{1,0:T(8,128)S(1)}, u32[]{:S(2)}, u32[]{:S(2)}) %collective-permute-start.21) | collective-permute-done | bytes 92192 | tf_op jit(solution)/shard_map/ppermute | solution.py:289
  113.1 0.1 collective-permute-start.22
  113.1 1.3 collective-permute-done.22.got_ref
  114.4 0.9 copy-done.7
  115.3 3.2 %middle.1 = (f32[32,576]{1,0:T(8,128)S(1)}, f32[32,576]{1,0:T(8,128)S(1)}, f32[48,48]{1,0:T(8,128)S(1)}, f32[16,16]{1,0:T(8,128)S(1)}, f32[16,16]{1,0:T(8,128)S(1)}) custom-call(f32[32,576]{1,0:T(8,128)S(1)} %copy-done.4, f32[40,576]{1,0:T(8,128)S(1)} %copy-done.7, f32[40,576]{1,0:T(8,128)S(1)} %add_add_fusion.mine_ref, ...), custom_call_target="tpu_custom_call" | custom-call | tf_op jit(solution)/shard_map/middle/pallas_call | solution.py:341
  118.5 2.5 %collective-permute-start.25 = (f32[48,48]{1,0:T(8,128)S(1)}, f32[48,48]{1,0:T(8,128)S(1)}, u32[]{:S(2)}, u32[]{:S(2)}) collective-permute-start(f32[48,48]{1,0:T(8,128)S(1)} %get-tuple-element.39), channel_id=1, source_target_pairs={{0,24},{1,25},{2,26},{3,27},{4,28},{5,29},{6,30},{7,31},{8,16},{9,... | collective-permute-start | bytes 27656 | tf_op jit(solution)/shard_map/ppermute | solution.py:289
  121.0 0.5 collective-permute-start.24
  121.5 0.5 collective-permute-start.23
  122.1 1.2 collective-permute-done.25
  123.3 1.6 %collective-permute-done.24 = f32[48,48]{1,0:T(8,128)S(1)} collective-permute-done((f32[48,48]{1,0:T(8,128)S(1)}, f32[48,48]{1,0:T(8,128)S(1)}, u32[]{:S(2)}, u32[]{:S(2)}) %collective-permute-start.24) | collective-permute-done | bytes 9248 | tf_op jit(solution)/shard_map/ppermute | solution.py:289
  124.9 0.5 collective-permute-done.23
  125.4 2.0 %collective-permute-start.28 = (f32[48,48]{1,0:T(8,128)S(1)}, f32[48,48]{1,0:T(8,128)S(1)}, u32[]{:S(2)}, u32[]{:S(2)}) collective-permute-start(f32[48,48]{1,0:T(8,128)S(1)} %add_add_fusion.2.refs_0_), channel_id=1, source_target_pairs={{0,6},{1,7},{2,4},{3,5},{4,2},{5,3},{6,0},{7,1},{8,14},{9,15},{10,... | collective-permute-start | bytes 27656 | tf_op jit(solution)/shard_map/ppermute | solution.py:289
  127.4 2.4 %collective-permute-start.26 = (f32[48,48]{1,0:T(8,128)S(1)}, f32[48,48]{1,0:T(8,128)S(1)}, u32[]{:S(2)}, u32[]{:S(2)}) collective-permute-start(f32[48,48]{1,0:T(8,128)S(1)} %add_add_fusion.2.refs_0_), channel_id=1, source_target_pairs={{0,2},{1,3},{2,0},{3,1},{4,6},{5,7},{6,4},{7,5},{8,10},{9,11},{10,... | collective-permute-start | bytes 27656 | tf_op jit(solution)/shard_map/ppermute | solution.py:289
  129.8 1.2 collective-permute-done.28.refs_3_
  131.1 1.1 collective-permute-done.27.refs_2_
  132.1 2.8 %last.1 = (f32[16,576]{1,0:T(8,128)}, f32[2,16,16]{2,1,0:T(8,128)}, f32[2,16,16]{2,1,0:T(8,128)}) custom-call(f32[32,576]{1,0:T(8,128)S(1)} %copy-done.4, f32[32,576]{1,0:T(8,128)S(1)} %get-tuple-element.35.q_ref, f32[32,576]{1,0:T(8,128)S(1)} %get-tuple-element.36.prod_ref, f32[16,16]{1,0:T(8,128)S(1)} %get-tuple-element.37.proj0_ref, ...), custom_call_target="tpu_custom_call" | custom-call | tf_op jit(solution)/shard_map/last/pallas_call | solution.py:350
  (59 shorter events, 0.4 us)
Async XLA Ops:
  0.6 49.5 %copy-start.25 = (f32[576]{0:T(1024)S(1)}, f32[576]{0:T(1024)}, u32[]{:S(2)}) copy-start(f32[576]{0:T(1024)} %param.4) | copy-start | bytes 6916
  0.6 1.6 %collective-permute-start = (f32[16,576]{1,0:T(8,128)}, f32[16,576]{1,0:T(8,128)S(1)}, u32[]{:S(2)}, u32[]{:S(2)}) collective-permute-start(f32[16,576]{1,0:T(8,128)} %bitcast.7), channel_id=1, source_target_pairs={{0,1},{1,0},{2,3},{3,2},{4,5},{5,4},{6,7},{7,6},{8,9},{9,8},{10,11... | collective-permute-start | bytes 110600 | tf_op jit(solution)/shard_map/ppermute | solution.py:289
  3.1 11.8 %copy-start.1 = (f32[32,576]{1,0:T(8,128)}, f32[32,576]{1,0:T(8,128)S(1)}, u32[]{:S(2)}) copy-start(f32[32,576]{1,0:T(8,128)S(1)} %pad_maximum_fusion.pair_ref.first_ref) | copy-start | bytes 221188
  3.1 7.5 %collective-permute-start.3 = (f32[32,576]{1,0:T(8,128)S(1)}, f32[32,576]{1,0:T(8,128)S(1)}, u32[]{:S(2)}, u32[]{:S(2)}) collective-permute-start(f32[32,576]{1,0:T(8,128)S(1)} %pad_maximum_fusion.pair_ref.first_ref), channel_id=1, source_target_pairs={{0,6},{1,25},{2,4},{3,27},{4,2},{5,29},{6,0},{7,31},{8,14},{9,17},... | collective-permute-start | bytes 221192 | tf_op jit(solution)/shard_map/ppermute | solution.py:289
  8.1 5.3 %collective-permute-start.2 = (f32[32,576]{1,0:T(8,128)S(1)}, f32[32,576]{1,0:T(8,128)S(1)}, u32[]{:S(2)}, u32[]{:S(2)}) collective-permute-start(f32[32,576]{1,0:T(8,128)S(1)} %pad_maximum_fusion.pair_ref.first_ref), channel_id=1, source_target_pairs={{0,4},{1,17},{2,6},{3,19},{4,0},{5,21},{6,2},{7,23},{8,12},{9,25},... | collective-permute-start | bytes 221192 | tf_op jit(solution)/shard_map/ppermute | solution.py:289
  8.1 5.3 %collective-permute-start.1 = (f32[32,576]{1,0:T(8,128)S(1)}, f32[32,576]{1,0:T(8,128)S(1)}, u32[]{:S(2)}, u32[]{:S(2)}) collective-permute-start(f32[32,576]{1,0:T(8,128)S(1)} %pad_maximum_fusion.pair_ref.first_ref), channel_id=1, source_target_pairs={{0,2},{1,9},{2,0},{3,11},{4,6},{5,13},{6,4},{7,15},{8,10},{9,1},{1... | collective-permute-start | bytes 221192 | tf_op jit(solution)/shard_map/ppermute | solution.py:289
  10.6 4.3 %copy-start.19 = (f32[32,576]{1,0:T(8,128)}, f32[32,576]{1,0:T(8,128)S(1)}, u32[]{:S(2)}) copy-start(f32[32,576]{1,0:T(8,128)S(1)} %collective-permute-done.3.refs_2_) | copy-start | bytes 221188
  10.6 3.3 %collective-permute-start.6 = (f32[32,576]{1,0:T(8,128)S(1)}, f32[32,576]{1,0:T(8,128)S(1)}, u32[]{:S(2)}, u32[]{:S(2)}) collective-permute-start(f32[32,576]{1,0:T(8,128)S(1)} %collective-permute-done.3.refs_2_), channel_id=1, source_target_pairs={{0,1},{1,0},{2,3},{3,2},{4,5},{5,4},{6,7},{7,6},{8,9},{9,8},{10,11... | collective-permute-start | bytes 221192 | tf_op jit(solution)/shard_map/ppermute | solution.py:289
  13.4 1.5 %copy-start.20 = (f32[32,576]{1,0:T(8,128)}, f32[32,576]{1,0:T(8,128)S(1)}, u32[]{:S(2)}) copy-start(f32[32,576]{1,0:T(8,128)S(1)} %collective-permute-done.2.refs_1_) | copy-start | bytes 221188
  13.4 1.3 collective-permute-start.5
  13.4 1.4 %copy-start.21 = (f32[32,576]{1,0:T(8,128)}, f32[32,576]{1,0:T(8,128)S(1)}, u32[]{:S(2)}) copy-start(f32[32,576]{1,0:T(8,128)S(1)} %collective-permute-done.1.refs_0_) | copy-start | bytes 221188
  13.4 1.4 %collective-permute-start.4 = (f32[32,576]{1,0:T(8,128)S(1)}, f32[32,576]{1,0:T(8,128)S(1)}, u32[]{:S(2)}, u32[]{:S(2)}) collective-permute-start(f32[32,576]{1,0:T(8,128)S(1)} %collective-permute-done.1.refs_0_), channel_id=1, source_target_pairs={{0,1},{1,0},{2,3},{3,2},{4,5},{5,4},{6,7},{7,6},{8,9},{9,8},{10,11... | collective-permute-start | bytes 221192 | tf_op jit(solution)/shard_map/ppermute | solution.py:289
  13.9 0.9 copy-start.22
  14.7 0.6 copy-start.23
  14.9 0.6 copy-start.24
  15.5 13.1 %copy-start = (f32[4,576,4608]{2,1,0:T(8,128)S(1)}, f32[4,576,4608]{2,1,0:T(8,128)}, u32[]{:S(2)}) copy-start(f32[4,576,4608]{2,1,0:T(8,128)} %param.3) | copy-start | bytes 127401984
  49.8 1.8 %collective-permute-start.7 = (f32[4,32,576]{2,1,0:T(8,128)}, f32[4,32,576]{2,1,0:T(8,128)S(1)}, u32[]{:S(2)}, u32[]{:S(2)}) collective-permute-start(f32[4,32,576]{2,1,0:T(8,128)} %get-tuple-element.24), channel_id=1, source_target_pairs={{0,1},{1,0},{2,3},{3,2},{4,5},{5,4},{6,7},{7,6},{8,9},{9,8},{10,11... | collective-permute-start | bytes 884744 | tf_op jit(solution)/shard_map/ppermute | solution.py:289
  51.6 0.9 copy-start.2
  52.5 1.0 copy-start.14
  53.5 61.0 %copy-start.4 = (f32[32,576]{1,0:T(8,128)S(1)}, f32[32,576]{1,0:T(8,128)}, u32[]{:S(2)}) copy-start(f32[32,576]{1,0:T(8,128)} %copy-done.1) | copy-start | bytes 221188
  53.5 4.5 %collective-permute-start.8 = (f32[32,576]{1,0:T(8,128)S(1)}, f32[32,576]{1,0:T(8,128)S(1)}, u32[]{:S(2)}, u32[]{:S(2)}) collective-permute-start(f32[32,576]{1,0:T(8,128)S(1)} %get-tuple-element.26), channel_id=1, source_target_pairs={{0,2},{1,9},{2,0},{3,11},{4,6},{5,13},{6,4},{7,15},{8,10},{9,1},{1... | collective-permute-start | bytes 221192 | tf_op jit(solution)/shard_map/ppermute | solution.py:289
  54.3 6.2 %collective-permute-start.9 = (f32[32,576]{1,0:T(8,128)S(1)}, f32[32,576]{1,0:T(8,128)S(1)}, u32[]{:S(2)}, u32[]{:S(2)}) collective-permute-start(f32[32,576]{1,0:T(8,128)S(1)} %get-tuple-element.27), channel_id=1, source_target_pairs={{0,4},{1,17},{2,6},{3,19},{4,0},{5,21},{6,2},{7,23},{8,12},{9,25},... | collective-permute-start | bytes 221192 | tf_op jit(solution)/shard_map/ppermute | solution.py:289
  55.8 6.3 %collective-permute-start.10 = (f32[32,576]{1,0:T(8,128)S(1)}, f32[32,576]{1,0:T(8,128)S(1)}, u32[]{:S(2)}, u32[]{:S(2)}) collective-permute-start(f32[32,576]{1,0:T(8,128)S(1)} %get-tuple-element.28), channel_id=1, source_target_pairs={{0,6},{1,25},{2,4},{3,27},{4,2},{5,29},{6,0},{7,31},{8,14},{9,17},... | collective-permute-start | bytes 221192 | tf_op jit(solution)/shard_map/ppermute | solution.py:289
  62.2 1.3 collective-permute-start.11
  63.5 0.9 copy-start.3
  64.8 10.1 %copy-start.5 = (f32[40,576]{1,0:T(8,128)}, f32[40,576]{1,0:T(8,128)S(1)}, u32[]{:S(2)}) copy-start(f32[40,576]{1,0:T(8,128)S(1)} %pair.1.pair_ref) | copy-start | bytes 276484
  64.8 6.5 %collective-permute-start.14 = (f32[40,576]{1,0:T(8,128)S(1)}, f32[40,576]{1,0:T(8,128)S(1)}, u32[]{:S(2)}, u32[]{:S(2)}) collective-permute-start(f32[40,576]{1,0:T(8,128)S(1)} %pair.1.pair_ref), channel_id=1, source_target_pairs={{0,6},{1,25},{2,4},{3,27},{4,2},{5,29},{6,0},{7,31},{8,14},{9,17},... | collective-permute-start | bytes 276488 | tf_op jit(solution)/shard_map/ppermute | solution.py:289
  66.9 6.5 %collective-permute-start.13 = (f32[40,576]{1,0:T(8,128)S(1)}, f32[40,576]{1,0:T(8,128)S(1)}, u32[]{:S(2)}, u32[]{:S(2)}) collective-permute-start(f32[40,576]{1,0:T(8,128)S(1)} %pair.1.pair_ref), channel_id=1, source_target_pairs={{0,4},{1,17},{2,6},{3,19},{4,0},{5,21},{6,2},{7,23},{8,12},{9,25},... | collective-permute-start | bytes 276488 | tf_op jit(solution)/shard_map/ppermute | solution.py:289
  66.9 6.5 %collective-permute-start.12 = (f32[40,576]{1,0:T(8,128)S(1)}, f32[40,576]{1,0:T(8,128)S(1)}, u32[]{:S(2)}, u32[]{:S(2)}) collective-permute-start(f32[40,576]{1,0:T(8,128)S(1)} %pair.1.pair_ref), channel_id=1, source_target_pairs={{0,2},{1,9},{2,0},{3,11},{4,6},{5,13},{6,4},{7,15},{8,10},{9,1},{1... | collective-permute-start | bytes 276488 | tf_op jit(solution)/shard_map/ppermute | solution.py:289
  71.3 3.6 %copy-start.16 = (f32[40,576]{1,0:T(8,128)}, f32[40,576]{1,0:T(8,128)S(1)}, u32[]{:S(2)}) copy-start(f32[40,576]{1,0:T(8,128)S(1)} %collective-permute-done.14.refs_2_) | copy-start | bytes 276484
  71.3 2.7 %collective-permute-start.17 = (f32[40,576]{1,0:T(8,128)S(1)}, f32[40,576]{1,0:T(8,128)S(1)}, u32[]{:S(2)}, u32[]{:S(2)}) collective-permute-start(f32[40,576]{1,0:T(8,128)S(1)} %collective-permute-done.14.refs_2_), channel_id=1, source_target_pairs={{0,1},{1,0},{2,3},{3,2},{4,5},{5,4},{6,7},{7,6},{8,9},{9,8},{10,11... | collective-permute-start | bytes 276488 | tf_op jit(solution)/shard_map/ppermute | solution.py:289
  73.4 1.5 %copy-start.17 = (f32[40,576]{1,0:T(8,128)}, f32[40,576]{1,0:T(8,128)S(1)}, u32[]{:S(2)}) copy-start(f32[40,576]{1,0:T(8,128)S(1)} %collective-permute-done.13.refs_1_) | copy-start | bytes 276484
  73.4 1.3 collective-permute-start.16
  73.5 1.5 %copy-start.18 = (f32[40,576]{1,0:T(8,128)}, f32[40,576]{1,0:T(8,128)S(1)}, u32[]{:S(2)}) copy-start(f32[40,576]{1,0:T(8,128)S(1)} %collective-permute-done.12.refs_0_) | copy-start | bytes 276484
  73.5 1.4 %collective-permute-start.15 = (f32[40,576]{1,0:T(8,128)S(1)}, f32[40,576]{1,0:T(8,128)S(1)}, u32[]{:S(2)}, u32[]{:S(2)}) collective-permute-start(f32[40,576]{1,0:T(8,128)S(1)} %collective-permute-done.12.refs_0_), channel_id=1, source_target_pairs={{0,1},{1,0},{2,3},{3,2},{4,5},{5,4},{6,7},{7,6},{8,9},{9,8},{10,11... | collective-permute-start | bytes 276488 | tf_op jit(solution)/shard_map/ppermute | solution.py:289
  74.0 1.0 copy-start.8
  74.8 0.6 copy-start.10
  75.4 0.6 copy-start.12
  97.3 1.8 %collective-permute-start.18 = (f32[4,32,576]{2,1,0:T(8,128)}, f32[4,32,576]{2,1,0:T(8,128)S(1)}, u32[]{:S(2)}, u32[]{:S(2)}) collective-permute-start(f32[4,32,576]{2,1,0:T(8,128)} %get-tuple-element.30), channel_id=1, source_target_pairs={{0,1},{1,0},{2,3},{3,2},{4,5},{5,4},{6,7},{7,6},{8,9},{9,8},{10,11... | collective-permute-start | bytes 884744 | tf_op jit(solution)/shard_map/ppermute | solution.py:289
  99.2 0.9 copy-start.6
  100.1 0.9 copy-start.9
  101.0 0.9 copy-start.11
  101.8 0.9 copy-start.13
  102.7 1.0 copy-start.15
  103.8 5.8 %collective-permute-start.19 = (f32[40,576]{1,0:T(8,128)S(1)}, f32[40,576]{1,0:T(8,128)S(1)}, u32[]{:S(2)}, u32[]{:S(2)}) collective-permute-start(f32[40,576]{1,0:T(8,128)S(1)} %get-tuple-element.32), channel_id=1, source_target_pairs={{0,2},{1,9},{2,0},{3,11},{4,6},{5,13},{6,4},{7,15},{8,10},{9,1},{1... | collective-permute-start | bytes 276488 | tf_op jit(solution)/shard_map/ppermute | solution.py:289
  103.9 5.7 %collective-permute-start.20 = (f32[40,576]{1,0:T(8,128)S(1)}, f32[40,576]{1,0:T(8,128)S(1)}, u32[]{:S(2)}, u32[]{:S(2)}) collective-permute-start(f32[40,576]{1,0:T(8,128)S(1)} %get-tuple-element.33), channel_id=1, source_target_pairs={{0,4},{1,17},{2,6},{3,19},{4,0},{5,21},{6,2},{7,23},{8,12},{9,25},... | collective-permute-start | bytes 276488 | tf_op jit(solution)/shard_map/ppermute | solution.py:289
  106.6 6.5 %collective-permute-start.21 = (f32[40,576]{1,0:T(8,128)S(1)}, f32[40,576]{1,0:T(8,128)S(1)}, u32[]{:S(2)}, u32[]{:S(2)}) collective-permute-start(f32[40,576]{1,0:T(8,128)S(1)} %get-tuple-element.34), channel_id=1, source_target_pairs={{0,6},{1,25},{2,4},{3,27},{4,2},{5,29},{6,0},{7,31},{8,14},{9,17},... | collective-permute-start | bytes 276488 | tf_op jit(solution)/shard_map/ppermute | solution.py:289
  113.1 1.4 %collective-permute-start.22 = (f32[40,576]{1,0:T(8,128)S(1)}, f32[40,576]{1,0:T(8,128)S(1)}, u32[]{:S(2)}, u32[]{:S(2)}) collective-permute-start(f32[40,576]{1,0:T(8,128)S(1)} %add_add_fusion.mine_ref), channel_id=1, source_target_pairs={{0,1},{1,0},{2,3},{3,2},{4,5},{5,4},{6,7},{7,6},{8,9},{9,8},{10,11... | collective-permute-start | bytes 276488 | tf_op jit(solution)/shard_map/ppermute | solution.py:289
  114.4 0.9 copy-start.7
  118.5 4.8 %collective-permute-start.25 = (f32[48,48]{1,0:T(8,128)S(1)}, f32[48,48]{1,0:T(8,128)S(1)}, u32[]{:S(2)}, u32[]{:S(2)}) collective-permute-start(f32[48,48]{1,0:T(8,128)S(1)} %get-tuple-element.39), channel_id=1, source_target_pairs={{0,24},{1,25},{2,26},{3,27},{4,28},{5,29},{6,30},{7,31},{8,16},{9,... | collective-permute-start | bytes 27656 | tf_op jit(solution)/shard_map/ppermute | solution.py:289
  121.0 3.8 %collective-permute-start.24 = (f32[48,48]{1,0:T(8,128)S(1)}, f32[48,48]{1,0:T(8,128)S(1)}, u32[]{:S(2)}, u32[]{:S(2)}) collective-permute-start(f32[48,48]{1,0:T(8,128)S(1)} %get-tuple-element.39), channel_id=1, source_target_pairs={{0,16},{1,17},{2,18},{3,19},{4,20},{5,21},{6,22},{7,23},{8,24},{9,... | collective-permute-start | bytes 27656 | tf_op jit(solution)/shard_map/ppermute | solution.py:289
  121.5 3.8 %collective-permute-start.23 = (f32[48,48]{1,0:T(8,128)S(1)}, f32[48,48]{1,0:T(8,128)S(1)}, u32[]{:S(2)}, u32[]{:S(2)}) collective-permute-start(f32[48,48]{1,0:T(8,128)S(1)} %get-tuple-element.39), channel_id=1, source_target_pairs={{0,8},{1,9},{2,10},{3,11},{4,12},{5,13},{6,14},{7,15},{8,0},{9,1},... | collective-permute-start | bytes 27656 | tf_op jit(solution)/shard_map/ppermute | solution.py:289
  125.4 5.7 %collective-permute-start.28 = (f32[48,48]{1,0:T(8,128)S(1)}, f32[48,48]{1,0:T(8,128)S(1)}, u32[]{:S(2)}, u32[]{:S(2)}) collective-permute-start(f32[48,48]{1,0:T(8,128)S(1)} %add_add_fusion.2.refs_0_), channel_id=1, source_target_pairs={{0,6},{1,7},{2,4},{3,5},{4,2},{5,3},{6,0},{7,1},{8,14},{9,15},{10,... | collective-permute-start | bytes 27656 | tf_op jit(solution)/shard_map/ppermute | solution.py:289
  127.4 4.7 %collective-permute-start.27 = (f32[48,48]{1,0:T(8,128)S(1)}, f32[48,48]{1,0:T(8,128)S(1)}, u32[]{:S(2)}, u32[]{:S(2)}) collective-permute-start(f32[48,48]{1,0:T(8,128)S(1)} %add_add_fusion.2.refs_0_), channel_id=1, source_target_pairs={{0,4},{1,5},{2,6},{3,7},{4,0},{5,1},{6,2},{7,3},{8,12},{9,13},{10,... | collective-permute-start | bytes 27656 | tf_op jit(solution)/shard_map/ppermute | solution.py:289
  127.4 4.7 %collective-permute-start.26 = (f32[48,48]{1,0:T(8,128)S(1)}, f32[48,48]{1,0:T(8,128)S(1)}, u32[]{:S(2)}, u32[]{:S(2)}) collective-permute-start(f32[48,48]{1,0:T(8,128)S(1)} %add_add_fusion.2.refs_0_), channel_id=1, source_target_pairs={{0,2},{1,3},{2,0},{3,1},{4,6},{5,7},{6,4},{7,5},{8,10},{9,11},{10,... | collective-permute-start | bytes 27656 | tf_op jit(solution)/shard_map/ppermute | solution.py:289

commit v2 on v1

--- a/solution.py
+++ b/solution.py
@@ -84,10 +84,28 @@
     return lax.dot_general(left, right, dims, preferred_element_type=F32, precision=precise)
 
 
-def product_kernel(k, n, group, tile, a_ref, pair_ref, *refs):
-    mine = refs[: group - 1]
-    theirs = refs[group - 1 : 2 * (group - 1)]
-    send_ref, keep_ref, xg, xr, rows, u_acc, v_acc = refs[2 * (group - 1) :]
+def order_kernel(k, own_ref, other_ref, out_ref):
+    even = place()[0] == 0
+    own, other = own_ref[...], other_ref[...]
+    out_ref[:k, :] = jnp.where(even, own, other)
+    out_ref[k:, :] = jnp.where(even, other, own)
+
+
+def product_kernel(k, n, group, tile, chunk, pieces, load, *refs):
+    sources, refs = refs[: 1 if load else pieces], refs[1 if load else pieces :]
+    pair_ref, mine, theirs = refs[0], refs[1:group], refs[group : 2 * group - 1]
+    send_ref, keep_ref, *refs = refs[2 * group - 1 :]
+    if load:
+        held, (xg, xr, rows, u_acc, v_acc, arrived) = refs[:pieces], refs[pieces:]
+    else:
+        held, (xg, xr, rows, u_acc, v_acc) = sources, refs
+    def fetch(p):
+        at = pl.ds(p * tile, tile)
+        return pltpu.make_async_copy(sources[0].at[at, :], held[p], arrived.at[p])
+
+    if load:
+        for p in range(pieces):
+            fetch(p).start()
     parity, z, r = place()
     even = parity == 0
 
@@ -111,18 +129,23 @@
 
     v_acc[...] = jnp.zeros_like(v_acc)
 
-    def step(t, carry):
-        at = pl.ds(pl.multiple_of(t * tile, tile), tile)
-        high, low = split(a_ref[at, :])
+    def step(piece, at, c, total):
+        cols = pl.ds(pl.multiple_of(c * chunk, chunk), chunk)
+        high, low = split(held[piece][:, cols])
         p = dot(xr[:, at], high, NN)
         q = dot(xr[:k, at], low, NN)
-        v_acc[...] += p[:k] + p[k:] + q
-        p = dot(xg[...], high, NT)
-        q = dot(xg[:k, :], low, NT)
-        u_acc[:, at] = p[:k] + p[k:] + q
-        return carry
-
-    lax.fori_loop(0, a_ref.shape[0] // tile, step, 0)
+        v_acc[:, cols] += p[:k] + p[k:] + q
+        p = dot(xg[:, cols], high, NT)
+        q = dot(xg[:k, cols], low, NT)
+        return total + p[:k] + p[k:] + q
+
+    for piece in range(pieces):
+        if load:
+            fetch(piece).wait()
+        at = slice(piece * tile, (piece + 1) * tile)
+        u_acc[:, at] = lax.fori_loop(
+            0, held[piece].shape[1] // chunk, functools.partial(step, piece, at), jnp.zeros((k, tile), F32)
+        )
 
     def by_z(out):
         for g in range(group):
@@ -153,7 +176,7 @@
 
 def combine_kernel(k, n, group, extra, keep_ref, got_ref, pair_ref, energy_ref, *refs):
     theirs = refs[: group - 1] if extra else ()
-    outs = refs[len(theirs) :]
+    outs = refs[len(refs) - group :]
     parity, z, r = place()
     even = parity == 0
     at = jnp.where(even, z, r)
@@ -259,17 +282,22 @@
     basis_ref[...] = dot32(inverse, rest, NN)
 
 
-def call(kernel, out_shape, n_in, scratch=(), limit=8 << 20, name=None):
+def call(kernel, out_shape, n_in, scratch=(), limit=1 << 20, name=None, load=False):
     many = isinstance(out_shape, (tuple, list))
-    return pl.pallas_call(
+    run = pl.pallas_call(
         kernel,
         out_shape=out_shape,
-        in_specs=[VMEM_SPEC] * n_in,
+        in_specs=[pl.BlockSpec(memory_space=pl.ANY) if load and i == 0 else VMEM_SPEC for i in range(n_in)],
         out_specs=tuple([VMEM_SPEC] * len(out_shape)) if many else VMEM_SPEC,
         scratch_shapes=list(scratch),
         compiler_params=pltpu.CompilerParams(vmem_limit_bytes=limit),
         name=name,
     )
+
+    def keep(i, v):
+        return v if load and i == 0 else pltpu.with_memory_space_constraint(v, pltpu.VMEM)
+
+    return lambda *args: run(*[keep(i, v) for i, v in enumerate(args)])
 
 
 def shape(*dims):
@@ -295,33 +323,35 @@
         return lambda r, c: (r ^ s) * n_col + c if c % 2 else r * n_col + (c ^ (2 * s))
 
     steps = range(1, group)
-    tile = 256 if rows % 256 == 0 else rows
-    a = pltpu.with_memory_space_constraint(coupling.reshape(rows, width), pltpu.VMEM)
+    tile = 256
+    pieces = rows // tile
+    chunk = width // 3
+    a = coupling.reshape(rows, width)
     energy = energies.reshape(1, n)
     own = block.T
     other = swap(own)
-    even = lax.rem(lax.axis_index("col"), 2) == 0
-    first = jnp.concatenate([jnp.where(even, own, other), jnp.where(even, other, own)], axis=0)
-
-    def products(pair, name):
+    first = call(functools.partial(order_kernel, k), shape(2 * k, n), 2, name="order")(own, other)
+
+    def products(a, pair, name, load=False):
         mine = [send(pair, spread(s)) for s in steps]
         theirs = [swap(y) for y in mine]
-        kept, gone = pltpu.VMEM, BF16
-        keep_send = call(
-            functools.partial(product_kernel, k, n, group, tile),
-            (shape(group, 2 * k, n), shape(group, 2 * k, n)),
-            2 + 2 * (group - 1),
+        out, keep, *held = call(
+            functools.partial(product_kernel, k, n, group, tile, chunk, pieces, load),
+            (shape(group, 2 * k, n), shape(group, 2 * k, n))
+            + ((shape(tile, width),) * pieces if load else ()),
+            len(a) + 2 * group - 1,
             scratch=[
                 pltpu.VMEM((2 * k, width), BF16),
                 pltpu.VMEM((2 * k, rows), BF16),
                 pltpu.VMEM((group, k, n), F32),
                 pltpu.VMEM((k, rows), F32),
                 pltpu.VMEM((k, width), F32),
-            ],
-            limit=14 << 20,
+            ]
+            + ([pltpu.SemaphoreType.DMA((pieces,))] if load else []),
+            limit=8 << 20,
             name=name,
-        )(a, pair, *mine, *theirs)
-        out, keep = keep_send
+            load=load,
+        )(*a, pair, *mine, *theirs)
         got = swap(out)
         extra = pair.shape[0] > 2 * k
         parts = call(
@@ -333,19 +363,18 @@
         total = parts[0]
         for s in steps:
             total = total + send(parts[s], spread(s))
-        return total, swap(total)
-
-    mine, got = products(first, "first")
+        return total, swap(total), held
+
+    mine, got, held = products([a], first, "first", load=True)
     pair = call(functools.partial(pair_kernel, k, n), shape(2 * k + 8, n), 3, name="pair")(first, mine, got)
-    mine, got = products(pair, "second")
+    mine, got, _ = products(held, pair, "second")
     q, prod, moments, proj0, fact0 = call(
         functools.partial(second_kernel, k, n, order),
         (shape(2 * k, n), shape(2 * k, n), shape(3 * k, 3 * k), shape(k, k), shape(k, k)),
         4,
         name="middle",
     )(first, pair, mine, got)
-    for s in [None]:
-        moments = sum([send(moments, lambda r, c, s=s: (r ^ s) * n_col + c) for s in steps], moments)
+    moments = sum([send(moments, lambda r, c, s=s: (r ^ s) * n_col + c) for s in steps], moments)
     parts = [moments] + [send(moments, lambda r, c, s=s: r * n_col + (c ^ (2 * s))) for s in steps]
     basis, proj, fact = call(
         functools.partial(last_kernel, k, n, order, group),
@@ -362,7 +391,8 @@
     def body(coupling, energies, block):
         n, k = block.shape
         paired = n_col == 2 * n_row and n_row & (n_row - 1) == 0 and n_row > 1
-        whole = n % 64 == 0 and k % 8 == 0 and 8 * k == 128
+        divides = coupling.shape[0] * n % 256 == 0
+        whole = divides and n % 64 == 0 and 8 * k == 128 and coupling.shape[2] % 384 == 0
         small = coupling.size * 4 <= 44 << 20
         if paired and whole and small:
             return on_device(n_row, n_col, coupling, energies, block)

time: 136 us -> 115 us (0.85)
  local copies, waits for them, and re-layouts: 23 us -> 0.78 us
  Pallas kernels: 48.9 us -> 52.6 us
    unnamed x52 -> x4, local copies, waits for them, and re-layouts: 23 us -> 0.78 us
    pallas_call x7 -> x8, Pallas kernels: 48.9 us -> 52.6 us  [call(): return lambda *args: run(*[keep(i, v) for i, v in enumerate(args)])]
  transfers between devices with their start and end apart: 29 -> 29, of which waited for: 23 -> 24; matrix products, arithmetic and copies ran while one was open for 0% -> 0% of each run, Pallas kernels for 0% -> 0%
where the time goes in v2:
time: 115 us
  Pallas kernels  52.6 us (46%)
  waiting for transfers between devices  31.6 us (27%)
  starting transfers between devices  29.5 us (26%)
    pallas_call x8, Pallas kernels, call(): return lambda *args: run(*[keep(i, v) for i, v in enumerate(args)])  52.6 us
    ppermute x29, waiting for transfers between devices, send(): lax.ppermute(value, axes, [(r * n_col + c, to(r, c)) for r, c in flat])  31.6 us
    ppermute x29, starting transfers between devices, send(): lax.ppermute(value, axes, [(r * n_col + c, to(r, c)) for r, c in flat])  29.5 us
  transfers between devices with their start and end apart: 29, of which 24 were waited for; matrix products, arithmetic and copies ran while one was open for 0% of the time, Pallas kernels for 0%

profile of v2, /device:TPU:0, one launch (start us, length us, event | category | flops | bytes accessed | tf_op | source)
XLA Modules:
  0.0 115.3 jit_solution(8325231088322935024)
XLA Ops:
  0.6 0.6 collective-permute-start
  1.2 1.1 collective-permute-done.other_ref
  2.3 0.8 copy-done
  3.1 5.0 %collective-permute-start.3 = (f32[32,576]{1,0:T(8,128)S(1)}, f32[32,576]{1,0:T(8,128)S(1)}, u32[]{:S(2)}, u32[]{:S(2)}) collective-permute-start(f32[32,576]{1,0:T(8,128)S(1)} %order.1.refs_1_.pair_ref.first_ref), channel_id=1, source_target_pairs={{0,6},{1,25},{2,4},{3,27},{4,2},{5,29},{6,0},{7,31},{8,14},{9,17},... | collective-permute-start | bytes 221192 | tf_op jit(solution)/shard_map/ppermute | solution.py:317
  8.1 0.0 collective-permute-start.2
  8.1 0.6 collective-permute-start.1
  8.7 1.9 %collective-permute-done.3.refs_4_ = f32[32,576]{1,0:T(8,128)S(1)} collective-permute-done((f32[32,576]{1,0:T(8,128)S(1)}, f32[32,576]{1,0:T(8,128)S(1)}, u32[]{:S(2)}, u32[]{:S(2)}) %collective-permute-start.3) | collective-permute-done | bytes 73760 | tf_op jit(solution)/shard_map/ppermute | solution.py:317
  10.6 0.0 collective-permute-start.6
  10.6 2.8 %collective-permute-done.2.refs_3_ = f32[32,576]{1,0:T(8,128)S(1)} collective-permute-done((f32[32,576]{1,0:T(8,128)S(1)}, f32[32,576]{1,0:T(8,128)S(1)}, u32[]{:S(2)}, u32[]{:S(2)}) %collective-permute-start.2) | collective-permute-done | bytes 73760 | tf_op jit(solution)/shard_map/ppermute | solution.py:317
  13.4 0.0 collective-permute-start.5
  13.4 0.0 collective-permute-done.1.refs_2_
  13.4 0.5 collective-permute-start.4
  13.9 0.0 collective-permute-done.6.refs_7_
  13.9 0.8 collective-permute-done.5.refs_6_
  14.7 0.2 collective-permute-done.4.refs_5_
  14.8 24.1 %first.1 = (f32[4,32,576]{2,1,0:T(8,128)S(1)}, f32[4,32,576]{2,1,0:T(8,128)S(1)}, f32[256,4608]{1,0:T(8,128)S(1)}, f32[256,4608]{1,0:T(8,128)S(1)}, f32[256,4608...) custom-call(f32[2304,4608]{1,0:T(8,128)} %bitcast.5, ...), custom_call_target="tpu_custom_call" | custom-call | tf_op jit(solution)/shard_map/first/pallas_call | solution.py:300
  39.0 0.4 collective-permute-start.7
  39.4 1.3 %collective-permute-done.7.got_ref = f32[4,32,576]{2,1,0:T(8,128)S(1)} collective-permute-done((f32[4,32,576]{2,1,0:T(8,128)S(1)}, f32[4,32,576]{2,1,0:T(8,128)S(1)}, u32[]{:S(2)}, u32[]{:S(2)}) %collective-permute-start.7) | collective-permute-done | bytes 294944 | tf_op jit(solution)/shard_map/ppermute | solution.py:317
  40.7 0.8 collective-permute-start.8
  41.5 1.5 %collective-permute-start.9 = (f32[32,576]{1,0:T(8,128)S(1)}, f32[32,576]{1,0:T(8,128)S(1)}, u32[]{:S(2)}, u32[]{:S(2)}) collective-permute-start(f32[32,576]{1,0:T(8,128)S(1)} %get-tuple-element.36), channel_id=1, source_target_pairs={{0,4},{1,17},{2,6},{3,19},{4,0},{5,21},{6,2},{7,23},{8,12},{9,25},... | collective-permute-start | bytes 221192 | tf_op jit(solution)/shard_map/ppermute | solution.py:317
  43.0 2.1 %collective-permute-start.10 = (f32[32,576]{1,0:T(8,128)S(1)}, f32[32,576]{1,0:T(8,128)S(1)}, u32[]{:S(2)}, u32[]{:S(2)}) collective-permute-start(f32[32,576]{1,0:T(8,128)S(1)} %get-tuple-element.37), channel_id=1, source_target_pairs={{0,6},{1,25},{2,4},{3,27},{4,2},{5,29},{6,0},{7,31},{8,14},{9,17},... | collective-permute-start | bytes 221192 | tf_op jit(solution)/shard_map/ppermute | solution.py:317
  45.2 0.1 collective-permute-done.8
  45.2 2.5 %collective-permute-done.9 = f32[32,576]{1,0:T(8,128)S(1)} collective-permute-done((f32[32,576]{1,0:T(8,128)S(1)}, f32[32,576]{1,0:T(8,128)S(1)}, u32[]{:S(2)}, u32[]{:S(2)}) %collective-permute-start.9) | collective-permute-done | bytes 73760 | tf_op jit(solution)/shard_map/ppermute | solution.py:317
  47.7 1.7 %collective-permute-done.10 = f32[32,576]{1,0:T(8,128)S(1)} collective-permute-done((f32[32,576]{1,0:T(8,128)S(1)}, f32[32,576]{1,0:T(8,128)S(1)}, u32[]{:S(2)}, u32[]{:S(2)}) %collective-permute-start.10) | collective-permute-done | bytes 73760 | tf_op jit(solution)/shard_map/ppermute | solution.py:317
  49.4 0.1 collective-permute-start.11
  49.5 1.3 %collective-permute-done.11.got_ref = f32[32,576]{1,0:T(8,128)S(1)} collective-permute-done((f32[32,576]{1,0:T(8,128)S(1)}, f32[32,576]{1,0:T(8,128)S(1)}, u32[]{:S(2)}, u32[]{:S(2)}) %collective-permute-start.11) | collective-permute-done | bytes 73760 | tf_op jit(solution)/shard_map/ppermute | solution.py:317
  50.7 0.4 pair.1.refs_9_.pair_ref
  51.1 2.2 %collective-permute-start.14 = (f32[40,576]{1,0:T(8,128)S(1)}, f32[40,576]{1,0:T(8,128)S(1)}, u32[]{:S(2)}, u32[]{:S(2)}) collective-permute-start(f32[40,576]{1,0:T(8,128)S(1)} %pair.1.refs_9_.pair_ref), channel_id=1, source_target_pairs={{0,6},{1,25},{2,4},{3,27},{4,2},{5,29},{6,0},{7,31},{8,14},{9,17},... | collective-permute-start | bytes 276488 | tf_op jit(solution)/shard_map/ppermute | solution.py:317
  53.2 0.0 collective-permute-start.13
  53.2 2.2 %collective-permute-start.12 = (f32[40,576]{1,0:T(8,128)S(1)}, f32[40,576]{1,0:T(8,128)S(1)}, u32[]{:S(2)}, u32[]{:S(2)}) collective-permute-start(f32[40,576]{1,0:T(8,128)S(1)} %pair.1.refs_9_.pair_ref), channel_id=1, source_target_pairs={{0,2},{1,9},{2,0},{3,11},{4,6},{5,13},{6,4},{7,15},{8,10},{9,1},{1... | collective-permute-start | bytes 276488 | tf_op jit(solution)/shard_map/ppermute | solution.py:317
  55.5 2.1 %collective-permute-done.14.refs_12_ = f32[40,576]{1,0:T(8,128)S(1)} collective-permute-done((f32[40,576]{1,0:T(8,128)S(1)}, f32[40,576]{1,0:T(8,128)S(1)}, u32[]{:S(2)}, u32[]{:S(2)}) %collective-permute-start.14) | collective-permute-done | bytes 92192 | tf_op jit(solution)/shard_map/ppermute | solution.py:317
  57.6 0.0 collective-permute-start.17
  57.6 2.1 %collective-permute-done.13.refs_11_ = f32[40,576]{1,0:T(8,128)S(1)} collective-permute-done((f32[40,576]{1,0:T(8,128)S(1)}, f32[40,576]{1,0:T(8,128)S(1)}, u32[]{:S(2)}, u32[]{:S(2)}) %collective-permute-start.13) | collective-permute-done | bytes 92192 | tf_op jit(solution)/shard_map/ppermute | solution.py:317
  59.8 0.0 collective-permute-start.16
  59.8 0.0 collective-permute-done.12.refs_10_
  59.8 0.5 collective-permute-start.15
  60.3 0.0 collective-permute-done.17.refs_15_.refs_2_
  60.3 0.8 collective-permute-done.16.refs_14_.refs_1_
  61.1 0.2 collective-permute-done.15.refs_13_.refs_0_
  61.2 22.0 %second.1 = (f32[4,32,576]{2,1,0:T(8,128)S(1)}, f32[4,32,576]{2,1,0:T(8,128)S(1)}) custom-call(f32[256,4608]{1,0:T(8,128)S(1)} %get-tuple-element.38.refs_0_, f32[256,4608]{1,0:T(8,128)S(1)} %get-tuple-element.39.refs_1_, f32[256,4608]{1,0:T(8,128)S(1)} %get-tuple-element.40.refs_2_, f32[256,4608]{1,0:T(8,128)S(1)} %get-tuple-element.41.refs_3_, ...), custom_call_target="tpu_custom_call" | custom-call | tf_op jit(solution)/shard_map/second/pallas_call | solution.py:300
  83.2 0.4 collective-permute-start.18
  83.6 1.3 %collective-permute-done.18.got_ref = f32[4,32,576]{2,1,0:T(8,128)S(1)} collective-permute-done((f32[4,32,576]{2,1,0:T(8,128)S(1)}, f32[4,32,576]{2,1,0:T(8,128)S(1)}, u32[]{:S(2)}, u32[]{:S(2)}) %collective-permute-start.18) | collective-permute-done | bytes 294944 | tf_op jit(solution)/shard_map/ppermute | solution.py:317
  85.0 0.3 collective-permute-start.19
  85.3 2.5 %collective-permute-start.20 = (f32[40,576]{1,0:T(8,128)S(1)}, f32[40,576]{1,0:T(8,128)S(1)}, u32[]{:S(2)}, u32[]{:S(2)}) collective-permute-start(f32[40,576]{1,0:T(8,128)S(1)} %get-tuple-element.51), channel_id=1, source_target_pairs={{0,4},{1,17},{2,6},{3,19},{4,0},{5,21},{6,2},{7,23},{8,12},{9,25},... | collective-permute-start | bytes 276488 | tf_op jit(solution)/shard_map/ppermute | solution.py:317
  87.8 1.7 %collective-permute-start.21 = (f32[40,576]{1,0:T(8,128)S(1)}, f32[40,576]{1,0:T(8,128)S(1)}, u32[]{:S(2)}, u32[]{:S(2)}) collective-permute-start(f32[40,576]{1,0:T(8,128)S(1)} %get-tuple-element.52), channel_id=1, source_target_pairs={{0,6},{1,25},{2,4},{3,27},{4,2},{5,29},{6,0},{7,31},{8,14},{9,17},... | collective-permute-start | bytes 276488 | tf_op jit(solution)/shard_map/ppermute | solution.py:317
  89.4 0.3 collective-permute-done.19
  89.7 1.1 collective-permute-done.20
  90.8 3.4 %collective-permute-done.21 = f32[40,576]{1,0:T(8,128)S(1)} collective-permute-done((f32[40,576]{1,0:T(8,128)S(1)}, f32[40,576]{1,0:T(8,128)S(1)}, u32[]{:S(2)}, u32[]{:S(2)}) %collective-permute-start.21) | collective-permute-done | bytes 92192 | tf_op jit(solution)/shard_map/ppermute | solution.py:317
  94.3 0.1 collective-permute-start.22
  94.4 1.3 %collective-permute-done.22.got_ref = f32[40,576]{1,0:T(8,128)S(1)} collective-permute-done((f32[40,576]{1,0:T(8,128)S(1)}, f32[40,576]{1,0:T(8,128)S(1)}, u32[]{:S(2)}, u32[]{:S(2)}) %collective-permute-start.22) | collective-permute-done | bytes 92192 | tf_op jit(solution)/shard_map/ppermute | solution.py:317
  95.7 3.2 %middle.1 = (f32[32,576]{1,0:T(8,128)S(1)}, f32[32,576]{1,0:T(8,128)S(1)}, f32[48,48]{1,0:T(8,128)S(1)}, f32[16,16]{1,0:T(8,128)S(1)}, f32[16,16]{1,0:T(8,128)S(1)}) custom-call(f32[32,576]{1,0:T(8,128)S(1)} %order.1.refs_1_.pair_ref.first_ref, f32[40,576]{1,0:T(8,128)S(1)} %pair.1.refs_9_.pair_ref, f32[40,576]{1,0:T(8,128)S(1)} %add_add_fusion.mine_ref, ...), custom_call_target="tpu_custom_call" | custom-call | tf_op jit(solution)/shard_map/middle/pallas_call | solution.py:300
  98.9 2.6 %collective-permute-start.25 = (f32[48,48]{1,0:T(8,128)S(1)}, f32[48,48]{1,0:T(8,128)S(1)}, u32[]{:S(2)}, u32[]{:S(2)}) collective-permute-start(f32[48,48]{1,0:T(8,128)S(1)} %get-tuple-element.57), channel_id=1, source_target_pairs={{0,24},{1,25},{2,26},{3,27},{4,28},{5,29},{6,30},{7,31},{8,16},{9,... | collective-permute-start | bytes 27656 | tf_op jit(solution)/shard_map/ppermute | solution.py:317
  101.4 0.5 collective-permute-start.24
  101.9 0.5 collective-permute-start.23
  102.4 1.2 %collective-permute-done.25 = f32[48,48]{1,0:T(8,128)S(1)} collective-permute-done((f32[48,48]{1,0:T(8,128)S(1)}, f32[48,48]{1,0:T(8,128)S(1)}, u32[]{:S(2)}, u32[]{:S(2)}) %collective-permute-start.25) | collective-permute-done | bytes 9248 | tf_op jit(solution)/shard_map/ppermute | solution.py:317
  103.6 1.6 %collective-permute-done.24 = f32[48,48]{1,0:T(8,128)S(1)} collective-permute-done((f32[48,48]{1,0:T(8,128)S(1)}, f32[48,48]{1,0:T(8,128)S(1)}, u32[]{:S(2)}, u32[]{:S(2)}) %collective-permute-start.24) | collective-permute-done | bytes 9248 | tf_op jit(solution)/shard_map/ppermute | solution.py:317
  105.2 0.5 collective-permute-done.23
  105.8 1.9 %collective-permute-start.28 = (f32[48,48]{1,0:T(8,128)S(1)}, f32[48,48]{1,0:T(8,128)S(1)}, u32[]{:S(2)}, u32[]{:S(2)}) collective-permute-start(f32[48,48]{1,0:T(8,128)S(1)} %add_add_fusion.2.refs_0_), channel_id=1, source_target_pairs={{0,6},{1,7},{2,4},{3,5},{4,2},{5,3},{6,0},{7,1},{8,14},{9,15},{10,... | collective-permute-start | bytes 27656 | tf_op jit(solution)/shard_map/ppermute | solution.py:317
  107.7 0.2 collective-permute-start.27
  107.9 2.3 %collective-permute-start.26 = (f32[48,48]{1,0:T(8,128)S(1)}, f32[48,48]{1,0:T(8,128)S(1)}, u32[]{:S(2)}, u32[]{:S(2)}) collective-permute-start(f32[48,48]{1,0:T(8,128)S(1)} %add_add_fusion.2.refs_0_), channel_id=1, source_target_pairs={{0,2},{1,3},{2,0},{3,1},{4,6},{5,7},{6,4},{7,5},{8,10},{9,11},{10,... | collective-permute-start | bytes 27656 | tf_op jit(solution)/shard_map/ppermute | solution.py:317
  110.2 1.2 %collective-permute-done.28.refs_3_ = f32[48,48]{1,0:T(8,128)S(1)} collective-permute-done((f32[48,48]{1,0:T(8,128)S(1)}, f32[48,48]{1,0:T(8,128)S(1)}, u32[]{:S(2)}, u32[]{:S(2)}) %collective-permute-start.28) | collective-permute-done | bytes 9248 | tf_op jit(solution)/shard_map/ppermute | solution.py:317
  111.5 1.0 collective-permute-done.27.refs_2_
  112.4 0.0 collective-permute-done.26.refs_1_
  112.4 2.8 %last.1 = (f32[16,576]{1,0:T(8,128)}, f32[2,16,16]{2,1,0:T(8,128)}, f32[2,16,16]{2,1,0:T(8,128)}) custom-call(f32[32,576]{1,0:T(8,128)S(1)} %order.1.refs_1_.pair_ref.first_ref, f32[32,576]{1,0:T(8,128)S(1)} %get-tuple-element.53.q_ref, f32[32,576]{1,0:T(8,128)S(1)} %get-tuple-element.54.prod_ref, f32[16,16]{1,0:T(8,128)S(1)} %get-tuple-element.55.proj0_ref, ...), custom_call_target="tpu_custom_call" | custom-call | tf_op jit(solution)/shard_map/last/pallas_call | solution.py:300
  (10 shorter events, 0.2 us)
Async XLA Ops:
  0.6 1.6 %collective-permute-start = (f32[16,576]{1,0:T(8,128)}, f32[16,576]{1,0:T(8,128)S(1)}, u32[]{:S(2)}, u32[]{:S(2)}) collective-permute-start(f32[16,576]{1,0:T(8,128)} %bitcast.3), channel_id=1, source_target_pairs={{0,1},{1,0},{2,3},{3,2},{4,5},{5,4},{6,7},{7,6},{8,9},{9,8},{10,11... | collective-permute-start | bytes 110600 | tf_op jit(solution)/shard_map/ppermute | solution.py:317
  2.3 0.8 copy-start
  3.1 7.5 %collective-permute-start.3 = (f32[32,576]{1,0:T(8,128)S(1)}, f32[32,576]{1,0:T(8,128)S(1)}, u32[]{:S(2)}, u32[]{:S(2)}) collective-permute-start(f32[32,576]{1,0:T(8,128)S(1)} %order.1.refs_1_.pair_ref.first_ref), channel_id=1, source_target_pairs={{0,6},{1,25},{2,4},{3,27},{4,2},{5,29},{6,0},{7,31},{8,14},{9,17},... | collective-permute-start | bytes 221192 | tf_op jit(solution)/shard_map/ppermute | solution.py:317
  8.1 5.3 %collective-permute-start.2 = (f32[32,576]{1,0:T(8,128)S(1)}, f32[32,576]{1,0:T(8,128)S(1)}, u32[]{:S(2)}, u32[]{:S(2)}) collective-permute-start(f32[32,576]{1,0:T(8,128)S(1)} %order.1.refs_1_.pair_ref.first_ref), channel_id=1, source_target_pairs={{0,4},{1,17},{2,6},{3,19},{4,0},{5,21},{6,2},{7,23},{8,12},{9,25},... | collective-permute-start | bytes 221192 | tf_op jit(solution)/shard_map/ppermute | solution.py:317
  8.1 5.3 %collective-permute-start.1 = (f32[32,576]{1,0:T(8,128)S(1)}, f32[32,576]{1,0:T(8,128)S(1)}, u32[]{:S(2)}, u32[]{:S(2)}) collective-permute-start(f32[32,576]{1,0:T(8,128)S(1)} %order.1.refs_1_.pair_ref.first_ref), channel_id=1, source_target_pairs={{0,2},{1,9},{2,0},{3,11},{4,6},{5,13},{6,4},{7,15},{8,10},{9,1},{1... | collective-permute-start | bytes 221192 | tf_op jit(solution)/shard_map/ppermute | solution.py:317
  10.6 3.3 %collective-permute-start.6 = (f32[32,576]{1,0:T(8,128)S(1)}, f32[32,576]{1,0:T(8,128)S(1)}, u32[]{:S(2)}, u32[]{:S(2)}) collective-permute-start(f32[32,576]{1,0:T(8,128)S(1)} %collective-permute-done.3.refs_4_), channel_id=1, source_target_pairs={{0,1},{1,0},{2,3},{3,2},{4,5},{5,4},{6,7},{7,6},{8,9},{9,8},{10,11... | collective-permute-start | bytes 221192 | tf_op jit(solution)/shard_map/ppermute | solution.py:317
  13.4 1.3 %collective-permute-start.5 = (f32[32,576]{1,0:T(8,128)S(1)}, f32[32,576]{1,0:T(8,128)S(1)}, u32[]{:S(2)}, u32[]{:S(2)}) collective-permute-start(f32[32,576]{1,0:T(8,128)S(1)} %collective-permute-done.2.refs_3_), channel_id=1, source_target_pairs={{0,1},{1,0},{2,3},{3,2},{4,5},{5,4},{6,7},{7,6},{8,9},{9,8},{10,11... | collective-permute-start | bytes 221192 | tf_op jit(solution)/shard_map/ppermute | solution.py:317
  13.4 1.4 %collective-permute-start.4 = (f32[32,576]{1,0:T(8,128)S(1)}, f32[32,576]{1,0:T(8,128)S(1)}, u32[]{:S(2)}, u32[]{:S(2)}) collective-permute-start(f32[32,576]{1,0:T(8,128)S(1)} %collective-permute-done.1.refs_2_), channel_id=1, source_target_pairs={{0,1},{1,0},{2,3},{3,2},{4,5},{5,4},{6,7},{7,6},{8,9},{9,8},{10,11... | collective-permute-start | bytes 221192 | tf_op jit(solution)/shard_map/ppermute | solution.py:317
  14.8 24.6 %copy-start.1 = (f32[576]{0:T(1024)S(1)}, f32[576]{0:T(1024)}, u32[]{:S(2)}) copy-start(f32[576]{0:T(1024)} %param.4) | copy-start | bytes 6916
  39.0 1.7 %collective-permute-start.7 = (f32[4,32,576]{2,1,0:T(8,128)S(1)}, f32[4,32,576]{2,1,0:T(8,128)S(1)}, u32[]{:S(2)}, u32[]{:S(2)}) collective-permute-start(f32[4,32,576]{2,1,0:T(8,128)S(1)} %get-tuple-element.33), channel_id=1, source_target_pairs={{0,1},{1,0},{2,3},{3,2},{4,5},{5,4},{6,7},{7,6},{8,9},{9,8},{10,11... | collective-permute-start | bytes 884744 | tf_op jit(solution)/shard_map/ppermute | solution.py:317
  40.7 4.5 %collective-permute-start.8 = (f32[32,576]{1,0:T(8,128)S(1)}, f32[32,576]{1,0:T(8,128)S(1)}, u32[]{:S(2)}, u32[]{:S(2)}) collective-permute-start(f32[32,576]{1,0:T(8,128)S(1)} %get-tuple-element.35), channel_id=1, source_target_pairs={{0,2},{1,9},{2,0},{3,11},{4,6},{5,13},{6,4},{7,15},{8,10},{9,1},{1... | collective-permute-start | bytes 221192 | tf_op jit(solution)/shard_map/ppermute | solution.py:317
  41.5 6.2 %collective-permute-start.9 = (f32[32,576]{1,0:T(8,128)S(1)}, f32[32,576]{1,0:T(8,128)S(1)}, u32[]{:S(2)}, u32[]{:S(2)}) collective-permute-start(f32[32,576]{1,0:T(8,128)S(1)} %get-tuple-element.36), channel_id=1, source_target_pairs={{0,4},{1,17},{2,6},{3,19},{4,0},{5,21},{6,2},{7,23},{8,12},{9,25},... | collective-permute-start | bytes 221192 | tf_op jit(solution)/shard_map/ppermute | solution.py:317
  43.0 6.3 %collective-permute-start.10 = (f32[32,576]{1,0:T(8,128)S(1)}, f32[32,576]{1,0:T(8,128)S(1)}, u32[]{:S(2)}, u32[]{:S(2)}) collective-permute-start(f32[32,576]{1,0:T(8,128)S(1)} %get-tuple-element.37), channel_id=1, source_target_pairs={{0,6},{1,25},{2,4},{3,27},{4,2},{5,29},{6,0},{7,31},{8,14},{9,17},... | collective-permute-start | bytes 221192 | tf_op jit(solution)/shard_map/ppermute | solution.py:317
  49.4 1.3 %collective-permute-start.11 = (f32[32,576]{1,0:T(8,128)S(1)}, f32[32,576]{1,0:T(8,128)S(1)}, u32[]{:S(2)}, u32[]{:S(2)}) collective-permute-start(f32[32,576]{1,0:T(8,128)S(1)} %add_add_fusion.1.mine_ref), channel_id=1, source_target_pairs={{0,1},{1,0},{2,3},{3,2},{4,5},{5,4},{6,7},{7,6},{8,9},{9,8},{10,11... | collective-permute-start | bytes 221192 | tf_op jit(solution)/shard_map/ppermute | solution.py:317
  51.1 6.5 %collective-permute-start.14 = (f32[40,576]{1,0:T(8,128)S(1)}, f32[40,576]{1,0:T(8,128)S(1)}, u32[]{:S(2)}, u32[]{:S(2)}) collective-permute-start(f32[40,576]{1,0:T(8,128)S(1)} %pair.1.refs_9_.pair_ref), channel_id=1, source_target_pairs={{0,6},{1,25},{2,4},{3,27},{4,2},{5,29},{6,0},{7,31},{8,14},{9,17},... | collective-permute-start | bytes 276488 | tf_op jit(solution)/shard_map/ppermute | solution.py:317
  53.2 6.5 %collective-permute-start.13 = (f32[40,576]{1,0:T(8,128)S(1)}, f32[40,576]{1,0:T(8,128)S(1)}, u32[]{:S(2)}, u32[]{:S(2)}) collective-permute-start(f32[40,576]{1,0:T(8,128)S(1)} %pair.1.refs_9_.pair_ref), channel_id=1, source_target_pairs={{0,4},{1,17},{2,6},{3,19},{4,0},{5,21},{6,2},{7,23},{8,12},{9,25},... | collective-permute-start | bytes 276488 | tf_op jit(solution)/shard_map/ppermute | solution.py:317
  53.2 6.5 %collective-permute-start.12 = (f32[40,576]{1,0:T(8,128)S(1)}, f32[40,576]{1,0:T(8,128)S(1)}, u32[]{:S(2)}, u32[]{:S(2)}) collective-permute-start(f32[40,576]{1,0:T(8,128)S(1)} %pair.1.refs_9_.pair_ref), channel_id=1, source_target_pairs={{0,2},{1,9},{2,0},{3,11},{4,6},{5,13},{6,4},{7,15},{8,10},{9,1},{1... | collective-permute-start | bytes 276488 | tf_op jit(solution)/shard_map/ppermute | solution.py:317
  57.6 2.7 %collective-permute-start.17 = (f32[40,576]{1,0:T(8,128)S(1)}, f32[40,576]{1,0:T(8,128)S(1)}, u32[]{:S(2)}, u32[]{:S(2)}) collective-permute-start(f32[40,576]{1,0:T(8,128)S(1)} %collective-permute-done.14.refs_12_), channel_id=1, source_target_pairs={{0,1},{1,0},{2,3},{3,2},{4,5},{5,4},{6,7},{7,6},{8,9},{9,8},{10,11... | collective-permute-start | bytes 276488 | tf_op jit(solution)/shard_map/ppermute | solution.py:317
  59.8 1.3 %collective-permute-start.16 = (f32[40,576]{1,0:T(8,128)S(1)}, f32[40,576]{1,0:T(8,128)S(1)}, u32[]{:S(2)}, u32[]{:S(2)}) collective-permute-start(f32[40,576]{1,0:T(8,128)S(1)} %collective-permute-done.13.refs_11_), channel_id=1, source_target_pairs={{0,1},{1,0},{2,3},{3,2},{4,5},{5,4},{6,7},{7,6},{8,9},{9,8},{10,11... | collective-permute-start | bytes 276488 | tf_op jit(solution)/shard_map/ppermute | solution.py:317
  59.8 1.5 %collective-permute-start.15 = (f32[40,576]{1,0:T(8,128)S(1)}, f32[40,576]{1,0:T(8,128)S(1)}, u32[]{:S(2)}, u32[]{:S(2)}) collective-permute-start(f32[40,576]{1,0:T(8,128)S(1)} %collective-permute-done.12.refs_10_), channel_id=1, source_target_pairs={{0,1},{1,0},{2,3},{3,2},{4,5},{5,4},{6,7},{7,6},{8,9},{9,8},{10,11... | collective-permute-start | bytes 276488 | tf_op jit(solution)/shard_map/ppermute | solution.py:317
  83.2 1.7 %collective-permute-start.18 = (f32[4,32,576]{2,1,0:T(8,128)S(1)}, f32[4,32,576]{2,1,0:T(8,128)S(1)}, u32[]{:S(2)}, u32[]{:S(2)}) collective-permute-start(f32[4,32,576]{2,1,0:T(8,128)S(1)} %get-tuple-element.48), channel_id=1, source_target_pairs={{0,1},{1,0},{2,3},{3,2},{4,5},{5,4},{6,7},{7,6},{8,9},{9,8},{10,11... | collective-permute-start | bytes 884744 | tf_op jit(solution)/shard_map/ppermute | solution.py:317
  85.0 4.7 %collective-permute-start.19 = (f32[40,576]{1,0:T(8,128)S(1)}, f32[40,576]{1,0:T(8,128)S(1)}, u32[]{:S(2)}, u32[]{:S(2)}) collective-permute-start(f32[40,576]{1,0:T(8,128)S(1)} %get-tuple-element.50), channel_id=1, source_target_pairs={{0,2},{1,9},{2,0},{3,11},{4,6},{5,13},{6,4},{7,15},{8,10},{9,1},{1... | collective-permute-start | bytes 276488 | tf_op jit(solution)/shard_map/ppermute | solution.py:317
  85.3 5.6 %collective-permute-start.20 = (f32[40,576]{1,0:T(8,128)S(1)}, f32[40,576]{1,0:T(8,128)S(1)}, u32[]{:S(2)}, u32[]{:S(2)}) collective-permute-start(f32[40,576]{1,0:T(8,128)S(1)} %get-tuple-element.51), channel_id=1, source_target_pairs={{0,4},{1,17},{2,6},{3,19},{4,0},{5,21},{6,2},{7,23},{8,12},{9,25},... | collective-permute-start | bytes 276488 | tf_op jit(solution)/shard_map/ppermute | solution.py:317
  87.8 6.5 %collective-permute-start.21 = (f32[40,576]{1,0:T(8,128)S(1)}, f32[40,576]{1,0:T(8,128)S(1)}, u32[]{:S(2)}, u32[]{:S(2)}) collective-permute-start(f32[40,576]{1,0:T(8,128)S(1)} %get-tuple-element.52), channel_id=1, source_target_pairs={{0,6},{1,25},{2,4},{3,27},{4,2},{5,29},{6,0},{7,31},{8,14},{9,17},... | collective-permute-start | bytes 276488 | tf_op jit(solution)/shard_map/ppermute | solution.py:317
  94.3 1.4 %collective-permute-start.22 = (f32[40,576]{1,0:T(8,128)S(1)}, f32[40,576]{1,0:T(8,128)S(1)}, u32[]{:S(2)}, u32[]{:S(2)}) collective-permute-start(f32[40,576]{1,0:T(8,128)S(1)} %add_add_fusion.mine_ref), channel_id=1, source_target_pairs={{0,1},{1,0},{2,3},{3,2},{4,5},{5,4},{6,7},{7,6},{8,9},{9,8},{10,11... | collective-permute-start | bytes 276488 | tf_op jit(solution)/shard_map/ppermute | solution.py:317
  98.9 4.8 %collective-permute-start.25 = (f32[48,48]{1,0:T(8,128)S(1)}, f32[48,48]{1,0:T(8,128)S(1)}, u32[]{:S(2)}, u32[]{:S(2)}) collective-permute-start(f32[48,48]{1,0:T(8,128)S(1)} %get-tuple-element.57), channel_id=1, source_target_pairs={{0,24},{1,25},{2,26},{3,27},{4,28},{5,29},{6,30},{7,31},{8,16},{9,... | collective-permute-start | bytes 27656 | tf_op jit(solution)/shard_map/ppermute | solution.py:317
  101.4 3.8 %collective-permute-start.24 = (f32[48,48]{1,0:T(8,128)S(1)}, f32[48,48]{1,0:T(8,128)S(1)}, u32[]{:S(2)}, u32[]{:S(2)}) collective-permute-start(f32[48,48]{1,0:T(8,128)S(1)} %get-tuple-element.57), channel_id=1, source_target_pairs={{0,16},{1,17},{2,18},{3,19},{4,20},{5,21},{6,22},{7,23},{8,24},{9,... | collective-permute-start | bytes 27656 | tf_op jit(solution)/shard_map/ppermute | solution.py:317
  101.9 3.8 %collective-permute-start.23 = (f32[48,48]{1,0:T(8,128)S(1)}, f32[48,48]{1,0:T(8,128)S(1)}, u32[]{:S(2)}, u32[]{:S(2)}) collective-permute-start(f32[48,48]{1,0:T(8,128)S(1)} %get-tuple-element.57), channel_id=1, source_target_pairs={{0,8},{1,9},{2,10},{3,11},{4,12},{5,13},{6,14},{7,15},{8,0},{9,1},... | collective-permute-start | bytes 27656 | tf_op jit(solution)/shard_map/ppermute | solution.py:317
  105.8 5.7 %collective-permute-start.28 = (f32[48,48]{1,0:T(8,128)S(1)}, f32[48,48]{1,0:T(8,128)S(1)}, u32[]{:S(2)}, u32[]{:S(2)}) collective-permute-start(f32[48,48]{1,0:T(8,128)S(1)} %add_add_fusion.2.refs_0_), channel_id=1, source_target_pairs={{0,6},{1,7},{2,4},{3,5},{4,2},{5,3},{6,0},{7,1},{8,14},{9,15},{10,... | collective-permute-start | bytes 27656 | tf_op jit(solution)/shard_map/ppermute | solution.py:317
  107.7 4.7 %collective-permute-start.27 = (f32[48,48]{1,0:T(8,128)S(1)}, f32[48,48]{1,0:T(8,128)S(1)}, u32[]{:S(2)}, u32[]{:S(2)}) collective-permute-start(f32[48,48]{1,0:T(8,128)S(1)} %add_add_fusion.2.refs_0_), channel_id=1, source_target_pairs={{0,4},{1,5},{2,6},{3,7},{4,0},{5,1},{6,2},{7,3},{8,12},{9,13},{10,... | collective-permute-start | bytes 27656 | tf_op jit(solution)/shard_map/ppermute | solution.py:317
  107.9 4.6 %collective-permute-start.26 = (f32[48,48]{1,0:T(8,128)S(1)}, f32[48,48]{1,0:T(8,128)S(1)}, u32[]{:S(2)}, u32[]{:S(2)}) collective-permute-start(f32[48,48]{1,0:T(8,128)S(1)} %add_add_fusion.2.refs_0_), channel_id=1, source_target_pairs={{0,2},{1,3},{2,0},{3,1},{4,6},{5,7},{6,4},{7,5},{8,10},{9,11},{10,... | collective-permute-start | bytes 27656 | tf_op jit(solution)/shard_map/ppermute | solution.py:317

commit v3 on v2

--- a/solution.py
+++ b/solution.py
@@ -91,77 +91,139 @@
     out_ref[k:, :] = jnp.where(even, other, own)
 
 
-def product_kernel(k, n, group, tile, chunk, pieces, load, *refs):
-    sources, refs = refs[: 1 if load else pieces], refs[1 if load else pieces :]
-    pair_ref, mine, theirs = refs[0], refs[1:group], refs[group : 2 * group - 1]
-    send_ref, keep_ref, *refs = refs[2 * group - 1 :]
+def pieces_of(part, group, n, rows):
+    found, at, end = [], part * rows, (part + 1) * rows
+    while at < end:
+        s, off = divmod(at, n)
+        count = min(n - off, end - at)
+        found.append((s, off, at - part * rows, count))
+        at += count
+    return found
+
+
+class Loader:
+    def __init__(self, source, arrived, n, group, parts, r, z):
+        self.source, self.arrived, self.n, self.group, self.parts, self.r, self.z = source, arrived, n, group, parts, r, z
+        self.rows = group * n // parts
+
+    def copies(self, number, part, s, into):
+        cols = pl.ds(pl.multiple_of(lax.bitwise_xor(self.z, s) * (2 * self.n), 128), 2 * self.n)
+        return [
+            pltpu.make_async_copy(
+                self.source.at[pl.ds(pl.multiple_of(lax.bitwise_xor(self.r, peer) * self.n + off, 8), count), cols],
+                into.at[pl.ds(at, count), :],
+                self.arrived.at[number, i],
+            )
+            for i, (peer, off, at, count) in enumerate(pieces_of(part, self.group, self.n, self.rows))
+        ]
+
+    def start(self, *where):
+        for copy in self.copies(*where):
+            copy.start()
+
+    def wait(self, *where):
+        for copy in self.copies(*where):
+            copy.wait()
+
+
+def both_halves(slab, at, k, n, first, second):
+    high, low = split(jnp.concatenate([first, second], axis=1))
+    slab[:k, at * 2 * n : (at + 1) * 2 * n] = high
+    slab[k:, at * 2 * n : (at + 1) * 2 * n] = low
+
+
+def early_kernel(k, n, group, tile, parts, load, *refs):
+    parity, z, r = place()
     if load:
-        held, (xg, xr, rows, u_acc, v_acc, arrived) = refs[:pieces], refs[pieces:]
+        source, pair_ref, u_ref, *held, xg, arrived = refs
+        loader = Loader(source, arrived, n, group, parts, r, z)
+        for p in range(parts):
+            loader.start(p, p, 0, held[p])
     else:
-        held, (xg, xr, rows, u_acc, v_acc) = sources, refs
-    def fetch(p):
-        at = pl.ds(p * tile, tile)
-        return pltpu.make_async_copy(sources[0].at[at, :], held[p], arrived.at[p])
-
-    if load:
-        for p in range(pieces):
-            fetch(p).start()
+        *held, pair_ref, u_ref, xg = refs
+    both_halves(xg, 0, k, n, pair_ref[:k, :], pair_ref[k : 2 * k, :])
+    rows = held[0].shape[0]
+
+    def step(p, t, carry):
+        high, low = split(held[p][pl.ds(pl.multiple_of(t * tile, tile), tile), :])
+        one = dot(xg[...], high, NT)
+        two = dot(xg[:k, :], low, NT)
+        u_ref[:, pl.ds(pl.multiple_of(p * rows + t * tile, tile), tile)] = one[:k] + one[k:] + two
+        return carry
+
+    for p in range(parts):
+        if load:
+            loader.wait(p, p, 0, held[p])
+        lax.fori_loop(0, rows // tile, functools.partial(step, p), 0)
+
+
+def main_kernel(k, n, group, tile, parts, load, *refs):
     parity, z, r = place()
     even = parity == 0
-
-    def put(slab, at, first, second):
-        high, low = split(jnp.concatenate([first, second], axis=1))
-        cols = pl.ds(pl.multiple_of(at * (2 * n), 2 * n), 2 * n)
-        slab[:k, cols] = high
-        slab[k:, cols] = low
-
-    pair = pair_ref[: 2 * k, :]
-    put(xg, z, pair[:k], pair[k:])
-    rows[pl.ds(r, 1)] = jnp.where(even, pair[:k], pair[k:])[None]
+    count = (group - 1) * parts
+    if load:
+        source, refs = refs[0], refs[1:]
+    else:
+        held, refs = refs[:count], refs[count:]
+    pair_ref, u0_ref, mine, theirs = refs[0], refs[1], refs[2 : group + 1], refs[group + 1 : 2 * group]
+    send_ref, keep_ref, own_ref, xr, *refs = refs[2 * group :]
+    if load:
+        held, refs = refs[:count], refs[count:]
+        xg, u_acc, v_acc, arrived = refs
+        loader = Loader(source, arrived, n, group, parts, r, z)
+        for i in range(count):
+            loader.start(i, i % parts, 1 + i // parts, held[i])
+    else:
+        xg, u_acc, v_acc = refs
+    rows = held[0].shape[0]
+
+    segments = [jnp.where(even, pair_ref[:k, :], pair_ref[k : 2 * k, :])]
     for s in range(1, group):
         y, w = mine[s - 1][: 2 * k, :], theirs[s - 1][: 2 * k, :]
         along_z = jnp.where(even, y, w)
         along_row = jnp.where(even, w, y)
-        put(xg, lax.bitwise_xor(z, s), along_z[:k], along_z[k:])
-        rows[pl.ds(lax.bitwise_xor(r, s), 1)] = jnp.where(even, along_row[:k], along_row[k:])[None]
+        both_halves(xg, s - 1, k, n, along_z[:k], along_z[k:])
+        segments.append(jnp.where(even, along_row[:k], along_row[k:]))
     for a in range(0, group, 2):
-        put(xr, a // 2, rows[a], rows[a + 1])
-
+        both_halves(xr, a // 2, k, n, segments[a], segments[a + 1])
+    u_acc[...] = u0_ref[...]
     v_acc[...] = jnp.zeros_like(v_acc)
 
-    def step(piece, at, c, total):
-        cols = pl.ds(pl.multiple_of(c * chunk, chunk), chunk)
-        high, low = split(held[piece][:, cols])
-        p = dot(xr[:, at], high, NN)
-        q = dot(xr[:k, at], low, NN)
-        v_acc[:, cols] += p[:k] + p[k:] + q
-        p = dot(xg[:, cols], high, NT)
-        q = dot(xg[:k, cols], low, NT)
-        return total + p[:k] + p[k:] + q
-
-    for piece in range(pieces):
+    def step(i, t, carry):
+        s, p = divmod(i, parts)
+        cols = slice(s * 2 * n, (s + 1) * 2 * n)
+        at = pl.ds(pl.multiple_of(p * rows + t * tile, tile), tile)
+        high, low = split(held[i][pl.ds(pl.multiple_of(t * tile, tile), tile), :])
+        one = dot(xr[:, at], high, NN)
+        two = dot(xr[:k, at], low, NN)
+        v_acc[:, cols] += one[:k] + one[k:] + two
+        one = dot(xg[:, cols], high, NT)
+        two = dot(xg[:k, cols], low, NT)
+        u_acc[:, at] += one[:k] + one[k:] + two
+        return carry
+
+    for i in range(count):
         if load:
-            fetch(piece).wait()
-        at = slice(piece * tile, (piece + 1) * tile)
-        u_acc[:, at] = lax.fori_loop(
-            0, held[piece].shape[1] // chunk, functools.partial(step, piece, at), jnp.zeros((k, tile), F32)
-        )
+            loader.wait(i, i % parts, 1 + i // parts, held[i])
+        lax.fori_loop(0, rows // tile, functools.partial(step, i), 0)
+
+    own_ref[...] = u_acc[:, :n]
 
     def by_z(out):
-        for g in range(group):
-            both = v_acc[:, 2 * n * g : 2 * n * (g + 1)]
-            out[g, :k, :] = both[:, :n]
-            out[g, k:, :] = both[:, n:]
+        for s in range(1, group):
+            both = v_acc[:, 2 * n * (s - 1) : 2 * n * s]
+            out[s - 1, :k, :] = both[:, :n]
+            out[s - 1, k:, :] = both[:, n:]
 
     def by_row(out, first):
+        at = slice(0, k) if first else slice(k, 2 * k)
+        rest = slice(k, 2 * k) if first else slice(0, k)
         for a in range(0, group, 2):
             both = u_acc[:, n * a : n * (a + 2)]
-            at = slice(0, k) if first else slice(k, 2 * k)
-            rest = slice(k, 2 * k) if first else slice(0, k)
-            out[a, at, :] = both[:, :n]
-            out[a + 1, at, :] = both[:, n:]
-            out[a, rest, :] = jnp.zeros((k, n), F32)
-            out[a + 1, rest, :] = jnp.zeros((k, n), F32)
+            for s in (a, a + 1):
+                if s:
+                    out[s - 1, at, :] = both[:, n * (s - a) : n * (s - a + 1)]
+                    out[s - 1, rest, :] = jnp.zeros((k, n), F32)
 
     @pl.when(even)
     def _():
@@ -174,27 +236,50 @@
         by_row(keep_ref, False)
 
 
-def combine_kernel(k, n, group, extra, keep_ref, got_ref, pair_ref, energy_ref, *refs):
-    theirs = refs[: group - 1] if extra else ()
-    outs = refs[len(refs) - group :]
-    parity, z, r = place()
-    even = parity == 0
-    at = jnp.where(even, z, r)
-    for s in range(group):
-        i = lax.bitwise_xor(at, s)
-        total = keep_ref[pl.ds(i, 1)][0] + got_ref[pl.ds(i, 1)][0]
-        if s == 0:
-            own = energy_ref[...] * pair_ref[: 2 * k, :]
-            row = lax.broadcasted_iota(jnp.int32, own.shape, 0)
-            total = total + jnp.where((row < k) == even, own, 0.0)
-        outs[s][: 2 * k, :] = total
+def late_kernel(k, n, group, tile, parts, extra, *refs):
+    held, refs = refs[:parts], refs[parts:]
+    xr, own_ref, pair_ref, energy_ref, *refs = refs
+    more, refs = (refs[0], refs[1:]) if extra else (None, refs)
+    out_ref, v_acc = refs
+    even = place()[0] == 0
+    rows = held[0].shape[0]
+    v_acc[...] = jnp.zeros_like(v_acc)
+
+    def step(p, t, carry):
+        at = pl.ds(pl.multiple_of(p * rows + t * tile, tile), tile)
+        high, low = split(held[p][pl.ds(pl.multiple_of(t * tile, tile), tile), :])
+        one = dot(xr[:, at], high, NN)
+        two = dot(xr[:k, at], low, NN)
+        v_acc[...] += one[:k] + one[k:] + two
+        return carry
+
+    for p in range(parts):
+        lax.fori_loop(0, rows // tile, functools.partial(step, p), 0)
+    own = jnp.where(even, pair_ref[:k, :], pair_ref[k : 2 * k, :])
+    own = energy_ref[...] * own + own_ref[...]
+    zero = jnp.zeros_like(own)
+    both = v_acc[...]
+    out_ref[:k, :] = both[:, :n] + jnp.where(even, own, zero)
+    out_ref[k : 2 * k, :] = both[:, n:] + jnp.where(even, zero, own)
+    if extra:
+        out_ref[2 * k :, :] = more[...]
+
+
+def combine_kernel(k, n, group, extra, keep_ref, got_ref, *refs):
+    if extra:
+        pair_ref, theirs, outs = refs[0], refs[1:group], refs[group:]
+    else:
+        outs = refs
+    for s in range(1, group):
+        outs[s - 1][: 2 * k, :] = keep_ref[s - 1] + got_ref[s - 1]
     if extra:
         part = pair_ref[2 * k :, :]
         for w in theirs:
             part = part + w[2 * k :, :]
-        part = jnp.where(even, part, jnp.zeros_like(part))
-        for s in range(group):
-            outs[s][2 * k :, :] = part
+        part = jnp.where(place()[0] == 0, part, jnp.zeros_like(part))
+        for s in range(1, group):
+            outs[s - 1][2 * k :, :] = part
+        outs[group - 1][...] = part
 
 
 def pair_kernel(k, n, first_ref, mine_ref, got_ref, out_ref):
@@ -282,7 +367,7 @@
     basis_ref[...] = dot32(inverse, rest, NN)
 
 
-def call(kernel, out_shape, n_in, scratch=(), limit=1 << 20, name=None, load=False):
+def call(kernel, out_shape, n_in, scratch=(), limit=1 << 20, name=None, load=False, flops=0):
     many = isinstance(out_shape, (tuple, list))
     run = pl.pallas_call(
         kernel,
@@ -291,6 +376,7 @@
         out_specs=tuple([VMEM_SPEC] * len(out_shape)) if many else VMEM_SPEC,
         scratch_shapes=list(scratch),
         compiler_params=pltpu.CompilerParams(vmem_limit_bytes=limit),
+        cost_estimate=pl.CostEstimate(flops=flops, transcendentals=0, bytes_accessed=flops // 128) if flops else None,
         name=name,
     )
 
@@ -324,8 +410,7 @@
 
     steps = range(1, group)
     tile = 256
-    pieces = rows // tile
-    chunk = width // 3
+    parts = 3
     a = coupling.reshape(rows, width)
     energy = energies.reshape(1, n)
     own = block.T
@@ -333,39 +418,64 @@
     first = call(functools.partial(order_kernel, k), shape(2 * k, n), 2, name="order")(own, other)
 
     def products(a, pair, name, load=False):
+        extra = pair.shape[0] > 2 * k
+        block = (shape(rows // parts, 2 * n),) * parts
+        sizes = (k, n, group, tile, parts)
+        work = rows * 2 * n * 256
+        count = (group - 1) * parts
+        most = max(len(pieces_of(p, group, n, rows // parts)) for p in range(parts))
         mine = [send(pair, spread(s)) for s in steps]
+        u0, *near = call(
+            functools.partial(early_kernel, *sizes, load),
+            (shape(k, rows),) + (block if load else ()),
+            2 if load else 1 + parts,
+            scratch=[pltpu.VMEM((2 * k, 2 * n), BF16)] + ([pltpu.SemaphoreType.DMA((parts, most))] if load else []),
+            limit=8 << 20,
+            name=name + "_early",
+            flops=2 * work,
+            load=load,
+        )(*([a] if load else a[:parts]), pair)
+        u0, *mine = lax.optimization_barrier((u0, *mine))
         theirs = [swap(y) for y in mine]
-        out, keep, *held = call(
-            functools.partial(product_kernel, k, n, group, tile, chunk, pieces, load),
-            (shape(group, 2 * k, n), shape(group, 2 * k, n))
-            + ((shape(tile, width),) * pieces if load else ()),
-            len(a) + 2 * group - 1,
+        out, keep, own, xr, *far = call(
+            functools.partial(main_kernel, *sizes, load),
+            (shape(group - 1, 2 * k, n), shape(group - 1, 2 * k, n), shape(k, n), jax.ShapeDtypeStruct((2 * k, rows), BF16))
+            + (block * (group - 1) if load else ()),
+            (1 if load else count) + 2 * group,
             scratch=[
-                pltpu.VMEM((2 * k, width), BF16),
-                pltpu.VMEM((2 * k, rows), BF16),
-                pltpu.VMEM((group, k, n), F32),
+                pltpu.VMEM((2 * k, (group - 1) * 2 * n), BF16),
                 pltpu.VMEM((k, rows), F32),
-                pltpu.VMEM((k, width), F32),
+                pltpu.VMEM((k, (group - 1) * 2 * n), F32),
             ]
-            + ([pltpu.SemaphoreType.DMA((pieces,))] if load else []),
+            + ([pltpu.SemaphoreType.DMA((count, most))] if load else []),
             limit=8 << 20,
             name=name,
             load=load,
-        )(*a, pair, *mine, *theirs)
+            flops=4 * work * (group - 1),
+        )(*([a] if load else a[parts:]), pair, u0, *mine, *theirs)
+        held = near + far if load else a
         got = swap(out)
-        extra = pair.shape[0] > 2 * k
-        parts = call(
+        parts_out = call(
             functools.partial(combine_kernel, k, n, group, extra),
-            tuple([shape(pair.shape[0], n)] * group),
-            4 + (group - 1 if extra else 0),
+            (shape(pair.shape[0], n),) * (group - 1) + ((shape(8, n),) if extra else ()),
+            2 + (group if extra else 0),
             name=name + "_combine",
-        )(keep, got, pair, energy, *(theirs if extra else ()))
-        total = parts[0]
-        for s in steps:
-            total = total + send(parts[s], spread(s))
+        )(keep, got, *((pair, *theirs) if extra else ()))
+        arrived = [send(parts_out[s - 1], spread(s)) for s in steps]
+        total = call(
+            functools.partial(late_kernel, *sizes, extra),
+            shape(pair.shape[0], n),
+            parts + 4 + extra,
+            scratch=[pltpu.VMEM((k, 2 * n), F32)],
+            limit=8 << 20,
+            name=name + "_late",
+            flops=2 * work,
+        )(*held[:parts], xr, own, pair, energy, *parts_out[group - 1 :])
+        for v in arrived:
+            total = total + v
         return total, swap(total), held
 
-    mine, got, held = products([a], first, "first", load=True)
+    mine, got, held = products(a, first, "first", load=True)
     pair = call(functools.partial(pair_kernel, k, n), shape(2 * k + 8, n), 3, name="pair")(first, mine, got)
     mine, got, _ = products(held, pair, "second")
     q, prod, moments, proj0, fact0 = call(
@@ -391,8 +501,8 @@
     def body(coupling, energies, block):
         n, k = block.shape
         paired = n_col == 2 * n_row and n_row & (n_row - 1) == 0 and n_row > 1
-        divides = coupling.shape[0] * n % 256 == 0
-        whole = divides and n % 64 == 0 and 8 * k == 128 and coupling.shape[2] % 384 == 0
+        divides = coupling.shape[0] * n % 768 == 0
+        whole = divides and n % 64 == 0 and 8 * k == 128 and coupling.shape[2] == coupling.shape[0] * n * 2
         small = coupling.size * 4 <= 44 << 20
         if paired and whole and small:
             return on_device(n_row, n_col, coupling, energies, block)

time: 115 us -> 109 us (0.948)
  waiting for transfers between devices: 31.6 us -> 19.5 us
  Pallas kernels: 52.6 us -> 58.1 us
    ppermute x29, waiting for transfers between devices: 31.6 us -> 19.5 us  [send(): lax.ppermute(value, axes, [(r * n_col + c, to(r, c)) for r, c in flat])]
    pallas_call x8 -> x12, Pallas kernels: 52.6 us -> 58.1 us  [call(): return lambda *args: run(*[keep(i, v) for i, v in enumerate(args)])]
  transfers between devices with their start and end apart: 29 -> 29, of which waited for: 24 -> 20; matrix products, arithmetic and copies ran while one was open for 0% -> 0% of each run, Pallas kernels for 0% -> 15%
where the time goes in v3:
time: 109 us; the launch traced here: 108 us
  Pallas kernels  58.1 us (53%)
  starting transfers between devices  29.2 us (27%)
  waiting for transfers between devices  19.5 us (18%)
    pallas_call x12, Pallas kernels, call(): return lambda *args: run(*[keep(i, v) for i, v in enumerate(args)])  58.1 us
    ppermute x29, starting transfers between devices, send(): lax.ppermute(value, axes, [(r * n_col + c, to(r, c)) for r, c in flat])  29.2 us
    ppermute x29, waiting for transfers between devices, send(): lax.ppermute(value, axes, [(r * n_col + c, to(r, c)) for r, c in flat])  19.5 us
  transfers between devices with their start and end apart: 29, of which 20 were waited for; matrix products, arithmetic and copies ran while one was open for 0% of the time, Pallas kernels for 15%

profile of v3, /device:TPU:0, one launch (start us, length us, event | category | flops | bytes accessed | tf_op | source)
XLA Modules:
  0.0 108.5 jit_solution(272641214905719961)
XLA Ops:
  0.6 0.6 collective-permute-start
  1.2 1.1 collective-permute-done.other_ref
  2.3 0.8 copy-done
  3.1 5.0 %collective-permute-start.3 = (f32[32,576]{1,0:T(8,128)S(1)}, f32[32,576]{1,0:T(8,128)S(1)}, u32[]{:S(2)}, u32[]{:S(2)}) collective-permute-start(f32[32,576]{1,0:T(8,128)S(1)} %order.1.refs_1_.refs_5_.first_ref), channel_id=1, source_target_pairs={{0,6},{1,25},{2,4},{3,27},{4,2},{5,29},{6,0},{7,31},{8,14},{9,17},... | collective-permute-start | bytes 221192 | tf_op jit(solution)/shard_map/ppermute | solution.py:403
  8.1 0.6 collective-permute-start.1
  8.7 5.9 %first_early.1 = (f32[16,2304]{1,0:T(8,128)S(1)}, f32[768,1152]{1,0:T(8,128)S(1)}, f32[768,1152]{1,0:T(8,128)S(1)}, f32[768,1152]{1,0:T(8,128)S(1)}) custom-call(f32[2304,4608]{1,0:T(8,128)} %bitcast.5, f32[32,576]{1,0:T(8,128)S(1)} %order.1.refs_1_.refs_5_.first_ref), custom_call_target="tpu_custom_call" | custom-call | flops 1358954496 | bytes 10616832 | tf_op jit(solution)/shard_map/first_early/pallas_call | solution.py:386
  14.6 0.0 collective-permute-done.2.refs_4_
  14.6 0.0 collective-permute-done.1.refs_3_
  14.6 0.0 copy-start.1
  14.6 0.1 collective-permute-start.4
  14.7 0.5 collective-permute-start.5
  15.2 0.1 collective-permute-start.6
  15.3 0.7 collective-permute-done.4.refs_6_
  16.0 0.2 collective-permute-done.5.refs_7_
  16.1 0.4 collective-permute-done.6.refs_8_
  16.5 18.9 %first.1 = (f32[3,32,576]{2,1,0:T(8,128)S(1)}, f32[3,32,576]{2,1,0:T(8,128)S(1)}, f32[16,576]{1,0:T(8,128)S(1)}, bf16[32,2304]{1,0:T(8,128)(2,1)S(1)}, f32[768,1...) custom-call(f32[2304,4608]{1,0:T(8,128)} %bitcast.6, ...), custom_call_target="tpu_custom_call" | custom-call | flops 8153726976 | bytes 63700992 | tf_op jit(solution)/shard_map/first/pallas_call | solution.py:386
  35.4 0.2 collective-permute-start.7
  35.6 1.3 %collective-permute-done.7.got_ref = f32[3,32,576]{2,1,0:T(8,128)S(1)} collective-permute-done((f32[3,32,576]{2,1,0:T(8,128)S(1)}, f32[3,32,576]{2,1,0:T(8,128)S(1)}, u32[]{:S(2)}, u32[]{:S(2)}) %collective-permute-start.7) | collective-permute-done | bytes 221216 | tf_op jit(solution)/shard_map/ppermute | solution.py:403
  37.0 1.4 %collective-permute-start.8 = (f32[32,576]{1,0:T(8,128)S(1)}, f32[32,576]{1,0:T(8,128)S(1)}, u32[]{:S(2)}, u32[]{:S(2)}) collective-permute-start(f32[32,576]{1,0:T(8,128)S(1)} %get-tuple-element.59), channel_id=1, source_target_pairs={{0,2},{1,9},{2,0},{3,11},{4,6},{5,13},{6,4},{7,15},{8,10},{9,1},{1... | collective-permute-start | bytes 221192 | tf_op jit(solution)/shard_map/ppermute | solution.py:403
  38.4 2.9 %collective-permute-start.9 = (f32[32,576]{1,0:T(8,128)S(1)}, f32[32,576]{1,0:T(8,128)S(1)}, u32[]{:S(2)}, u32[]{:S(2)}) collective-permute-start(f32[32,576]{1,0:T(8,128)S(1)} %get-tuple-element.60), channel_id=1, source_target_pairs={{0,4},{1,17},{2,6},{3,19},{4,0},{5,21},{6,2},{7,23},{8,12},{9,25},... | collective-permute-start | bytes 221192 | tf_op jit(solution)/shard_map/ppermute | solution.py:403
  41.4 0.1 collective-permute-start.10
  41.4 3.0 %first_late.1 = f32[32,576]{1,0:T(8,128)S(1)} custom-call(f32[768,1152]{1,0:T(8,128)S(1)} %get-tuple-element.47.refs_0_, f32[768,1152]{1,0:T(8,128)S(1)} %get-tuple-element.48.refs_1_, f32[768,1152]{1,0:T(8,128)S(1)} %get-tuple-element.49.refs_2_, bf16[32,2304]{1,0:T(8,128)(2,1)S(1)} %get-tuple-element.55.refs_3_, f32[16,576]{1,0:T(8,128)S(1)} %get-tuple-element.56.refs_4_, ...), custom_call_target="tpu_custom_call" | custom-call | flops 1358954496 | bytes 10616832 | tf_op jit(solution)/shard_map/first_late/pallas_call | solution.py:386
  44.5 0.0 collective-permute-done.8
  44.5 0.2 collective-permute-done.9
  44.6 2.9 %collective-permute-done.10 = f32[32,576]{1,0:T(8,128)S(1)} collective-permute-done((f32[32,576]{1,0:T(8,128)S(1)}, f32[32,576]{1,0:T(8,128)S(1)}, u32[]{:S(2)}, u32[]{:S(2)}) %collective-permute-start.10) | collective-permute-done | bytes 73760 | tf_op jit(solution)/shard_map/ppermute | solution.py:403
  47.6 0.1 collective-permute-start.11
  47.7 1.3 %collective-permute-done.11.got_ref = f32[32,576]{1,0:T(8,128)S(1)} collective-permute-done((f32[32,576]{1,0:T(8,128)S(1)}, f32[32,576]{1,0:T(8,128)S(1)}, u32[]{:S(2)}, u32[]{:S(2)}) %collective-permute-start.11) | collective-permute-done | bytes 73760 | tf_op jit(solution)/shard_map/ppermute | solution.py:403
  49.0 0.4 pair.1.refs_3_.refs_9_.refs_0_.refs_5_.pair_ref
  49.3 1.0 collective-permute-start.14
  50.3 3.4 %collective-permute-start.12 = (f32[40,576]{1,0:T(8,128)S(1)}, f32[40,576]{1,0:T(8,128)S(1)}, u32[]{:S(2)}, u32[]{:S(2)}) collective-permute-start(f32[40,576]{1,0:T(8,128)S(1)} %pair.1.refs_3_.refs_9_.refs_0_.refs_5_.pair_ref), channel_id=1, source_target_pairs={{0,2},{1,9},{2,0},{3,11},{4,6},{5,13},{6,4},{7,15},{8,10},{9,1},{1... | collective-permute-start | bytes 276488 | tf_op jit(solution)/shard_map/ppermute | solution.py:403
  53.7 3.9 %second_early.1.refs_10_ = f32[16,2304]{1,0:T(8,128)S(1)} custom-call(f32[768,1152]{1,0:T(8,128)S(1)} %get-tuple-element.47.refs_0_, f32[768,1152]{1,0:T(8,128)S(1)} %get-tuple-element.48.refs_1_, f32[768,1152]{1,0:T(8,128)S(1)} %get-tuple-element.49.refs_2_, f32[40,576]{1,0:T(8,128)S(1)} %pair.1.refs_3_.refs_9_.refs_0_.refs_5_.pair_ref), custom_call_target="tpu_custom_call" | custom-call | flops 1358954496 | bytes 10616832 | tf_op jit(solution)/shard_map/second_early/pallas_call | solution.py:386
  57.6 0.0 collective-permute-done.14.refs_13_
  57.6 0.4 collective-permute-done.13.refs_12_
  58.0 0.0 collective-permute-done.12.refs_11_
  58.0 0.0 collective-permute-start.15
  58.0 0.5 collective-permute-start.16
  58.5 0.0 collective-permute-start.17
  58.5 0.8 collective-permute-done.15.refs_14_.refs_1_
  59.3 0.2 collective-permute-done.16.refs_15_.refs_2_
  59.4 0.4 collective-permute-done.17.refs_16_.refs_3_
  59.8 17.0 %second.1 = (f32[3,32,576]{2,1,0:T(8,128)S(1)}, f32[3,32,576]{2,1,0:T(8,128)S(1)}, f32[16,576]{1,0:T(8,128)S(1)}, bf16[32,2304]{1,0:T(8,128)(2,1)S(1)}) custom-call(f32[768,1152]{1,0:T(8,128)S(1)} %get-tuple-element.62.refs_0_, f32[768,1152]{1,0:T(8,128)S(1)} %get-tuple-element.63.refs_1_, f32[768,1152]{1,0:T(8,128)S(1)} %get-tuple-element.64.refs_2_, ...), custom_call_target="tpu_custom_call" | custom-call | flops 8153726976 | bytes 63700992 | tf_op jit(solution)/shard_map/second/pallas_call | solution.py:386
  76.8 0.2 collective-permute-start.18
  77.0 1.4 %collective-permute-done.18.got_ref = f32[3,32,576]{2,1,0:T(8,128)S(1)} collective-permute-done((f32[3,32,576]{2,1,0:T(8,128)S(1)}, f32[3,32,576]{2,1,0:T(8,128)S(1)}, u32[]{:S(2)}, u32[]{:S(2)}) %collective-permute-start.18) | collective-permute-done | bytes 221216 | tf_op jit(solution)/shard_map/ppermute | solution.py:403
  78.4 0.5 collective-permute-start.19
  78.9 1.2 %collective-permute-start.20 = (f32[40,576]{1,0:T(8,128)S(1)}, f32[40,576]{1,0:T(8,128)S(1)}, u32[]{:S(2)}, u32[]{:S(2)}) collective-permute-start(f32[40,576]{1,0:T(8,128)S(1)} %get-tuple-element.81), channel_id=1, source_target_pairs={{0,4},{1,17},{2,6},{3,19},{4,0},{5,21},{6,2},{7,23},{8,12},{9,25},... | collective-permute-start | bytes 276488 | tf_op jit(solution)/shard_map/ppermute | solution.py:403
  80.0 2.8 %collective-permute-start.21 = (f32[40,576]{1,0:T(8,128)S(1)}, f32[40,576]{1,0:T(8,128)S(1)}, u32[]{:S(2)}, u32[]{:S(2)}) collective-permute-start(f32[40,576]{1,0:T(8,128)S(1)} %get-tuple-element.82), channel_id=1, source_target_pairs={{0,6},{1,25},{2,4},{3,27},{4,2},{5,29},{6,0},{7,31},{8,14},{9,17},... | collective-permute-start | bytes 276488 | tf_op jit(solution)/shard_map/ppermute | solution.py:403
  82.9 3.0 %second_late.1 = f32[40,576]{1,0:T(8,128)S(1)} custom-call(f32[768,1152]{1,0:T(8,128)S(1)} %get-tuple-element.47.refs_0_, f32[768,1152]{1,0:T(8,128)S(1)} %get-tuple-element.48.refs_1_, f32[768,1152]{1,0:T(8,128)S(1)} %get-tuple-element.49.refs_2_, bf16[32,2304]{1,0:T(8,128)(2,1)S(1)} %get-tuple-element.75.refs_3_, f32[16,576]{1,0:T(8,128)S(1)} %get-tuple-element.76.refs_4_, ...), custom_call_target="tpu_custom_call" | custom-call | flops 1358954496 | bytes 10616832 | tf_op jit(solution)/shard_map/second_late/pallas_call | solution.py:386
  85.9 0.0 collective-permute-done.19
  85.9 0.8 collective-permute-done.21
  86.7 0.1 collective-permute-start.22
  86.8 1.3 %collective-permute-done.22.got_ref = f32[40,576]{1,0:T(8,128)S(1)} collective-permute-done((f32[40,576]{1,0:T(8,128)S(1)}, f32[40,576]{1,0:T(8,128)S(1)}, u32[]{:S(2)}, u32[]{:S(2)}) %collective-permute-start.22) | collective-permute-done | bytes 92192 | tf_op jit(solution)/shard_map/ppermute | solution.py:403
  88.1 3.2 %middle.1 = (f32[32,576]{1,0:T(8,128)S(1)}, f32[32,576]{1,0:T(8,128)S(1)}, f32[48,48]{1,0:T(8,128)S(1)}, f32[16,16]{1,0:T(8,128)S(1)}, f32[16,16]{1,0:T(8,128)S(1)}) custom-call(f32[32,576]{1,0:T(8,128)S(1)} %order.1.refs_1_.refs_5_.first_ref, f32[40,576]{1,0:T(8,128)S(1)} %pair.1.refs_3_.refs_9_.refs_0_.refs_5_.pair_ref, ...), custom_call_target="tpu_custom_call" | custom-call | tf_op jit(solution)/shard_map/middle/pallas_call | solution.py:386
  91.3 2.5 %collective-permute-start.25 = (f32[48,48]{1,0:T(8,128)S(1)}, f32[48,48]{1,0:T(8,128)S(1)}, u32[]{:S(2)}, u32[]{:S(2)}) collective-permute-start(f32[48,48]{1,0:T(8,128)S(1)} %get-tuple-element.87), channel_id=1, source_target_pairs={{0,24},{1,25},{2,26},{3,27},{4,28},{5,29},{6,30},{7,31},{8,16},{9,... | collective-permute-start | bytes 27656 | tf_op jit(solution)/shard_map/ppermute | solution.py:403
  93.8 0.5 collective-permute-start.24
  94.3 0.5 collective-permute-start.23
  94.9 1.2 %collective-permute-done.25 = f32[48,48]{1,0:T(8,128)S(1)} collective-permute-done((f32[48,48]{1,0:T(8,128)S(1)}, f32[48,48]{1,0:T(8,128)S(1)}, u32[]{:S(2)}, u32[]{:S(2)}) %collective-permute-start.25) | collective-permute-done | bytes 9248 | tf_op jit(solution)/shard_map/ppermute | solution.py:403
  96.1 1.6 %collective-permute-done.24 = f32[48,48]{1,0:T(8,128)S(1)} collective-permute-done((f32[48,48]{1,0:T(8,128)S(1)}, f32[48,48]{1,0:T(8,128)S(1)}, u32[]{:S(2)}, u32[]{:S(2)}) %collective-permute-start.24) | collective-permute-done | bytes 9248 | tf_op jit(solution)/shard_map/ppermute | solution.py:403
  97.7 0.5 collective-permute-done.23
  98.2 2.8 %collective-permute-start.28 = (f32[48,48]{1,0:T(8,128)S(1)}, f32[48,48]{1,0:T(8,128)S(1)}, u32[]{:S(2)}, u32[]{:S(2)}) collective-permute-start(f32[48,48]{1,0:T(8,128)S(1)} %add_add_fusion.2.refs_0_), channel_id=1, source_target_pairs={{0,6},{1,7},{2,4},{3,5},{4,2},{5,3},{6,0},{7,1},{8,14},{9,15},{10,... | collective-permute-start | bytes 27656 | tf_op jit(solution)/shard_map/ppermute | solution.py:403
  100.9 0.4 collective-permute-start.27
  101.3 1.3 %collective-permute-start.26 = (f32[48,48]{1,0:T(8,128)S(1)}, f32[48,48]{1,0:T(8,128)S(1)}, u32[]{:S(2)}, u32[]{:S(2)}) collective-permute-start(f32[48,48]{1,0:T(8,128)S(1)} %add_add_fusion.2.refs_0_), channel_id=1, source_target_pairs={{0,2},{1,3},{2,0},{3,1},{4,6},{5,7},{6,4},{7,5},{8,10},{9,11},{10,... | collective-permute-start | bytes 27656 | tf_op jit(solution)/shard_map/ppermute | solution.py:403
  102.6 1.3 %collective-permute-done.28.refs_3_ = f32[48,48]{1,0:T(8,128)S(1)} collective-permute-done((f32[48,48]{1,0:T(8,128)S(1)}, f32[48,48]{1,0:T(8,128)S(1)}, u32[]{:S(2)}, u32[]{:S(2)}) %collective-permute-start.28) | collective-permute-done | bytes 9248 | tf_op jit(solution)/shard_map/ppermute | solution.py:403
  103.9 1.7 %collective-permute-done.27.refs_2_ = f32[48,48]{1,0:T(8,128)S(1)} collective-permute-done((f32[48,48]{1,0:T(8,128)S(1)}, f32[48,48]{1,0:T(8,128)S(1)}, u32[]{:S(2)}, u32[]{:S(2)}) %collective-permute-start.27) | collective-permute-done | bytes 9248 | tf_op jit(solution)/shard_map/ppermute | solution.py:403
  105.7 2.8 %last.1 = (f32[16,576]{1,0:T(8,128)}, f32[2,16,16]{2,1,0:T(8,128)}, f32[2,16,16]{2,1,0:T(8,128)}) custom-call(f32[32,576]{1,0:T(8,128)S(1)} %order.1.refs_1_.refs_5_.first_ref, f32[32,576]{1,0:T(8,128)S(1)} %get-tuple-element.83.q_ref, f32[32,576]{1,0:T(8,128)S(1)} %get-tuple-element.84.prod_ref, f32[16,16]{1,0:T(8,128)S(1)} %get-tuple-element.85.proj0_ref, ...), custom_call_target="tpu_custom_call" | custom-call | tf_op jit(solution)/shard_map/last/pallas_call | solution.py:386
  (14 shorter events, 0.2 us)
Async XLA Ops:
  0.6 1.6 %collective-permute-start = (f32[16,576]{1,0:T(8,128)}, f32[16,576]{1,0:T(8,128)S(1)}, u32[]{:S(2)}, u32[]{:S(2)}) collective-permute-start(f32[16,576]{1,0:T(8,128)} %bitcast.3), channel_id=1, source_target_pairs={{0,1},{1,0},{2,3},{3,2},{4,5},{5,4},{6,7},{7,6},{8,9},{9,8},{10,11... | collective-permute-start | bytes 110600 | tf_op jit(solution)/shard_map/ppermute | solution.py:403
  2.3 0.8 copy-start
  3.1 11.5 %collective-permute-start.3 = (f32[32,576]{1,0:T(8,128)S(1)}, f32[32,576]{1,0:T(8,128)S(1)}, u32[]{:S(2)}, u32[]{:S(2)}) collective-permute-start(f32[32,576]{1,0:T(8,128)S(1)} %order.1.refs_1_.refs_5_.first_ref), channel_id=1, source_target_pairs={{0,6},{1,25},{2,4},{3,27},{4,2},{5,29},{6,0},{7,31},{8,14},{9,17},... | collective-permute-start | bytes 221192 | tf_op jit(solution)/shard_map/ppermute | solution.py:403
  8.1 6.5 %collective-permute-start.2 = (f32[32,576]{1,0:T(8,128)S(1)}, f32[32,576]{1,0:T(8,128)S(1)}, u32[]{:S(2)}, u32[]{:S(2)}) collective-permute-start(f32[32,576]{1,0:T(8,128)S(1)} %order.1.refs_1_.refs_5_.first_ref), channel_id=1, source_target_pairs={{0,4},{1,17},{2,6},{3,19},{4,0},{5,21},{6,2},{7,23},{8,12},{9,25},... | collective-permute-start | bytes 221192 | tf_op jit(solution)/shard_map/ppermute | solution.py:403
  8.1 6.5 %collective-permute-start.1 = (f32[32,576]{1,0:T(8,128)S(1)}, f32[32,576]{1,0:T(8,128)S(1)}, u32[]{:S(2)}, u32[]{:S(2)}) collective-permute-start(f32[32,576]{1,0:T(8,128)S(1)} %order.1.refs_1_.refs_5_.first_ref), channel_id=1, source_target_pairs={{0,2},{1,9},{2,0},{3,11},{4,6},{5,13},{6,4},{7,15},{8,10},{9,1},{1... | collective-permute-start | bytes 221192 | tf_op jit(solution)/shard_map/ppermute | solution.py:403
  14.6 21.0 %copy-start.1 = (f32[576]{0:T(1024)S(1)}, f32[576]{0:T(1024)}, u32[]{:S(2)}) copy-start(f32[576]{0:T(1024)} %param.4) | copy-start | bytes 6916
  14.6 1.3 %collective-permute-start.4 = (f32[32,576]{1,0:T(8,128)S(1)}, f32[32,576]{1,0:T(8,128)S(1)}, u32[]{:S(2)}, u32[]{:S(2)}) collective-permute-start(f32[32,576]{1,0:T(8,128)S(1)} %collective-permute-done.1.refs_3_), channel_id=1, source_target_pairs={{0,1},{1,0},{2,3},{3,2},{4,5},{5,4},{6,7},{7,6},{8,9},{9,8},{10,11... | collective-permute-start | bytes 221192 | tf_op jit(solution)/shard_map/ppermute | solution.py:403
  14.7 1.4 %collective-permute-start.5 = (f32[32,576]{1,0:T(8,128)S(1)}, f32[32,576]{1,0:T(8,128)S(1)}, u32[]{:S(2)}, u32[]{:S(2)}) collective-permute-start(f32[32,576]{1,0:T(8,128)S(1)} %collective-permute-done.2.refs_4_), channel_id=1, source_target_pairs={{0,1},{1,0},{2,3},{3,2},{4,5},{5,4},{6,7},{7,6},{8,9},{9,8},{10,11... | collective-permute-start | bytes 221192 | tf_op jit(solution)/shard_map/ppermute | solution.py:403
  15.2 1.3 %collective-permute-start.6 = (f32[32,576]{1,0:T(8,128)S(1)}, f32[32,576]{1,0:T(8,128)S(1)}, u32[]{:S(2)}, u32[]{:S(2)}) collective-permute-start(f32[32,576]{1,0:T(8,128)S(1)} %collective-permute-done.3.refs_5_), channel_id=1, source_target_pairs={{0,1},{1,0},{2,3},{3,2},{4,5},{5,4},{6,7},{7,6},{8,9},{9,8},{10,11... | collective-permute-start | bytes 221192 | tf_op jit(solution)/shard_map/ppermute | solution.py:403
  35.4 1.6 %collective-permute-start.7 = (f32[3,32,576]{2,1,0:T(8,128)S(1)}, f32[3,32,576]{2,1,0:T(8,128)S(1)}, u32[]{:S(2)}, u32[]{:S(2)}) collective-permute-start(f32[3,32,576]{2,1,0:T(8,128)S(1)} %get-tuple-element.58), channel_id=1, source_target_pairs={{0,1},{1,0},{2,3},{3,2},{4,5},{5,4},{6,7},{7,6},{8,9},{9,8},{10,11... | collective-permute-start | bytes 663560 | tf_op jit(solution)/shard_map/ppermute | solution.py:403
  37.0 7.5 %collective-permute-start.8 = (f32[32,576]{1,0:T(8,128)S(1)}, f32[32,576]{1,0:T(8,128)S(1)}, u32[]{:S(2)}, u32[]{:S(2)}) collective-permute-start(f32[32,576]{1,0:T(8,128)S(1)} %get-tuple-element.59), channel_id=1, source_target_pairs={{0,2},{1,9},{2,0},{3,11},{4,6},{5,13},{6,4},{7,15},{8,10},{9,1},{1... | collective-permute-start | bytes 221192 | tf_op jit(solution)/shard_map/ppermute | solution.py:403
  38.4 6.2 %collective-permute-start.9 = (f32[32,576]{1,0:T(8,128)S(1)}, f32[32,576]{1,0:T(8,128)S(1)}, u32[]{:S(2)}, u32[]{:S(2)}) collective-permute-start(f32[32,576]{1,0:T(8,128)S(1)} %get-tuple-element.60), channel_id=1, source_target_pairs={{0,4},{1,17},{2,6},{3,19},{4,0},{5,21},{6,2},{7,23},{8,12},{9,25},... | collective-permute-start | bytes 221192 | tf_op jit(solution)/shard_map/ppermute | solution.py:403
  41.4 6.2 %collective-permute-start.10 = (f32[32,576]{1,0:T(8,128)S(1)}, f32[32,576]{1,0:T(8,128)S(1)}, u32[]{:S(2)}, u32[]{:S(2)}) collective-permute-start(f32[32,576]{1,0:T(8,128)S(1)} %get-tuple-element.61), channel_id=1, source_target_pairs={{0,6},{1,25},{2,4},{3,27},{4,2},{5,29},{6,0},{7,31},{8,14},{9,17},... | collective-permute-start | bytes 221192 | tf_op jit(solution)/shard_map/ppermute | solution.py:403
  47.6 1.3 %collective-permute-start.11 = (f32[32,576]{1,0:T(8,128)S(1)}, f32[32,576]{1,0:T(8,128)S(1)}, u32[]{:S(2)}, u32[]{:S(2)}) collective-permute-start(f32[32,576]{1,0:T(8,128)S(1)} %add_add_fusion.1.mine_ref), channel_id=1, source_target_pairs={{0,1},{1,0},{2,3},{3,2},{4,5},{5,4},{6,7},{7,6},{8,9},{9,8},{10,11... | collective-permute-start | bytes 221192 | tf_op jit(solution)/shard_map/ppermute | solution.py:403
  49.3 8.3 %collective-permute-start.14 = (f32[40,576]{1,0:T(8,128)S(1)}, f32[40,576]{1,0:T(8,128)S(1)}, u32[]{:S(2)}, u32[]{:S(2)}) collective-permute-start(f32[40,576]{1,0:T(8,128)S(1)} %pair.1.refs_3_.refs_9_.refs_0_.refs_5_.pair_ref), channel_id=1, source_target_pairs={{0,6},{1,25},{2,4},{3,27},{4,2},{5,29},{6,0},{7,31},{8,14},{9,17},... | collective-permute-start | bytes 276488 | tf_op jit(solution)/shard_map/ppermute | solution.py:403
  50.3 7.7 %collective-permute-start.13 = (f32[40,576]{1,0:T(8,128)S(1)}, f32[40,576]{1,0:T(8,128)S(1)}, u32[]{:S(2)}, u32[]{:S(2)}) collective-permute-start(f32[40,576]{1,0:T(8,128)S(1)} %pair.1.refs_3_.refs_9_.refs_0_.refs_5_.pair_ref), channel_id=1, source_target_pairs={{0,4},{1,17},{2,6},{3,19},{4,0},{5,21},{6,2},{7,23},{8,12},{9,25},... | collective-permute-start | bytes 276488 | tf_op jit(solution)/shard_map/ppermute | solution.py:403
  50.3 7.7 %collective-permute-start.12 = (f32[40,576]{1,0:T(8,128)S(1)}, f32[40,576]{1,0:T(8,128)S(1)}, u32[]{:S(2)}, u32[]{:S(2)}) collective-permute-start(f32[40,576]{1,0:T(8,128)S(1)} %pair.1.refs_3_.refs_9_.refs_0_.refs_5_.pair_ref), channel_id=1, source_target_pairs={{0,2},{1,9},{2,0},{3,11},{4,6},{5,13},{6,4},{7,15},{8,10},{9,1},{1... | collective-permute-start | bytes 276488 | tf_op jit(solution)/shard_map/ppermute | solution.py:403
  58.0 1.3 %collective-permute-start.15 = (f32[40,576]{1,0:T(8,128)S(1)}, f32[40,576]{1,0:T(8,128)S(1)}, u32[]{:S(2)}, u32[]{:S(2)}) collective-permute-start(f32[40,576]{1,0:T(8,128)S(1)} %collective-permute-done.12.refs_11_), channel_id=1, source_target_pairs={{0,1},{1,0},{2,3},{3,2},{4,5},{5,4},{6,7},{7,6},{8,9},{9,8},{10,11... | collective-permute-start | bytes 276488 | tf_op jit(solution)/shard_map/ppermute | solution.py:403
  58.0 1.5 %collective-permute-start.16 = (f32[40,576]{1,0:T(8,128)S(1)}, f32[40,576]{1,0:T(8,128)S(1)}, u32[]{:S(2)}, u32[]{:S(2)}) collective-permute-start(f32[40,576]{1,0:T(8,128)S(1)} %collective-permute-done.13.refs_12_), channel_id=1, source_target_pairs={{0,1},{1,0},{2,3},{3,2},{4,5},{5,4},{6,7},{7,6},{8,9},{9,8},{10,11... | collective-permute-start | bytes 276488 | tf_op jit(solution)/shard_map/ppermute | solution.py:403
  58.5 1.3 %collective-permute-start.17 = (f32[40,576]{1,0:T(8,128)S(1)}, f32[40,576]{1,0:T(8,128)S(1)}, u32[]{:S(2)}, u32[]{:S(2)}) collective-permute-start(f32[40,576]{1,0:T(8,128)S(1)} %collective-permute-done.14.refs_13_), channel_id=1, source_target_pairs={{0,1},{1,0},{2,3},{3,2},{4,5},{5,4},{6,7},{7,6},{8,9},{9,8},{10,11... | collective-permute-start | bytes 276488 | tf_op jit(solution)/shard_map/ppermute | solution.py:403
  76.8 1.6 %collective-permute-start.18 = (f32[3,32,576]{2,1,0:T(8,128)S(1)}, f32[3,32,576]{2,1,0:T(8,128)S(1)}, u32[]{:S(2)}, u32[]{:S(2)}) collective-permute-start(f32[3,32,576]{2,1,0:T(8,128)S(1)} %get-tuple-element.78), channel_id=1, source_target_pairs={{0,1},{1,0},{2,3},{3,2},{4,5},{5,4},{6,7},{7,6},{8,9},{9,8},{10,11... | collective-permute-start | bytes 663560 | tf_op jit(solution)/shard_map/ppermute | solution.py:403
  78.4 7.5 %collective-permute-start.19 = (f32[40,576]{1,0:T(8,128)S(1)}, f32[40,576]{1,0:T(8,128)S(1)}, u32[]{:S(2)}, u32[]{:S(2)}) collective-permute-start(f32[40,576]{1,0:T(8,128)S(1)} %get-tuple-element.80), channel_id=1, source_target_pairs={{0,2},{1,9},{2,0},{3,11},{4,6},{5,13},{6,4},{7,15},{8,10},{9,1},{1... | collective-permute-start | bytes 276488 | tf_op jit(solution)/shard_map/ppermute | solution.py:403
  78.9 7.1 %collective-permute-start.20 = (f32[40,576]{1,0:T(8,128)S(1)}, f32[40,576]{1,0:T(8,128)S(1)}, u32[]{:S(2)}, u32[]{:S(2)}) collective-permute-start(f32[40,576]{1,0:T(8,128)S(1)} %get-tuple-element.81), channel_id=1, source_target_pairs={{0,4},{1,17},{2,6},{3,19},{4,0},{5,21},{6,2},{7,23},{8,12},{9,25},... | collective-permute-start | bytes 276488 | tf_op jit(solution)/shard_map/ppermute | solution.py:403
  80.0 6.7 %collective-permute-start.21 = (f32[40,576]{1,0:T(8,128)S(1)}, f32[40,576]{1,0:T(8,128)S(1)}, u32[]{:S(2)}, u32[]{:S(2)}) collective-permute-start(f32[40,576]{1,0:T(8,128)S(1)} %get-tuple-element.82), channel_id=1, source_target_pairs={{0,6},{1,25},{2,4},{3,27},{4,2},{5,29},{6,0},{7,31},{8,14},{9,17},... | collective-permute-start | bytes 276488 | tf_op jit(solution)/shard_map/ppermute | solution.py:403
  86.7 1.4 %collective-permute-start.22 = (f32[40,576]{1,0:T(8,128)S(1)}, f32[40,576]{1,0:T(8,128)S(1)}, u32[]{:S(2)}, u32[]{:S(2)}) collective-permute-start(f32[40,576]{1,0:T(8,128)S(1)} %add_add_fusion.mine_ref), channel_id=1, source_target_pairs={{0,1},{1,0},{2,3},{3,2},{4,5},{5,4},{6,7},{7,6},{8,9},{9,8},{10,11... | collective-permute-start | bytes 276488 | tf_op jit(solution)/shard_map/ppermute | solution.py:403
  91.3 4.8 %collective-permute-start.25 = (f32[48,48]{1,0:T(8,128)S(1)}, f32[48,48]{1,0:T(8,128)S(1)}, u32[]{:S(2)}, u32[]{:S(2)}) collective-permute-start(f32[48,48]{1,0:T(8,128)S(1)} %get-tuple-element.87), channel_id=1, source_target_pairs={{0,24},{1,25},{2,26},{3,27},{4,28},{5,29},{6,30},{7,31},{8,16},{9,... | collective-permute-start | bytes 27656 | tf_op jit(solution)/shard_map/ppermute | solution.py:403
  93.8 3.8 %collective-permute-start.24 = (f32[48,48]{1,0:T(8,128)S(1)}, f32[48,48]{1,0:T(8,128)S(1)}, u32[]{:S(2)}, u32[]{:S(2)}) collective-permute-start(f32[48,48]{1,0:T(8,128)S(1)} %get-tuple-element.87), channel_id=1, source_target_pairs={{0,16},{1,17},{2,18},{3,19},{4,20},{5,21},{6,22},{7,23},{8,24},{9,... | collective-permute-start | bytes 27656 | tf_op jit(solution)/shard_map/ppermute | solution.py:403
  94.3 3.8 %collective-permute-start.23 = (f32[48,48]{1,0:T(8,128)S(1)}, f32[48,48]{1,0:T(8,128)S(1)}, u32[]{:S(2)}, u32[]{:S(2)}) collective-permute-start(f32[48,48]{1,0:T(8,128)S(1)} %get-tuple-element.87), channel_id=1, source_target_pairs={{0,8},{1,9},{2,10},{3,11},{4,12},{5,13},{6,14},{7,15},{8,0},{9,1},... | collective-permute-start | bytes 27656 | tf_op jit(solution)/shard_map/ppermute | solution.py:403
  98.2 5.8 %collective-permute-start.28 = (f32[48,48]{1,0:T(8,128)S(1)}, f32[48,48]{1,0:T(8,128)S(1)}, u32[]{:S(2)}, u32[]{:S(2)}) collective-permute-start(f32[48,48]{1,0:T(8,128)S(1)} %add_add_fusion.2.refs_0_), channel_id=1, source_target_pairs={{0,6},{1,7},{2,4},{3,5},{4,2},{5,3},{6,0},{7,1},{8,14},{9,15},{10,... | collective-permute-start | bytes 27656 | tf_op jit(solution)/shard_map/ppermute | solution.py:403
  100.9 4.7 %collective-permute-start.27 = (f32[48,48]{1,0:T(8,128)S(1)}, f32[48,48]{1,0:T(8,128)S(1)}, u32[]{:S(2)}, u32[]{:S(2)}) collective-permute-start(f32[48,48]{1,0:T(8,128)S(1)} %add_add_fusion.2.refs_0_), channel_id=1, source_target_pairs={{0,4},{1,5},{2,6},{3,7},{4,0},{5,1},{6,2},{7,3},{8,12},{9,13},{10,... | collective-permute-start | bytes 27656 | tf_op jit(solution)/shard_map/ppermute | solution.py:403
  101.3 4.4 %collective-permute-start.26 = (f32[48,48]{1,0:T(8,128)S(1)}, f32[48,48]{1,0:T(8,128)S(1)}, u32[]{:S(2)}, u32[]{:S(2)}) collective-permute-start(f32[48,48]{1,0:T(8,128)S(1)} %add_add_fusion.2.refs_0_), channel_id=1, source_target_pairs={{0,2},{1,3},{2,0},{3,1},{4,6},{5,7},{6,4},{7,5},{8,10},{9,11},{10,... | collective-permute-start | bytes 27656 | tf_op jit(solution)/shard_map/ppermute | solution.py:403

commit v4 on v3

v4 whole, which is shorter than its diff:
```python
import functools

import jax
import jax.numpy as jnp
from jax import lax
from jax.experimental import pallas as pl
from jax.experimental.pallas import tpu as pltpu
from jax.sharding import PartitionSpec as P

ITERS = 2
F32 = jnp.float32
BF16 = jnp.bfloat16

precise = lax.Precision.HIGHEST

NN = (((1,), (0,)), ((), ()))
NT = (((1,), (1,)), ((), ()))
TN = (((0,), (0,)), ((), ()))

VMEM_SPEC = pl.BlockSpec(memory_space=pltpu.VMEM)


def generic(coupling, energies, block):
    order = block.shape[0] * lax.axis_size("row") * lax.axis_size("col")
    segment = block.shape[0]
    width = block.shape[1]
    column = lax.axis_index("col")
    current, energy_rows = (
        lax.all_gather(block, "col", axis=0, tiled=True),
        lax.all_gather(energies, "col", axis=0, tiled=True),
    )
    prior = jnp.zeros_like(current)
    projection_list = []
    factor_list = []
    for section in range(ITERS):
        own_rows = lax.dynamic_slice_in_dim(current, column * segment, segment, 0)
        spread = lax.all_gather(own_rows, "row", axis=0, tiled=True)
        spread = spread.reshape(coupling.shape[0], segment, width)
        direct = lax.psum_scatter(
            jnp.einsum("aig,gk->aik", coupling, current, precision=precise),
            "row",
            scatter_dimension=0,
            tiled=True,
        ).reshape(segment, width)
        partial_value = jnp.einsum("aig,aik->gk", coupling, spread, precision=precise)
        transposed = lax.psum(partial_value, "col")
        direct_rows = lax.all_gather(direct, "col", axis=0, tiled=True)
        product = energy_rows[:, None] * current + direct_rows + transposed
        stacked = jnp.concatenate([current, prior, product], axis=1)
        moments = lax.psum(jnp.einsum("nk,nl->kl", stacked, stacked, precision=precise), "row") / order
        projection = moments[:width, 2 * width :]
        cross = moments[width : 2 * width, 2 * width :]
        weights = jnp.concatenate([-projection, -cross, jnp.eye(width, dtype=F32)], axis=0)
        gram_matrix = jnp.dot(weights.T, jnp.dot(moments, weights, precision=precise), precision=precise)
        factor = jnp.linalg.cholesky(gram_matrix)
        residual = (
            product
            - jnp.dot(current, projection, precision=precise)
            - jnp.dot(prior, cross, precision=precise)
        )
        prior = current
        current = jax.scipy.linalg.solve_triangular(factor, residual.T, lower=True).T
        projection_list.append(projection)
        factor_list.append(factor)
    basis = lax.dynamic_slice_in_dim(current, column * segment, segment, 0)
    return (basis, jnp.stack(projection_list), jnp.stack(factor_list))


def place():
    column = lax.axis_index("col")
    return lax.rem(column, 2), lax.div(column, 2), lax.axis_index("row")


def split(value):
    high = value.astype(BF16)
    return high, (value - high.astype(F32)).astype(BF16)


def dot(left, right, dims):
    return lax.dot_general(left, right, dims, preferred_element_type=F32)


def dot32(left, right, dims):
    return lax.dot_general(left, right, dims, preferred_element_type=F32, precision=precise)


def own_half(value, even, n):
    return jnp.where(even, value[:, :n], value[:, n : 2 * n])


def in_half(value, even):
    zero = jnp.zeros_like(value)
    return jnp.concatenate([jnp.where(even, value, zero), jnp.where(even, zero, value)], axis=1)


def pieces_of(part, group, n, rows):
    found, at, end = [], part * rows, (part + 1) * rows
    while at < end:
        s, off = divmod(at, n)
        count = min(n - off, end - at)
        found.append((s, off, at - part * rows, count))
        at += count
    return found


class Loader:
    def __init__(self, source, arrived, n, group, parts, first, held):
        _, z, r = place()
        self.held, self.first = held, first

        def copies(i):
            cols = pl.ds(pl.multiple_of(lax.bitwise_xor(z, (first + i) // parts) * (2 * n), 128), 2 * n)
            return [
                pltpu.make_async_copy(
                    source.at[pl.ds(pl.multiple_of(lax.bitwise_xor(r, peer) * n + off, 8), count), cols],
                    held[i].at[pl.ds(at, count), :],
                    arrived.at[i, j],
                )
                for j, (peer, off, at, count) in enumerate(
                    pieces_of((first + i) % parts, group, n, group * n // parts)
                )
            ]

        self.copies = copies
        for i in range(len(held)):
            for copy in copies(i):
                copy.start()

    def wait(self, i):
        for copy in self.copies(i):
            copy.wait()


def begin_kernel(k, n, group, parts, source, block_ref, own_ref, *refs):
    *held, arrived, ready = refs
    copy = pltpu.make_async_copy(block_ref, own_ref, ready)
    copy.start()
    loader = Loader(source, arrived, n, group, parts, 0, held)
    copy.wait()
    for i in range(len(held)):
        loader.wait(i)


def order_kernel(k, n, own_ref, other_ref, out_ref):
    even = place()[0] == 0
    own, other = own_ref[...], other_ref[...]
    out_ref[...] = jnp.concatenate([jnp.where(even, own, other), jnp.where(even, other, own)], axis=1)


def put(slab, at, k, value):
    high, low = split(value)
    slab[:k, at : at + value.shape[1]] = high
    slab[k:, at : at + value.shape[1]] = low


def early_kernel(k, n, group, tile, parts, given, new, *refs):
    source, refs = (refs[0], refs[1:]) if new else (None, refs)
    held, refs = list(refs[:given]), refs[given:]
    pair_ref, u_ref, *refs = refs
    if new:
        *fresh, xg, arrived = refs
        loader = Loader(source, arrived, n, group, parts, given, fresh)
        held = held + fresh
    else:
        (xg,) = refs
    put(xg, 0, k, pair_ref[:, : 2 * n])
    rows = held[0].shape[0]

    def step(p, t, carry):
        high, low = split(held[p][pl.ds(pl.multiple_of(t * tile, tile), tile), :])
        one = dot(xg[...], high, NT)
        two = dot(xg[:k, :], low, NT)
        u_ref[:, pl.ds(pl.multiple_of(p * rows + t * tile, tile), tile)] = one[:k] + one[k:] + two
        return carry

    for p in range(parts):
        if p >= given:
            loader.wait(p - given)
        lax.fori_loop(0, rows // tile, functools.partial(step, p), 0)
    for p in range(parts, given + new):
        loader.wait(p - given)


def turned(s, group, even):
    return jnp.logical_not(even) if s == group - 1 else even


def main_kernel(k, n, group, tile, parts, given, new, *refs):
    even = place()[0] == 0
    source, refs = (refs[0], refs[1:]) if new else (None, refs)
    held, refs = list(refs[:given]), refs[given:]
    pair_ref, u0_ref, mine, theirs = refs[0], refs[1], refs[2 : group + 1], refs[group + 1 : 2 * group]
    send_ref, keep_ref, own_ref, xr, *refs = refs[2 * group :]
    if new:
        *fresh, xg, u_acc, v_acc, arrived = refs
        loader = Loader(source, arrived, n, group, parts, parts + given, fresh)
        held = held + fresh
    else:
        xg, u_acc, v_acc = refs
    rows = held[0].shape[0]

    segments = [own_half(pair_ref, even, n)]
    for s in range(1, group):
        y, w = mine[s - 1][:, : 2 * n], theirs[s - 1][:, : 2 * n]
        along = turned(s, group, even)
        put(xg, (s - 1) * 2 * n, k, jnp.where(along, y, w))
        segments.append(own_half(jnp.where(along, w, y), even, n))
    for a in range(0, group, 2):
        put(xr, a * n, k, jnp.concatenate(segments[a : a + 2], axis=1))
    u_acc[...] = u0_ref[...]
    v_acc[...] = jnp.zeros_like(v_acc)

    def step(i, t, carry):
        s, p = divmod(i, parts)
        cols = slice(s * 2 * n, (s + 1) * 2 * n)
        at = pl.ds(pl.multiple_of(p * rows + t * tile, tile), tile)
        high, low = split(held[i][pl.ds(pl.multiple_of(t * tile, tile), tile), :])
        one = dot(xr[:, at], high, NN)
        two = dot(xr[:k, at], low, NN)
        v_acc[:, cols] += one[:k] + one[k:] + two
        one = dot(xg[:, cols], high, NT)
        two = dot(xg[:k, cols], low, NT)
        u_acc[:, at] += one[:k] + one[k:] + two
        return carry

    for i in range(len(held)):
        if i >= given:
            loader.wait(i - given)
        lax.fori_loop(0, rows // tile, functools.partial(step, i), 0)

    own_ref[...] = u_acc[:, :n]
    for s in range(1, group):
        along = turned(s, group, even)
        by_z = v_acc[:, 2 * n * (s - 1) : 2 * n * s]
        by_row = in_half(u_acc[:, n * s : n * (s + 1)], even)
        keep_ref[s - 1] = jnp.where(along, by_z, by_row)
        send_ref[s - 1] = jnp.where(along, by_row, by_z)


def late_kernel(k, n, group, tile, parts, extra, *refs):
    held, refs = refs[:parts], refs[parts:]
    xr, own_ref, pair_ref, energy_ref, *refs = refs
    more, refs = (refs[0], refs[1:]) if extra else (None, refs)
    out_ref, v_acc = refs
    even = place()[0] == 0
    rows = held[0].shape[0]
    v_acc[...] = jnp.zeros_like(v_acc)

    def step(p, t, carry):
        at = pl.ds(pl.multiple_of(p * rows + t * tile, tile), tile)
        high, low = split(held[p][pl.ds(pl.multiple_of(t * tile, tile), tile), :])
        one = dot(xr[:, at], high, NN)
        two = dot(xr[:k, at], low, NN)
        v_acc[...] += one[:k] + one[k:] + two
        return carry

    for p in range(parts):
        lax.fori_loop(0, rows // tile, functools.partial(step, p), 0)
    own = energy_ref[...] * own_half(pair_ref, even, n) + own_ref[...]
    out_ref[:, : 2 * n] = v_acc[...] + in_half(own, even)
    if extra:
        part = more[...]
        out_ref[:, 2 * n :] = jnp.where(even, part, jnp.zeros_like(part))


def combine_kernel(k, n, group, extra, keep_ref, got_ref, *refs):
    even = place()[0] == 0
    if extra:
        pair_ref, mine, theirs, outs = refs[0], refs[1:group], refs[group : 2 * group - 1], refs[2 * group - 1 :]
        part = pair_ref[:, 2 * n :]
        for s in range(1, group):
            along = turned(s, group, even)
            part = part + jnp.where(along, theirs[s - 1][:, 2 * n :], mine[s - 1][:, 2 * n :])
        outs[group - 1][...] = part
    else:
        outs = refs
    for s in range(1, group):
        outs[s - 1][:, : 2 * n] = keep_ref[s - 1] + got_ref[s - 1]
        if extra:
            outs[s - 1][:, 2 * n :] = jnp.where(turned(s, group, even), part, jnp.zeros_like(part))


def pair_kernel(k, n, first_ref, mine_ref, got_ref, out_ref):
    value = mine_ref[...] + got_ref[...]
    s = jnp.concatenate([first_ref[...], value], axis=0)
    moments = dot32(s, s, NT)
    out_ref[:, : 2 * n] = value
    out_ref[:, 2 * n :] = jnp.zeros((k, 8 * k), F32)
    out_ref[:, 2 * n : 2 * n + 2 * k] = moments[:k]
    out_ref[:, 2 * n + 2 * k : 2 * n + 4 * k] = moments[k:]


def factor_of(gram):
    k = gram.shape[0]
    rows = lax.broadcasted_iota(jnp.int32, (k, 2 * k), 0)
    cols = lax.broadcasted_iota(jnp.int32, (k, 2 * k), 1)
    row = lax.broadcasted_iota(jnp.int32, (k, 1), 0)
    both = jnp.concatenate([gram, jnp.where(rows == cols, 1.0, 0.0)[:, :k]], axis=1)
    lower = jnp.zeros((k, k), F32)
    for j in range(k):
        scale = 1.0 / jnp.sqrt(both[j : j + 1, j : j + 1])
        column = jnp.where(row >= j, both[:, j : j + 1] * scale, 0.0)
        lower = jnp.where(cols[:, :k] == j, column, lower)
        lead = both[j : j + 1, :] * scale
        below = jnp.where(row > j, column, 0.0)
        both = jnp.where(rows == j, lead, both - below * lead)
    return lower, both[:, k:]


def gram_of(moments, coefficients):
    k = moments.shape[0]
    w = coefficients.shape[1]
    parts = jnp.concatenate([-coefficients, eye(w)], axis=0)
    return dot32(parts, dot32(moments, parts, NN), TN)


def eye(k):
    return jnp.where(
        lax.broadcasted_iota(jnp.int32, (k, k), 0) == lax.broadcasted_iota(jnp.int32, (k, k), 1), 1.0, 0.0
    ).astype(F32)


def second_kernel(k, n, order, first_ref, pair_ref, mine_ref, got_ref, q_ref, prod_ref, mom_ref, base_ref, proj_ref, fact_ref):
    packed = mine_ref[:, 2 * n :] + got_ref[:, 2 * n :]
    moments = jnp.concatenate([packed[:, : 2 * k], packed[:, 2 * k : 4 * k]], axis=0) * (1.0 / order)
    projection = moments[:k, k:]
    lower, inverse = factor_of(gram_of(moments, projection))
    proj_ref[...] = projection
    fact_ref[...] = lower
    x, y = first_ref[...], pair_ref[:, : 2 * n]
    w = mine_ref[:, : 2 * n] + got_ref[:, : 2 * n]
    q = dot32(inverse, y - dot32(projection, x, TN), NN)
    prod = dot32(inverse, w - dot32(projection, y, TN), NN)
    q_ref[...] = q
    prod_ref[...] = prod
    s = jnp.concatenate([q, x, prod], axis=0)
    total = dot32(s, s, NT)
    mom_ref[...] = total
    base_ref[...] = jnp.where(place()[0] == 0, total, jnp.zeros_like(total))


def last_kernel(k, n, order, first_ref, q_ref, prod_ref, proj0_ref, fact0_ref, mine_ref, got_ref, basis_ref, proj_ref, fact_ref):
    moments = (mine_ref[...] + got_ref[...]) * (1.0 / order)
    coefficients = moments[: 2 * k, 2 * k :]
    lower, inverse = factor_of(gram_of(moments, coefficients))
    proj_ref[0] = proj0_ref[...]
    proj_ref[1] = coefficients[:k]
    fact_ref[0] = fact0_ref[...]
    fact_ref[1] = lower
    even = place()[0] == 0
    rest = (
        own_half(prod_ref, even, n)
        - dot32(coefficients[:k], own_half(q_ref, even, n), TN)
        - dot32(coefficients[k:], own_half(first_ref, even, n), TN)
    )
    basis_ref[...] = dot32(inverse, rest, NN)


def call(kernel, out_shape, n_in, scratch=(), limit=1 << 20, name=None, far=0, flops=0):
    many = isinstance(out_shape, (tuple, list))
    run = pl.pallas_call(
        kernel,
        out_shape=out_shape,
        in_specs=[pl.BlockSpec(memory_space=pl.ANY) if i < far else VMEM_SPEC for i in range(n_in)],
        out_specs=tuple([VMEM_SPEC] * len(out_shape)) if many else VMEM_SPEC,
        scratch_shapes=list(scratch),
        compiler_params=pltpu.CompilerParams(vmem_limit_bytes=limit),
        cost_estimate=pl.CostEstimate(flops=flops, transcendentals=0, bytes_accessed=flops // 128) if flops else None,
        name=name,
    )
    return lambda *args: run(
        *[v if i < far else pltpu.with_memory_space_constraint(v, pltpu.VMEM) for i, v in enumerate(args)]
    )


def shape(*dims):
    return jax.ShapeDtypeStruct(dims, F32)


def on_device(n_row, n_col, coupling, energies, block):
    n, k = block.shape
    group = n_row
    order = n * n_row * n_col
    rows = coupling.shape[0] * n
    width = coupling.shape[2]
    axes = ("row", "col")
    flat = [(r, c) for r in range(n_row) for c in range(n_col)]

    def send(value, to):
        pairs = [(r * n_col + c, to(r, c)) for r, c in flat]
        return lax.ppermute(value, axes, [p for p in pairs if p[1] is not None])

    def swap(value):
        return send(value, lambda r, c: r * n_col + (c ^ 1))

    def chip(r, c, s_row, s_z):
        return (r ^ s_row) * n_col + (c ^ (2 * s_z))

    def spread(s):
        def to(r, c):
            along_z = (c % 2 == 0) != (s == group - 1)
            return chip(r, c, 0, s) if along_z else chip(r, c, s, 0)

        return to

    steps = range(1, group)
    tile, parts = 256, 3
    total_pieces = group * parts
    block_shape = shape(rows // parts, 2 * n)
    most = max(len(pieces_of(p, group, n, rows // parts)) for p in range(parts))
    semaphores = lambda count: [pltpu.SemaphoreType.DMA((count, most))]
    work = rows * 2 * n * 256
    a = coupling.reshape(rows, width)
    energy = energies.reshape(1, n)

    other = swap(block.T)
    own, *held = call(
        functools.partial(begin_kernel, k, n, group, parts),
        (shape(k, n), block_shape),
        2,
        scratch=semaphores(1) + [pltpu.SemaphoreType.DMA],
        name="begin",
        far=2,
        flops=work // 4,
    )(a, block.T)
    first = call(functools.partial(order_kernel, k, n), shape(k, 2 * n), 2, name="order")(own, other)

    def products(held, pair, name):
        extra = pair.shape[1] > 2 * n
        sizes = (k, n, group, tile, parts)
        load = len(held) < total_pieces
        mine = [send(pair, spread(s)) for s in steps]
        near = held[:parts]
        new = parts + 1 - len(near) if load else 0
        u0, *fresh = call(
            functools.partial(early_kernel, *sizes, len(near), new),
            (shape(k, rows),) + (block_shape,) * new,
            load + len(near) + 1,
            scratch=[pltpu.VMEM((2 * k, 2 * n), BF16)] + (semaphores(new) if new else []),
            limit=8 << 20,
            name=name + "_early",
            far=int(load),
            flops=2 * work,
        )(*([a] if load else []), *near, pair)
        held = held + fresh
        u0, *mine = lax.optimization_barrier((u0, *mine))
        theirs = [swap(y) for y in mine]
        new = total_pieces - len(held)
        out, keep, mine_u, xr, *fresh = call(
            functools.partial(main_kernel, *sizes, len(held) - parts, new),
            (shape(group - 1, k, 2 * n), shape(group - 1, k, 2 * n), shape(k, n), jax.ShapeDtypeStruct((2 * k, rows), BF16))
            + (block_shape,) * new,
            load + len(held) - parts + 2 * group,
            scratch=[
                pltpu.VMEM((2 * k, (group - 1) * 2 * n), BF16),
                pltpu.VMEM((k, rows), F32),
                pltpu.VMEM((k, (group - 1) * 2 * n), F32),
            ]
            + (semaphores(new) if new else []),
            limit=8 << 20,
            name=name,
            far=int(load),
            flops=4 * work * (group - 1),
        )(*([a] if load else []), *held[parts:], pair, u0, *mine, *theirs)
        held = held + fresh
        got = swap(out)
        sums = call(
            functools.partial(combine_kernel, k, n, group, extra),
            (shape(k, pair.shape[1]),) * (group - 1) + ((shape(k, 8 * k),) if extra else ()),
            2 + (2 * group - 1 if extra else 0),
            name=name + "_combine",
        )(keep, got, *((pair, *mine, *theirs) if extra else ()))
        arrived = [send(sums[s - 1], spread(s)) for s in steps]
        total = call(
            functools.partial(late_kernel, *sizes, extra),
            shape(k, pair.shape[1]),
            parts + 4 + extra,
            scratch=[pltpu.VMEM((k, 2 * n), F32)],
            limit=8 << 20,
            name=name + "_late",
            flops=2 * work,
        )(*held[:parts], xr, mine_u, pair, energy, *sums[group - 1 :])
        for v in arrived:
            total = total + v
        return total, swap(total), held

    mine, got, held = products(held, first, "first")
    pair = call(functools.partial(pair_kernel, k, n), shape(k, 2 * n + 8 * k), 3, name="pair")(first, mine, got)
    mine, got, held = products(held, pair, "second")
    q, prod, moments, total, proj0, fact0 = call(
        functools.partial(second_kernel, k, n, order),
        (shape(k, 2 * n), shape(k, 2 * n), shape(3 * k, 3 * k), shape(3 * k, 3 * k), shape(k, k), shape(k, k)),
        4,
        name="middle",
    )(first, pair, mine, got)
    half = group * group // 2
    for i in range(1, half + 1):

        def to(r, c, i=i):
            s = half - 1 + i if c % 2 else i
            return None if c % 2 == 0 and i == half else chip(r, c, s // group, s % group)

        total = total + send(moments, to)
    basis, proj, fact = call(
        functools.partial(last_kernel, k, n, order),
        (shape(k, n), shape(2, k, k), shape(2, k, k)),
        7,
        name="last",
    )(first, q, prod, proj0, fact0, total, swap(total))
    return basis.T, proj, fact


def solution(mesh):
    n_row, n_col = mesh.shape["row"], mesh.shape["col"]

    def body(coupling, energies, block):
        n, k = block.shape
        paired = n_col == 2 * n_row and n_row & (n_row - 1) == 0 and n_row > 1
        divides = coupling.shape[0] * n % 768 == 0
        whole = divides and n % 64 == 0 and 8 * k == 128 and coupling.shape[2] == coupling.shape[0] * n * 2
        small = coupling.size * 4 <= 44 << 20
        if paired and whole and small:
            return on_device(n_row, n_col, coupling, energies, block)
        return generic(coupling, energies, block)

    placed = (P(None, "col", "row"), P(("row", "col")), P(("row", "col"), None))
    return jax.shard_map(
        body,
        mesh=mesh,
        in_specs=placed,
        out_specs=(P(("row", "col"), None), P(), P()),
        check_vma=False,
    )
```

time: 109 us -> 118 us (1.083)
  local copies, waits for them, and re-layouts: 0.79 us -> 13.9 us
  starting transfers between devices: 29.2 us -> 35.4 us
  waiting for transfers between devices: 19.5 us -> 13.5 us
  Pallas kernels: 58.1 us -> 54.2 us
    unnamed x4 -> x6, local copies, waits for them, and re-layouts: 0.78 us -> 13.9 us
    ppermute x29 -> x32, starting transfers between devices: 29.2 us -> 35.4 us  [send(): return lax.ppermute(value, axes, [p for p in pairs if p[1] is not None])]
    ppermute x29 -> x32, waiting for transfers between devices: 19.5 us -> 13.5 us  [send(): return lax.ppermute(value, axes, [p for p in pairs if p[1] is not None])]
    pallas_call x12 -> x13, Pallas kernels: 58.1 us -> 54.2 us  [call(): run(*[v if i < far else pltpu.with_memory_space_constraint(v, pltpu.VMEM)...]
  transfers between devices with their start and end apart: 29 -> 32, of which waited for: 20 -> 15; matrix products, arithmetic and copies ran while one was open for 0% -> 0% of each run, Pallas kernels for 15% -> 12%
where the time goes in v4:
time: 118 us
  Pallas kernels  54.2 us (46%)
  starting transfers between devices  35.4 us (30%)
  local copies, waits for them, and re-layouts  13.9 us (12%)
  waiting for transfers between devices  13.5 us (11%)
    pallas_call x13, Pallas kernels, call(): run(*[v if i < far else pltpu.with_memory_space_constraint(v, pltpu.VMEM)...  54.2 us
    ppermute x32, starting transfers between devices, send(): return lax.ppermute(value, axes, [p for p in pairs if p[1] is not None])  35.4 us
    unnamed x6, local copies, waits for them, and re-layouts  13.9 us
    ppermute x32, waiting for transfers between devices, send(): return lax.ppermute(value, axes, [p for p in pairs if p[1] is not None])  13.5 us
  transfers between devices with their start and end apart: 32, of which 15 were waited for; matrix products, arithmetic and copies ran while one was open for 0% of the time, Pallas kernels for 12%

profile of v4, /device:TPU:0, one launch (start us, length us, event | category | flops | bytes accessed | tf_op | source)
XLA Modules:
  0.0 117.9 jit_solution(17002949875546653506)
XLA Ops:
  0.6 0.6 collective-permute-start
  1.2 13.1 %copy-done = f32[4,576,4608]{2,1,0:T(8,128)S(1)} copy-done((f32[4,576,4608]{2,1,0:T(8,128)S(1)}, f32[4,576,4608]{2,1,0:T(8,128)}, u32[]{:S(2)}) %copy-start) | copy-done | bytes 42467352
  14.3 0.8 copy-done.1
  15.1 0.5 begin.1
  15.5 0.0 collective-permute-done.other_ref
  15.5 0.1 order.1.refs_2_.refs_5_.first_ref
  15.6 3.5 %collective-permute-start.3 = (f32[16,1152]{1,0:T(8,128)S(1)}, f32[16,1152]{1,0:T(8,128)S(1)}, u32[]{:S(2)}, u32[]{:S(2)}) collective-permute-start(f32[16,1152]{1,0:T(8,128)S(1)} %order.1.refs_2_.refs_5_.first_ref), channel_id=1, source_target_pairs={{0,24},{1,7},{2,26},{3,5},{4,28},{5,3},{6,30},{7,1},{8,16},{9,15},... | collective-permute-start | bytes 221192 | tf_op jit(solution)/shard_map/ppermute | solution.py:391
  19.1 2.6 %collective-permute-start.2 = (f32[16,1152]{1,0:T(8,128)S(1)}, f32[16,1152]{1,0:T(8,128)S(1)}, u32[]{:S(2)}, u32[]{:S(2)}) collective-permute-start(f32[16,1152]{1,0:T(8,128)S(1)} %order.1.refs_2_.refs_5_.first_ref), channel_id=1, source_target_pairs={{0,4},{1,17},{2,6},{3,19},{4,0},{5,21},{6,2},{7,23},{8,12},{9,25},... | collective-permute-start | bytes 221192 | tf_op jit(solution)/shard_map/ppermute | solution.py:391
  21.7 1.6 %collective-permute-start.1 = (f32[16,1152]{1,0:T(8,128)S(1)}, f32[16,1152]{1,0:T(8,128)S(1)}, u32[]{:S(2)}, u32[]{:S(2)}) collective-permute-start(f32[16,1152]{1,0:T(8,128)S(1)} %order.1.refs_2_.refs_5_.first_ref), channel_id=1, source_target_pairs={{0,2},{1,9},{2,0},{3,11},{4,6},{5,13},{6,4},{7,15},{8,10},{9,1},{1... | collective-permute-start | bytes 221192 | tf_op jit(solution)/shard_map/ppermute | solution.py:391
  23.3 4.6 %first_early.1 = (f32[16,2304]{1,0:T(8,128)S(1)}, f32[768,1152]{1,0:T(8,128)S(1)}, f32[768,1152]{1,0:T(8,128)S(1)}, f32[768,1152]{1,0:T(8,128)S(1)}) custom-call(f32[2304,4608]{1,0:T(8,128)} %bitcast.3, f32[768,1152]{1,0:T(8,128)S(1)} %get-tuple-element.50.refs_1_.refs_0_, f32[16,1152]{1,0:T(8,128)S(1)} %order.1.refs_2_.refs_5_.first_ref), custom_call_target="tpu_custom_call" | custom-call | flops 1358954496 | bytes 10616832 | tf_op jit(solution)/shard_map/first_early/pallas_call | solution.py:371
  27.9 0.0 collective-permute-done.3.refs_6_
  27.9 0.1 collective-permute-start.4
  28.0 0.5 collective-permute-start.5
  28.5 0.1 collective-permute-start.6
  28.6 0.7 collective-permute-done.4.refs_7_
  29.3 0.2 collective-permute-done.5.refs_8_
  29.4 0.4 collective-permute-done.6.refs_9_
  29.8 16.9 %first.1 = (f32[3,16,1152]{2,1,0:T(8,128)S(1)}, f32[3,16,1152]{2,1,0:T(8,128)S(1)}, f32[16,576]{1,0:T(8,128)S(1)}, bf16[32,2304]{1,0:T(8,128)(2,1)S(1)}, f32[768...) custom-call(f32[2304,4608]{1,0:T(8,128)} %bitcast.4, ...), custom_call_target="tpu_custom_call" | custom-call | flops 8153726976 | bytes 63700992 | tf_op jit(solution)/shard_map/first/pallas_call | solution.py:371
  46.7 0.2 collective-permute-start.7
  47.0 1.3 %collective-permute-done.7.got_ref = f32[3,16,1152]{2,1,0:T(8,128)S(1)} collective-permute-done((f32[3,16,1152]{2,1,0:T(8,128)S(1)}, f32[3,16,1152]{2,1,0:T(8,128)S(1)}, u32[]{:S(2)}, u32[]{:S(2)}) %collective-permute-start.7) | collective-permute-done | bytes 221216 | tf_op jit(solution)/shard_map/ppermute | solution.py:391
  48.3 0.5 collective-permute-start.8
  48.8 0.7 collective-permute-start.9
  49.6 1.3 %collective-permute-start.10 = (f32[16,1152]{1,0:T(8,128)S(1)}, f32[16,1152]{1,0:T(8,128)S(1)}, u32[]{:S(2)}, u32[]{:S(2)}) collective-permute-start(f32[16,1152]{1,0:T(8,128)S(1)} %get-tuple-element.65), channel_id=1, source_target_pairs={{0,24},{1,7},{2,26},{3,5},{4,28},{5,3},{6,30},{7,1},{8,16},{9,15},... | collective-permute-start | bytes 221192 | tf_op jit(solution)/shard_map/ppermute | solution.py:391
  50.8 2.8 %first_late.1 = f32[16,1152]{1,0:T(8,128)S(1)} custom-call(f32[768,1152]{1,0:T(8,128)S(1)} %get-tuple-element.50.refs_1_.refs_0_, f32[768,1152]{1,0:T(8,128)S(1)} %get-tuple-element.51.refs_1_, f32[768,1152]{1,0:T(8,128)S(1)} %get-tuple-element.52.refs_2_, bf16[32,2304]{1,0:T(8,128)(2,1)S(1)} %get-tuple-element.59.refs_3_, ...), custom_call_target="tpu_custom_call" | custom-call | flops 1358954496 | bytes 10616832 | tf_op jit(solution)/shard_map/first_late/pallas_call | solution.py:371
  53.7 2.0 %collective-permute-done.9 = f32[16,1152]{1,0:T(8,128)S(1)} collective-permute-done((f32[16,1152]{1,0:T(8,128)S(1)}, f32[16,1152]{1,0:T(8,128)S(1)}, u32[]{:S(2)}, u32[]{:S(2)}) %collective-permute-start.9) | collective-permute-done | bytes 73760 | tf_op jit(solution)/shard_map/ppermute | solution.py:391
  55.7 0.1 collective-permute-start.11
  55.8 1.3 %collective-permute-done.11.got_ref = f32[16,1152]{1,0:T(8,128)S(1)} collective-permute-done((f32[16,1152]{1,0:T(8,128)S(1)}, f32[16,1152]{1,0:T(8,128)S(1)}, u32[]{:S(2)}, u32[]{:S(2)}) %collective-permute-start.11) | collective-permute-done | bytes 73760 | tf_op jit(solution)/shard_map/ppermute | solution.py:391
  57.0 0.3 pair.1.refs_3_.refs_9_.refs_0_.refs_5_.pair_ref
  57.4 1.1 collective-permute-start.14
  58.4 0.8 collective-permute-start.13
  59.2 1.6 %collective-permute-start.12 = (f32[16,1280]{1,0:T(8,128)S(1)}, f32[16,1280]{1,0:T(8,128)S(1)}, u32[]{:S(2)}, u32[]{:S(2)}) collective-permute-start(f32[16,1280]{1,0:T(8,128)S(1)} %pair.1.refs_3_.refs_9_.refs_0_.refs_5_.pair_ref), channel_id=1, source_target_pairs={{0,2},{1,9},{2,0},{3,11},{4,6},{5,13},{6,4},{7,15},{8,10},{9,1},{1... | collective-permute-start | bytes 245768 | tf_op jit(solution)/shard_map/ppermute | solution.py:391
  60.8 3.8 %second_early.1.refs_10_ = f32[16,2304]{1,0:T(8,128)S(1)} custom-call(f32[768,1152]{1,0:T(8,128)S(1)} %get-tuple-element.50.refs_1_.refs_0_, f32[768,1152]{1,0:T(8,128)S(1)} %get-tuple-element.51.refs_1_, f32[768,1152]{1,0:T(8,128)S(1)} %get-tuple-element.52.refs_2_, f32[16,1280]{1,0:T(8,128)S(1)} %pair.1.refs_3_.refs_9_.refs_0_.refs_5_.pair_ref), custom_call_target="tpu_custom_call" | custom-call | flops 1358954496 | bytes 10616832 | tf_op jit(solution)/shard_map/second_early/pallas_call | solution.py:371
  64.6 0.0 collective-permute-done.14.refs_13_.refs_3_
  64.6 0.0 collective-permute-done.13.refs_12_.refs_2_
  64.7 0.0 collective-permute-done.12.refs_11_.refs_1_
  64.7 0.1 collective-permute-start.15
  64.7 0.5 collective-permute-start.16
  65.2 0.1 collective-permute-start.17
  65.3 0.7 collective-permute-done.15.refs_14_.refs_4_
  66.0 0.2 collective-permute-done.16.refs_15_.refs_5_
  66.2 0.4 collective-permute-done.17.refs_16_.refs_6_
  66.5 16.7 %second.1 = (f32[3,16,1152]{2,1,0:T(8,128)S(1)}, f32[3,16,1152]{2,1,0:T(8,128)S(1)}, f32[16,576]{1,0:T(8,128)S(1)}, bf16[32,2304]{1,0:T(8,128)(2,1)S(1)}) custom-call(f32[768,1152]{1,0:T(8,128)S(1)} %get-tuple-element.53.refs_1_.refs_0_, f32[768,1152]{1,0:T(8,128)S(1)} %get-tuple-element.66.refs_1_, f32[768,1152]{1,0:T(8,128)S(1)} %get-tuple-element.67.refs_2_, ...), custom_call_target="tpu_custom_call" | custom-call | flops 8153726976 | bytes 63700992 | tf_op jit(solution)/shard_map/second/pallas_call | solution.py:371
  83.2 0.2 collective-permute-start.18
  83.4 1.3 %collective-permute-done.18.got_ref = f32[3,16,1152]{2,1,0:T(8,128)S(1)} collective-permute-done((f32[3,16,1152]{2,1,0:T(8,128)S(1)}, f32[3,16,1152]{2,1,0:T(8,128)S(1)}, u32[]{:S(2)}, u32[]{:S(2)}) %collective-permute-start.18) | collective-permute-done | bytes 221216 | tf_op jit(solution)/shard_map/ppermute | solution.py:391
  84.8 0.6 collective-permute-start.19
  85.4 2.2 %collective-permute-start.20 = (f32[16,1280]{1,0:T(8,128)S(1)}, f32[16,1280]{1,0:T(8,128)S(1)}, u32[]{:S(2)}, u32[]{:S(2)}) collective-permute-start(f32[16,1280]{1,0:T(8,128)S(1)} %get-tuple-element.84), channel_id=1, source_target_pairs={{0,4},{1,17},{2,6},{3,19},{4,0},{5,21},{6,2},{7,23},{8,12},{9,25},... | collective-permute-start | bytes 245768 | tf_op jit(solution)/shard_map/ppermute | solution.py:391
  87.6 1.8 %collective-permute-start.21 = (f32[16,1280]{1,0:T(8,128)S(1)}, f32[16,1280]{1,0:T(8,128)S(1)}, u32[]{:S(2)}, u32[]{:S(2)}) collective-permute-start(f32[16,1280]{1,0:T(8,128)S(1)} %get-tuple-element.85), channel_id=1, source_target_pairs={{0,24},{1,7},{2,26},{3,5},{4,28},{5,3},{6,30},{7,1},{8,16},{9,15},... | collective-permute-start | bytes 245768 | tf_op jit(solution)/shard_map/ppermute | solution.py:391
  89.4 2.8 %second_late.1 = f32[16,1280]{1,0:T(8,128)S(1)} custom-call(f32[768,1152]{1,0:T(8,128)S(1)} %get-tuple-element.50.refs_1_.refs_0_, f32[768,1152]{1,0:T(8,128)S(1)} %get-tuple-element.51.refs_1_, f32[768,1152]{1,0:T(8,128)S(1)} %get-tuple-element.52.refs_2_, bf16[32,2304]{1,0:T(8,128)(2,1)S(1)} %get-tuple-element.78.refs_3_, ...), custom_call_target="tpu_custom_call" | custom-call | flops 1358954496 | bytes 10616832 | tf_op jit(solution)/shard_map/second_late/pallas_call | solution.py:371
  92.3 1.0 collective-permute-done.20
  93.2 0.1 collective-permute-start.22
  93.3 1.3 %collective-permute-done.22.got_ref = f32[16,1280]{1,0:T(8,128)S(1)} collective-permute-done((f32[16,1280]{1,0:T(8,128)S(1)}, f32[16,1280]{1,0:T(8,128)S(1)}, u32[]{:S(2)}, u32[]{:S(2)}) %collective-permute-start.22) | collective-permute-done | bytes 81952 | tf_op jit(solution)/shard_map/ppermute | solution.py:391
  94.6 2.8 %middle.1 = (f32[16,1152]{1,0:T(8,128)S(1)}, f32[16,1152]{1,0:T(8,128)S(1)}, f32[48,48]{1,0:T(8,128)S(1)}, f32[48,48]{1,0:T(8,128)S(1)}, f32[16,16]{1,0:T(8,128)S(1)}, /*index=5*/f32[16,16]{1,0:T(8,128)S(1)}) custom-call(f32[16,1152]{1,0:T(8,128)S(1)} %order.1.refs_2_.refs_5_.first_ref, f32[16,1280]{1,0:T(8,128)S(1)} %pair.1.refs_3_.refs_9_.refs_0_.refs_5_.pair_ref, ...), custom_call_target="tpu_custom_call" | custom-call | tf_op jit(solution)/shard_map/middle/pallas_call | solution.py:371
  97.4 0.7 collective-permute-start.30
  98.0 2.3 %collective-permute-start.29 = (f32[48,48]{1,0:T(8,128)S(1)}, f32[48,48]{1,0:T(8,128)S(1)}, u32[]{:S(2)}, u32[]{:S(2)}) collective-permute-start(f32[48,48]{1,0:T(8,128)S(1)} %get-tuple-element.91), channel_id=1, source_target_pairs={{0,14},{1,29},{2,12},{3,31},{4,10},{5,25},{6,8},{7,27},{8,6},{9,21... | collective-permute-start | bytes 27656 | tf_op jit(solution)/shard_map/ppermute | solution.py:391
  100.3 0.3 collective-permute-start.28
  100.6 2.8 %collective-permute-start.27 = (f32[48,48]{1,0:T(8,128)S(1)}, f32[48,48]{1,0:T(8,128)S(1)}, u32[]{:S(2)}, u32[]{:S(2)}) collective-permute-start(f32[48,48]{1,0:T(8,128)S(1)} %get-tuple-element.91), channel_id=1, source_target_pairs={{0,10},{1,25},{2,8},{3,27},{4,14},{5,29},{6,12},{7,31},{8,2},{9,17... | collective-permute-start | bytes 27656 | tf_op jit(solution)/shard_map/ppermute | solution.py:391
  103.4 1.4 %collective-permute-start.26 = (f32[48,48]{1,0:T(8,128)S(1)}, f32[48,48]{1,0:T(8,128)S(1)}, u32[]{:S(2)}, u32[]{:S(2)}) collective-permute-start(f32[48,48]{1,0:T(8,128)S(1)} %get-tuple-element.91), channel_id=1, source_target_pairs={{0,8},{1,23},{2,10},{3,21},{4,12},{5,19},{6,14},{7,17},{8,0},{9,31... | collective-permute-start | bytes 27656 | tf_op jit(solution)/shard_map/ppermute | solution.py:391
  104.9 1.7 %collective-permute-start.25 = (f32[48,48]{1,0:T(8,128)S(1)}, f32[48,48]{1,0:T(8,128)S(1)}, u32[]{:S(2)}, u32[]{:S(2)}) collective-permute-start(f32[48,48]{1,0:T(8,128)S(1)} %get-tuple-element.91), channel_id=1, source_target_pairs={{0,6},{1,21},{2,4},{3,23},{4,2},{5,17},{6,0},{7,19},{8,14},{9,29},... | collective-permute-start | bytes 27656 | tf_op jit(solution)/shard_map/ppermute | solution.py:391
  106.6 2.7 %collective-permute-start.23 = (f32[48,48]{1,0:T(8,128)S(1)}, f32[48,48]{1,0:T(8,128)S(1)}, u32[]{:S(2)}, u32[]{:S(2)}) collective-permute-start(f32[48,48]{1,0:T(8,128)S(1)} %get-tuple-element.91), channel_id=1, source_target_pairs={{0,2},{1,17},{2,0},{3,19},{4,6},{5,21},{6,4},{7,23},{8,10},{9,25},... | collective-permute-start | bytes 27656 | tf_op jit(solution)/shard_map/ppermute | solution.py:391
  109.3 1.2 %collective-permute-done.25 = f32[48,48]{1,0:T(8,128)S(1)} collective-permute-done((f32[48,48]{1,0:T(8,128)S(1)}, f32[48,48]{1,0:T(8,128)S(1)}, u32[]{:S(2)}, u32[]{:S(2)}) %collective-permute-start.25) | collective-permute-done | bytes 9248 | tf_op jit(solution)/shard_map/ppermute | solution.py:391
  110.5 0.8 collective-permute-done.24
  111.3 2.9 %collective-permute-start.31 = (f32[48,48]{1,0:T(8,128)S(1)}, f32[48,48]{1,0:T(8,128)S(1)}, u32[]{:S(2)}, u32[]{:S(2)}) collective-permute-start(f32[48,48]{1,0:T(8,128)S(1)} %add_add_fusion.2.mine_ref), channel_id=1, source_target_pairs={{0,1},{1,0},{2,3},{3,2},{4,5},{5,4},{6,7},{7,6},{8,9},{9,8},{10,11... | collective-permute-start | bytes 27656 | tf_op jit(solution)/shard_map/ppermute | solution.py:391
  114.2 0.8 collective-permute-done.31.got_ref
  115.0 2.8 %last.1 = (f32[16,576]{1,0:T(8,128)}, f32[2,16,16]{2,1,0:T(8,128)}, f32[2,16,16]{2,1,0:T(8,128)}) custom-call(f32[16,1152]{1,0:T(8,128)S(1)} %order.1.refs_2_.refs_5_.first_ref, f32[16,1152]{1,0:T(8,128)S(1)} %get-tuple-element.86.q_ref, f32[16,1152]{1,0:T(8,128)S(1)} %get-tuple-element.87.prod_ref, f32[16,16]{1,0:T(8,128)S(1)} %get-tuple-element.88.proj0_ref, ...), custom_call_target="tpu_custom_call" | custom-call | tf_op jit(solution)/shard_map/last/pallas_call | solution.py:371
  (23 shorter events, 0.2 us)
Async XLA Ops:
  0.6 14.9 %collective-permute-start = (f32[16,576]{1,0:T(8,128)}, f32[16,576]{1,0:T(8,128)S(1)}, u32[]{:S(2)}, u32[]{:S(2)}) collective-permute-start(f32[16,576]{1,0:T(8,128)} %bitcast.6), channel_id=1, source_target_pairs={{0,1},{1,0},{2,3},{3,2},{4,5},{5,4},{6,7},{7,6},{8,9},{9,8},{10,11... | collective-permute-start | bytes 110600 | tf_op jit(solution)/shard_map/ppermute | solution.py:391
  1.2 13.1 %copy-start = (f32[4,576,4608]{2,1,0:T(8,128)S(1)}, f32[4,576,4608]{2,1,0:T(8,128)}, u32[]{:S(2)}) copy-start(f32[4,576,4608]{2,1,0:T(8,128)} %param.3) | copy-start | bytes 127401984
  14.3 0.8 copy-start.1
  15.6 12.3 %collective-permute-start.3 = (f32[16,1152]{1,0:T(8,128)S(1)}, f32[16,1152]{1,0:T(8,128)S(1)}, u32[]{:S(2)}, u32[]{:S(2)}) collective-permute-start(f32[16,1152]{1,0:T(8,128)S(1)} %order.1.refs_2_.refs_5_.first_ref), channel_id=1, source_target_pairs={{0,24},{1,7},{2,26},{3,5},{4,28},{5,3},{6,30},{7,1},{8,16},{9,15},... | collective-permute-start | bytes 221192 | tf_op jit(solution)/shard_map/ppermute | solution.py:391
  19.1 8.8 %collective-permute-start.2 = (f32[16,1152]{1,0:T(8,128)S(1)}, f32[16,1152]{1,0:T(8,128)S(1)}, u32[]{:S(2)}, u32[]{:S(2)}) collective-permute-start(f32[16,1152]{1,0:T(8,128)S(1)} %order.1.refs_2_.refs_5_.first_ref), channel_id=1, source_target_pairs={{0,4},{1,17},{2,6},{3,19},{4,0},{5,21},{6,2},{7,23},{8,12},{9,25},... | collective-permute-start | bytes 221192 | tf_op jit(solution)/shard_map/ppermute | solution.py:391
  21.7 6.2 %collective-permute-start.1 = (f32[16,1152]{1,0:T(8,128)S(1)}, f32[16,1152]{1,0:T(8,128)S(1)}, u32[]{:S(2)}, u32[]{:S(2)}) collective-permute-start(f32[16,1152]{1,0:T(8,128)S(1)} %order.1.refs_2_.refs_5_.first_ref), channel_id=1, source_target_pairs={{0,2},{1,9},{2,0},{3,11},{4,6},{5,13},{6,4},{7,15},{8,10},{9,1},{1... | collective-permute-start | bytes 221192 | tf_op jit(solution)/shard_map/ppermute | solution.py:391
  27.9 1.3 %collective-permute-start.4 = (f32[16,1152]{1,0:T(8,128)S(1)}, f32[16,1152]{1,0:T(8,128)S(1)}, u32[]{:S(2)}, u32[]{:S(2)}) collective-permute-start(f32[16,1152]{1,0:T(8,128)S(1)} %collective-permute-done.1.refs_4_), channel_id=1, source_target_pairs={{0,1},{1,0},{2,3},{3,2},{4,5},{5,4},{6,7},{7,6},{8,9},{9,8},{10,11... | collective-permute-start | bytes 221192 | tf_op jit(solution)/shard_map/ppermute | solution.py:391
  28.0 1.4 %collective-permute-start.5 = (f32[16,1152]{1,0:T(8,128)S(1)}, f32[16,1152]{1,0:T(8,128)S(1)}, u32[]{:S(2)}, u32[]{:S(2)}) collective-permute-start(f32[16,1152]{1,0:T(8,128)S(1)} %collective-permute-done.2.refs_5_), channel_id=1, source_target_pairs={{0,1},{1,0},{2,3},{3,2},{4,5},{5,4},{6,7},{7,6},{8,9},{9,8},{10,11... | collective-permute-start | bytes 221192 | tf_op jit(solution)/shard_map/ppermute | solution.py:391
  28.5 1.3 %collective-permute-start.6 = (f32[16,1152]{1,0:T(8,128)S(1)}, f32[16,1152]{1,0:T(8,128)S(1)}, u32[]{:S(2)}, u32[]{:S(2)}) collective-permute-start(f32[16,1152]{1,0:T(8,128)S(1)} %collective-permute-done.3.refs_6_), channel_id=1, source_target_pairs={{0,1},{1,0},{2,3},{3,2},{4,5},{5,4},{6,7},{7,6},{8,9},{9,8},{10,11... | collective-permute-start | bytes 221192 | tf_op jit(solution)/shard_map/ppermute | solution.py:391
  29.8 17.2 %copy-start.2 = (f32[576]{0:T(1024)S(1)}, f32[576]{0:T(1024)}, u32[]{:S(2)}) copy-start(f32[576]{0:T(1024)} %param.4) | copy-start | bytes 6916
  46.7 1.5 %collective-permute-start.7 = (f32[3,16,1152]{2,1,0:T(8,128)S(1)}, f32[3,16,1152]{2,1,0:T(8,128)S(1)}, u32[]{:S(2)}, u32[]{:S(2)}) collective-permute-start(f32[3,16,1152]{2,1,0:T(8,128)S(1)} %get-tuple-element.62), channel_id=1, source_target_pairs={{0,1},{1,0},{2,3},{3,2},{4,5},{5,4},{6,7},{7,6},{8,9},{9,8},{10,11... | collective-permute-start | bytes 663560 | tf_op jit(solution)/shard_map/ppermute | solution.py:391
  48.3 5.4 %collective-permute-start.8 = (f32[16,1152]{1,0:T(8,128)S(1)}, f32[16,1152]{1,0:T(8,128)S(1)}, u32[]{:S(2)}, u32[]{:S(2)}) collective-permute-start(f32[16,1152]{1,0:T(8,128)S(1)} %get-tuple-element.63), channel_id=1, source_target_pairs={{0,2},{1,9},{2,0},{3,11},{4,6},{5,13},{6,4},{7,15},{8,10},{9,1},{1... | collective-permute-start | bytes 221192 | tf_op jit(solution)/shard_map/ppermute | solution.py:391
  48.8 6.8 %collective-permute-start.9 = (f32[16,1152]{1,0:T(8,128)S(1)}, f32[16,1152]{1,0:T(8,128)S(1)}, u32[]{:S(2)}, u32[]{:S(2)}) collective-permute-start(f32[16,1152]{1,0:T(8,128)S(1)} %get-tuple-element.64), channel_id=1, source_target_pairs={{0,4},{1,17},{2,6},{3,19},{4,0},{5,21},{6,2},{7,23},{8,12},{9,25},... | collective-permute-start | bytes 221192 | tf_op jit(solution)/shard_map/ppermute | solution.py:391
  49.6 6.1 %collective-permute-start.10 = (f32[16,1152]{1,0:T(8,128)S(1)}, f32[16,1152]{1,0:T(8,128)S(1)}, u32[]{:S(2)}, u32[]{:S(2)}) collective-permute-start(f32[16,1152]{1,0:T(8,128)S(1)} %get-tuple-element.65), channel_id=1, source_target_pairs={{0,24},{1,7},{2,26},{3,5},{4,28},{5,3},{6,30},{7,1},{8,16},{9,15},... | collective-permute-start | bytes 221192 | tf_op jit(solution)/shard_map/ppermute | solution.py:391
  55.7 1.3 %collective-permute-start.11 = (f32[16,1152]{1,0:T(8,128)S(1)}, f32[16,1152]{1,0:T(8,128)S(1)}, u32[]{:S(2)}, u32[]{:S(2)}) collective-permute-start(f32[16,1152]{1,0:T(8,128)S(1)} %add_add_fusion.1.mine_ref), channel_id=1, source_target_pairs={{0,1},{1,0},{2,3},{3,2},{4,5},{5,4},{6,7},{7,6},{8,9},{9,8},{10,11... | collective-permute-start | bytes 221192 | tf_op jit(solution)/shard_map/ppermute | solution.py:391
  57.4 7.3 %collective-permute-start.14 = (f32[16,1280]{1,0:T(8,128)S(1)}, f32[16,1280]{1,0:T(8,128)S(1)}, u32[]{:S(2)}, u32[]{:S(2)}) collective-permute-start(f32[16,1280]{1,0:T(8,128)S(1)} %pair.1.refs_3_.refs_9_.refs_0_.refs_5_.pair_ref), channel_id=1, source_target_pairs={{0,24},{1,7},{2,26},{3,5},{4,28},{5,3},{6,30},{7,1},{8,16},{9,15},... | collective-permute-start | bytes 245768 | tf_op jit(solution)/shard_map/ppermute | solution.py:391
  58.4 6.2 %collective-permute-start.13 = (f32[16,1280]{1,0:T(8,128)S(1)}, f32[16,1280]{1,0:T(8,128)S(1)}, u32[]{:S(2)}, u32[]{:S(2)}) collective-permute-start(f32[16,1280]{1,0:T(8,128)S(1)} %pair.1.refs_3_.refs_9_.refs_0_.refs_5_.pair_ref), channel_id=1, source_target_pairs={{0,4},{1,17},{2,6},{3,19},{4,0},{5,21},{6,2},{7,23},{8,12},{9,25},... | collective-permute-start | bytes 245768 | tf_op jit(solution)/shard_map/ppermute | solution.py:391
  59.2 5.4 %collective-permute-start.12 = (f32[16,1280]{1,0:T(8,128)S(1)}, f32[16,1280]{1,0:T(8,128)S(1)}, u32[]{:S(2)}, u32[]{:S(2)}) collective-permute-start(f32[16,1280]{1,0:T(8,128)S(1)} %pair.1.refs_3_.refs_9_.refs_0_.refs_5_.pair_ref), channel_id=1, source_target_pairs={{0,2},{1,9},{2,0},{3,11},{4,6},{5,13},{6,4},{7,15},{8,10},{9,1},{1... | collective-permute-start | bytes 245768 | tf_op jit(solution)/shard_map/ppermute | solution.py:391
  64.7 1.3 %collective-permute-start.15 = (f32[16,1280]{1,0:T(8,128)S(1)}, f32[16,1280]{1,0:T(8,128)S(1)}, u32[]{:S(2)}, u32[]{:S(2)}) collective-permute-start(f32[16,1280]{1,0:T(8,128)S(1)} %collective-permute-done.12.refs_11_.refs_1_), channel_id=1, source_target_pairs={{0,1},{1,0},{2,3},{3,2},{4,5},{5,4},{6,7},{7,6},{8,9},{9,8},{10,11... | collective-permute-start | bytes 245768 | tf_op jit(solution)/shard_map/ppermute | solution.py:391
  64.7 1.4 %collective-permute-start.16 = (f32[16,1280]{1,0:T(8,128)S(1)}, f32[16,1280]{1,0:T(8,128)S(1)}, u32[]{:S(2)}, u32[]{:S(2)}) collective-permute-start(f32[16,1280]{1,0:T(8,128)S(1)} %collective-permute-done.13.refs_12_.refs_2_), channel_id=1, source_target_pairs={{0,1},{1,0},{2,3},{3,2},{4,5},{5,4},{6,7},{7,6},{8,9},{9,8},{10,11... | collective-permute-start | bytes 245768 | tf_op jit(solution)/shard_map/ppermute | solution.py:391
  65.2 1.3 %collective-permute-start.17 = (f32[16,1280]{1,0:T(8,128)S(1)}, f32[16,1280]{1,0:T(8,128)S(1)}, u32[]{:S(2)}, u32[]{:S(2)}) collective-permute-start(f32[16,1280]{1,0:T(8,128)S(1)} %collective-permute-done.14.refs_13_.refs_3_), channel_id=1, source_target_pairs={{0,1},{1,0},{2,3},{3,2},{4,5},{5,4},{6,7},{7,6},{8,9},{9,8},{10,11... | collective-permute-start | bytes 245768 | tf_op jit(solution)/shard_map/ppermute | solution.py:391
  83.2 1.5 %collective-permute-start.18 = (f32[3,16,1152]{2,1,0:T(8,128)S(1)}, f32[3,16,1152]{2,1,0:T(8,128)S(1)}, u32[]{:S(2)}, u32[]{:S(2)}) collective-permute-start(f32[3,16,1152]{2,1,0:T(8,128)S(1)} %get-tuple-element.81), channel_id=1, source_target_pairs={{0,1},{1,0},{2,3},{3,2},{4,5},{5,4},{6,7},{7,6},{8,9},{9,8},{10,11... | collective-permute-start | bytes 663560 | tf_op jit(solution)/shard_map/ppermute | solution.py:391
  84.8 7.5 %collective-permute-start.19 = (f32[16,1280]{1,0:T(8,128)S(1)}, f32[16,1280]{1,0:T(8,128)S(1)}, u32[]{:S(2)}, u32[]{:S(2)}) collective-permute-start(f32[16,1280]{1,0:T(8,128)S(1)} %get-tuple-element.83), channel_id=1, source_target_pairs={{0,2},{1,9},{2,0},{3,11},{4,6},{5,13},{6,4},{7,15},{8,10},{9,1},{1... | collective-permute-start | bytes 245768 | tf_op jit(solution)/shard_map/ppermute | solution.py:391
  85.4 7.8 %collective-permute-start.20 = (f32[16,1280]{1,0:T(8,128)S(1)}, f32[16,1280]{1,0:T(8,128)S(1)}, u32[]{:S(2)}, u32[]{:S(2)}) collective-permute-start(f32[16,1280]{1,0:T(8,128)S(1)} %get-tuple-element.84), channel_id=1, source_target_pairs={{0,4},{1,17},{2,6},{3,19},{4,0},{5,21},{6,2},{7,23},{8,12},{9,25},... | collective-permute-start | bytes 245768 | tf_op jit(solution)/shard_map/ppermute | solution.py:391
  87.6 5.6 %collective-permute-start.21 = (f32[16,1280]{1,0:T(8,128)S(1)}, f32[16,1280]{1,0:T(8,128)S(1)}, u32[]{:S(2)}, u32[]{:S(2)}) collective-permute-start(f32[16,1280]{1,0:T(8,128)S(1)} %get-tuple-element.85), channel_id=1, source_target_pairs={{0,24},{1,7},{2,26},{3,5},{4,28},{5,3},{6,30},{7,1},{8,16},{9,15},... | collective-permute-start | bytes 245768 | tf_op jit(solution)/shard_map/ppermute | solution.py:391
  93.2 1.3 %collective-permute-start.22 = (f32[16,1280]{1,0:T(8,128)S(1)}, f32[16,1280]{1,0:T(8,128)S(1)}, u32[]{:S(2)}, u32[]{:S(2)}) collective-permute-start(f32[16,1280]{1,0:T(8,128)S(1)} %add_add_fusion.mine_ref), channel_id=1, source_target_pairs={{0,1},{1,0},{2,3},{3,2},{4,5},{5,4},{6,7},{7,6},{8,9},{9,8},{10,11... | collective-permute-start | bytes 245768 | tf_op jit(solution)/shard_map/ppermute | solution.py:391
  97.4 7.5 %collective-permute-start.30 = (f32[48,48]{1,0:T(8,128)S(1)}, f32[48,48]{1,0:T(8,128)S(1)}, u32[]{:S(2)}, u32[]{:S(2)}) collective-permute-start(f32[48,48]{1,0:T(8,128)S(1)} %get-tuple-element.91), channel_id=1, source_target_pairs={{1,31},{3,29},{5,27},{7,25},{9,23},{11,21},{13,19},{15,17},{17,15}... | collective-permute-start | bytes 27656 | tf_op jit(solution)/shard_map/ppermute | solution.py:391
  98.0 8.5 %collective-permute-start.29 = (f32[48,48]{1,0:T(8,128)S(1)}, f32[48,48]{1,0:T(8,128)S(1)}, u32[]{:S(2)}, u32[]{:S(2)}) collective-permute-start(f32[48,48]{1,0:T(8,128)S(1)} %get-tuple-element.91), channel_id=1, source_target_pairs={{0,14},{1,29},{2,12},{3,31},{4,10},{5,25},{6,8},{7,27},{8,6},{9,21... | collective-permute-start | bytes 27656 | tf_op jit(solution)/shard_map/ppermute | solution.py:391
  100.3 6.3 %collective-permute-start.28 = (f32[48,48]{1,0:T(8,128)S(1)}, f32[48,48]{1,0:T(8,128)S(1)}, u32[]{:S(2)}, u32[]{:S(2)}) collective-permute-start(f32[48,48]{1,0:T(8,128)S(1)} %get-tuple-element.91), channel_id=1, source_target_pairs={{0,12},{1,27},{2,14},{3,25},{4,8},{5,31},{6,10},{7,29},{8,4},{9,19... | collective-permute-start | bytes 27656 | tf_op jit(solution)/shard_map/ppermute | solution.py:391
  100.6 8.6 %collective-permute-start.27 = (f32[48,48]{1,0:T(8,128)S(1)}, f32[48,48]{1,0:T(8,128)S(1)}, u32[]{:S(2)}, u32[]{:S(2)}) collective-permute-start(f32[48,48]{1,0:T(8,128)S(1)} %get-tuple-element.91), channel_id=1, source_target_pairs={{0,10},{1,25},{2,8},{3,27},{4,14},{5,29},{6,12},{7,31},{8,2},{9,17... | collective-permute-start | bytes 27656 | tf_op jit(solution)/shard_map/ppermute | solution.py:391
  103.4 5.8 %collective-permute-start.26 = (f32[48,48]{1,0:T(8,128)S(1)}, f32[48,48]{1,0:T(8,128)S(1)}, u32[]{:S(2)}, u32[]{:S(2)}) collective-permute-start(f32[48,48]{1,0:T(8,128)S(1)} %get-tuple-element.91), channel_id=1, source_target_pairs={{0,8},{1,23},{2,10},{3,21},{4,12},{5,19},{6,14},{7,17},{8,0},{9,31... | collective-permute-start | bytes 27656 | tf_op jit(solution)/shard_map/ppermute | solution.py:391
  104.9 5.6 %collective-permute-start.25 = (f32[48,48]{1,0:T(8,128)S(1)}, f32[48,48]{1,0:T(8,128)S(1)}, u32[]{:S(2)}, u32[]{:S(2)}) collective-permute-start(f32[48,48]{1,0:T(8,128)S(1)} %get-tuple-element.91), channel_id=1, source_target_pairs={{0,6},{1,21},{2,4},{3,23},{4,2},{5,17},{6,0},{7,19},{8,14},{9,29},... | collective-permute-start | bytes 27656 | tf_op jit(solution)/shard_map/ppermute | solution.py:391
  106.6 4.7 %collective-permute-start.24 = (f32[48,48]{1,0:T(8,128)S(1)}, f32[48,48]{1,0:T(8,128)S(1)}, u32[]{:S(2)}, u32[]{:S(2)}) collective-permute-start(f32[48,48]{1,0:T(8,128)S(1)} %get-tuple-element.91), channel_id=1, source_target_pairs={{0,4},{1,19},{2,6},{3,17},{4,0},{5,23},{6,2},{7,21},{8,12},{9,27},... | collective-permute-start | bytes 27656 | tf_op jit(solution)/shard_map/ppermute | solution.py:391
  106.6 4.7 %collective-permute-start.23 = (f32[48,48]{1,0:T(8,128)S(1)}, f32[48,48]{1,0:T(8,128)S(1)}, u32[]{:S(2)}, u32[]{:S(2)}) collective-permute-start(f32[48,48]{1,0:T(8,128)S(1)} %get-tuple-element.91), channel_id=1, source_target_pairs={{0,2},{1,17},{2,0},{3,19},{4,6},{5,21},{6,4},{7,23},{8,10},{9,25},... | collective-permute-start | bytes 27656 | tf_op jit(solution)/shard_map/ppermute | solution.py:391
  111.3 3.7 %collective-permute-start.31 = (f32[48,48]{1,0:T(8,128)S(1)}, f32[48,48]{1,0:T(8,128)S(1)}, u32[]{:S(2)}, u32[]{:S(2)}) collective-permute-start(f32[48,48]{1,0:T(8,128)S(1)} %add_add_fusion.2.mine_ref), channel_id=1, source_target_pairs={{0,1},{1,0},{2,3},{3,2},{4,5},{5,4},{6,7},{7,6},{8,9},{9,8},{10,11... | collective-permute-start | bytes 27656 | tf_op jit(solution)/shard_map/ppermute | solution.py:391

commit v5 on v4

--- a/solution.py
+++ b/solution.py
@@ -369,7 +369,7 @@
         name=name,
     )
     return lambda *args: run(
-        *[v if i < far else pltpu.with_memory_space_constraint(v, pltpu.VMEM) for i, v in enumerate(args)]
+        *[pltpu.with_memory_space_constraint(v, pltpu.HBM if i < far else pltpu.VMEM) for i, v in enumerate(args)]
     )
 
 

time: 118 us -> 106 us (0.90)
  local copies, waits for them, and re-layouts: 13.9 us -> 0.01 us
  Pallas kernels: 54.2 us -> 56.5 us
    unnamed x6 -> x2, local copies, waits for them, and re-layouts: 13.9 us -> 0.01 us
    pallas_call x13, Pallas kernels: 54.2 us -> 56.5 us  [call(): run(*[pltpu.with_memory_space_constraint(v, pltpu.HBM if i < far else plt...]
  transfers between devices with their start and end apart: 32 -> 32, of which waited for: 15 -> 16; matrix products, arithmetic and copies ran while one was open for 0% -> 0% of each run, Pallas kernels for 12% -> 16%
where the time goes in v5:
time: 106 us
  Pallas kernels  56.5 us (53%)
  starting transfers between devices  35 us (33%)
  waiting for transfers between devices  13.5 us (13%)
    pallas_call x13, Pallas kernels, call(): run(*[pltpu.with_memory_space_constraint(v, pltpu.HBM if i < far else plt...  56.5 us
    ppermute x32, starting transfers between devices, send(): return lax.ppermute(value, axes, [p for p in pairs if p[1] is not None])  35 us
    ppermute x32, waiting for transfers between devices, send(): return lax.ppermute(value, axes, [p for p in pairs if p[1] is not None])  13.5 us
  transfers between devices with their start and end apart: 32, of which 16 were waited for; matrix products, arithmetic and copies ran while one was open for 0% of the time, Pallas kernels for 16%

profile of v5, /device:TPU:0, one launch (start us, length us, event | category | flops | bytes accessed | tf_op | source)
XLA Modules:
  0.0 105.8 jit_solution(16957222454892416461)
XLA Ops:
  0.6 0.6 collective-permute-start
  1.2 2.0 %begin.1 = (f32[16,576]{1,0:T(8,128)S(1)}, f32[768,1152]{1,0:T(8,128)S(1)}) custom-call(f32[2304,4608]{1,0:T(8,128)} %bitcast.3, f32[16,576]{1,0:T(8,128)} %bitcast.7), custom_call_target="tpu_custom_call" | custom-call | flops 169869312 | bytes 1327104 | tf_op jit(solution)/shard_map/begin/pallas_call | solution.py:371
  3.2 0.0 collective-permute-done.other_ref
  3.2 0.1 order.1.refs_2_.refs_5_.first_ref
  3.3 3.5 %collective-permute-start.3 = (f32[16,1152]{1,0:T(8,128)S(1)}, f32[16,1152]{1,0:T(8,128)S(1)}, u32[]{:S(2)}, u32[]{:S(2)}) collective-permute-start(f32[16,1152]{1,0:T(8,128)S(1)} %order.1.refs_2_.refs_5_.first_ref), channel_id=1, source_target_pairs={{0,24},{1,7},{2,26},{3,5},{4,28},{5,3},{6,30},{7,1},{8,16},{9,15},... | collective-permute-start | bytes 221192 | tf_op jit(solution)/shard_map/ppermute | solution.py:391
  6.8 2.6 %collective-permute-start.2 = (f32[16,1152]{1,0:T(8,128)S(1)}, f32[16,1152]{1,0:T(8,128)S(1)}, u32[]{:S(2)}, u32[]{:S(2)}) collective-permute-start(f32[16,1152]{1,0:T(8,128)S(1)} %order.1.refs_2_.refs_5_.first_ref), channel_id=1, source_target_pairs={{0,4},{1,17},{2,6},{3,19},{4,0},{5,21},{6,2},{7,23},{8,12},{9,25},... | collective-permute-start | bytes 221192 | tf_op jit(solution)/shard_map/ppermute | solution.py:391
  9.4 1.6 %collective-permute-start.1 = (f32[16,1152]{1,0:T(8,128)S(1)}, f32[16,1152]{1,0:T(8,128)S(1)}, u32[]{:S(2)}, u32[]{:S(2)}) collective-permute-start(f32[16,1152]{1,0:T(8,128)S(1)} %order.1.refs_2_.refs_5_.first_ref), channel_id=1, source_target_pairs={{0,2},{1,9},{2,0},{3,11},{4,6},{5,13},{6,4},{7,15},{8,10},{9,1},{1... | collective-permute-start | bytes 221192 | tf_op jit(solution)/shard_map/ppermute | solution.py:391
  11.0 4.6 %first_early.1 = (f32[16,2304]{1,0:T(8,128)S(1)}, f32[768,1152]{1,0:T(8,128)S(1)}, f32[768,1152]{1,0:T(8,128)S(1)}, f32[768,1152]{1,0:T(8,128)S(1)}) custom-call(f32[2304,4608]{1,0:T(8,128)} %bitcast.4, f32[768,1152]{1,0:T(8,128)S(1)} %get-tuple-element.50.refs_1_.refs_0_, f32[16,1152]{1,0:T(8,128)S(1)} %order.1.refs_2_.refs_5_.first_ref), custom_call_target="tpu_custom_call" | custom-call | flops 1358954496 | bytes 10616832 | tf_op jit(solution)/shard_map/first_early/pallas_call | solution.py:371
  15.6 0.0 collective-permute-done.3.refs_6_
  15.6 0.0 collective-permute-done.2.refs_5_
  15.6 0.1 collective-permute-start.4
  15.7 0.5 collective-permute-start.5
  16.2 0.1 collective-permute-start.6
  16.3 0.7 collective-permute-done.4.refs_7_
  17.0 0.2 collective-permute-done.5.refs_8_
  17.1 0.4 collective-permute-done.6.refs_9_
  17.5 17.0 %first.1 = (f32[3,16,1152]{2,1,0:T(8,128)S(1)}, f32[3,16,1152]{2,1,0:T(8,128)S(1)}, f32[16,576]{1,0:T(8,128)S(1)}, bf16[32,2304]{1,0:T(8,128)(2,1)S(1)}, f32[768...) custom-call(f32[2304,4608]{1,0:T(8,128)} %bitcast.5, ...), custom_call_target="tpu_custom_call" | custom-call | flops 8153726976 | bytes 63700992 | tf_op jit(solution)/shard_map/first/pallas_call | solution.py:371
  34.5 0.2 collective-permute-start.7
  34.7 1.3 %collective-permute-done.7.got_ref = f32[3,16,1152]{2,1,0:T(8,128)S(1)} collective-permute-done((f32[3,16,1152]{2,1,0:T(8,128)S(1)}, f32[3,16,1152]{2,1,0:T(8,128)S(1)}, u32[]{:S(2)}, u32[]{:S(2)}) %collective-permute-start.7) | collective-permute-done | bytes 221216 | tf_op jit(solution)/shard_map/ppermute | solution.py:391
  36.1 0.5 collective-permute-start.8
  36.6 0.7 collective-permute-start.9
  37.3 1.3 %collective-permute-start.10 = (f32[16,1152]{1,0:T(8,128)S(1)}, f32[16,1152]{1,0:T(8,128)S(1)}, u32[]{:S(2)}, u32[]{:S(2)}) collective-permute-start(f32[16,1152]{1,0:T(8,128)S(1)} %get-tuple-element.65), channel_id=1, source_target_pairs={{0,24},{1,7},{2,26},{3,5},{4,28},{5,3},{6,30},{7,1},{8,16},{9,15},... | collective-permute-start | bytes 221192 | tf_op jit(solution)/shard_map/ppermute | solution.py:391
  38.6 3.1 %first_late.1 = f32[16,1152]{1,0:T(8,128)S(1)} custom-call(f32[768,1152]{1,0:T(8,128)S(1)} %get-tuple-element.50.refs_1_.refs_0_, f32[768,1152]{1,0:T(8,128)S(1)} %get-tuple-element.51.refs_1_, f32[768,1152]{1,0:T(8,128)S(1)} %get-tuple-element.52.refs_2_, bf16[32,2304]{1,0:T(8,128)(2,1)S(1)} %get-tuple-element.59.refs_3_, ...), custom_call_target="tpu_custom_call" | custom-call | flops 1358954496 | bytes 10616832 | tf_op jit(solution)/shard_map/first_late/pallas_call | solution.py:371
  41.7 0.0 collective-permute-done.8
  41.7 1.7 %collective-permute-done.9 = f32[16,1152]{1,0:T(8,128)S(1)} collective-permute-done((f32[16,1152]{1,0:T(8,128)S(1)}, f32[16,1152]{1,0:T(8,128)S(1)}, u32[]{:S(2)}, u32[]{:S(2)}) %collective-permute-start.9) | collective-permute-done | bytes 73760 | tf_op jit(solution)/shard_map/ppermute | solution.py:391
  43.5 0.1 collective-permute-start.11
  43.5 1.3 %collective-permute-done.11.got_ref = f32[16,1152]{1,0:T(8,128)S(1)} collective-permute-done((f32[16,1152]{1,0:T(8,128)S(1)}, f32[16,1152]{1,0:T(8,128)S(1)}, u32[]{:S(2)}, u32[]{:S(2)}) %collective-permute-start.11) | collective-permute-done | bytes 73760 | tf_op jit(solution)/shard_map/ppermute | solution.py:391
  44.8 0.3 pair.1.refs_3_.refs_9_.refs_0_.refs_5_.pair_ref
  45.1 1.1 %collective-permute-start.14 = (f32[16,1280]{1,0:T(8,128)S(1)}, f32[16,1280]{1,0:T(8,128)S(1)}, u32[]{:S(2)}, u32[]{:S(2)}) collective-permute-start(f32[16,1280]{1,0:T(8,128)S(1)} %pair.1.refs_3_.refs_9_.refs_0_.refs_5_.pair_ref), channel_id=1, source_target_pairs={{0,24},{1,7},{2,26},{3,5},{4,28},{5,3},{6,30},{7,1},{8,16},{9,15},... | collective-permute-start | bytes 245768 | tf_op jit(solution)/shard_map/ppermute | solution.py:391
  46.2 1.0 collective-permute-start.13
  47.3 1.6 %collective-permute-start.12 = (f32[16,1280]{1,0:T(8,128)S(1)}, f32[16,1280]{1,0:T(8,128)S(1)}, u32[]{:S(2)}, u32[]{:S(2)}) collective-permute-start(f32[16,1280]{1,0:T(8,128)S(1)} %pair.1.refs_3_.refs_9_.refs_0_.refs_5_.pair_ref), channel_id=1, source_target_pairs={{0,2},{1,9},{2,0},{3,11},{4,6},{5,13},{6,4},{7,15},{8,10},{9,1},{1... | collective-permute-start | bytes 245768 | tf_op jit(solution)/shard_map/ppermute | solution.py:391
  48.8 3.8 %second_early.1.refs_10_ = f32[16,2304]{1,0:T(8,128)S(1)} custom-call(f32[768,1152]{1,0:T(8,128)S(1)} %get-tuple-element.50.refs_1_.refs_0_, f32[768,1152]{1,0:T(8,128)S(1)} %get-tuple-element.51.refs_1_, f32[768,1152]{1,0:T(8,128)S(1)} %get-tuple-element.52.refs_2_, f32[16,1280]{1,0:T(8,128)S(1)} %pair.1.refs_3_.refs_9_.refs_0_.refs_5_.pair_ref), custom_call_target="tpu_custom_call" | custom-call | flops 1358954496 | bytes 10616832 | tf_op jit(solution)/shard_map/second_early/pallas_call | solution.py:371
  52.6 0.0 collective-permute-done.14.refs_13_.refs_3_
  52.7 0.0 collective-permute-done.13.refs_12_.refs_2_
  52.7 0.1 collective-permute-start.15
  52.8 0.5 collective-permute-start.16
  53.3 0.1 collective-permute-start.17
  53.4 0.7 collective-permute-done.15.refs_14_.refs_4_
  54.0 0.2 collective-permute-done.16.refs_15_.refs_5_
  54.2 0.4 collective-permute-done.17.refs_16_.refs_6_
  54.6 16.8 %second.1 = (f32[3,16,1152]{2,1,0:T(8,128)S(1)}, f32[3,16,1152]{2,1,0:T(8,128)S(1)}, f32[16,576]{1,0:T(8,128)S(1)}, bf16[32,2304]{1,0:T(8,128)(2,1)S(1)}) custom-call(f32[768,1152]{1,0:T(8,128)S(1)} %get-tuple-element.53.refs_1_.refs_0_, f32[768,1152]{1,0:T(8,128)S(1)} %get-tuple-element.66.refs_1_, f32[768,1152]{1,0:T(8,128)S(1)} %get-tuple-element.67.refs_2_, ...), custom_call_target="tpu_custom_call" | custom-call | flops 8153726976 | bytes 63700992 | tf_op jit(solution)/shard_map/second/pallas_call | solution.py:371
  71.4 0.2 collective-permute-start.18
  71.6 1.3 %collective-permute-done.18.got_ref = f32[3,16,1152]{2,1,0:T(8,128)S(1)} collective-permute-done((f32[3,16,1152]{2,1,0:T(8,128)S(1)}, f32[3,16,1152]{2,1,0:T(8,128)S(1)}, u32[]{:S(2)}, u32[]{:S(2)}) %collective-permute-start.18) | collective-permute-done | bytes 221216 | tf_op jit(solution)/shard_map/ppermute | solution.py:391
  72.9 0.6 collective-permute-start.19
  73.5 2.0 %collective-permute-start.20 = (f32[16,1280]{1,0:T(8,128)S(1)}, f32[16,1280]{1,0:T(8,128)S(1)}, u32[]{:S(2)}, u32[]{:S(2)}) collective-permute-start(f32[16,1280]{1,0:T(8,128)S(1)} %get-tuple-element.84), channel_id=1, source_target_pairs={{0,4},{1,17},{2,6},{3,19},{4,0},{5,21},{6,2},{7,23},{8,12},{9,25},... | collective-permute-start | bytes 245768 | tf_op jit(solution)/shard_map/ppermute | solution.py:391
  75.5 1.8 %collective-permute-start.21 = (f32[16,1280]{1,0:T(8,128)S(1)}, f32[16,1280]{1,0:T(8,128)S(1)}, u32[]{:S(2)}, u32[]{:S(2)}) collective-permute-start(f32[16,1280]{1,0:T(8,128)S(1)} %get-tuple-element.85), channel_id=1, source_target_pairs={{0,24},{1,7},{2,26},{3,5},{4,28},{5,3},{6,30},{7,1},{8,16},{9,15},... | collective-permute-start | bytes 245768 | tf_op jit(solution)/shard_map/ppermute | solution.py:391
  77.3 3.1 %second_late.1 = f32[16,1280]{1,0:T(8,128)S(1)} custom-call(f32[768,1152]{1,0:T(8,128)S(1)} %get-tuple-element.50.refs_1_.refs_0_, f32[768,1152]{1,0:T(8,128)S(1)} %get-tuple-element.51.refs_1_, f32[768,1152]{1,0:T(8,128)S(1)} %get-tuple-element.52.refs_2_, bf16[32,2304]{1,0:T(8,128)(2,1)S(1)} %get-tuple-element.78.refs_3_, ...), custom_call_target="tpu_custom_call" | custom-call | flops 1358954496 | bytes 10616832 | tf_op jit(solution)/shard_map/second_late/pallas_call | solution.py:371
  80.4 1.0 collective-permute-done.20
  81.4 0.1 collective-permute-start.22
  81.5 1.3 %collective-permute-done.22.got_ref = f32[16,1280]{1,0:T(8,128)S(1)} collective-permute-done((f32[16,1280]{1,0:T(8,128)S(1)}, f32[16,1280]{1,0:T(8,128)S(1)}, u32[]{:S(2)}, u32[]{:S(2)}) %collective-permute-start.22) | collective-permute-done | bytes 81952 | tf_op jit(solution)/shard_map/ppermute | solution.py:391
  82.7 2.8 %middle.1 = (f32[16,1152]{1,0:T(8,128)S(1)}, f32[16,1152]{1,0:T(8,128)S(1)}, f32[48,48]{1,0:T(8,128)S(1)}, f32[48,48]{1,0:T(8,128)S(1)}, f32[16,16]{1,0:T(8,128)S(1)}, /*index=5*/f32[16,16]{1,0:T(8,128)S(1)}) custom-call(f32[16,1152]{1,0:T(8,128)S(1)} %order.1.refs_2_.refs_5_.first_ref, f32[16,1280]{1,0:T(8,128)S(1)} %pair.1.refs_3_.refs_9_.refs_0_.refs_5_.pair_ref, ...), custom_call_target="tpu_custom_call" | custom-call | tf_op jit(solution)/shard_map/middle/pallas_call | solution.py:371
  85.5 0.7 collective-permute-start.30
  86.2 2.1 %collective-permute-start.29 = (f32[48,48]{1,0:T(8,128)S(1)}, f32[48,48]{1,0:T(8,128)S(1)}, u32[]{:S(2)}, u32[]{:S(2)}) collective-permute-start(f32[48,48]{1,0:T(8,128)S(1)} %get-tuple-element.91), channel_id=1, source_target_pairs={{0,14},{1,29},{2,12},{3,31},{4,10},{5,25},{6,8},{7,27},{8,6},{9,21... | collective-permute-start | bytes 27656 | tf_op jit(solution)/shard_map/ppermute | solution.py:391
  88.3 0.3 collective-permute-start.28
  88.5 2.8 %collective-permute-start.27 = (f32[48,48]{1,0:T(8,128)S(1)}, f32[48,48]{1,0:T(8,128)S(1)}, u32[]{:S(2)}, u32[]{:S(2)}) collective-permute-start(f32[48,48]{1,0:T(8,128)S(1)} %get-tuple-element.91), channel_id=1, source_target_pairs={{0,10},{1,25},{2,8},{3,27},{4,14},{5,29},{6,12},{7,31},{8,2},{9,17... | collective-permute-start | bytes 27656 | tf_op jit(solution)/shard_map/ppermute | solution.py:391
  91.3 1.7 %collective-permute-start.26 = (f32[48,48]{1,0:T(8,128)S(1)}, f32[48,48]{1,0:T(8,128)S(1)}, u32[]{:S(2)}, u32[]{:S(2)}) collective-permute-start(f32[48,48]{1,0:T(8,128)S(1)} %get-tuple-element.91), channel_id=1, source_target_pairs={{0,8},{1,23},{2,10},{3,21},{4,12},{5,19},{6,14},{7,17},{8,0},{9,31... | collective-permute-start | bytes 27656 | tf_op jit(solution)/shard_map/ppermute | solution.py:391
  93.0 1.5 %collective-permute-start.25 = (f32[48,48]{1,0:T(8,128)S(1)}, f32[48,48]{1,0:T(8,128)S(1)}, u32[]{:S(2)}, u32[]{:S(2)}) collective-permute-start(f32[48,48]{1,0:T(8,128)S(1)} %get-tuple-element.91), channel_id=1, source_target_pairs={{0,6},{1,21},{2,4},{3,23},{4,2},{5,17},{6,0},{7,19},{8,14},{9,29},... | collective-permute-start | bytes 27656 | tf_op jit(solution)/shard_map/ppermute | solution.py:391
  94.5 2.9 %collective-permute-start.23 = (f32[48,48]{1,0:T(8,128)S(1)}, f32[48,48]{1,0:T(8,128)S(1)}, u32[]{:S(2)}, u32[]{:S(2)}) collective-permute-start(f32[48,48]{1,0:T(8,128)S(1)} %get-tuple-element.91), channel_id=1, source_target_pairs={{0,2},{1,17},{2,0},{3,19},{4,6},{5,21},{6,4},{7,23},{8,10},{9,25},... | collective-permute-start | bytes 27656 | tf_op jit(solution)/shard_map/ppermute | solution.py:391
  97.4 1.2 %collective-permute-done.25 = f32[48,48]{1,0:T(8,128)S(1)} collective-permute-done((f32[48,48]{1,0:T(8,128)S(1)}, f32[48,48]{1,0:T(8,128)S(1)}, u32[]{:S(2)}, u32[]{:S(2)}) %collective-permute-start.25) | collective-permute-done | bytes 9248 | tf_op jit(solution)/shard_map/ppermute | solution.py:391
  98.6 0.6 collective-permute-done.24
  99.2 0.5 collective-permute-done.23
  99.8 2.4 %collective-permute-start.31 = (f32[48,48]{1,0:T(8,128)S(1)}, f32[48,48]{1,0:T(8,128)S(1)}, u32[]{:S(2)}, u32[]{:S(2)}) collective-permute-start(f32[48,48]{1,0:T(8,128)S(1)} %add_add_fusion.2.mine_ref), channel_id=1, source_target_pairs={{0,1},{1,0},{2,3},{3,2},{4,5},{5,4},{6,7},{7,6},{8,9},{9,8},{10,11... | collective-permute-start | bytes 27656 | tf_op jit(solution)/shard_map/ppermute | solution.py:391
  102.1 0.8 collective-permute-done.31.got_ref
  103.0 2.8 %last.1 = (f32[16,576]{1,0:T(8,128)}, f32[2,16,16]{2,1,0:T(8,128)}, f32[2,16,16]{2,1,0:T(8,128)}) custom-call(f32[16,1152]{1,0:T(8,128)S(1)} %order.1.refs_2_.refs_5_.first_ref, f32[16,1152]{1,0:T(8,128)S(1)} %get-tuple-element.86.q_ref, f32[16,1152]{1,0:T(8,128)S(1)} %get-tuple-element.87.prod_ref, f32[16,16]{1,0:T(8,128)S(1)} %get-tuple-element.88.proj0_ref, ...), custom_call_target="tpu_custom_call" | custom-call | tf_op jit(solution)/shard_map/last/pallas_call | solution.py:371
  (19 shorter events, 0.2 us)
Async XLA Ops:
  0.6 2.6 %collective-permute-start = (f32[16,576]{1,0:T(8,128)}, f32[16,576]{1,0:T(8,128)S(1)}, u32[]{:S(2)}, u32[]{:S(2)}) collective-permute-start(f32[16,576]{1,0:T(8,128)} %bitcast.6), channel_id=1, source_target_pairs={{0,1},{1,0},{2,3},{3,2},{4,5},{5,4},{6,7},{7,6},{8,9},{9,8},{10,11... | collective-permute-start | bytes 110600 | tf_op jit(solution)/shard_map/ppermute | solution.py:391
  3.3 12.3 %collective-permute-start.3 = (f32[16,1152]{1,0:T(8,128)S(1)}, f32[16,1152]{1,0:T(8,128)S(1)}, u32[]{:S(2)}, u32[]{:S(2)}) collective-permute-start(f32[16,1152]{1,0:T(8,128)S(1)} %order.1.refs_2_.refs_5_.first_ref), channel_id=1, source_target_pairs={{0,24},{1,7},{2,26},{3,5},{4,28},{5,3},{6,30},{7,1},{8,16},{9,15},... | collective-permute-start | bytes 221192 | tf_op jit(solution)/shard_map/ppermute | solution.py:391
  6.8 8.8 %collective-permute-start.2 = (f32[16,1152]{1,0:T(8,128)S(1)}, f32[16,1152]{1,0:T(8,128)S(1)}, u32[]{:S(2)}, u32[]{:S(2)}) collective-permute-start(f32[16,1152]{1,0:T(8,128)S(1)} %order.1.refs_2_.refs_5_.first_ref), channel_id=1, source_target_pairs={{0,4},{1,17},{2,6},{3,19},{4,0},{5,21},{6,2},{7,23},{8,12},{9,25},... | collective-permute-start | bytes 221192 | tf_op jit(solution)/shard_map/ppermute | solution.py:391
  9.4 6.2 %collective-permute-start.1 = (f32[16,1152]{1,0:T(8,128)S(1)}, f32[16,1152]{1,0:T(8,128)S(1)}, u32[]{:S(2)}, u32[]{:S(2)}) collective-permute-start(f32[16,1152]{1,0:T(8,128)S(1)} %order.1.refs_2_.refs_5_.first_ref), channel_id=1, source_target_pairs={{0,2},{1,9},{2,0},{3,11},{4,6},{5,13},{6,4},{7,15},{8,10},{9,1},{1... | collective-permute-start | bytes 221192 | tf_op jit(solution)/shard_map/ppermute | solution.py:391
  15.6 1.3 %collective-permute-start.4 = (f32[16,1152]{1,0:T(8,128)S(1)}, f32[16,1152]{1,0:T(8,128)S(1)}, u32[]{:S(2)}, u32[]{:S(2)}) collective-permute-start(f32[16,1152]{1,0:T(8,128)S(1)} %collective-permute-done.1.refs_4_), channel_id=1, source_target_pairs={{0,1},{1,0},{2,3},{3,2},{4,5},{5,4},{6,7},{7,6},{8,9},{9,8},{10,11... | collective-permute-start | bytes 221192 | tf_op jit(solution)/shard_map/ppermute | solution.py:391
  15.7 1.4 %collective-permute-start.5 = (f32[16,1152]{1,0:T(8,128)S(1)}, f32[16,1152]{1,0:T(8,128)S(1)}, u32[]{:S(2)}, u32[]{:S(2)}) collective-permute-start(f32[16,1152]{1,0:T(8,128)S(1)} %collective-permute-done.2.refs_5_), channel_id=1, source_target_pairs={{0,1},{1,0},{2,3},{3,2},{4,5},{5,4},{6,7},{7,6},{8,9},{9,8},{10,11... | collective-permute-start | bytes 221192 | tf_op jit(solution)/shard_map/ppermute | solution.py:391
  16.2 1.3 %collective-permute-start.6 = (f32[16,1152]{1,0:T(8,128)S(1)}, f32[16,1152]{1,0:T(8,128)S(1)}, u32[]{:S(2)}, u32[]{:S(2)}) collective-permute-start(f32[16,1152]{1,0:T(8,128)S(1)} %collective-permute-done.3.refs_6_), channel_id=1, source_target_pairs={{0,1},{1,0},{2,3},{3,2},{4,5},{5,4},{6,7},{7,6},{8,9},{9,8},{10,11... | collective-permute-start | bytes 221192 | tf_op jit(solution)/shard_map/ppermute | solution.py:391
  17.5 17.3 %copy-start = (f32[576]{0:T(1024)S(1)}, f32[576]{0:T(1024)}, u32[]{:S(2)}) copy-start(f32[576]{0:T(1024)} %param.4) | copy-start | bytes 6916
  34.5 1.5 %collective-permute-start.7 = (f32[3,16,1152]{2,1,0:T(8,128)S(1)}, f32[3,16,1152]{2,1,0:T(8,128)S(1)}, u32[]{:S(2)}, u32[]{:S(2)}) collective-permute-start(f32[3,16,1152]{2,1,0:T(8,128)S(1)} %get-tuple-element.62), channel_id=1, source_target_pairs={{0,1},{1,0},{2,3},{3,2},{4,5},{5,4},{6,7},{7,6},{8,9},{9,8},{10,11... | collective-permute-start | bytes 663560 | tf_op jit(solution)/shard_map/ppermute | solution.py:391
  36.1 5.6 %collective-permute-start.8 = (f32[16,1152]{1,0:T(8,128)S(1)}, f32[16,1152]{1,0:T(8,128)S(1)}, u32[]{:S(2)}, u32[]{:S(2)}) collective-permute-start(f32[16,1152]{1,0:T(8,128)S(1)} %get-tuple-element.63), channel_id=1, source_target_pairs={{0,2},{1,9},{2,0},{3,11},{4,6},{5,13},{6,4},{7,15},{8,10},{9,1},{1... | collective-permute-start | bytes 221192 | tf_op jit(solution)/shard_map/ppermute | solution.py:391
  36.6 6.8 %collective-permute-start.9 = (f32[16,1152]{1,0:T(8,128)S(1)}, f32[16,1152]{1,0:T(8,128)S(1)}, u32[]{:S(2)}, u32[]{:S(2)}) collective-permute-start(f32[16,1152]{1,0:T(8,128)S(1)} %get-tuple-element.64), channel_id=1, source_target_pairs={{0,4},{1,17},{2,6},{3,19},{4,0},{5,21},{6,2},{7,23},{8,12},{9,25},... | collective-permute-start | bytes 221192 | tf_op jit(solution)/shard_map/ppermute | solution.py:391
  37.3 6.1 %collective-permute-start.10 = (f32[16,1152]{1,0:T(8,128)S(1)}, f32[16,1152]{1,0:T(8,128)S(1)}, u32[]{:S(2)}, u32[]{:S(2)}) collective-permute-start(f32[16,1152]{1,0:T(8,128)S(1)} %get-tuple-element.65), channel_id=1, source_target_pairs={{0,24},{1,7},{2,26},{3,5},{4,28},{5,3},{6,30},{7,1},{8,16},{9,15},... | collective-permute-start | bytes 221192 | tf_op jit(solution)/shard_map/ppermute | solution.py:391
  43.5 1.3 %collective-permute-start.11 = (f32[16,1152]{1,0:T(8,128)S(1)}, f32[16,1152]{1,0:T(8,128)S(1)}, u32[]{:S(2)}, u32[]{:S(2)}) collective-permute-start(f32[16,1152]{1,0:T(8,128)S(1)} %add_add_fusion.1.mine_ref), channel_id=1, source_target_pairs={{0,1},{1,0},{2,3},{3,2},{4,5},{5,4},{6,7},{7,6},{8,9},{9,8},{10,11... | collective-permute-start | bytes 221192 | tf_op jit(solution)/shard_map/ppermute | solution.py:391
  45.1 7.5 %collective-permute-start.14 = (f32[16,1280]{1,0:T(8,128)S(1)}, f32[16,1280]{1,0:T(8,128)S(1)}, u32[]{:S(2)}, u32[]{:S(2)}) collective-permute-start(f32[16,1280]{1,0:T(8,128)S(1)} %pair.1.refs_3_.refs_9_.refs_0_.refs_5_.pair_ref), channel_id=1, source_target_pairs={{0,24},{1,7},{2,26},{3,5},{4,28},{5,3},{6,30},{7,1},{8,16},{9,15},... | collective-permute-start | bytes 245768 | tf_op jit(solution)/shard_map/ppermute | solution.py:391
  46.2 6.5 %collective-permute-start.13 = (f32[16,1280]{1,0:T(8,128)S(1)}, f32[16,1280]{1,0:T(8,128)S(1)}, u32[]{:S(2)}, u32[]{:S(2)}) collective-permute-start(f32[16,1280]{1,0:T(8,128)S(1)} %pair.1.refs_3_.refs_9_.refs_0_.refs_5_.pair_ref), channel_id=1, source_target_pairs={{0,4},{1,17},{2,6},{3,19},{4,0},{5,21},{6,2},{7,23},{8,12},{9,25},... | collective-permute-start | bytes 245768 | tf_op jit(solution)/shard_map/ppermute | solution.py:391
  47.3 5.4 %collective-permute-start.12 = (f32[16,1280]{1,0:T(8,128)S(1)}, f32[16,1280]{1,0:T(8,128)S(1)}, u32[]{:S(2)}, u32[]{:S(2)}) collective-permute-start(f32[16,1280]{1,0:T(8,128)S(1)} %pair.1.refs_3_.refs_9_.refs_0_.refs_5_.pair_ref), channel_id=1, source_target_pairs={{0,2},{1,9},{2,0},{3,11},{4,6},{5,13},{6,4},{7,15},{8,10},{9,1},{1... | collective-permute-start | bytes 245768 | tf_op jit(solution)/shard_map/ppermute | solution.py:391
  52.7 1.3 %collective-permute-start.15 = (f32[16,1280]{1,0:T(8,128)S(1)}, f32[16,1280]{1,0:T(8,128)S(1)}, u32[]{:S(2)}, u32[]{:S(2)}) collective-permute-start(f32[16,1280]{1,0:T(8,128)S(1)} %collective-permute-done.12.refs_11_.refs_1_), channel_id=1, source_target_pairs={{0,1},{1,0},{2,3},{3,2},{4,5},{5,4},{6,7},{7,6},{8,9},{9,8},{10,11... | collective-permute-start | bytes 245768 | tf_op jit(solution)/shard_map/ppermute | solution.py:391
  52.8 1.4 %collective-permute-start.16 = (f32[16,1280]{1,0:T(8,128)S(1)}, f32[16,1280]{1,0:T(8,128)S(1)}, u32[]{:S(2)}, u32[]{:S(2)}) collective-permute-start(f32[16,1280]{1,0:T(8,128)S(1)} %collective-permute-done.13.refs_12_.refs_2_), channel_id=1, source_target_pairs={{0,1},{1,0},{2,3},{3,2},{4,5},{5,4},{6,7},{7,6},{8,9},{9,8},{10,11... | collective-permute-start | bytes 245768 | tf_op jit(solution)/shard_map/ppermute | solution.py:391
  53.3 1.3 %collective-permute-start.17 = (f32[16,1280]{1,0:T(8,128)S(1)}, f32[16,1280]{1,0:T(8,128)S(1)}, u32[]{:S(2)}, u32[]{:S(2)}) collective-permute-start(f32[16,1280]{1,0:T(8,128)S(1)} %collective-permute-done.14.refs_13_.refs_3_), channel_id=1, source_target_pairs={{0,1},{1,0},{2,3},{3,2},{4,5},{5,4},{6,7},{7,6},{8,9},{9,8},{10,11... | collective-permute-start | bytes 245768 | tf_op jit(solution)/shard_map/ppermute | solution.py:391
  71.4 1.5 %collective-permute-start.18 = (f32[3,16,1152]{2,1,0:T(8,128)S(1)}, f32[3,16,1152]{2,1,0:T(8,128)S(1)}, u32[]{:S(2)}, u32[]{:S(2)}) collective-permute-start(f32[3,16,1152]{2,1,0:T(8,128)S(1)} %get-tuple-element.81), channel_id=1, source_target_pairs={{0,1},{1,0},{2,3},{3,2},{4,5},{5,4},{6,7},{7,6},{8,9},{9,8},{10,11... | collective-permute-start | bytes 663560 | tf_op jit(solution)/shard_map/ppermute | solution.py:391
  72.9 7.5 %collective-permute-start.19 = (f32[16,1280]{1,0:T(8,128)S(1)}, f32[16,1280]{1,0:T(8,128)S(1)}, u32[]{:S(2)}, u32[]{:S(2)}) collective-permute-start(f32[16,1280]{1,0:T(8,128)S(1)} %get-tuple-element.83), channel_id=1, source_target_pairs={{0,2},{1,9},{2,0},{3,11},{4,6},{5,13},{6,4},{7,15},{8,10},{9,1},{1... | collective-permute-start | bytes 245768 | tf_op jit(solution)/shard_map/ppermute | solution.py:391
  73.5 7.9 %collective-permute-start.20 = (f32[16,1280]{1,0:T(8,128)S(1)}, f32[16,1280]{1,0:T(8,128)S(1)}, u32[]{:S(2)}, u32[]{:S(2)}) collective-permute-start(f32[16,1280]{1,0:T(8,128)S(1)} %get-tuple-element.84), channel_id=1, source_target_pairs={{0,4},{1,17},{2,6},{3,19},{4,0},{5,21},{6,2},{7,23},{8,12},{9,25},... | collective-permute-start | bytes 245768 | tf_op jit(solution)/shard_map/ppermute | solution.py:391
  75.5 5.9 %collective-permute-start.21 = (f32[16,1280]{1,0:T(8,128)S(1)}, f32[16,1280]{1,0:T(8,128)S(1)}, u32[]{:S(2)}, u32[]{:S(2)}) collective-permute-start(f32[16,1280]{1,0:T(8,128)S(1)} %get-tuple-element.85), channel_id=1, source_target_pairs={{0,24},{1,7},{2,26},{3,5},{4,28},{5,3},{6,30},{7,1},{8,16},{9,15},... | collective-permute-start | bytes 245768 | tf_op jit(solution)/shard_map/ppermute | solution.py:391
  81.4 1.3 %collective-permute-start.22 = (f32[16,1280]{1,0:T(8,128)S(1)}, f32[16,1280]{1,0:T(8,128)S(1)}, u32[]{:S(2)}, u32[]{:S(2)}) collective-permute-start(f32[16,1280]{1,0:T(8,128)S(1)} %add_add_fusion.mine_ref), channel_id=1, source_target_pairs={{0,1},{1,0},{2,3},{3,2},{4,5},{5,4},{6,7},{7,6},{8,9},{9,8},{10,11... | collective-permute-start | bytes 245768 | tf_op jit(solution)/shard_map/ppermute | solution.py:391
  85.5 7.5 %collective-permute-start.30 = (f32[48,48]{1,0:T(8,128)S(1)}, f32[48,48]{1,0:T(8,128)S(1)}, u32[]{:S(2)}, u32[]{:S(2)}) collective-permute-start(f32[48,48]{1,0:T(8,128)S(1)} %get-tuple-element.91), channel_id=1, source_target_pairs={{1,31},{3,29},{5,27},{7,25},{9,23},{11,21},{13,19},{15,17},{17,15}... | collective-permute-start | bytes 27656 | tf_op jit(solution)/shard_map/ppermute | solution.py:391
  86.2 8.3 %collective-permute-start.29 = (f32[48,48]{1,0:T(8,128)S(1)}, f32[48,48]{1,0:T(8,128)S(1)}, u32[]{:S(2)}, u32[]{:S(2)}) collective-permute-start(f32[48,48]{1,0:T(8,128)S(1)} %get-tuple-element.91), channel_id=1, source_target_pairs={{0,14},{1,29},{2,12},{3,31},{4,10},{5,25},{6,8},{7,27},{8,6},{9,21... | collective-permute-start | bytes 27656 | tf_op jit(solution)/shard_map/ppermute | solution.py:391
  88.3 6.2 %collective-permute-start.28 = (f32[48,48]{1,0:T(8,128)S(1)}, f32[48,48]{1,0:T(8,128)S(1)}, u32[]{:S(2)}, u32[]{:S(2)}) collective-permute-start(f32[48,48]{1,0:T(8,128)S(1)} %get-tuple-element.91), channel_id=1, source_target_pairs={{0,12},{1,27},{2,14},{3,25},{4,8},{5,31},{6,10},{7,29},{8,4},{9,19... | collective-permute-start | bytes 27656 | tf_op jit(solution)/shard_map/ppermute | solution.py:391
  88.5 8.9 %collective-permute-start.27 = (f32[48,48]{1,0:T(8,128)S(1)}, f32[48,48]{1,0:T(8,128)S(1)}, u32[]{:S(2)}, u32[]{:S(2)}) collective-permute-start(f32[48,48]{1,0:T(8,128)S(1)} %get-tuple-element.91), channel_id=1, source_target_pairs={{0,10},{1,25},{2,8},{3,27},{4,14},{5,29},{6,12},{7,31},{8,2},{9,17... | collective-permute-start | bytes 27656 | tf_op jit(solution)/shard_map/ppermute | solution.py:391
  91.3 6.1 %collective-permute-start.26 = (f32[48,48]{1,0:T(8,128)S(1)}, f32[48,48]{1,0:T(8,128)S(1)}, u32[]{:S(2)}, u32[]{:S(2)}) collective-permute-start(f32[48,48]{1,0:T(8,128)S(1)} %get-tuple-element.91), channel_id=1, source_target_pairs={{0,8},{1,23},{2,10},{3,21},{4,12},{5,19},{6,14},{7,17},{8,0},{9,31... | collective-permute-start | bytes 27656 | tf_op jit(solution)/shard_map/ppermute | solution.py:391
  93.0 5.6 %collective-permute-start.25 = (f32[48,48]{1,0:T(8,128)S(1)}, f32[48,48]{1,0:T(8,128)S(1)}, u32[]{:S(2)}, u32[]{:S(2)}) collective-permute-start(f32[48,48]{1,0:T(8,128)S(1)} %get-tuple-element.91), channel_id=1, source_target_pairs={{0,6},{1,21},{2,4},{3,23},{4,2},{5,17},{6,0},{7,19},{8,14},{9,29},... | collective-permute-start | bytes 27656 | tf_op jit(solution)/shard_map/ppermute | solution.py:391
  94.5 4.8 %collective-permute-start.24 = (f32[48,48]{1,0:T(8,128)S(1)}, f32[48,48]{1,0:T(8,128)S(1)}, u32[]{:S(2)}, u32[]{:S(2)}) collective-permute-start(f32[48,48]{1,0:T(8,128)S(1)} %get-tuple-element.91), channel_id=1, source_target_pairs={{0,4},{1,19},{2,6},{3,17},{4,0},{5,23},{6,2},{7,21},{8,12},{9,27},... | collective-permute-start | bytes 27656 | tf_op jit(solution)/shard_map/ppermute | solution.py:391
  94.5 5.2 %collective-permute-start.23 = (f32[48,48]{1,0:T(8,128)S(1)}, f32[48,48]{1,0:T(8,128)S(1)}, u32[]{:S(2)}, u32[]{:S(2)}) collective-permute-start(f32[48,48]{1,0:T(8,128)S(1)} %get-tuple-element.91), channel_id=1, source_target_pairs={{0,2},{1,17},{2,0},{3,19},{4,6},{5,21},{6,4},{7,23},{8,10},{9,25},... | collective-permute-start | bytes 27656 | tf_op jit(solution)/shard_map/ppermute | solution.py:391
  99.8 3.2 %collective-permute-start.31 = (f32[48,48]{1,0:T(8,128)S(1)}, f32[48,48]{1,0:T(8,128)S(1)}, u32[]{:S(2)}, u32[]{:S(2)}) collective-permute-start(f32[48,48]{1,0:T(8,128)S(1)} %add_add_fusion.2.mine_ref), channel_id=1, source_target_pairs={{0,1},{1,0},{2,3},{3,2},{4,5},{5,4},{6,7},{7,6},{8,9},{9,8},{10,11... | collective-permute-start | bytes 27656 | tf_op jit(solution)/shard_map/ppermute | solution.py:391

commit v6 on v5

--- a/solution.py
+++ b/solution.py
@@ -103,22 +103,26 @@
     return found
 
 
+def order_of(group, parts):
+    near = [(0, p) for p in range(parts)]
+    lead = [(s, 0) for s in range(1, group)]
+    return near + lead + [(s, p) for s in range(1, group) for p in range(1, parts)]
+
+
 class Loader:
-    def __init__(self, source, arrived, n, group, parts, first, held):
+    def __init__(self, source, arrived, n, group, parts, where, held):
         _, z, r = place()
-        self.held, self.first = held, first
 
         def copies(i):
-            cols = pl.ds(pl.multiple_of(lax.bitwise_xor(z, (first + i) // parts) * (2 * n), 128), 2 * n)
+            s, part = where[i]
+            cols = pl.ds(pl.multiple_of(lax.bitwise_xor(z, s) * (2 * n), 128), 2 * n)
             return [
                 pltpu.make_async_copy(
                     source.at[pl.ds(pl.multiple_of(lax.bitwise_xor(r, peer) * n + off, 8), count), cols],
                     held[i].at[pl.ds(at, count), :],
                     arrived.at[i, j],
                 )
-                for j, (peer, off, at, count) in enumerate(
-                    pieces_of((first + i) % parts, group, n, group * n // parts)
-                )
+                for j, (peer, off, at, count) in enumerate(pieces_of(part, group, n, group * n // parts))
             ]
 
         self.copies = copies
@@ -131,11 +135,59 @@
             copy.wait()
 
 
+class Pieces:
+    def __init__(self, n, group, parts, given, new, scratch, refs):
+        order = order_of(group, parts)
+        refs = list(refs)
+        source = refs.pop(0) if len(new) else None
+        held = {order[i]: refs.pop(0) for i in given}
+        self.waits = {}
+        if len(new):
+            arrived = refs.pop()
+            at = len(refs) - scratch - len(new)
+            fresh, refs = refs[at : at + len(new)], refs[:at] + refs[at + len(new) :]
+            where = [order[i] for i in new]
+            self.loader = Loader(source, arrived, n, group, parts, where, fresh)
+            self.waits = {key: i for i, key in enumerate(where)}
+            held.update(zip(where, fresh))
+        self.held, self.refs = held, refs
+
+    def get(self, s, p):
+        if (s, p) in self.waits:
+            self.loader.wait(self.waits.pop((s, p)))
+        return self.held[s, p]
+
+    def finish(self):
+        for key in list(self.waits):
+            self.get(*key)
+
+
+def tiles_of(piece, tile, first, last, step):
+    def body(t, carry):
+        high, low = split(piece[pl.ds(pl.multiple_of(t * tile, tile), tile), :])
+        step(t, high, low)
+        return carry
+
+    lax.fori_loop(first, last, body, 0)
+
+
+def across(xg, cols, k, high, low):
+    one = dot(xg[:, cols], high, NT)
+    two = dot(xg[:k, cols], low, NT)
+    return one[:k] + one[k:] + two
+
+
+def along(xr, at, k, high, low):
+    one = dot(xr[:, at], high, NN)
+    two = dot(xr[:k, at], low, NN)
+    return one[:k] + one[k:] + two
+
+
 def begin_kernel(k, n, group, parts, source, block_ref, own_ref, *refs):
     *held, arrived, ready = refs
     copy = pltpu.make_async_copy(block_ref, own_ref, ready)
     copy.start()
-    loader = Loader(source, arrived, n, group, parts, 0, held)
+    loader = Loader(source, arrived, n, group, parts, order_of(group, parts), held)
     copy.wait()
     for i in range(len(held)):
         loader.wait(i)
@@ -153,110 +205,115 @@
     slab[k:, at : at + value.shape[1]] = low
 
 
-def early_kernel(k, n, group, tile, parts, given, new, *refs):
-    source, refs = (refs[0], refs[1:]) if new else (None, refs)
-    held, refs = list(refs[:given]), refs[given:]
-    pair_ref, u_ref, *refs = refs
-    if new:
-        *fresh, xg, arrived = refs
-        loader = Loader(source, arrived, n, group, parts, given, fresh)
-        held = held + fresh
-    else:
-        (xg,) = refs
-    put(xg, 0, k, pair_ref[:, : 2 * n])
-    rows = held[0].shape[0]
-
-    def step(p, t, carry):
-        high, low = split(held[p][pl.ds(pl.multiple_of(t * tile, tile), tile), :])
-        one = dot(xg[...], high, NT)
-        two = dot(xg[:k, :], low, NT)
-        u_ref[:, pl.ds(pl.multiple_of(p * rows + t * tile, tile), tile)] = one[:k] + one[k:] + two
-        return carry
-
-    for p in range(parts):
-        if p >= given:
-            loader.wait(p - given)
-        lax.fori_loop(0, rows // tile, functools.partial(step, p), 0)
-    for p in range(parts, given + new):
-        loader.wait(p - given)
-
-
 def turned(s, group, even):
     return jnp.logical_not(even) if s == group - 1 else even
 
 
+def early_kernel(k, n, group, tile, parts, given, new, *refs):
+    pieces = Pieces(n, group, parts, given, new, 1, refs)
+    xg = pieces.refs.pop(-1)
+    pair_ref, u_ref = pieces.refs
+    put(xg, 0, k, pair_ref[:, : 2 * n])
+    for p in range(parts):
+        piece = pieces.get(0, p)
+        rows = piece.shape[0]
+
+        def step(t, high, low):
+            u_ref[:, pl.ds(pl.multiple_of(p * rows + t * tile, tile), tile)] = across(xg, slice(None), k, high, low)
+
+        tiles_of(piece, tile, 0, rows // tile, step)
+    pieces.finish()
+
+
+def own_kernel(k, n, group, tile, parts, given, new, *refs):
+    pieces = Pieces(n, group, parts, given, new, 1, refs)
+    xr = pieces.refs.pop(-1)
+    pair_ref, v_ref = pieces.refs
+    even = place()[0] == 0
+    put(xr, 0, k, own_half(pair_ref, even, n))
+    v_ref[...] = jnp.zeros_like(v_ref)
+    for s in range(1, group):
+        cols = slice((s - 1) * 2 * n, s * 2 * n)
+
+        def step(t, high, low):
+            v_ref[:, cols] += along(xr, pl.ds(pl.multiple_of(t * tile, tile), tile), k, high, low)
+
+        tiles_of(pieces.get(s, 0), tile, 0, n // tile, step)
+    pieces.finish()
+
+
 def main_kernel(k, n, group, tile, parts, given, new, *refs):
+    pieces = Pieces(n, group, parts, given, new, 2, refs)
+    u_acc, v_acc = pieces.refs[-2:]
+    refs = pieces.refs[:-2]
+    pair_ref, u0_ref, v0_ref, mine, theirs = refs[0], refs[1], refs[2], refs[3 : group + 2], refs[group + 2 : 2 * group + 1]
+    send_ref, keep_ref, own_ref, xr, xg = refs[2 * group + 1 :]
     even = place()[0] == 0
-    source, refs = (refs[0], refs[1:]) if new else (None, refs)
-    held, refs = list(refs[:given]), refs[given:]
-    pair_ref, u0_ref, mine, theirs = refs[0], refs[1], refs[2 : group + 1], refs[group + 1 : 2 * group]
-    send_ref, keep_ref, own_ref, xr, *refs = refs[2 * group :]
-    if new:
-        *fresh, xg, u_acc, v_acc, arrived = refs
-        loader = Loader(source, arrived, n, group, parts, parts + given, fresh)
-        held = held + fresh
-    else:
-        xg, u_acc, v_acc = refs
-    rows = held[0].shape[0]
 
     segments = [own_half(pair_ref, even, n)]
     for s in range(1, group):
         y, w = mine[s - 1][:, : 2 * n], theirs[s - 1][:, : 2 * n]
-        along = turned(s, group, even)
-        put(xg, (s - 1) * 2 * n, k, jnp.where(along, y, w))
-        segments.append(own_half(jnp.where(along, w, y), even, n))
+        to_z = turned(s, group, even)
+        put(xg, (s - 1) * 2 * n, k, jnp.where(to_z, y, w))
+        segments.append(own_half(jnp.where(to_z, w, y), even, n))
     for a in range(0, group, 2):
         put(xr, a * n, k, jnp.concatenate(segments[a : a + 2], axis=1))
     u_acc[...] = u0_ref[...]
-    v_acc[...] = jnp.zeros_like(v_acc)
-
-    def step(i, t, carry):
-        s, p = divmod(i, parts)
-        cols = slice(s * 2 * n, (s + 1) * 2 * n)
-        at = pl.ds(pl.multiple_of(p * rows + t * tile, tile), tile)
-        high, low = split(held[i][pl.ds(pl.multiple_of(t * tile, tile), tile), :])
-        one = dot(xr[:, at], high, NN)
-        two = dot(xr[:k, at], low, NN)
-        v_acc[:, cols] += one[:k] + one[k:] + two
-        one = dot(xg[:, cols], high, NT)
-        two = dot(xg[:k, cols], low, NT)
-        u_acc[:, at] += one[:k] + one[k:] + two
-        return carry
-
-    for i in range(len(held)):
-        if i >= given:
-            loader.wait(i - given)
-        lax.fori_loop(0, rows // tile, functools.partial(step, i), 0)
+    v_acc[...] = v0_ref[...]
+
+    for s, p in order_of(group, parts)[parts:]:
+        piece = pieces.get(s, p)
+        rows = piece.shape[0]
+        cols = slice((s - 1) * 2 * n, s * 2 * n)
+
+        def step(t, high, low):
+            at = pl.ds(pl.multiple_of(p * rows + t * tile, tile), tile)
+            v_acc[:, cols] += along(xr, at, k, high, low)
+            u_acc[:, at] += across(xg, cols, k, high, low)
+
+        tiles_of(piece, tile, n // tile if p == 0 else 0, rows // tile, step)
 
     own_ref[...] = u_acc[:, :n]
     for s in range(1, group):
-        along = turned(s, group, even)
+        to_z = turned(s, group, even)
         by_z = v_acc[:, 2 * n * (s - 1) : 2 * n * s]
         by_row = in_half(u_acc[:, n * s : n * (s + 1)], even)
-        keep_ref[s - 1] = jnp.where(along, by_z, by_row)
-        send_ref[s - 1] = jnp.where(along, by_row, by_z)
+        keep_ref[s - 1] = jnp.where(to_z, by_z, by_row)
+        send_ref[s - 1] = jnp.where(to_z, by_row, by_z)
+
+
+def near_kernel(k, n, tile, piece, xr, v_ref):
+    v_ref[...] = jnp.zeros_like(v_ref)
+
+    def step(t, high, low):
+        v_ref[...] += along(xr, pl.ds(pl.multiple_of(t * tile, tile), tile), k, high, low)
+
+    tiles_of(piece, tile, 0, piece.shape[0] // tile, step)
 
 
 def late_kernel(k, n, group, tile, parts, extra, *refs):
-    held, refs = refs[:parts], refs[parts:]
-    xr, own_ref, pair_ref, energy_ref, *refs = refs
+    near, lead, refs = refs[: parts - 1], refs[parts - 1 : parts + group - 2], refs[parts + group - 2 :]
+    xr, xg, v_ref, own_ref, pair_ref, energy_ref, *refs = refs
     more, refs = (refs[0], refs[1:]) if extra else (None, refs)
-    out_ref, v_acc = refs
+    out_ref, v_acc, u_acc = refs
     even = place()[0] == 0
-    rows = held[0].shape[0]
-    v_acc[...] = jnp.zeros_like(v_acc)
-
-    def step(p, t, carry):
-        at = pl.ds(pl.multiple_of(p * rows + t * tile, tile), tile)
-        high, low = split(held[p][pl.ds(pl.multiple_of(t * tile, tile), tile), :])
-        one = dot(xr[:, at], high, NN)
-        two = dot(xr[:k, at], low, NN)
-        v_acc[...] += one[:k] + one[k:] + two
-        return carry
-
-    for p in range(parts):
-        lax.fori_loop(0, rows // tile, functools.partial(step, p), 0)
-    own = energy_ref[...] * own_half(pair_ref, even, n) + own_ref[...]
+    v_acc[...] = v_ref[...]
+    u_acc[...] = own_ref[...]
+    for p in range(1, parts):
+        rows = near[p - 1].shape[0]
+
+        def step(t, high, low):
+            v_acc[...] += along(xr, pl.ds(pl.multiple_of(p * rows + t * tile, tile), tile), k, high, low)
+
+        tiles_of(near[p - 1], tile, 0, rows // tile, step)
+    for s in range(1, group):
+        cols = slice((s - 1) * 2 * n, s * 2 * n)
+
+        def step(t, high, low):
+            u_acc[:, pl.ds(pl.multiple_of(t * tile, tile), tile)] += across(xg, cols, k, high, low)
+
+        tiles_of(lead[s - 1], tile, 0, n // tile, step)
+    own = energy_ref[...] * own_half(pair_ref, even, n) + u_acc[...]
     out_ref[:, : 2 * n] = v_acc[...] + in_half(own, even)
     if extra:
         part = more[...]
@@ -269,8 +326,8 @@
         pair_ref, mine, theirs, outs = refs[0], refs[1:group], refs[group : 2 * group - 1], refs[2 * group - 1 :]
         part = pair_ref[:, 2 * n :]
         for s in range(1, group):
-            along = turned(s, group, even)
-            part = part + jnp.where(along, theirs[s - 1][:, 2 * n :], mine[s - 1][:, 2 * n :])
+            to_z = turned(s, group, even)
+            part = part + jnp.where(to_z, theirs[s - 1][:, 2 * n :], mine[s - 1][:, 2 * n :])
         outs[group - 1][...] = part
     else:
         outs = refs
@@ -295,16 +352,15 @@
     rows = lax.broadcasted_iota(jnp.int32, (k, 2 * k), 0)
     cols = lax.broadcasted_iota(jnp.int32, (k, 2 * k), 1)
     row = lax.broadcasted_iota(jnp.int32, (k, 1), 0)
-    both = jnp.concatenate([gram, jnp.where(rows == cols, 1.0, 0.0)[:, :k]], axis=1)
-    lower = jnp.zeros((k, k), F32)
-    for j in range(k):
-        scale = 1.0 / jnp.sqrt(both[j : j + 1, j : j + 1])
-        column = jnp.where(row >= j, both[:, j : j + 1] * scale, 0.0)
-        lower = jnp.where(cols[:, :k] == j, column, lower)
-        lead = both[j : j + 1, :] * scale
-        below = jnp.where(row > j, column, 0.0)
-        both = jnp.where(rows == j, lead, both - below * lead)
-    return lower, both[:, k:]
+    both = jnp.concatenate([gram, eye(k)], axis=1)
+    for j in range(k - 1):
+        lead = both[j : j + 1, :]
+        lead = lead * (1.0 / both[j : j + 1, j : j + 1])
+        both = both - jnp.where(row > j, both[:, j : j + 1], 0.0) * lead
+    pivots = jnp.sum(jnp.where(rows == cols, both, 0.0), axis=1, keepdims=True)
+    both = both * (1.0 / jnp.sqrt(pivots))
+    upper = jnp.where(rows <= cols, both, 0.0)[:, :k]
+    return dot32(upper, eye(k), TN), both[:, k:]
 
 
 def gram_of(moments, coefficients):
@@ -320,7 +376,7 @@
     ).astype(F32)
 
 
-def second_kernel(k, n, order, first_ref, pair_ref, mine_ref, got_ref, q_ref, prod_ref, mom_ref, base_ref, proj_ref, fact_ref):
+def second_kernel(k, n, order, first_ref, pair_ref, mine_ref, got_ref, q_ref, prod_ref, mom_ref, proj_ref, fact_ref):
     packed = mine_ref[:, 2 * n :] + got_ref[:, 2 * n :]
     moments = jnp.concatenate([packed[:, : 2 * k], packed[:, 2 * k : 4 * k]], axis=0) * (1.0 / order)
     projection = moments[:k, k:]
@@ -329,18 +385,21 @@
     fact_ref[...] = lower
     x, y = first_ref[...], pair_ref[:, : 2 * n]
     w = mine_ref[:, : 2 * n] + got_ref[:, : 2 * n]
-    q = dot32(inverse, y - dot32(projection, x, TN), NN)
-    prod = dot32(inverse, w - dot32(projection, y, TN), NN)
+    rest = jnp.concatenate([y, w], axis=1) - dot32(projection, jnp.concatenate([x, y], axis=1), TN)
+    both = dot32(inverse, rest, NN)
+    q, prod = both[:, : 2 * n], both[:, 2 * n :]
     q_ref[...] = q
     prod_ref[...] = prod
     s = jnp.concatenate([q, x, prod], axis=0)
-    total = dot32(s, s, NT)
-    mom_ref[...] = total
-    base_ref[...] = jnp.where(place()[0] == 0, total, jnp.zeros_like(total))
-
-
-def last_kernel(k, n, order, first_ref, q_ref, prod_ref, proj0_ref, fact0_ref, mine_ref, got_ref, basis_ref, proj_ref, fact_ref):
-    moments = (mine_ref[...] + got_ref[...]) * (1.0 / order)
+    mom_ref[...] = dot32(s, s, NT)
+
+
+def last_kernel(k, n, order, first_ref, q_ref, prod_ref, proj0_ref, fact0_ref, *refs):
+    *sums, basis_ref, proj_ref, fact_ref = refs
+    total = sums[0][...]
+    for m in sums[1:]:
+        total = total + m[...]
+    moments = total * (1.0 / order)
     coefficients = moments[: 2 * k, 2 * k :]
     lower, inverse = factor_of(gram_of(moments, coefficients))
     proj_ref[0] = proj0_ref[...]
@@ -348,11 +407,8 @@
     fact_ref[0] = fact0_ref[...]
     fact_ref[1] = lower
     even = place()[0] == 0
-    rest = (
-        own_half(prod_ref, even, n)
-        - dot32(coefficients[:k], own_half(q_ref, even, n), TN)
-        - dot32(coefficients[k:], own_half(first_ref, even, n), TN)
-    )
+    before = jnp.concatenate([own_half(q_ref, even, n), own_half(first_ref, even, n)], axis=0)
+    rest = own_half(prod_ref, even, n) - dot32(coefficients, before, TN)
     basis_ref[...] = dot32(inverse, rest, NN)
 
 
@@ -429,41 +485,72 @@
         extra = pair.shape[1] > 2 * n
         sizes = (k, n, group, tile, parts)
         load = len(held) < total_pieces
+
+        def matrix_call(kernel, need, upto, out_shapes, args, scratch, label, flops):
+            given = [i for i in need if i < len(held)]
+            new = range(len(held), max(upto, len(held)))
+            outs = call(
+                functools.partial(kernel, *sizes, given, new),
+                tuple(out_shapes) + (block_shape,) * len(new),
+                (len(new) > 0) + len(given) + len(args),
+                scratch=list(scratch) + (semaphores(len(new)) if new else []),
+                limit=8 << 20,
+                name=name + label,
+                far=int(len(new) > 0),
+                flops=flops,
+            )(*([a] if new else []), *[held[i] for i in given], *args)
+            held.extend(outs[len(out_shapes) :])
+            return outs[: len(out_shapes)]
+
         mine = [send(pair, spread(s)) for s in steps]
-        near = held[:parts]
-        new = parts + 1 - len(near) if load else 0
-        u0, *fresh = call(
-            functools.partial(early_kernel, *sizes, len(near), new),
-            (shape(k, rows),) + (block_shape,) * new,
-            load + len(near) + 1,
-            scratch=[pltpu.VMEM((2 * k, 2 * n), BF16)] + (semaphores(new) if new else []),
+        (u0,) = matrix_call(
+            early_kernel,
+            range(parts),
+            parts + 1,
+            [shape(k, rows)],
+            [pair],
+            [pltpu.VMEM((2 * k, 2 * n), BF16)],
+            "_early",
+            2 * work,
+        )
+        u0, same, *mine = lax.optimization_barrier((u0, pair, *mine))
+        theirs = [swap(y) for y in mine]
+        (v0,) = matrix_call(
+            own_kernel,
+            range(parts, parts + group - 1),
+            parts + group - 1,
+            [shape(k, (group - 1) * 2 * n)],
+            [same],
+            [pltpu.VMEM((2 * k, n), BF16)],
+            "_own",
+            work,
+        )
+        out, keep, mine_u, xr, xg = matrix_call(
+            main_kernel,
+            range(parts, total_pieces),
+            total_pieces,
+            [
+                shape(group - 1, k, 2 * n),
+                shape(group - 1, k, 2 * n),
+                shape(k, n),
+                jax.ShapeDtypeStruct((2 * k, rows), BF16),
+                jax.ShapeDtypeStruct((2 * k, (group - 1) * 2 * n), BF16),
+            ],
+            [pair, u0, v0, *mine, *theirs],
+            [pltpu.VMEM((k, rows), F32), pltpu.VMEM((k, (group - 1) * 2 * n), F32)],
+            "",
+            8 * work,
+        )
+        got = swap(out)
+        near = call(
+            functools.partial(near_kernel, k, n, tile),
+            shape(k, 2 * n),
+            2,
             limit=8 << 20,
-            name=name + "_early",
-            far=int(load),
-            flops=2 * work,
-        )(*([a] if load else []), *near, pair)
-        held = held + fresh
-        u0, *mine = lax.optimization_barrier((u0, *mine))
-        theirs = [swap(y) for y in mine]
-        new = total_pieces - len(held)
-        out, keep, mine_u, xr, *fresh = call(
-            functools.partial(main_kernel, *sizes, len(held) - parts, new),
-            (shape(group - 1, k, 2 * n), shape(group - 1, k, 2 * n), shape(k, n), jax.ShapeDtypeStruct((2 * k, rows), BF16))
-            + (block_shape,) * new,
-            load + len(held) - parts + 2 * group,
-            scratch=[
-                pltpu.VMEM((2 * k, (group - 1) * 2 * n), BF16),
-                pltpu.VMEM((k, rows), F32),
-                pltpu.VMEM((k, (group - 1) * 2 * n), F32),
-            ]
-            + (semaphores(new) if new else []),
-            limit=8 << 20,
-            name=name,
-            far=int(load),
-            flops=4 * work * (group - 1),
-        )(*([a] if load else []), *held[parts:], pair, u0, *mine, *theirs)
-        held = held + fresh
-        got = swap(out)
+            name=name + "_near",
+            flops=work,
+        )(held[0], xr)
+        got, near = lax.optimization_barrier((got, near))
         sums = call(
             functools.partial(combine_kernel, k, n, group, extra),
             (shape(k, pair.shape[1]),) * (group - 1) + ((shape(k, 8 * k),) if extra else ()),
@@ -474,12 +561,12 @@
         total = call(
             functools.partial(late_kernel, *sizes, extra),
             shape(k, pair.shape[1]),
-            parts + 4 + extra,
-            scratch=[pltpu.VMEM((k, 2 * n), F32)],
+            parts - 1 + group - 1 + 6 + extra,
+            scratch=[pltpu.VMEM((k, 2 * n), F32), pltpu.VMEM((k, n), F32)],
             limit=8 << 20,
             name=name + "_late",
-            flops=2 * work,
-        )(*held[:parts], xr, mine_u, pair, energy, *sums[group - 1 :])
+            flops=3 * work,
+        )(*held[1 : parts + group - 1], xr, xg, near, mine_u, pair, energy, *sums[group - 1 :])
         for v in arrived:
             total = total + v
         return total, swap(total), held
@@ -487,26 +574,20 @@
     mine, got, held = products(held, first, "first")
     pair = call(functools.partial(pair_kernel, k, n), shape(k, 2 * n + 8 * k), 3, name="pair")(first, mine, got)
     mine, got, held = products(held, pair, "second")
-    q, prod, moments, total, proj0, fact0 = call(
+    q, prod, moments, proj0, fact0 = call(
         functools.partial(second_kernel, k, n, order),
-        (shape(k, 2 * n), shape(k, 2 * n), shape(3 * k, 3 * k), shape(3 * k, 3 * k), shape(k, k), shape(k, k)),
+        (shape(k, 2 * n), shape(k, 2 * n), shape(3 * k, 3 * k), shape(k, k), shape(k, k)),
         4,
         name="middle",
     )(first, pair, mine, got)
-    half = group * group // 2
-    for i in range(1, half + 1):
-
-        def to(r, c, i=i):
-            s = half - 1 + i if c % 2 else i
-            return None if c % 2 == 0 and i == half else chip(r, c, s // group, s % group)
-
-        total = total + send(moments, to)
+    moments = sum([send(moments, lambda r, c, s=s: chip(r, c, s, 0)) for s in steps], moments)
+    sums = [moments] + [send(moments, lambda r, c, s=s: chip(r, c, 0, s)) for s in steps]
     basis, proj, fact = call(
         functools.partial(last_kernel, k, n, order),
         (shape(k, n), shape(2, k, k), shape(2, k, k)),
-        7,
+        5 + group,
         name="last",
-    )(first, q, prod, proj0, fact0, total, swap(total))
+    )(first, q, prod, proj0, fact0, *sums)
     return basis.T, proj, fact
 
 
@@ -517,7 +598,7 @@
         n, k = block.shape
         paired = n_col == 2 * n_row and n_row & (n_row - 1) == 0 and n_row > 1
         divides = coupling.shape[0] * n % 768 == 0
-        whole = divides and n % 64 == 0 and 8 * k == 128 and coupling.shape[2] == coupling.shape[0] * n * 2
+        whole = divides and n % 64 == 0 and n >= 256 and 8 * k == 128 and coupling.shape[2] == coupling.shape[0] * n * 2
         small = coupling.size * 4 <= 44 << 20
         if paired and whole and small:
             return on_device(n_row, n_col, coupling, energies, block)

time: 106 us -> 100 us (0.943)
  starting transfers between devices: 35 us -> 29.7 us
  waiting for transfers between devices: 13.5 us -> 8.37 us
  Pallas kernels: 56.5 us -> 60.8 us
    ppermute x32 -> x29, starting transfers between devices: 35 us -> 29.7 us  [send(): return lax.ppermute(value, axes, [p for p in pairs if p[1] is not None])]
    ppermute x32 -> x29, waiting for transfers between devices: 13.5 us -> 8.37 us  [send(): return lax.ppermute(value, axes, [p for p in pairs if p[1] is not None])]
    pallas_call x13 -> x17, Pallas kernels: 56.5 us -> 60.8 us  [call(): run(*[pltpu.with_memory_space_constraint(v, pltpu.HBM if i < far else plt...]
  transfers between devices with their start and end apart: 32 -> 29, of which waited for: 16 -> 10; matrix products, arithmetic and copies ran while one was open for 0% -> 0% of each run, Pallas kernels for 16% -> 27%
where the time goes in v6:
time: 100 us; the launch traced here: 99.8 us
  Pallas kernels  60.8 us (61%)
  starting transfers between devices  29.7 us (30%)
  waiting for transfers between devices  8.37 us (8%)
    pallas_call x17, Pallas kernels, call(): run(*[pltpu.with_memory_space_constraint(v, pltpu.HBM if i < far else plt...  60.8 us
    ppermute x29, starting transfers between devices, send(): return lax.ppermute(value, axes, [p for p in pairs if p[1] is not None])  29.7 us
    ppermute x29, waiting for transfers between devices, send(): return lax.ppermute(value, axes, [p for p in pairs if p[1] is not None])  8.37 us
  transfers between devices with their start and end apart: 29, of which 10 were waited for; matrix products, arithmetic and copies ran while one was open for 0% of the time, Pallas kernels for 27%

profile of v6, /device:TPU:0, one launch (start us, length us, event | category | flops | bytes accessed | tf_op | source)
XLA Modules:
  0.0 99.8 jit_solution(14833086248161222820)
XLA Ops:
  0.6 0.6 collective-permute-start
  1.2 2.0 %begin.1 = (f32[16,576]{1,0:T(8,128)S(1)}, f32[768,1152]{1,0:T(8,128)S(1)}) custom-call(f32[2304,4608]{1,0:T(8,128)} %bitcast.3, f32[16,576]{1,0:T(8,128)} %bitcast.8), custom_call_target="tpu_custom_call" | custom-call | flops 169869312 | bytes 1327104 | tf_op jit(solution)/shard_map/begin/pallas_call | solution.py:427
  3.2 0.1 order.1.refs_2_.refs_4_.refs_9_.first_ref
  3.3 3.5 %collective-permute-start.3 = (f32[16,1152]{1,0:T(8,128)S(1)}, f32[16,1152]{1,0:T(8,128)S(1)}, u32[]{:S(2)}, u32[]{:S(2)}) collective-permute-start(f32[16,1152]{1,0:T(8,128)S(1)} %order.1.refs_2_.refs_4_.refs_9_.first_ref), channel_id=1, source_target_pairs={{0,24},{1,7},{2,26},{3,5},{4,28},{5,3},{6,30},{7,1},{8,16},{9,15},... | collective-permute-start | bytes 221192 | tf_op jit(solution)/shard_map/ppermute | solution.py:447
  6.8 2.6 %collective-permute-start.2 = (f32[16,1152]{1,0:T(8,128)S(1)}, f32[16,1152]{1,0:T(8,128)S(1)}, u32[]{:S(2)}, u32[]{:S(2)}) collective-permute-start(f32[16,1152]{1,0:T(8,128)S(1)} %order.1.refs_2_.refs_4_.refs_9_.first_ref), channel_id=1, source_target_pairs={{0,4},{1,17},{2,6},{3,19},{4,0},{5,21},{6,2},{7,23},{8,12},{9,25},... | collective-permute-start | bytes 221192 | tf_op jit(solution)/shard_map/ppermute | solution.py:447
  9.4 1.6 %collective-permute-start.1 = (f32[16,1152]{1,0:T(8,128)S(1)}, f32[16,1152]{1,0:T(8,128)S(1)}, u32[]{:S(2)}, u32[]{:S(2)}) collective-permute-start(f32[16,1152]{1,0:T(8,128)S(1)} %order.1.refs_2_.refs_4_.refs_9_.first_ref), channel_id=1, source_target_pairs={{0,2},{1,9},{2,0},{3,11},{4,6},{5,13},{6,4},{7,15},{8,10},{9,1},{1... | collective-permute-start | bytes 221192 | tf_op jit(solution)/shard_map/ppermute | solution.py:447
  11.0 4.6 %first_early.1 = (f32[16,2304]{1,0:T(8,128)S(1)}, f32[768,1152]{1,0:T(8,128)S(1)}, f32[768,1152]{1,0:T(8,128)S(1)}, f32[768,1152]{1,0:T(8,128)S(1)}) custom-call(f32[2304,4608]{1,0:T(8,128)} %bitcast.4, f32[768,1152]{1,0:T(8,128)S(1)} %get-tuple-element.58.refs_1_.piece.refs_0_, f32[16,1152]{1,0:T(8,128)S(1)} %order.1.refs_2_.refs_4_.refs_9_.first_ref), custom_call_target="tpu_custom_call" | custom-call | flops 1358954496 | bytes 10616832 | tf_op jit(solution)/shard_map/first_early/pallas_call | solution.py:427
  15.6 0.0 collective-permute-done.3.refs_9_
  15.6 0.0 collective-permute-done.1.refs_7_
  15.6 0.1 collective-permute-start.4
  15.7 0.5 collective-permute-start.5
  16.2 0.1 collective-permute-start.6
  16.3 3.7 %first_own.1 = (f32[16,3456]{1,0:T(8,128)S(1)}, f32[768,1152]{1,0:T(8,128)S(1)}, f32[768,1152]{1,0:T(8,128)S(1)}) custom-call(f32[2304,4608]{1,0:T(8,128)} %bitcast.5, f32[768,1152]{1,0:T(8,128)S(1)} %get-tuple-element.61.refs_1_.refs_2_.refs_0_, f32[16,1152]{1,0:T(8,128)S(1)} %order.1.refs_2_.refs_4_.refs_9_.first_ref), custom_call_target="tpu_custom_call" | custom-call | flops 679477248 | bytes 5308416 | tf_op jit(solution)/shard_map/first_own/pallas_call | solution.py:427
  20.0 0.0 collective-permute-done.4.refs_10_
  20.0 0.0 collective-permute-done.6.refs_12_
  20.0 0.0 copy-start
  20.0 14.8 %first.1 = (f32[3,16,1152]{2,1,0:T(8,128)S(1)}, f32[3,16,1152]{2,1,0:T(8,128)S(1)}, f32[16,576]{1,0:T(8,128)S(1)}, bf16[32,2304]{1,0:T(8,128)(2,1)S(1)}, bf16[32...) custom-call(f32[2304,4608]{1,0:T(8,128)} %bitcast.6, ...), custom_call_target="tpu_custom_call" | custom-call | flops 5435817984 | bytes 42467328 | tf_op jit(solution)/shard_map/first/pallas_call | solution.py:427
  34.8 0.5 collective-permute-start.7
  35.3 1.0 first_near.1.refs_7_
  36.3 0.1 collective-permute-done.7.got_ref
  36.5 0.5 collective-permute-start.8
  37.0 0.7 collective-permute-start.9
  37.7 1.3 %collective-permute-start.10 = (f32[16,1152]{1,0:T(8,128)S(1)}, f32[16,1152]{1,0:T(8,128)S(1)}, u32[]{:S(2)}, u32[]{:S(2)}) collective-permute-start(f32[16,1152]{1,0:T(8,128)S(1)} %get-tuple-element.80), channel_id=1, source_target_pairs={{0,24},{1,7},{2,26},{3,5},{4,28},{5,3},{6,30},{7,1},{8,16},{9,15},... | collective-permute-start | bytes 221192 | tf_op jit(solution)/shard_map/ppermute | solution.py:447
  39.0 4.6 %first_late.1 = f32[16,1152]{1,0:T(8,128)S(1)} custom-call(f32[768,1152]{1,0:T(8,128)S(1)} %get-tuple-element.59.refs_0_.refs_1_, f32[768,1152]{1,0:T(8,128)S(1)} %get-tuple-element.60.refs_1_.refs_2_, f32[768,1152]{1,0:T(8,128)S(1)} %get-tuple-element.61.refs_1_.refs_2_.refs_0_, f32[768,1152]{1,0:T(8,128)S(1)} %get-tuple-element.64.refs_2_.refs_3_.refs_1_, ...), custom_call_target="tpu_custom_call" | custom-call | flops 2038431744 | bytes 15925248 | tf_op jit(solution)/shard_map/first_late/pallas_call | solution.py:427
  43.6 0.0 collective-permute-done.8
  43.6 0.2 collective-permute-done.9
  43.8 0.0 collective-permute-done.10
  43.8 0.1 collective-permute-start.11
  43.9 1.3 %collective-permute-done.11.got_ref = f32[16,1152]{1,0:T(8,128)S(1)} collective-permute-done((f32[16,1152]{1,0:T(8,128)S(1)}, f32[16,1152]{1,0:T(8,128)S(1)}, u32[]{:S(2)}, u32[]{:S(2)}) %collective-permute-start.11) | collective-permute-done | bytes 73760 | tf_op jit(solution)/shard_map/ppermute | solution.py:447
  45.2 0.3 pair.1.refs_3_.refs_9_.refs_0_.pair_ref
  45.5 1.5 %collective-permute-start.14 = (f32[16,1280]{1,0:T(8,128)S(1)}, f32[16,1280]{1,0:T(8,128)S(1)}, u32[]{:S(2)}, u32[]{:S(2)}) collective-permute-start(f32[16,1280]{1,0:T(8,128)S(1)} %pair.1.refs_3_.refs_9_.refs_0_.pair_ref), channel_id=1, source_target_pairs={{0,24},{1,7},{2,26},{3,5},{4,28},{5,3},{6,30},{7,1},{8,16},{9,15},... | collective-permute-start | bytes 245768 | tf_op jit(solution)/shard_map/ppermute | solution.py:447
  47.0 2.2 %collective-permute-start.13 = (f32[16,1280]{1,0:T(8,128)S(1)}, f32[16,1280]{1,0:T(8,128)S(1)}, u32[]{:S(2)}, u32[]{:S(2)}) collective-permute-start(f32[16,1280]{1,0:T(8,128)S(1)} %pair.1.refs_3_.refs_9_.refs_0_.pair_ref), channel_id=1, source_target_pairs={{0,4},{1,17},{2,6},{3,19},{4,0},{5,21},{6,2},{7,23},{8,12},{9,25},... | collective-permute-start | bytes 245768 | tf_op jit(solution)/shard_map/ppermute | solution.py:447
  49.2 1.6 %collective-permute-start.12 = (f32[16,1280]{1,0:T(8,128)S(1)}, f32[16,1280]{1,0:T(8,128)S(1)}, u32[]{:S(2)}, u32[]{:S(2)}) collective-permute-start(f32[16,1280]{1,0:T(8,128)S(1)} %pair.1.refs_3_.refs_9_.refs_0_.pair_ref), channel_id=1, source_target_pairs={{0,2},{1,9},{2,0},{3,11},{4,6},{5,13},{6,4},{7,15},{8,10},{9,1},{1... | collective-permute-start | bytes 245768 | tf_op jit(solution)/shard_map/ppermute | solution.py:447
  50.7 3.8 %second_early.1.refs_10_ = f32[16,2304]{1,0:T(8,128)S(1)} custom-call(f32[768,1152]{1,0:T(8,128)S(1)} %get-tuple-element.58.refs_1_.piece.refs_0_, f32[768,1152]{1,0:T(8,128)S(1)} %get-tuple-element.59.refs_0_.refs_1_, f32[768,1152]{1,0:T(8,128)S(1)} %get-tuple-element.60.refs_1_.refs_2_, f32[16,1280]{1,0:T(8,128)S(1)} %pair.1.refs_3_.refs_9_.refs_0_.pair_ref), custom_call_target="tpu_custom_call" | custom-call | flops 1358954496 | bytes 10616832 | tf_op jit(solution)/shard_map/second_early/pallas_call | solution.py:427
  54.5 0.0 collective-permute-done.14.refs_14_.refs_3_
  54.6 0.0 collective-permute-done.13.refs_13_.refs_2_
  54.6 0.1 collective-permute-start.15
  54.7 0.5 collective-permute-start.16
  55.2 0.1 collective-permute-start.17
  55.2 2.0 %second_own.1.refs_11_ = f32[16,3456]{1,0:T(8,128)S(1)} custom-call(f32[768,1152]{1,0:T(8,128)S(1)} %get-tuple-element.61.refs_1_.refs_2_.refs_0_, f32[768,1152]{1,0:T(8,128)S(1)} %get-tuple-element.64.refs_2_.refs_3_.refs_1_, f32[768,1152]{1,0:T(8,128)S(1)} %get-tuple-element.65.refs_3_.refs_4_.refs_2_, f32[16,1280]{1,0:T(8,128)S(1)} %pair.1.refs_3_.refs_9_.refs_0_.pair_ref), custom_call_target="tpu_custom_call" | custom-call | flops 679477248 | bytes 5308416 | tf_op jit(solution)/shard_map/second_own/pallas_call | solution.py:427
  57.3 0.0 collective-permute-done.16.refs_16_.refs_5_
  57.3 12.9 %second.1 = (f32[3,16,1152]{2,1,0:T(8,128)S(1)}, f32[3,16,1152]{2,1,0:T(8,128)S(1)}, f32[16,576]{1,0:T(8,128)S(1)}, bf16[32,2304]{1,0:T(8,128)(2,1)S(1)}, bf16[32,3456]{1,0:T(8,128)(2,1)S(1)}) custom-call(f32[768,1152]{1,0:T(8,128)S(1)} %get-tuple-element.61.refs_1_.refs_2_.refs_0_, f32[768,1152]{1,0:T(8,128)S(1)} %get-tuple-element.64.refs_2_.refs_3_.refs_1_, ...), custom_call_target="tpu_custom_call" | custom-call | flops 5435817984 | bytes 42467328 | tf_op jit(solution)/shard_map/second/pallas_call | solution.py:427
  70.2 0.5 collective-permute-start.18
  70.7 1.0 second_near.1.refs_7_
  71.7 0.1 collective-permute-done.18.got_ref
  71.8 0.6 collective-permute-start.19
  72.4 1.7 %collective-permute-start.20 = (f32[16,1280]{1,0:T(8,128)S(1)}, f32[16,1280]{1,0:T(8,128)S(1)}, u32[]{:S(2)}, u32[]{:S(2)}) collective-permute-start(f32[16,1280]{1,0:T(8,128)S(1)} %get-tuple-element.101), channel_id=1, source_target_pairs={{0,4},{1,17},{2,6},{3,19},{4,0},{5,21},{6,2},{7,23},{8,12},{9,25},... | collective-permute-start | bytes 245768 | tf_op jit(solution)/shard_map/ppermute | solution.py:447
  74.1 1.1 %collective-permute-start.21 = (f32[16,1280]{1,0:T(8,128)S(1)}, f32[16,1280]{1,0:T(8,128)S(1)}, u32[]{:S(2)}, u32[]{:S(2)}) collective-permute-start(f32[16,1280]{1,0:T(8,128)S(1)} %get-tuple-element.102), channel_id=1, source_target_pairs={{0,24},{1,7},{2,26},{3,5},{4,28},{5,3},{6,30},{7,1},{8,16},{9,15},... | collective-permute-start | bytes 245768 | tf_op jit(solution)/shard_map/ppermute | solution.py:447
  75.2 4.6 %second_late.1 = f32[16,1280]{1,0:T(8,128)S(1)} custom-call(f32[768,1152]{1,0:T(8,128)S(1)} %get-tuple-element.59.refs_0_.refs_1_, f32[768,1152]{1,0:T(8,128)S(1)} %get-tuple-element.60.refs_1_.refs_2_, f32[768,1152]{1,0:T(8,128)S(1)} %get-tuple-element.61.refs_1_.refs_2_.refs_0_, f32[768,1152]{1,0:T(8,128)S(1)} %get-tuple-element.64.refs_2_.refs_3_.refs_1_, ...), custom_call_target="tpu_custom_call" | custom-call | flops 2038431744 | bytes 15925248 | tf_op jit(solution)/shard_map/second_late/pallas_call | solution.py:427
  79.7 0.0 collective-permute-done.19
  79.8 0.1 collective-permute-start.22
  79.9 1.3 %collective-permute-done.22.got_ref = f32[16,1280]{1,0:T(8,128)S(1)} collective-permute-done((f32[16,1280]{1,0:T(8,128)S(1)}, f32[16,1280]{1,0:T(8,128)S(1)}, u32[]{:S(2)}, u32[]{:S(2)}) %collective-permute-start.22) | collective-permute-done | bytes 81952 | tf_op jit(solution)/shard_map/ppermute | solution.py:447
  81.1 2.6 %middle.1 = (f32[16,1152]{1,0:T(8,128)S(1)}, f32[16,1152]{1,0:T(8,128)S(1)}, f32[48,48]{1,0:T(8,128)S(1)}, f32[16,16]{1,0:T(8,128)S(1)}, f32[16,16]{1,0:T(8,128)S(1)}) custom-call(f32[16,1152]{1,0:T(8,128)S(1)} %order.1.refs_2_.refs_4_.refs_9_.first_ref, f32[16,1280]{1,0:T(8,128)S(1)} %pair.1.refs_3_.refs_9_.refs_0_.pair_ref, ...), custom_call_target="tpu_custom_call" | custom-call | tf_op jit(solution)/shard_map/middle/pallas_call | solution.py:427
  83.8 1.9 %collective-permute-start.25 = (f32[48,48]{1,0:T(8,128)S(1)}, f32[48,48]{1,0:T(8,128)S(1)}, u32[]{:S(2)}, u32[]{:S(2)}) collective-permute-start(f32[48,48]{1,0:T(8,128)S(1)} %get-tuple-element.107), channel_id=1, source_target_pairs={{0,24},{1,25},{2,26},{3,27},{4,28},{5,29},{6,30},{7,31},{8,16},{9,... | collective-permute-start | bytes 27656 | tf_op jit(solution)/shard_map/ppermute | solution.py:447
  85.7 0.5 collective-permute-start.24
  86.2 1.1 %collective-permute-start.23 = (f32[48,48]{1,0:T(8,128)S(1)}, f32[48,48]{1,0:T(8,128)S(1)}, u32[]{:S(2)}, u32[]{:S(2)}) collective-permute-start(f32[48,48]{1,0:T(8,128)S(1)} %get-tuple-element.107), channel_id=1, source_target_pairs={{0,8},{1,9},{2,10},{3,11},{4,12},{5,13},{6,14},{7,15},{8,0},{9,1},... | collective-permute-start | bytes 27656 | tf_op jit(solution)/shard_map/ppermute | solution.py:447
  87.3 1.3 %collective-permute-done.25 = f32[48,48]{1,0:T(8,128)S(1)} collective-permute-done((f32[48,48]{1,0:T(8,128)S(1)}, f32[48,48]{1,0:T(8,128)S(1)}, u32[]{:S(2)}, u32[]{:S(2)}) %collective-permute-start.25) | collective-permute-done | bytes 9248 | tf_op jit(solution)/shard_map/ppermute | solution.py:447
  88.7 0.8 collective-permute-done.24
  89.5 0.5 collective-permute-done.23
  90.0 2.3 %collective-permute-start.28 = (f32[48,48]{1,0:T(8,128)S(1)}, f32[48,48]{1,0:T(8,128)S(1)}, u32[]{:S(2)}, u32[]{:S(2)}) collective-permute-start(f32[48,48]{1,0:T(8,128)S(1)} %add_add_fusion.2.refs_0_), channel_id=1, source_target_pairs={{0,6},{1,7},{2,4},{3,5},{4,2},{5,3},{6,0},{7,1},{8,14},{9,15},{10,... | collective-permute-start | bytes 27656 | tf_op jit(solution)/shard_map/ppermute | solution.py:447
  92.3 2.2 %collective-permute-start.26 = (f32[48,48]{1,0:T(8,128)S(1)}, f32[48,48]{1,0:T(8,128)S(1)}, u32[]{:S(2)}, u32[]{:S(2)}) collective-permute-start(f32[48,48]{1,0:T(8,128)S(1)} %add_add_fusion.2.refs_0_), channel_id=1, source_target_pairs={{0,2},{1,3},{2,0},{3,1},{4,6},{5,7},{6,4},{7,5},{8,10},{9,11},{10,... | collective-permute-start | bytes 27656 | tf_op jit(solution)/shard_map/ppermute | solution.py:447
  94.5 1.2 %collective-permute-done.28.refs_3_ = f32[48,48]{1,0:T(8,128)S(1)} collective-permute-done((f32[48,48]{1,0:T(8,128)S(1)}, f32[48,48]{1,0:T(8,128)S(1)}, u32[]{:S(2)}, u32[]{:S(2)}) %collective-permute-start.28) | collective-permute-done | bytes 9248 | tf_op jit(solution)/shard_map/ppermute | solution.py:447
  95.7 1.3 %collective-permute-done.27.refs_2_ = f32[48,48]{1,0:T(8,128)S(1)} collective-permute-done((f32[48,48]{1,0:T(8,128)S(1)}, f32[48,48]{1,0:T(8,128)S(1)}, u32[]{:S(2)}, u32[]{:S(2)}) %collective-permute-start.27) | collective-permute-done | bytes 9248 | tf_op jit(solution)/shard_map/ppermute | solution.py:447
  97.0 2.8 %last.1 = (f32[16,576]{1,0:T(8,128)}, f32[2,16,16]{2,1,0:T(8,128)}, f32[2,16,16]{2,1,0:T(8,128)}) custom-call(f32[16,1152]{1,0:T(8,128)S(1)} %order.1.refs_2_.refs_4_.refs_9_.first_ref, f32[16,1152]{1,0:T(8,128)S(1)} %get-tuple-element.103.q_ref, f32[16,1152]{1,0:T(8,128)S(1)} %get-tuple-element.104.prod_ref, f32[16,16]{1,0:T(8,128)S(1)} %get-tuple-element.105.proj0_ref, ...), custom_call_target="tpu_custom_call" | custom-call | tf_op jit(solution)/shard_map/last/pallas_call | solution.py:427
  (17 shorter events, 0.1 us)
Async XLA Ops:
  0.6 2.6 %collective-permute-start = (f32[16,576]{1,0:T(8,128)}, f32[16,576]{1,0:T(8,128)S(1)}, u32[]{:S(2)}, u32[]{:S(2)}) collective-permute-start(f32[16,576]{1,0:T(8,128)} %bitcast.7), channel_id=1, source_target_pairs={{0,1},{1,0},{2,3},{3,2},{4,5},{5,4},{6,7},{7,6},{8,9},{9,8},{10,11... | collective-permute-start | bytes 110600 | tf_op jit(solution)/shard_map/ppermute | solution.py:447
  3.3 12.3 %collective-permute-start.3 = (f32[16,1152]{1,0:T(8,128)S(1)}, f32[16,1152]{1,0:T(8,128)S(1)}, u32[]{:S(2)}, u32[]{:S(2)}) collective-permute-start(f32[16,1152]{1,0:T(8,128)S(1)} %order.1.refs_2_.refs_4_.refs_9_.first_ref), channel_id=1, source_target_pairs={{0,24},{1,7},{2,26},{3,5},{4,28},{5,3},{6,30},{7,1},{8,16},{9,15},... | collective-permute-start | bytes 221192 | tf_op jit(solution)/shard_map/ppermute | solution.py:447
  6.8 8.8 %collective-permute-start.2 = (f32[16,1152]{1,0:T(8,128)S(1)}, f32[16,1152]{1,0:T(8,128)S(1)}, u32[]{:S(2)}, u32[]{:S(2)}) collective-permute-start(f32[16,1152]{1,0:T(8,128)S(1)} %order.1.refs_2_.refs_4_.refs_9_.first_ref), channel_id=1, source_target_pairs={{0,4},{1,17},{2,6},{3,19},{4,0},{5,21},{6,2},{7,23},{8,12},{9,25},... | collective-permute-start | bytes 221192 | tf_op jit(solution)/shard_map/ppermute | solution.py:447
  9.4 6.2 %collective-permute-start.1 = (f32[16,1152]{1,0:T(8,128)S(1)}, f32[16,1152]{1,0:T(8,128)S(1)}, u32[]{:S(2)}, u32[]{:S(2)}) collective-permute-start(f32[16,1152]{1,0:T(8,128)S(1)} %order.1.refs_2_.refs_4_.refs_9_.first_ref), channel_id=1, source_target_pairs={{0,2},{1,9},{2,0},{3,11},{4,6},{5,13},{6,4},{7,15},{8,10},{9,1},{1... | collective-permute-start | bytes 221192 | tf_op jit(solution)/shard_map/ppermute | solution.py:447
  15.6 4.4 %collective-permute-start.4 = (f32[16,1152]{1,0:T(8,128)S(1)}, f32[16,1152]{1,0:T(8,128)S(1)}, u32[]{:S(2)}, u32[]{:S(2)}) collective-permute-start(f32[16,1152]{1,0:T(8,128)S(1)} %collective-permute-done.1.refs_7_), channel_id=1, source_target_pairs={{0,1},{1,0},{2,3},{3,2},{4,5},{5,4},{6,7},{7,6},{8,9},{9,8},{10,11... | collective-permute-start | bytes 221192 | tf_op jit(solution)/shard_map/ppermute | solution.py:447
  15.7 4.3 %collective-permute-start.5 = (f32[16,1152]{1,0:T(8,128)S(1)}, f32[16,1152]{1,0:T(8,128)S(1)}, u32[]{:S(2)}, u32[]{:S(2)}) collective-permute-start(f32[16,1152]{1,0:T(8,128)S(1)} %collective-permute-done.2.refs_8_), channel_id=1, source_target_pairs={{0,1},{1,0},{2,3},{3,2},{4,5},{5,4},{6,7},{7,6},{8,9},{9,8},{10,11... | collective-permute-start | bytes 221192 | tf_op jit(solution)/shard_map/ppermute | solution.py:447
  16.2 3.8 %collective-permute-start.6 = (f32[16,1152]{1,0:T(8,128)S(1)}, f32[16,1152]{1,0:T(8,128)S(1)}, u32[]{:S(2)}, u32[]{:S(2)}) collective-permute-start(f32[16,1152]{1,0:T(8,128)S(1)} %collective-permute-done.3.refs_9_), channel_id=1, source_target_pairs={{0,1},{1,0},{2,3},{3,2},{4,5},{5,4},{6,7},{7,6},{8,9},{9,8},{10,11... | collective-permute-start | bytes 221192 | tf_op jit(solution)/shard_map/ppermute | solution.py:447
  20.0 15.3 %copy-start = (f32[576]{0:T(1024)S(1)}, f32[576]{0:T(1024)}, u32[]{:S(2)}) copy-start(f32[576]{0:T(1024)} %param.4) | copy-start | bytes 6916
  34.8 1.6 %collective-permute-start.7 = (f32[3,16,1152]{2,1,0:T(8,128)S(1)}, f32[3,16,1152]{2,1,0:T(8,128)S(1)}, u32[]{:S(2)}, u32[]{:S(2)}) collective-permute-start(f32[3,16,1152]{2,1,0:T(8,128)S(1)} %get-tuple-element.73), channel_id=1, source_target_pairs={{0,1},{1,0},{2,3},{3,2},{4,5},{5,4},{6,7},{7,6},{8,9},{9,8},{10,11... | collective-permute-start | bytes 663560 | tf_op jit(solution)/shard_map/ppermute | solution.py:447
  36.5 7.1 %collective-permute-start.8 = (f32[16,1152]{1,0:T(8,128)S(1)}, f32[16,1152]{1,0:T(8,128)S(1)}, u32[]{:S(2)}, u32[]{:S(2)}) collective-permute-start(f32[16,1152]{1,0:T(8,128)S(1)} %get-tuple-element.78), channel_id=1, source_target_pairs={{0,2},{1,9},{2,0},{3,11},{4,6},{5,13},{6,4},{7,15},{8,10},{9,1},{1... | collective-permute-start | bytes 221192 | tf_op jit(solution)/shard_map/ppermute | solution.py:447
  37.0 6.8 %collective-permute-start.9 = (f32[16,1152]{1,0:T(8,128)S(1)}, f32[16,1152]{1,0:T(8,128)S(1)}, u32[]{:S(2)}, u32[]{:S(2)}) collective-permute-start(f32[16,1152]{1,0:T(8,128)S(1)} %get-tuple-element.79), channel_id=1, source_target_pairs={{0,4},{1,17},{2,6},{3,19},{4,0},{5,21},{6,2},{7,23},{8,12},{9,25},... | collective-permute-start | bytes 221192 | tf_op jit(solution)/shard_map/ppermute | solution.py:447
  37.7 6.1 %collective-permute-start.10 = (f32[16,1152]{1,0:T(8,128)S(1)}, f32[16,1152]{1,0:T(8,128)S(1)}, u32[]{:S(2)}, u32[]{:S(2)}) collective-permute-start(f32[16,1152]{1,0:T(8,128)S(1)} %get-tuple-element.80), channel_id=1, source_target_pairs={{0,24},{1,7},{2,26},{3,5},{4,28},{5,3},{6,30},{7,1},{8,16},{9,15},... | collective-permute-start | bytes 221192 | tf_op jit(solution)/shard_map/ppermute | solution.py:447
  43.8 1.3 %collective-permute-start.11 = (f32[16,1152]{1,0:T(8,128)S(1)}, f32[16,1152]{1,0:T(8,128)S(1)}, u32[]{:S(2)}, u32[]{:S(2)}) collective-permute-start(f32[16,1152]{1,0:T(8,128)S(1)} %add_add_fusion.1.mine_ref), channel_id=1, source_target_pairs={{0,1},{1,0},{2,3},{3,2},{4,5},{5,4},{6,7},{7,6},{8,9},{9,8},{10,11... | collective-permute-start | bytes 221192 | tf_op jit(solution)/shard_map/ppermute | solution.py:447
  45.5 9.0 %collective-permute-start.14 = (f32[16,1280]{1,0:T(8,128)S(1)}, f32[16,1280]{1,0:T(8,128)S(1)}, u32[]{:S(2)}, u32[]{:S(2)}) collective-permute-start(f32[16,1280]{1,0:T(8,128)S(1)} %pair.1.refs_3_.refs_9_.refs_0_.pair_ref), channel_id=1, source_target_pairs={{0,24},{1,7},{2,26},{3,5},{4,28},{5,3},{6,30},{7,1},{8,16},{9,15},... | collective-permute-start | bytes 245768 | tf_op jit(solution)/shard_map/ppermute | solution.py:447
  47.0 7.6 %collective-permute-start.13 = (f32[16,1280]{1,0:T(8,128)S(1)}, f32[16,1280]{1,0:T(8,128)S(1)}, u32[]{:S(2)}, u32[]{:S(2)}) collective-permute-start(f32[16,1280]{1,0:T(8,128)S(1)} %pair.1.refs_3_.refs_9_.refs_0_.pair_ref), channel_id=1, source_target_pairs={{0,4},{1,17},{2,6},{3,19},{4,0},{5,21},{6,2},{7,23},{8,12},{9,25},... | collective-permute-start | bytes 245768 | tf_op jit(solution)/shard_map/ppermute | solution.py:447
  49.2 5.4 %collective-permute-start.12 = (f32[16,1280]{1,0:T(8,128)S(1)}, f32[16,1280]{1,0:T(8,128)S(1)}, u32[]{:S(2)}, u32[]{:S(2)}) collective-permute-start(f32[16,1280]{1,0:T(8,128)S(1)} %pair.1.refs_3_.refs_9_.refs_0_.pair_ref), channel_id=1, source_target_pairs={{0,2},{1,9},{2,0},{3,11},{4,6},{5,13},{6,4},{7,15},{8,10},{9,1},{1... | collective-permute-start | bytes 245768 | tf_op jit(solution)/shard_map/ppermute | solution.py:447
  54.6 2.7 %collective-permute-start.15 = (f32[16,1280]{1,0:T(8,128)S(1)}, f32[16,1280]{1,0:T(8,128)S(1)}, u32[]{:S(2)}, u32[]{:S(2)}) collective-permute-start(f32[16,1280]{1,0:T(8,128)S(1)} %collective-permute-done.12.refs_12_.refs_1_), channel_id=1, source_target_pairs={{0,1},{1,0},{2,3},{3,2},{4,5},{5,4},{6,7},{7,6},{8,9},{9,8},{10,11... | collective-permute-start | bytes 245768 | tf_op jit(solution)/shard_map/ppermute | solution.py:447
  54.7 2.6 %collective-permute-start.16 = (f32[16,1280]{1,0:T(8,128)S(1)}, f32[16,1280]{1,0:T(8,128)S(1)}, u32[]{:S(2)}, u32[]{:S(2)}) collective-permute-start(f32[16,1280]{1,0:T(8,128)S(1)} %collective-permute-done.13.refs_13_.refs_2_), channel_id=1, source_target_pairs={{0,1},{1,0},{2,3},{3,2},{4,5},{5,4},{6,7},{7,6},{8,9},{9,8},{10,11... | collective-permute-start | bytes 245768 | tf_op jit(solution)/shard_map/ppermute | solution.py:447
  55.2 2.1 %collective-permute-start.17 = (f32[16,1280]{1,0:T(8,128)S(1)}, f32[16,1280]{1,0:T(8,128)S(1)}, u32[]{:S(2)}, u32[]{:S(2)}) collective-permute-start(f32[16,1280]{1,0:T(8,128)S(1)} %collective-permute-done.14.refs_14_.refs_3_), channel_id=1, source_target_pairs={{0,1},{1,0},{2,3},{3,2},{4,5},{5,4},{6,7},{7,6},{8,9},{9,8},{10,11... | collective-permute-start | bytes 245768 | tf_op jit(solution)/shard_map/ppermute | solution.py:447
  70.2 1.6 %collective-permute-start.18 = (f32[3,16,1152]{2,1,0:T(8,128)S(1)}, f32[3,16,1152]{2,1,0:T(8,128)S(1)}, u32[]{:S(2)}, u32[]{:S(2)}) collective-permute-start(f32[3,16,1152]{2,1,0:T(8,128)S(1)} %get-tuple-element.94), channel_id=1, source_target_pairs={{0,1},{1,0},{2,3},{3,2},{4,5},{5,4},{6,7},{7,6},{8,9},{9,8},{10,11... | collective-permute-start | bytes 663560 | tf_op jit(solution)/shard_map/ppermute | solution.py:447
  71.8 7.9 %collective-permute-start.19 = (f32[16,1280]{1,0:T(8,128)S(1)}, f32[16,1280]{1,0:T(8,128)S(1)}, u32[]{:S(2)}, u32[]{:S(2)}) collective-permute-start(f32[16,1280]{1,0:T(8,128)S(1)} %get-tuple-element.100), channel_id=1, source_target_pairs={{0,2},{1,9},{2,0},{3,11},{4,6},{5,13},{6,4},{7,15},{8,10},{9,1},{1... | collective-permute-start | bytes 245768 | tf_op jit(solution)/shard_map/ppermute | solution.py:447
  72.4 7.3 %collective-permute-start.20 = (f32[16,1280]{1,0:T(8,128)S(1)}, f32[16,1280]{1,0:T(8,128)S(1)}, u32[]{:S(2)}, u32[]{:S(2)}) collective-permute-start(f32[16,1280]{1,0:T(8,128)S(1)} %get-tuple-element.101), channel_id=1, source_target_pairs={{0,4},{1,17},{2,6},{3,19},{4,0},{5,21},{6,2},{7,23},{8,12},{9,25},... | collective-permute-start | bytes 245768 | tf_op jit(solution)/shard_map/ppermute | solution.py:447
  74.1 5.7 %collective-permute-start.21 = (f32[16,1280]{1,0:T(8,128)S(1)}, f32[16,1280]{1,0:T(8,128)S(1)}, u32[]{:S(2)}, u32[]{:S(2)}) collective-permute-start(f32[16,1280]{1,0:T(8,128)S(1)} %get-tuple-element.102), channel_id=1, source_target_pairs={{0,24},{1,7},{2,26},{3,5},{4,28},{5,3},{6,30},{7,1},{8,16},{9,15},... | collective-permute-start | bytes 245768 | tf_op jit(solution)/shard_map/ppermute | solution.py:447
  79.8 1.3 %collective-permute-start.22 = (f32[16,1280]{1,0:T(8,128)S(1)}, f32[16,1280]{1,0:T(8,128)S(1)}, u32[]{:S(2)}, u32[]{:S(2)}) collective-permute-start(f32[16,1280]{1,0:T(8,128)S(1)} %add_add_fusion.mine_ref), channel_id=1, source_target_pairs={{0,1},{1,0},{2,3},{3,2},{4,5},{5,4},{6,7},{7,6},{8,9},{9,8},{10,11... | collective-permute-start | bytes 245768 | tf_op jit(solution)/shard_map/ppermute | solution.py:447
  83.8 4.9 %collective-permute-start.25 = (f32[48,48]{1,0:T(8,128)S(1)}, f32[48,48]{1,0:T(8,128)S(1)}, u32[]{:S(2)}, u32[]{:S(2)}) collective-permute-start(f32[48,48]{1,0:T(8,128)S(1)} %get-tuple-element.107), channel_id=1, source_target_pairs={{0,24},{1,25},{2,26},{3,27},{4,28},{5,29},{6,30},{7,31},{8,16},{9,... | collective-permute-start | bytes 27656 | tf_op jit(solution)/shard_map/ppermute | solution.py:447
  85.7 3.8 %collective-permute-start.24 = (f32[48,48]{1,0:T(8,128)S(1)}, f32[48,48]{1,0:T(8,128)S(1)}, u32[]{:S(2)}, u32[]{:S(2)}) collective-permute-start(f32[48,48]{1,0:T(8,128)S(1)} %get-tuple-element.107), channel_id=1, source_target_pairs={{0,16},{1,17},{2,18},{3,19},{4,20},{5,21},{6,22},{7,23},{8,24},{9,... | collective-permute-start | bytes 27656 | tf_op jit(solution)/shard_map/ppermute | solution.py:447
  86.2 3.8 %collective-permute-start.23 = (f32[48,48]{1,0:T(8,128)S(1)}, f32[48,48]{1,0:T(8,128)S(1)}, u32[]{:S(2)}, u32[]{:S(2)}) collective-permute-start(f32[48,48]{1,0:T(8,128)S(1)} %get-tuple-element.107), channel_id=1, source_target_pairs={{0,8},{1,9},{2,10},{3,11},{4,12},{5,13},{6,14},{7,15},{8,0},{9,1},... | collective-permute-start | bytes 27656 | tf_op jit(solution)/shard_map/ppermute | solution.py:447
  90.0 5.7 %collective-permute-start.28 = (f32[48,48]{1,0:T(8,128)S(1)}, f32[48,48]{1,0:T(8,128)S(1)}, u32[]{:S(2)}, u32[]{:S(2)}) collective-permute-start(f32[48,48]{1,0:T(8,128)S(1)} %add_add_fusion.2.refs_0_), channel_id=1, source_target_pairs={{0,6},{1,7},{2,4},{3,5},{4,2},{5,3},{6,0},{7,1},{8,14},{9,15},{10,... | collective-permute-start | bytes 27656 | tf_op jit(solution)/shard_map/ppermute | solution.py:447
  92.3 4.7 %collective-permute-start.27 = (f32[48,48]{1,0:T(8,128)S(1)}, f32[48,48]{1,0:T(8,128)S(1)}, u32[]{:S(2)}, u32[]{:S(2)}) collective-permute-start(f32[48,48]{1,0:T(8,128)S(1)} %add_add_fusion.2.refs_0_), channel_id=1, source_target_pairs={{0,4},{1,5},{2,6},{3,7},{4,0},{5,1},{6,2},{7,3},{8,12},{9,13},{10,... | collective-permute-start | bytes 27656 | tf_op jit(solution)/shard_map/ppermute | solution.py:447
  92.3 4.7 %collective-permute-start.26 = (f32[48,48]{1,0:T(8,128)S(1)}, f32[48,48]{1,0:T(8,128)S(1)}, u32[]{:S(2)}, u32[]{:S(2)}) collective-permute-start(f32[48,48]{1,0:T(8,128)S(1)} %add_add_fusion.2.refs_0_), channel_id=1, source_target_pairs={{0,2},{1,3},{2,0},{3,1},{4,6},{5,7},{6,4},{7,5},{8,10},{9,11},{10,... | collective-permute-start | bytes 27656 | tf_op jit(solution)/shard_map/ppermute | solution.py:447

commit v7 on v6

--- a/solution.py
+++ b/solution.py
@@ -502,11 +502,11 @@
             held.extend(outs[len(out_shapes) :])
             return outs[: len(out_shapes)]
 
-        mine = [send(pair, spread(s)) for s in steps]
+        mine = [send(pair, spread(s)) for s in reversed(steps)][::-1]
         (u0,) = matrix_call(
             early_kernel,
             range(parts),
-            parts + 1,
+            parts + 2,
             [shape(k, rows)],
             [pair],
             [pltpu.VMEM((2 * k, 2 * n), BF16)],
@@ -518,7 +518,7 @@
         (v0,) = matrix_call(
             own_kernel,
             range(parts, parts + group - 1),
-            parts + group - 1,
+            parts + group,
             [shape(k, (group - 1) * 2 * n)],
             [same],
             [pltpu.VMEM((2 * k, n), BF16)],
@@ -580,8 +580,8 @@
         4,
         name="middle",
     )(first, pair, mine, got)
-    moments = sum([send(moments, lambda r, c, s=s: chip(r, c, s, 0)) for s in steps], moments)
-    sums = [moments] + [send(moments, lambda r, c, s=s: chip(r, c, 0, s)) for s in steps]
+    moments = sum([send(moments, lambda r, c, s=s: chip(r, c, s, 0)) for s in reversed(steps)], moments)
+    sums = [moments] + [send(moments, lambda r, c, s=s: chip(r, c, 0, s)) for s in reversed(steps)]
     basis, proj, fact = call(
         functools.partial(last_kernel, k, n, order),
         (shape(k, n), shape(2, k, k), shape(2, k, k)),

time: 100 us -> 101 us (1.010)
  waiting for transfers between devices: 8.37 us -> 11.4 us
  Pallas kernels: 60.8 us -> 59.1 us
    ppermute x29, waiting for transfers between devices: 8.37 us -> 11.4 us  [send(): return lax.ppermute(value, axes, [p for p in pairs if p[1] is not None])]
    pallas_call x17, Pallas kernels: 60.8 us -> 59.1 us  [call(): run(*[pltpu.with_memory_space_constraint(v, pltpu.HBM if i < far else plt...]
where the time goes in v7:
time: 101 us
  Pallas kernels  59.1 us (59%)
  starting transfers between devices  29.1 us (29%)
  waiting for transfers between devices  11.4 us (11%)
    pallas_call x17, Pallas kernels, call(): run(*[pltpu.with_memory_space_constraint(v, pltpu.HBM if i < far else plt...  59.1 us
    ppermute x29, starting transfers between devices, send(): return lax.ppermute(value, axes, [p for p in pairs if p[1] is not None])  29.1 us
    ppermute x29, waiting for transfers between devices, send(): return lax.ppermute(value, axes, [p for p in pairs if p[1] is not None])  11.4 us
  transfers between devices with their start and end apart: 29, of which 10 were waited for; matrix products, arithmetic and copies ran while one was open for 0% of the time, Pallas kernels for 27%

profile of v7, /device:TPU:0, one launch (start us, length us, event | category | flops | bytes accessed | tf_op | source)
XLA Modules:
  0.0 100.5 jit_solution(16832051690774913772)
XLA Ops:
  0.6 0.6 collective-permute-start
  1.2 2.0 %begin.1 = (f32[16,576]{1,0:T(8,128)S(1)}, f32[768,1152]{1,0:T(8,128)S(1)}) custom-call(f32[2304,4608]{1,0:T(8,128)} %bitcast.3, f32[16,576]{1,0:T(8,128)} %bitcast.8), custom_call_target="tpu_custom_call" | custom-call | flops 169869312 | bytes 1327104 | tf_op jit(solution)/shard_map/begin/pallas_call | solution.py:427
  3.2 0.1 order.1.refs_2_.refs_3_.refs_5_.refs_9_.first_ref
  3.3 3.5 %collective-permute-start.3 = (f32[16,1152]{1,0:T(8,128)S(1)}, f32[16,1152]{1,0:T(8,128)S(1)}, u32[]{:S(2)}, u32[]{:S(2)}) collective-permute-start(f32[16,1152]{1,0:T(8,128)S(1)} %order.1.refs_2_.refs_3_.refs_5_.refs_9_.first_ref), channel_id=1, source_target_pairs={{0,24},{1,7},{2,26},{3,5},{4,28},{5,3},{6,30},{7,1},{8,16},{9,15},... | collective-permute-start | bytes 221192 | tf_op jit(solution)/shard_map/ppermute | solution.py:447
  6.8 2.6 %collective-permute-start.2 = (f32[16,1152]{1,0:T(8,128)S(1)}, f32[16,1152]{1,0:T(8,128)S(1)}, u32[]{:S(2)}, u32[]{:S(2)}) collective-permute-start(f32[16,1152]{1,0:T(8,128)S(1)} %order.1.refs_2_.refs_3_.refs_5_.refs_9_.first_ref), channel_id=1, source_target_pairs={{0,4},{1,17},{2,6},{3,19},{4,0},{5,21},{6,2},{7,23},{8,12},{9,25},... | collective-permute-start | bytes 221192 | tf_op jit(solution)/shard_map/ppermute | solution.py:447
  9.4 1.6 %collective-permute-start.1 = (f32[16,1152]{1,0:T(8,128)S(1)}, f32[16,1152]{1,0:T(8,128)S(1)}, u32[]{:S(2)}, u32[]{:S(2)}) collective-permute-start(f32[16,1152]{1,0:T(8,128)S(1)} %order.1.refs_2_.refs_3_.refs_5_.refs_9_.first_ref), channel_id=1, source_target_pairs={{0,2},{1,9},{2,0},{3,11},{4,6},{5,13},{6,4},{7,15},{8,10},{9,1},{1... | collective-permute-start | bytes 221192 | tf_op jit(solution)/shard_map/ppermute | solution.py:447
  11.0 5.1 %first_early.1 = (f32[16,2304]{1,0:T(8,128)S(1)}, f32[768,1152]{1,0:T(8,128)S(1)}, f32[768,1152]{1,0:T(8,128)S(1)}, f32[768,1152]{1,0:T(8,128)S(1)}, f32[768,1152]{1,0:T(8,128)S(1)}) custom-call(f32[2304,4608]{1,0:T(8,128)} %bitcast.4, f32[768,1152]{1,0:T(8,128)S(1)} %get-tuple-element.58.refs_1_.piece.refs_0_, ...), custom_call_target="tpu_custom_call" | custom-call | flops 1358954496 | bytes 10616832 | tf_op jit(solution)/shard_map/first_early/pallas_call | solution.py:427
  16.1 0.0 collective-permute-done.1.refs_8_
  16.1 0.1 collective-permute-start.4
  16.2 0.5 collective-permute-start.5
  16.7 0.1 collective-permute-start.6
  16.8 3.1 %first_own.1 = (f32[16,3456]{1,0:T(8,128)S(1)}, f32[768,1152]{1,0:T(8,128)S(1)}, f32[768,1152]{1,0:T(8,128)S(1)}) custom-call(f32[2304,4608]{1,0:T(8,128)} %bitcast.5, f32[768,1152]{1,0:T(8,128)S(1)} %get-tuple-element.61.refs_1_.refs_2_.refs_0_, f32[768,1152]{1,0:T(8,128)S(1)} %get-tuple-element.62.refs_2_.refs_3_.refs_1_, ...), custom_call_target="tpu_custom_call" | custom-call | flops 679477248 | bytes 5308416 | tf_op jit(solution)/shard_map/first_own/pallas_call | solution.py:427
  19.9 0.0 collective-permute-done.4.refs_11_
  19.9 0.0 collective-permute-done.6.refs_13_
  19.9 0.0 copy-start
  19.9 13.0 %first.1 = (f32[3,16,1152]{2,1,0:T(8,128)S(1)}, f32[3,16,1152]{2,1,0:T(8,128)S(1)}, f32[16,576]{1,0:T(8,128)S(1)}, bf16[32,2304]{1,0:T(8,128)(2,1)S(1)}, bf16[32...) custom-call(f32[2304,4608]{1,0:T(8,128)} %bitcast.6, ...), custom_call_target="tpu_custom_call" | custom-call | flops 5435817984 | bytes 42467328 | tf_op jit(solution)/shard_map/first/pallas_call | solution.py:427
  33.0 0.5 collective-permute-start.7
  33.5 1.0 first_near.1.refs_7_
  34.4 0.1 collective-permute-done.7.got_ref
  34.6 0.7 collective-permute-start.8
  35.3 0.1 collective-permute-start.9
  35.5 1.2 %collective-permute-start.10 = (f32[16,1152]{1,0:T(8,128)S(1)}, f32[16,1152]{1,0:T(8,128)S(1)}, u32[]{:S(2)}, u32[]{:S(2)}) collective-permute-start(f32[16,1152]{1,0:T(8,128)S(1)} %get-tuple-element.81), channel_id=1, source_target_pairs={{0,24},{1,7},{2,26},{3,5},{4,28},{5,3},{6,30},{7,1},{8,16},{9,15},... | collective-permute-start | bytes 221192 | tf_op jit(solution)/shard_map/ppermute | solution.py:447
  36.7 4.6 %first_late.1 = f32[16,1152]{1,0:T(8,128)S(1)} custom-call(f32[768,1152]{1,0:T(8,128)S(1)} %get-tuple-element.59.refs_0_.refs_1_, f32[768,1152]{1,0:T(8,128)S(1)} %get-tuple-element.60.refs_1_.refs_2_, f32[768,1152]{1,0:T(8,128)S(1)} %get-tuple-element.61.refs_1_.refs_2_.refs_0_, f32[768,1152]{1,0:T(8,128)S(1)} %get-tuple-element.62.refs_2_.refs_3_.refs_1_, ...), custom_call_target="tpu_custom_call" | custom-call | flops 2038431744 | bytes 15925248 | tf_op jit(solution)/shard_map/first_late/pallas_call | solution.py:427
  41.3 0.0 collective-permute-done.8
  41.3 0.9 collective-permute-done.9
  42.2 0.1 collective-permute-start.11
  42.3 1.3 %collective-permute-done.11.got_ref = f32[16,1152]{1,0:T(8,128)S(1)} collective-permute-done((f32[16,1152]{1,0:T(8,128)S(1)}, f32[16,1152]{1,0:T(8,128)S(1)}, u32[]{:S(2)}, u32[]{:S(2)}) %collective-permute-start.11) | collective-permute-done | bytes 73760 | tf_op jit(solution)/shard_map/ppermute | solution.py:447
  43.5 0.3 pair.1.refs_3_.refs_9_.refs_0_.pair_ref
  43.8 0.9 collective-permute-start.14
  44.7 2.8 %collective-permute-start.13 = (f32[16,1280]{1,0:T(8,128)S(1)}, f32[16,1280]{1,0:T(8,128)S(1)}, u32[]{:S(2)}, u32[]{:S(2)}) collective-permute-start(f32[16,1280]{1,0:T(8,128)S(1)} %pair.1.refs_3_.refs_9_.refs_0_.pair_ref), channel_id=1, source_target_pairs={{0,4},{1,17},{2,6},{3,19},{4,0},{5,21},{6,2},{7,23},{8,12},{9,25},... | collective-permute-start | bytes 245768 | tf_op jit(solution)/shard_map/ppermute | solution.py:447
  47.5 1.4 %collective-permute-start.12 = (f32[16,1280]{1,0:T(8,128)S(1)}, f32[16,1280]{1,0:T(8,128)S(1)}, u32[]{:S(2)}, u32[]{:S(2)}) collective-permute-start(f32[16,1280]{1,0:T(8,128)S(1)} %pair.1.refs_3_.refs_9_.refs_0_.pair_ref), channel_id=1, source_target_pairs={{0,2},{1,9},{2,0},{3,11},{4,6},{5,13},{6,4},{7,15},{8,10},{9,1},{1... | collective-permute-start | bytes 245768 | tf_op jit(solution)/shard_map/ppermute | solution.py:447
  48.9 3.8 %second_early.1.refs_10_ = f32[16,2304]{1,0:T(8,128)S(1)} custom-call(f32[768,1152]{1,0:T(8,128)S(1)} %get-tuple-element.58.refs_1_.piece.refs_0_, f32[768,1152]{1,0:T(8,128)S(1)} %get-tuple-element.59.refs_0_.refs_1_, f32[768,1152]{1,0:T(8,128)S(1)} %get-tuple-element.60.refs_1_.refs_2_, f32[16,1280]{1,0:T(8,128)S(1)} %pair.1.refs_3_.refs_9_.refs_0_.pair_ref), custom_call_target="tpu_custom_call" | custom-call | flops 1358954496 | bytes 10616832 | tf_op jit(solution)/shard_map/second_early/pallas_call | solution.py:427
  52.7 0.0 collective-permute-done.14.refs_14_.refs_3_
  52.7 0.0 collective-permute-done.13.refs_13_.refs_2_
  52.7 0.0 collective-permute-done.12.refs_12_.refs_1_
  52.7 0.1 collective-permute-start.15
  52.8 0.5 collective-permute-start.16
  53.3 0.1 collective-permute-start.17
  53.4 2.0 %second_own.1.refs_11_ = f32[16,3456]{1,0:T(8,128)S(1)} custom-call(f32[768,1152]{1,0:T(8,128)S(1)} %get-tuple-element.61.refs_1_.refs_2_.refs_0_, f32[768,1152]{1,0:T(8,128)S(1)} %get-tuple-element.62.refs_2_.refs_3_.refs_1_, f32[768,1152]{1,0:T(8,128)S(1)} %get-tuple-element.65.refs_3_.refs_4_.refs_2_, f32[16,1280]{1,0:T(8,128)S(1)} %pair.1.refs_3_.refs_9_.refs_0_.pair_ref), custom_call_target="tpu_custom_call" | custom-call | flops 679477248 | bytes 5308416 | tf_op jit(solution)/shard_map/second_own/pallas_call | solution.py:427
  55.4 0.0 collective-permute-done.15.refs_15_.refs_4_
  55.4 0.0 collective-permute-done.16.refs_16_.refs_5_
  55.5 13.0 %second.1 = (f32[3,16,1152]{2,1,0:T(8,128)S(1)}, f32[3,16,1152]{2,1,0:T(8,128)S(1)}, f32[16,576]{1,0:T(8,128)S(1)}, bf16[32,2304]{1,0:T(8,128)(2,1)S(1)}, bf16[32,3456]{1,0:T(8,128)(2,1)S(1)}) custom-call(f32[768,1152]{1,0:T(8,128)S(1)} %get-tuple-element.61.refs_1_.refs_2_.refs_0_, f32[768,1152]{1,0:T(8,128)S(1)} %get-tuple-element.62.refs_2_.refs_3_.refs_1_, ...), custom_call_target="tpu_custom_call" | custom-call | flops 5435817984 | bytes 42467328 | tf_op jit(solution)/shard_map/second/pallas_call | solution.py:427
  68.5 0.5 collective-permute-start.18
  69.0 1.0 second_near.1.refs_7_
  69.9 0.1 collective-permute-done.18.got_ref
  70.1 0.7 collective-permute-start.19
  70.8 1.7 %collective-permute-start.20 = (f32[16,1280]{1,0:T(8,128)S(1)}, f32[16,1280]{1,0:T(8,128)S(1)}, u32[]{:S(2)}, u32[]{:S(2)}) collective-permute-start(f32[16,1280]{1,0:T(8,128)S(1)} %get-tuple-element.101), channel_id=1, source_target_pairs={{0,4},{1,17},{2,6},{3,19},{4,0},{5,21},{6,2},{7,23},{8,12},{9,25},... | collective-permute-start | bytes 245768 | tf_op jit(solution)/shard_map/ppermute | solution.py:447
  72.5 1.0 collective-permute-start.21
  73.4 4.6 %second_late.1 = f32[16,1280]{1,0:T(8,128)S(1)} custom-call(f32[768,1152]{1,0:T(8,128)S(1)} %get-tuple-element.59.refs_0_.refs_1_, f32[768,1152]{1,0:T(8,128)S(1)} %get-tuple-element.60.refs_1_.refs_2_, f32[768,1152]{1,0:T(8,128)S(1)} %get-tuple-element.61.refs_1_.refs_2_.refs_0_, f32[768,1152]{1,0:T(8,128)S(1)} %get-tuple-element.62.refs_2_.refs_3_.refs_1_, ...), custom_call_target="tpu_custom_call" | custom-call | flops 2038431744 | bytes 15925248 | tf_op jit(solution)/shard_map/second_late/pallas_call | solution.py:427
  78.1 0.1 collective-permute-start.22
  78.1 1.3 %collective-permute-done.22.got_ref = f32[16,1280]{1,0:T(8,128)S(1)} collective-permute-done((f32[16,1280]{1,0:T(8,128)S(1)}, f32[16,1280]{1,0:T(8,128)S(1)}, u32[]{:S(2)}, u32[]{:S(2)}) %collective-permute-start.22) | collective-permute-done | bytes 81952 | tf_op jit(solution)/shard_map/ppermute | solution.py:447
  79.4 2.6 %middle.1 = (f32[16,1152]{1,0:T(8,128)S(1)}, f32[16,1152]{1,0:T(8,128)S(1)}, f32[48,48]{1,0:T(8,128)S(1)}, f32[16,16]{1,0:T(8,128)S(1)}, f32[16,16]{1,0:T(8,128)S(1)}) custom-call(f32[16,1152]{1,0:T(8,128)S(1)} %order.1.refs_2_.refs_3_.refs_5_.refs_9_.first_ref, f32[16,1280]{1,0:T(8,128)S(1)} %pair.1.refs_3_.refs_9_.refs_0_.pair_ref, ...), custom_call_target="tpu_custom_call" | custom-call | tf_op jit(solution)/shard_map/middle/pallas_call | solution.py:427
  82.0 0.9 collective-permute-start.25
  83.0 1.6 %collective-permute-start.24 = (f32[48,48]{1,0:T(8,128)S(1)}, f32[48,48]{1,0:T(8,128)S(1)}, u32[]{:S(2)}, u32[]{:S(2)}) collective-permute-start(f32[48,48]{1,0:T(8,128)S(1)} %get-tuple-element.107), channel_id=1, source_target_pairs={{0,16},{1,17},{2,18},{3,19},{4,20},{5,21},{6,22},{7,23},{8,24},{9,... | collective-permute-start | bytes 27656 | tf_op jit(solution)/shard_map/ppermute | solution.py:447
  84.6 1.0 collective-permute-start.23
  85.6 0.3 collective-permute-done.25
  85.9 0.9 collective-permute-done.24
  86.8 2.5 %collective-permute-done.23 = f32[48,48]{1,0:T(8,128)S(1)} collective-permute-done((f32[48,48]{1,0:T(8,128)S(1)}, f32[48,48]{1,0:T(8,128)S(1)}, u32[]{:S(2)}, u32[]{:S(2)}) %collective-permute-start.23) | collective-permute-done | bytes 9248 | tf_op jit(solution)/shard_map/ppermute | solution.py:447
  89.4 0.1 collective-permute-start.28
  89.5 2.6 %collective-permute-start.27 = (f32[48,48]{1,0:T(8,128)S(1)}, f32[48,48]{1,0:T(8,128)S(1)}, u32[]{:S(2)}, u32[]{:S(2)}) collective-permute-start(f32[48,48]{1,0:T(8,128)S(1)} %add_add_fusion.2.refs_0_), channel_id=1, source_target_pairs={{0,4},{1,5},{2,6},{3,7},{4,0},{5,1},{6,2},{7,3},{8,12},{9,13},{10,... | collective-permute-start | bytes 27656 | tf_op jit(solution)/shard_map/ppermute | solution.py:447
  92.1 1.7 %collective-permute-start.26 = (f32[48,48]{1,0:T(8,128)S(1)}, f32[48,48]{1,0:T(8,128)S(1)}, u32[]{:S(2)}, u32[]{:S(2)}) collective-permute-start(f32[48,48]{1,0:T(8,128)S(1)} %add_add_fusion.2.refs_0_), channel_id=1, source_target_pairs={{0,6},{1,7},{2,4},{3,5},{4,2},{5,3},{6,0},{7,1},{8,14},{9,15},{10,... | collective-permute-start | bytes 27656 | tf_op jit(solution)/shard_map/ppermute | solution.py:447
  93.8 0.4 collective-permute-done.27.refs_2_
  94.2 3.5 %collective-permute-done.26.refs_1_ = f32[48,48]{1,0:T(8,128)S(1)} collective-permute-done((f32[48,48]{1,0:T(8,128)S(1)}, f32[48,48]{1,0:T(8,128)S(1)}, u32[]{:S(2)}, u32[]{:S(2)}) %collective-permute-start.26) | collective-permute-done | bytes 9248 | tf_op jit(solution)/shard_map/ppermute | solution.py:447
  97.7 2.8 %last.1 = (f32[16,576]{1,0:T(8,128)}, f32[2,16,16]{2,1,0:T(8,128)}, f32[2,16,16]{2,1,0:T(8,128)}) custom-call(f32[16,1152]{1,0:T(8,128)S(1)} %order.1.refs_2_.refs_3_.refs_5_.refs_9_.first_ref, f32[16,1152]{1,0:T(8,128)S(1)} %get-tuple-element.103.q_ref, f32[16,1152]{1,0:T(8,128)S(1)} %get-tuple-element.104.prod_ref, ...), custom_call_target="tpu_custom_call" | custom-call | tf_op jit(solution)/shard_map/last/pallas_call | solution.py:427
  (17 shorter events, 0.1 us)
Async XLA Ops:
  0.6 2.6 %collective-permute-start = (f32[16,576]{1,0:T(8,128)}, f32[16,576]{1,0:T(8,128)S(1)}, u32[]{:S(2)}, u32[]{:S(2)}) collective-permute-start(f32[16,576]{1,0:T(8,128)} %bitcast.7), channel_id=1, source_target_pairs={{0,1},{1,0},{2,3},{3,2},{4,5},{5,4},{6,7},{7,6},{8,9},{9,8},{10,11... | collective-permute-start | bytes 110600 | tf_op jit(solution)/shard_map/ppermute | solution.py:447
  3.3 12.8 %collective-permute-start.3 = (f32[16,1152]{1,0:T(8,128)S(1)}, f32[16,1152]{1,0:T(8,128)S(1)}, u32[]{:S(2)}, u32[]{:S(2)}) collective-permute-start(f32[16,1152]{1,0:T(8,128)S(1)} %order.1.refs_2_.refs_3_.refs_5_.refs_9_.first_ref), channel_id=1, source_target_pairs={{0,24},{1,7},{2,26},{3,5},{4,28},{5,3},{6,30},{7,1},{8,16},{9,15},... | collective-permute-start | bytes 221192 | tf_op jit(solution)/shard_map/ppermute | solution.py:447
  6.8 9.3 %collective-permute-start.2 = (f32[16,1152]{1,0:T(8,128)S(1)}, f32[16,1152]{1,0:T(8,128)S(1)}, u32[]{:S(2)}, u32[]{:S(2)}) collective-permute-start(f32[16,1152]{1,0:T(8,128)S(1)} %order.1.refs_2_.refs_3_.refs_5_.refs_9_.first_ref), channel_id=1, source_target_pairs={{0,4},{1,17},{2,6},{3,19},{4,0},{5,21},{6,2},{7,23},{8,12},{9,25},... | collective-permute-start | bytes 221192 | tf_op jit(solution)/shard_map/ppermute | solution.py:447
  9.4 6.7 %collective-permute-start.1 = (f32[16,1152]{1,0:T(8,128)S(1)}, f32[16,1152]{1,0:T(8,128)S(1)}, u32[]{:S(2)}, u32[]{:S(2)}) collective-permute-start(f32[16,1152]{1,0:T(8,128)S(1)} %order.1.refs_2_.refs_3_.refs_5_.refs_9_.first_ref), channel_id=1, source_target_pairs={{0,2},{1,9},{2,0},{3,11},{4,6},{5,13},{6,4},{7,15},{8,10},{9,1},{1... | collective-permute-start | bytes 221192 | tf_op jit(solution)/shard_map/ppermute | solution.py:447
  16.1 3.8 %collective-permute-start.4 = (f32[16,1152]{1,0:T(8,128)S(1)}, f32[16,1152]{1,0:T(8,128)S(1)}, u32[]{:S(2)}, u32[]{:S(2)}) collective-permute-start(f32[16,1152]{1,0:T(8,128)S(1)} %collective-permute-done.1.refs_8_), channel_id=1, source_target_pairs={{0,1},{1,0},{2,3},{3,2},{4,5},{5,4},{6,7},{7,6},{8,9},{9,8},{10,11... | collective-permute-start | bytes 221192 | tf_op jit(solution)/shard_map/ppermute | solution.py:447
  16.2 3.7 %collective-permute-start.5 = (f32[16,1152]{1,0:T(8,128)S(1)}, f32[16,1152]{1,0:T(8,128)S(1)}, u32[]{:S(2)}, u32[]{:S(2)}) collective-permute-start(f32[16,1152]{1,0:T(8,128)S(1)} %collective-permute-done.2.refs_9_), channel_id=1, source_target_pairs={{0,1},{1,0},{2,3},{3,2},{4,5},{5,4},{6,7},{7,6},{8,9},{9,8},{10,11... | collective-permute-start | bytes 221192 | tf_op jit(solution)/shard_map/ppermute | solution.py:447
  16.7 3.2 %collective-permute-start.6 = (f32[16,1152]{1,0:T(8,128)S(1)}, f32[16,1152]{1,0:T(8,128)S(1)}, u32[]{:S(2)}, u32[]{:S(2)}) collective-permute-start(f32[16,1152]{1,0:T(8,128)S(1)} %collective-permute-done.3.refs_10_), channel_id=1, source_target_pairs={{0,1},{1,0},{2,3},{3,2},{4,5},{5,4},{6,7},{7,6},{8,9},{9,8},{10,11... | collective-permute-start | bytes 221192 | tf_op jit(solution)/shard_map/ppermute | solution.py:447
  19.9 13.6 %copy-start = (f32[576]{0:T(1024)S(1)}, f32[576]{0:T(1024)}, u32[]{:S(2)}) copy-start(f32[576]{0:T(1024)} %param.4) | copy-start | bytes 6916
  33.0 1.6 %collective-permute-start.7 = (f32[3,16,1152]{2,1,0:T(8,128)S(1)}, f32[3,16,1152]{2,1,0:T(8,128)S(1)}, u32[]{:S(2)}, u32[]{:S(2)}) collective-permute-start(f32[3,16,1152]{2,1,0:T(8,128)S(1)} %get-tuple-element.74), channel_id=1, source_target_pairs={{0,1},{1,0},{2,3},{3,2},{4,5},{5,4},{6,7},{7,6},{8,9},{9,8},{10,11... | collective-permute-start | bytes 663560 | tf_op jit(solution)/shard_map/ppermute | solution.py:447
  34.6 6.6 %collective-permute-start.8 = (f32[16,1152]{1,0:T(8,128)S(1)}, f32[16,1152]{1,0:T(8,128)S(1)}, u32[]{:S(2)}, u32[]{:S(2)}) collective-permute-start(f32[16,1152]{1,0:T(8,128)S(1)} %get-tuple-element.79), channel_id=1, source_target_pairs={{0,2},{1,9},{2,0},{3,11},{4,6},{5,13},{6,4},{7,15},{8,10},{9,1},{1... | collective-permute-start | bytes 221192 | tf_op jit(solution)/shard_map/ppermute | solution.py:447
  35.3 6.8 %collective-permute-start.9 = (f32[16,1152]{1,0:T(8,128)S(1)}, f32[16,1152]{1,0:T(8,128)S(1)}, u32[]{:S(2)}, u32[]{:S(2)}) collective-permute-start(f32[16,1152]{1,0:T(8,128)S(1)} %get-tuple-element.80), channel_id=1, source_target_pairs={{0,4},{1,17},{2,6},{3,19},{4,0},{5,21},{6,2},{7,23},{8,12},{9,25},... | collective-permute-start | bytes 221192 | tf_op jit(solution)/shard_map/ppermute | solution.py:447
  35.5 6.7 %collective-permute-start.10 = (f32[16,1152]{1,0:T(8,128)S(1)}, f32[16,1152]{1,0:T(8,128)S(1)}, u32[]{:S(2)}, u32[]{:S(2)}) collective-permute-start(f32[16,1152]{1,0:T(8,128)S(1)} %get-tuple-element.81), channel_id=1, source_target_pairs={{0,24},{1,7},{2,26},{3,5},{4,28},{5,3},{6,30},{7,1},{8,16},{9,15},... | collective-permute-start | bytes 221192 | tf_op jit(solution)/shard_map/ppermute | solution.py:447
  42.2 1.3 %collective-permute-start.11 = (f32[16,1152]{1,0:T(8,128)S(1)}, f32[16,1152]{1,0:T(8,128)S(1)}, u32[]{:S(2)}, u32[]{:S(2)}) collective-permute-start(f32[16,1152]{1,0:T(8,128)S(1)} %add_add_fusion.1.mine_ref), channel_id=1, source_target_pairs={{0,1},{1,0},{2,3},{3,2},{4,5},{5,4},{6,7},{7,6},{8,9},{9,8},{10,11... | collective-permute-start | bytes 221192 | tf_op jit(solution)/shard_map/ppermute | solution.py:447
  43.8 8.8 %collective-permute-start.14 = (f32[16,1280]{1,0:T(8,128)S(1)}, f32[16,1280]{1,0:T(8,128)S(1)}, u32[]{:S(2)}, u32[]{:S(2)}) collective-permute-start(f32[16,1280]{1,0:T(8,128)S(1)} %pair.1.refs_3_.refs_9_.refs_0_.pair_ref), channel_id=1, source_target_pairs={{0,24},{1,7},{2,26},{3,5},{4,28},{5,3},{6,30},{7,1},{8,16},{9,15},... | collective-permute-start | bytes 245768 | tf_op jit(solution)/shard_map/ppermute | solution.py:447
  44.7 8.0 %collective-permute-start.13 = (f32[16,1280]{1,0:T(8,128)S(1)}, f32[16,1280]{1,0:T(8,128)S(1)}, u32[]{:S(2)}, u32[]{:S(2)}) collective-permute-start(f32[16,1280]{1,0:T(8,128)S(1)} %pair.1.refs_3_.refs_9_.refs_0_.pair_ref), channel_id=1, source_target_pairs={{0,4},{1,17},{2,6},{3,19},{4,0},{5,21},{6,2},{7,23},{8,12},{9,25},... | collective-permute-start | bytes 245768 | tf_op jit(solution)/shard_map/ppermute | solution.py:447
  47.5 5.2 %collective-permute-start.12 = (f32[16,1280]{1,0:T(8,128)S(1)}, f32[16,1280]{1,0:T(8,128)S(1)}, u32[]{:S(2)}, u32[]{:S(2)}) collective-permute-start(f32[16,1280]{1,0:T(8,128)S(1)} %pair.1.refs_3_.refs_9_.refs_0_.pair_ref), channel_id=1, source_target_pairs={{0,2},{1,9},{2,0},{3,11},{4,6},{5,13},{6,4},{7,15},{8,10},{9,1},{1... | collective-permute-start | bytes 245768 | tf_op jit(solution)/shard_map/ppermute | solution.py:447
  52.7 2.7 %collective-permute-start.15 = (f32[16,1280]{1,0:T(8,128)S(1)}, f32[16,1280]{1,0:T(8,128)S(1)}, u32[]{:S(2)}, u32[]{:S(2)}) collective-permute-start(f32[16,1280]{1,0:T(8,128)S(1)} %collective-permute-done.12.refs_12_.refs_1_), channel_id=1, source_target_pairs={{0,1},{1,0},{2,3},{3,2},{4,5},{5,4},{6,7},{7,6},{8,9},{9,8},{10,11... | collective-permute-start | bytes 245768 | tf_op jit(solution)/shard_map/ppermute | solution.py:447
  52.8 2.6 %collective-permute-start.16 = (f32[16,1280]{1,0:T(8,128)S(1)}, f32[16,1280]{1,0:T(8,128)S(1)}, u32[]{:S(2)}, u32[]{:S(2)}) collective-permute-start(f32[16,1280]{1,0:T(8,128)S(1)} %collective-permute-done.13.refs_13_.refs_2_), channel_id=1, source_target_pairs={{0,1},{1,0},{2,3},{3,2},{4,5},{5,4},{6,7},{7,6},{8,9},{9,8},{10,11... | collective-permute-start | bytes 245768 | tf_op jit(solution)/shard_map/ppermute | solution.py:447
  53.3 2.1 %collective-permute-start.17 = (f32[16,1280]{1,0:T(8,128)S(1)}, f32[16,1280]{1,0:T(8,128)S(1)}, u32[]{:S(2)}, u32[]{:S(2)}) collective-permute-start(f32[16,1280]{1,0:T(8,128)S(1)} %collective-permute-done.14.refs_14_.refs_3_), channel_id=1, source_target_pairs={{0,1},{1,0},{2,3},{3,2},{4,5},{5,4},{6,7},{7,6},{8,9},{9,8},{10,11... | collective-permute-start | bytes 245768 | tf_op jit(solution)/shard_map/ppermute | solution.py:447
  68.5 1.6 %collective-permute-start.18 = (f32[3,16,1152]{2,1,0:T(8,128)S(1)}, f32[3,16,1152]{2,1,0:T(8,128)S(1)}, u32[]{:S(2)}, u32[]{:S(2)}) collective-permute-start(f32[3,16,1152]{2,1,0:T(8,128)S(1)} %get-tuple-element.94), channel_id=1, source_target_pairs={{0,1},{1,0},{2,3},{3,2},{4,5},{5,4},{6,7},{7,6},{8,9},{9,8},{10,11... | collective-permute-start | bytes 663560 | tf_op jit(solution)/shard_map/ppermute | solution.py:447
  70.1 7.9 %collective-permute-start.19 = (f32[16,1280]{1,0:T(8,128)S(1)}, f32[16,1280]{1,0:T(8,128)S(1)}, u32[]{:S(2)}, u32[]{:S(2)}) collective-permute-start(f32[16,1280]{1,0:T(8,128)S(1)} %get-tuple-element.100), channel_id=1, source_target_pairs={{0,2},{1,9},{2,0},{3,11},{4,6},{5,13},{6,4},{7,15},{8,10},{9,1},{1... | collective-permute-start | bytes 245768 | tf_op jit(solution)/shard_map/ppermute | solution.py:447
  70.8 7.2 %collective-permute-start.20 = (f32[16,1280]{1,0:T(8,128)S(1)}, f32[16,1280]{1,0:T(8,128)S(1)}, u32[]{:S(2)}, u32[]{:S(2)}) collective-permute-start(f32[16,1280]{1,0:T(8,128)S(1)} %get-tuple-element.101), channel_id=1, source_target_pairs={{0,4},{1,17},{2,6},{3,19},{4,0},{5,21},{6,2},{7,23},{8,12},{9,25},... | collective-permute-start | bytes 245768 | tf_op jit(solution)/shard_map/ppermute | solution.py:447
  72.5 5.6 %collective-permute-start.21 = (f32[16,1280]{1,0:T(8,128)S(1)}, f32[16,1280]{1,0:T(8,128)S(1)}, u32[]{:S(2)}, u32[]{:S(2)}) collective-permute-start(f32[16,1280]{1,0:T(8,128)S(1)} %get-tuple-element.102), channel_id=1, source_target_pairs={{0,24},{1,7},{2,26},{3,5},{4,28},{5,3},{6,30},{7,1},{8,16},{9,15},... | collective-permute-start | bytes 245768 | tf_op jit(solution)/shard_map/ppermute | solution.py:447
  78.1 1.3 %collective-permute-start.22 = (f32[16,1280]{1,0:T(8,128)S(1)}, f32[16,1280]{1,0:T(8,128)S(1)}, u32[]{:S(2)}, u32[]{:S(2)}) collective-permute-start(f32[16,1280]{1,0:T(8,128)S(1)} %add_add_fusion.mine_ref), channel_id=1, source_target_pairs={{0,1},{1,0},{2,3},{3,2},{4,5},{5,4},{6,7},{7,6},{8,9},{9,8},{10,11... | collective-permute-start | bytes 245768 | tf_op jit(solution)/shard_map/ppermute | solution.py:447
  82.0 3.9 %collective-permute-start.25 = (f32[48,48]{1,0:T(8,128)S(1)}, f32[48,48]{1,0:T(8,128)S(1)}, u32[]{:S(2)}, u32[]{:S(2)}) collective-permute-start(f32[48,48]{1,0:T(8,128)S(1)} %get-tuple-element.107), channel_id=1, source_target_pairs={{0,8},{1,9},{2,10},{3,11},{4,12},{5,13},{6,14},{7,15},{8,0},{9,1},... | collective-permute-start | bytes 27656 | tf_op jit(solution)/shard_map/ppermute | solution.py:447
  83.0 3.8 %collective-permute-start.24 = (f32[48,48]{1,0:T(8,128)S(1)}, f32[48,48]{1,0:T(8,128)S(1)}, u32[]{:S(2)}, u32[]{:S(2)}) collective-permute-start(f32[48,48]{1,0:T(8,128)S(1)} %get-tuple-element.107), channel_id=1, source_target_pairs={{0,16},{1,17},{2,18},{3,19},{4,20},{5,21},{6,22},{7,23},{8,24},{9,... | collective-permute-start | bytes 27656 | tf_op jit(solution)/shard_map/ppermute | solution.py:447
  84.6 4.7 %collective-permute-start.23 = (f32[48,48]{1,0:T(8,128)S(1)}, f32[48,48]{1,0:T(8,128)S(1)}, u32[]{:S(2)}, u32[]{:S(2)}) collective-permute-start(f32[48,48]{1,0:T(8,128)S(1)} %get-tuple-element.107), channel_id=1, source_target_pairs={{0,24},{1,25},{2,26},{3,27},{4,28},{5,29},{6,30},{7,31},{8,16},{9,... | collective-permute-start | bytes 27656 | tf_op jit(solution)/shard_map/ppermute | solution.py:447
  89.4 4.5 %collective-permute-start.28 = (f32[48,48]{1,0:T(8,128)S(1)}, f32[48,48]{1,0:T(8,128)S(1)}, u32[]{:S(2)}, u32[]{:S(2)}) collective-permute-start(f32[48,48]{1,0:T(8,128)S(1)} %add_add_fusion.2.refs_0_), channel_id=1, source_target_pairs={{0,2},{1,3},{2,0},{3,1},{4,6},{5,7},{6,4},{7,5},{8,10},{9,11},{10,... | collective-permute-start | bytes 27656 | tf_op jit(solution)/shard_map/ppermute | solution.py:447
  89.5 4.7 %collective-permute-start.27 = (f32[48,48]{1,0:T(8,128)S(1)}, f32[48,48]{1,0:T(8,128)S(1)}, u32[]{:S(2)}, u32[]{:S(2)}) collective-permute-start(f32[48,48]{1,0:T(8,128)S(1)} %add_add_fusion.2.refs_0_), channel_id=1, source_target_pairs={{0,4},{1,5},{2,6},{3,7},{4,0},{5,1},{6,2},{7,3},{8,12},{9,13},{10,... | collective-permute-start | bytes 27656 | tf_op jit(solution)/shard_map/ppermute | solution.py:447
  92.1 5.6 %collective-permute-start.26 = (f32[48,48]{1,0:T(8,128)S(1)}, f32[48,48]{1,0:T(8,128)S(1)}, u32[]{:S(2)}, u32[]{:S(2)}) collective-permute-start(f32[48,48]{1,0:T(8,128)S(1)} %add_add_fusion.2.refs_0_), channel_id=1, source_target_pairs={{0,6},{1,7},{2,4},{3,5},{4,2},{5,3},{6,0},{7,1},{8,14},{9,15},{10,... | collective-permute-start | bytes 27656 | tf_op jit(solution)/shard_map/ppermute | solution.py:447

commit v8 on v6

--- a/solution.py
+++ b/solution.py
@@ -506,7 +506,7 @@
         (u0,) = matrix_call(
             early_kernel,
             range(parts),
-            parts + 1,
+            parts + 2,
             [shape(k, rows)],
             [pair],
             [pltpu.VMEM((2 * k, 2 * n), BF16)],
@@ -518,7 +518,7 @@
         (v0,) = matrix_call(
             own_kernel,
             range(parts, parts + group - 1),
-            parts + group - 1,
+            parts + group,
             [shape(k, (group - 1) * 2 * n)],
             [same],
             [pltpu.VMEM((2 * k, n), BF16)],

time: 100 us -> 98.3 us (0.983)
  Pallas kernels: 60.8 us -> 59.1 us
    pallas_call x17, Pallas kernels: 60.8 us -> 59.1 us  [call(): run(*[pltpu.with_memory_space_constraint(v, pltpu.HBM if i < far else plt...]
  transfers between devices with their start and end apart: 29 -> 29, of which waited for: 10 -> 10; matrix products, arithmetic and copies ran while one was open for 0% -> 0% of each run, Pallas kernels for 27% -> 28%
where the time goes in v8:
time: 98.3 us; the launch traced here: 98.1 us
  Pallas kernels  59.1 us (60%)
  starting transfers between devices  29.1 us (30%)
  waiting for transfers between devices  9.02 us (9%)
    pallas_call x17, Pallas kernels, call(): run(*[pltpu.with_memory_space_constraint(v, pltpu.HBM if i < far else plt...  59.1 us
    ppermute x29, starting transfers between devices, send(): return lax.ppermute(value, axes, [p for p in pairs if p[1] is not None])  29.1 us
    ppermute x29, waiting for transfers between devices, send(): return lax.ppermute(value, axes, [p for p in pairs if p[1] is not None])  9.02 us
  transfers between devices with their start and end apart: 29, of which 10 were waited for; matrix products, arithmetic and copies ran while one was open for 0% of the time, Pallas kernels for 28%

profile of v8, /device:TPU:0, one launch (start us, length us, event | category | flops | bytes accessed | tf_op | source)
XLA Modules:
  0.0 98.1 jit_solution(3667614946417528563)
XLA Ops:
  0.6 0.6 collective-permute-start
  1.2 2.0 %begin.1 = (f32[16,576]{1,0:T(8,128)S(1)}, f32[768,1152]{1,0:T(8,128)S(1)}) custom-call(f32[2304,4608]{1,0:T(8,128)} %bitcast.3, f32[16,576]{1,0:T(8,128)} %bitcast.8), custom_call_target="tpu_custom_call" | custom-call | flops 169869312 | bytes 1327104 | tf_op jit(solution)/shard_map/begin/pallas_call | solution.py:427
  3.2 0.0 collective-permute-done.other_ref
  3.2 0.1 order.1.refs_2_.refs_3_.refs_5_.refs_9_.first_ref
  3.3 3.5 %collective-permute-start.3 = (f32[16,1152]{1,0:T(8,128)S(1)}, f32[16,1152]{1,0:T(8,128)S(1)}, u32[]{:S(2)}, u32[]{:S(2)}) collective-permute-start(f32[16,1152]{1,0:T(8,128)S(1)} %order.1.refs_2_.refs_3_.refs_5_.refs_9_.first_ref), channel_id=1, source_target_pairs={{0,24},{1,7},{2,26},{3,5},{4,28},{5,3},{6,30},{7,1},{8,16},{9,15},... | collective-permute-start | bytes 221192 | tf_op jit(solution)/shard_map/ppermute | solution.py:447
  6.8 2.6 %collective-permute-start.2 = (f32[16,1152]{1,0:T(8,128)S(1)}, f32[16,1152]{1,0:T(8,128)S(1)}, u32[]{:S(2)}, u32[]{:S(2)}) collective-permute-start(f32[16,1152]{1,0:T(8,128)S(1)} %order.1.refs_2_.refs_3_.refs_5_.refs_9_.first_ref), channel_id=1, source_target_pairs={{0,4},{1,17},{2,6},{3,19},{4,0},{5,21},{6,2},{7,23},{8,12},{9,25},... | collective-permute-start | bytes 221192 | tf_op jit(solution)/shard_map/ppermute | solution.py:447
  9.4 1.6 %collective-permute-start.1 = (f32[16,1152]{1,0:T(8,128)S(1)}, f32[16,1152]{1,0:T(8,128)S(1)}, u32[]{:S(2)}, u32[]{:S(2)}) collective-permute-start(f32[16,1152]{1,0:T(8,128)S(1)} %order.1.refs_2_.refs_3_.refs_5_.refs_9_.first_ref), channel_id=1, source_target_pairs={{0,2},{1,9},{2,0},{3,11},{4,6},{5,13},{6,4},{7,15},{8,10},{9,1},{1... | collective-permute-start | bytes 221192 | tf_op jit(solution)/shard_map/ppermute | solution.py:447
  11.0 5.1 %first_early.1 = (f32[16,2304]{1,0:T(8,128)S(1)}, f32[768,1152]{1,0:T(8,128)S(1)}, f32[768,1152]{1,0:T(8,128)S(1)}, f32[768,1152]{1,0:T(8,128)S(1)}, f32[768,1152]{1,0:T(8,128)S(1)}) custom-call(f32[2304,4608]{1,0:T(8,128)} %bitcast.4, f32[768,1152]{1,0:T(8,128)S(1)} %get-tuple-element.58.refs_1_.piece.refs_0_, ...), custom_call_target="tpu_custom_call" | custom-call | flops 1358954496 | bytes 10616832 | tf_op jit(solution)/shard_map/first_early/pallas_call | solution.py:427
  16.1 0.0 collective-permute-done.3.refs_10_
  16.1 0.0 collective-permute-done.2.refs_9_
  16.1 0.1 collective-permute-start.4
  16.2 0.5 collective-permute-start.5
  16.7 0.1 collective-permute-start.6
  16.8 3.1 %first_own.1 = (f32[16,3456]{1,0:T(8,128)S(1)}, f32[768,1152]{1,0:T(8,128)S(1)}, f32[768,1152]{1,0:T(8,128)S(1)}) custom-call(f32[2304,4608]{1,0:T(8,128)} %bitcast.5, f32[768,1152]{1,0:T(8,128)S(1)} %get-tuple-element.61.refs_1_.refs_2_.refs_0_, f32[768,1152]{1,0:T(8,128)S(1)} %get-tuple-element.62.refs_2_.refs_3_.refs_1_, ...), custom_call_target="tpu_custom_call" | custom-call | flops 679477248 | bytes 5308416 | tf_op jit(solution)/shard_map/first_own/pallas_call | solution.py:427
  19.9 0.0 collective-permute-done.4.refs_11_
  19.9 0.0 collective-permute-done.5.refs_12_
  19.9 0.0 copy-start
  19.9 13.0 %first.1 = (f32[3,16,1152]{2,1,0:T(8,128)S(1)}, f32[3,16,1152]{2,1,0:T(8,128)S(1)}, f32[16,576]{1,0:T(8,128)S(1)}, bf16[32,2304]{1,0:T(8,128)(2,1)S(1)}, bf16[32...) custom-call(f32[2304,4608]{1,0:T(8,128)} %bitcast.6, ...), custom_call_target="tpu_custom_call" | custom-call | flops 5435817984 | bytes 42467328 | tf_op jit(solution)/shard_map/first/pallas_call | solution.py:427
  33.0 0.5 collective-permute-start.7
  33.5 1.0 first_near.1.refs_7_
  34.4 0.1 collective-permute-done.7.got_ref
  34.6 0.7 collective-permute-start.8
  35.3 0.1 collective-permute-start.9
  35.5 1.2 %collective-permute-start.10 = (f32[16,1152]{1,0:T(8,128)S(1)}, f32[16,1152]{1,0:T(8,128)S(1)}, u32[]{:S(2)}, u32[]{:S(2)}) collective-permute-start(f32[16,1152]{1,0:T(8,128)S(1)} %get-tuple-element.81), channel_id=1, source_target_pairs={{0,24},{1,7},{2,26},{3,5},{4,28},{5,3},{6,30},{7,1},{8,16},{9,15},... | collective-permute-start | bytes 221192 | tf_op jit(solution)/shard_map/ppermute | solution.py:447
  36.7 4.6 %first_late.1 = f32[16,1152]{1,0:T(8,128)S(1)} custom-call(f32[768,1152]{1,0:T(8,128)S(1)} %get-tuple-element.59.refs_0_.refs_1_, f32[768,1152]{1,0:T(8,128)S(1)} %get-tuple-element.60.refs_1_.refs_2_, f32[768,1152]{1,0:T(8,128)S(1)} %get-tuple-element.61.refs_1_.refs_2_.refs_0_, f32[768,1152]{1,0:T(8,128)S(1)} %get-tuple-element.62.refs_2_.refs_3_.refs_1_, ...), custom_call_target="tpu_custom_call" | custom-call | flops 2038431744 | bytes 15925248 | tf_op jit(solution)/shard_map/first_late/pallas_call | solution.py:427
  41.3 0.9 collective-permute-done.9
  42.1 0.0 collective-permute-done.10
  42.2 0.1 collective-permute-start.11
  42.3 1.3 %collective-permute-done.11.got_ref = f32[16,1152]{1,0:T(8,128)S(1)} collective-permute-done((f32[16,1152]{1,0:T(8,128)S(1)}, f32[16,1152]{1,0:T(8,128)S(1)}, u32[]{:S(2)}, u32[]{:S(2)}) %collective-permute-start.11) | collective-permute-done | bytes 73760 | tf_op jit(solution)/shard_map/ppermute | solution.py:447
  43.5 0.3 pair.1.refs_3_.refs_9_.refs_0_.pair_ref
  43.8 0.9 collective-permute-start.14
  44.7 2.8 %collective-permute-start.13 = (f32[16,1280]{1,0:T(8,128)S(1)}, f32[16,1280]{1,0:T(8,128)S(1)}, u32[]{:S(2)}, u32[]{:S(2)}) collective-permute-start(f32[16,1280]{1,0:T(8,128)S(1)} %pair.1.refs_3_.refs_9_.refs_0_.pair_ref), channel_id=1, source_target_pairs={{0,4},{1,17},{2,6},{3,19},{4,0},{5,21},{6,2},{7,23},{8,12},{9,25},... | collective-permute-start | bytes 245768 | tf_op jit(solution)/shard_map/ppermute | solution.py:447
  47.5 1.4 %collective-permute-start.12 = (f32[16,1280]{1,0:T(8,128)S(1)}, f32[16,1280]{1,0:T(8,128)S(1)}, u32[]{:S(2)}, u32[]{:S(2)}) collective-permute-start(f32[16,1280]{1,0:T(8,128)S(1)} %pair.1.refs_3_.refs_9_.refs_0_.pair_ref), channel_id=1, source_target_pairs={{0,2},{1,9},{2,0},{3,11},{4,6},{5,13},{6,4},{7,15},{8,10},{9,1},{1... | collective-permute-start | bytes 245768 | tf_op jit(solution)/shard_map/ppermute | solution.py:447
  48.9 3.8 %second_early.1.refs_10_ = f32[16,2304]{1,0:T(8,128)S(1)} custom-call(f32[768,1152]{1,0:T(8,128)S(1)} %get-tuple-element.58.refs_1_.piece.refs_0_, f32[768,1152]{1,0:T(8,128)S(1)} %get-tuple-element.59.refs_0_.refs_1_, f32[768,1152]{1,0:T(8,128)S(1)} %get-tuple-element.60.refs_1_.refs_2_, f32[16,1280]{1,0:T(8,128)S(1)} %pair.1.refs_3_.refs_9_.refs_0_.pair_ref), custom_call_target="tpu_custom_call" | custom-call | flops 1358954496 | bytes 10616832 | tf_op jit(solution)/shard_map/second_early/pallas_call | solution.py:427
  52.7 0.0 collective-permute-done.14.refs_14_.refs_3_
  52.7 0.0 collective-permute-done.13.refs_13_.refs_2_
  52.7 0.0 collective-permute-done.12.refs_12_.refs_1_
  52.7 0.1 collective-permute-start.15
  52.8 0.5 collective-permute-start.16
  53.3 0.1 collective-permute-start.17
  53.4 2.0 %second_own.1.refs_11_ = f32[16,3456]{1,0:T(8,128)S(1)} custom-call(f32[768,1152]{1,0:T(8,128)S(1)} %get-tuple-element.61.refs_1_.refs_2_.refs_0_, f32[768,1152]{1,0:T(8,128)S(1)} %get-tuple-element.62.refs_2_.refs_3_.refs_1_, f32[768,1152]{1,0:T(8,128)S(1)} %get-tuple-element.65.refs_3_.refs_4_.refs_2_, f32[16,1280]{1,0:T(8,128)S(1)} %pair.1.refs_3_.refs_9_.refs_0_.pair_ref), custom_call_target="tpu_custom_call" | custom-call | flops 679477248 | bytes 5308416 | tf_op jit(solution)/shard_map/second_own/pallas_call | solution.py:427
  55.4 0.0 collective-permute-done.16.refs_16_.refs_5_
  55.5 13.0 %second.1 = (f32[3,16,1152]{2,1,0:T(8,128)S(1)}, f32[3,16,1152]{2,1,0:T(8,128)S(1)}, f32[16,576]{1,0:T(8,128)S(1)}, bf16[32,2304]{1,0:T(8,128)(2,1)S(1)}, bf16[32,3456]{1,0:T(8,128)(2,1)S(1)}) custom-call(f32[768,1152]{1,0:T(8,128)S(1)} %get-tuple-element.61.refs_1_.refs_2_.refs_0_, f32[768,1152]{1,0:T(8,128)S(1)} %get-tuple-element.62.refs_2_.refs_3_.refs_1_, ...), custom_call_target="tpu_custom_call" | custom-call | flops 5435817984 | bytes 42467328 | tf_op jit(solution)/shard_map/second/pallas_call | solution.py:427
  68.5 0.5 collective-permute-start.18
  69.0 1.0 second_near.1.refs_7_
  69.9 0.1 collective-permute-done.18.got_ref
  70.1 0.7 collective-permute-start.19
  70.8 1.7 %collective-permute-start.20 = (f32[16,1280]{1,0:T(8,128)S(1)}, f32[16,1280]{1,0:T(8,128)S(1)}, u32[]{:S(2)}, u32[]{:S(2)}) collective-permute-start(f32[16,1280]{1,0:T(8,128)S(1)} %get-tuple-element.101), channel_id=1, source_target_pairs={{0,4},{1,17},{2,6},{3,19},{4,0},{5,21},{6,2},{7,23},{8,12},{9,25},... | collective-permute-start | bytes 245768 | tf_op jit(solution)/shard_map/ppermute | solution.py:447
  72.5 1.0 collective-permute-start.21
  73.4 4.6 %second_late.1 = f32[16,1280]{1,0:T(8,128)S(1)} custom-call(f32[768,1152]{1,0:T(8,128)S(1)} %get-tuple-element.59.refs_0_.refs_1_, f32[768,1152]{1,0:T(8,128)S(1)} %get-tuple-element.60.refs_1_.refs_2_, f32[768,1152]{1,0:T(8,128)S(1)} %get-tuple-element.61.refs_1_.refs_2_.refs_0_, f32[768,1152]{1,0:T(8,128)S(1)} %get-tuple-element.62.refs_2_.refs_3_.refs_1_, ...), custom_call_target="tpu_custom_call" | custom-call | flops 2038431744 | bytes 15925248 | tf_op jit(solution)/shard_map/second_late/pallas_call | solution.py:427
  78.1 0.1 collective-permute-start.22
  78.1 1.3 %collective-permute-done.22.got_ref = f32[16,1280]{1,0:T(8,128)S(1)} collective-permute-done((f32[16,1280]{1,0:T(8,128)S(1)}, f32[16,1280]{1,0:T(8,128)S(1)}, u32[]{:S(2)}, u32[]{:S(2)}) %collective-permute-start.22) | collective-permute-done | bytes 81952 | tf_op jit(solution)/shard_map/ppermute | solution.py:447
  79.4 2.6 %middle.1 = (f32[16,1152]{1,0:T(8,128)S(1)}, f32[16,1152]{1,0:T(8,128)S(1)}, f32[48,48]{1,0:T(8,128)S(1)}, f32[16,16]{1,0:T(8,128)S(1)}, f32[16,16]{1,0:T(8,128)S(1)}) custom-call(f32[16,1152]{1,0:T(8,128)S(1)} %order.1.refs_2_.refs_3_.refs_5_.refs_9_.first_ref, f32[16,1280]{1,0:T(8,128)S(1)} %pair.1.refs_3_.refs_9_.refs_0_.pair_ref, ...), custom_call_target="tpu_custom_call" | custom-call | tf_op jit(solution)/shard_map/middle/pallas_call | solution.py:427
  82.0 2.0 %collective-permute-start.25 = (f32[48,48]{1,0:T(8,128)S(1)}, f32[48,48]{1,0:T(8,128)S(1)}, u32[]{:S(2)}, u32[]{:S(2)}) collective-permute-start(f32[48,48]{1,0:T(8,128)S(1)} %get-tuple-element.107), channel_id=1, source_target_pairs={{0,24},{1,25},{2,26},{3,27},{4,28},{5,29},{6,30},{7,31},{8,16},{9,... | collective-permute-start | bytes 27656 | tf_op jit(solution)/shard_map/ppermute | solution.py:447
  84.1 0.4 collective-permute-start.24
  84.4 1.1 %collective-permute-start.23 = (f32[48,48]{1,0:T(8,128)S(1)}, f32[48,48]{1,0:T(8,128)S(1)}, u32[]{:S(2)}, u32[]{:S(2)}) collective-permute-start(f32[48,48]{1,0:T(8,128)S(1)} %get-tuple-element.107), channel_id=1, source_target_pairs={{0,8},{1,9},{2,10},{3,11},{4,12},{5,13},{6,14},{7,15},{8,0},{9,1},... | collective-permute-start | bytes 27656 | tf_op jit(solution)/shard_map/ppermute | solution.py:447
  85.6 1.3 %collective-permute-done.25 = f32[48,48]{1,0:T(8,128)S(1)} collective-permute-done((f32[48,48]{1,0:T(8,128)S(1)}, f32[48,48]{1,0:T(8,128)S(1)}, u32[]{:S(2)}, u32[]{:S(2)}) %collective-permute-start.25) | collective-permute-done | bytes 9248 | tf_op jit(solution)/shard_map/ppermute | solution.py:447
  86.9 1.0 collective-permute-done.24
  87.9 0.4 collective-permute-done.23
  88.3 2.3 %collective-permute-start.28 = (f32[48,48]{1,0:T(8,128)S(1)}, f32[48,48]{1,0:T(8,128)S(1)}, u32[]{:S(2)}, u32[]{:S(2)}) collective-permute-start(f32[48,48]{1,0:T(8,128)S(1)} %add_add_fusion.2.refs_0_), channel_id=1, source_target_pairs={{0,6},{1,7},{2,4},{3,5},{4,2},{5,3},{6,0},{7,1},{8,14},{9,15},{10,... | collective-permute-start | bytes 27656 | tf_op jit(solution)/shard_map/ppermute | solution.py:447
  90.6 2.2 %collective-permute-start.26 = (f32[48,48]{1,0:T(8,128)S(1)}, f32[48,48]{1,0:T(8,128)S(1)}, u32[]{:S(2)}, u32[]{:S(2)}) collective-permute-start(f32[48,48]{1,0:T(8,128)S(1)} %add_add_fusion.2.refs_0_), channel_id=1, source_target_pairs={{0,2},{1,3},{2,0},{3,1},{4,6},{5,7},{6,4},{7,5},{8,10},{9,11},{10,... | collective-permute-start | bytes 27656 | tf_op jit(solution)/shard_map/ppermute | solution.py:447
  92.7 1.2 %collective-permute-done.28.refs_3_ = f32[48,48]{1,0:T(8,128)S(1)} collective-permute-done((f32[48,48]{1,0:T(8,128)S(1)}, f32[48,48]{1,0:T(8,128)S(1)}, u32[]{:S(2)}, u32[]{:S(2)}) %collective-permute-start.28) | collective-permute-done | bytes 9248 | tf_op jit(solution)/shard_map/ppermute | solution.py:447
  94.0 1.3 %collective-permute-done.27.refs_2_ = f32[48,48]{1,0:T(8,128)S(1)} collective-permute-done((f32[48,48]{1,0:T(8,128)S(1)}, f32[48,48]{1,0:T(8,128)S(1)}, u32[]{:S(2)}, u32[]{:S(2)}) %collective-permute-start.27) | collective-permute-done | bytes 9248 | tf_op jit(solution)/shard_map/ppermute | solution.py:447
  95.3 2.8 %last.1 = (f32[16,576]{1,0:T(8,128)}, f32[2,16,16]{2,1,0:T(8,128)}, f32[2,16,16]{2,1,0:T(8,128)}) custom-call(f32[16,1152]{1,0:T(8,128)S(1)} %order.1.refs_2_.refs_3_.refs_5_.refs_9_.first_ref, f32[16,1152]{1,0:T(8,128)S(1)} %get-tuple-element.103.q_ref, f32[16,1152]{1,0:T(8,128)S(1)} %get-tuple-element.104.prod_ref, ...), custom_call_target="tpu_custom_call" | custom-call | tf_op jit(solution)/shard_map/last/pallas_call | solution.py:427
  (17 shorter events, 0.1 us)
Async XLA Ops:
  0.6 2.6 %collective-permute-start = (f32[16,576]{1,0:T(8,128)}, f32[16,576]{1,0:T(8,128)S(1)}, u32[]{:S(2)}, u32[]{:S(2)}) collective-permute-start(f32[16,576]{1,0:T(8,128)} %bitcast.7), channel_id=1, source_target_pairs={{0,1},{1,0},{2,3},{3,2},{4,5},{5,4},{6,7},{7,6},{8,9},{9,8},{10,11... | collective-permute-start | bytes 110600 | tf_op jit(solution)/shard_map/ppermute | solution.py:447
  3.3 12.8 %collective-permute-start.3 = (f32[16,1152]{1,0:T(8,128)S(1)}, f32[16,1152]{1,0:T(8,128)S(1)}, u32[]{:S(2)}, u32[]{:S(2)}) collective-permute-start(f32[16,1152]{1,0:T(8,128)S(1)} %order.1.refs_2_.refs_3_.refs_5_.refs_9_.first_ref), channel_id=1, source_target_pairs={{0,24},{1,7},{2,26},{3,5},{4,28},{5,3},{6,30},{7,1},{8,16},{9,15},... | collective-permute-start | bytes 221192 | tf_op jit(solution)/shard_map/ppermute | solution.py:447
  6.8 9.3 %collective-permute-start.2 = (f32[16,1152]{1,0:T(8,128)S(1)}, f32[16,1152]{1,0:T(8,128)S(1)}, u32[]{:S(2)}, u32[]{:S(2)}) collective-permute-start(f32[16,1152]{1,0:T(8,128)S(1)} %order.1.refs_2_.refs_3_.refs_5_.refs_9_.first_ref), channel_id=1, source_target_pairs={{0,4},{1,17},{2,6},{3,19},{4,0},{5,21},{6,2},{7,23},{8,12},{9,25},... | collective-permute-start | bytes 221192 | tf_op jit(solution)/shard_map/ppermute | solution.py:447
  9.4 6.7 %collective-permute-start.1 = (f32[16,1152]{1,0:T(8,128)S(1)}, f32[16,1152]{1,0:T(8,128)S(1)}, u32[]{:S(2)}, u32[]{:S(2)}) collective-permute-start(f32[16,1152]{1,0:T(8,128)S(1)} %order.1.refs_2_.refs_3_.refs_5_.refs_9_.first_ref), channel_id=1, source_target_pairs={{0,2},{1,9},{2,0},{3,11},{4,6},{5,13},{6,4},{7,15},{8,10},{9,1},{1... | collective-permute-start | bytes 221192 | tf_op jit(solution)/shard_map/ppermute | solution.py:447
  16.1 3.8 %collective-permute-start.4 = (f32[16,1152]{1,0:T(8,128)S(1)}, f32[16,1152]{1,0:T(8,128)S(1)}, u32[]{:S(2)}, u32[]{:S(2)}) collective-permute-start(f32[16,1152]{1,0:T(8,128)S(1)} %collective-permute-done.1.refs_8_), channel_id=1, source_target_pairs={{0,1},{1,0},{2,3},{3,2},{4,5},{5,4},{6,7},{7,6},{8,9},{9,8},{10,11... | collective-permute-start | bytes 221192 | tf_op jit(solution)/shard_map/ppermute | solution.py:447
  16.2 3.7 %collective-permute-start.5 = (f32[16,1152]{1,0:T(8,128)S(1)}, f32[16,1152]{1,0:T(8,128)S(1)}, u32[]{:S(2)}, u32[]{:S(2)}) collective-permute-start(f32[16,1152]{1,0:T(8,128)S(1)} %collective-permute-done.2.refs_9_), channel_id=1, source_target_pairs={{0,1},{1,0},{2,3},{3,2},{4,5},{5,4},{6,7},{7,6},{8,9},{9,8},{10,11... | collective-permute-start | bytes 221192 | tf_op jit(solution)/shard_map/ppermute | solution.py:447
  16.7 3.2 %collective-permute-start.6 = (f32[16,1152]{1,0:T(8,128)S(1)}, f32[16,1152]{1,0:T(8,128)S(1)}, u32[]{:S(2)}, u32[]{:S(2)}) collective-permute-start(f32[16,1152]{1,0:T(8,128)S(1)} %collective-permute-done.3.refs_10_), channel_id=1, source_target_pairs={{0,1},{1,0},{2,3},{3,2},{4,5},{5,4},{6,7},{7,6},{8,9},{9,8},{10,11... | collective-permute-start | bytes 221192 | tf_op jit(solution)/shard_map/ppermute | solution.py:447
  19.9 13.6 %copy-start = (f32[576]{0:T(1024)S(1)}, f32[576]{0:T(1024)}, u32[]{:S(2)}) copy-start(f32[576]{0:T(1024)} %param.4) | copy-start | bytes 6916
  33.0 1.6 %collective-permute-start.7 = (f32[3,16,1152]{2,1,0:T(8,128)S(1)}, f32[3,16,1152]{2,1,0:T(8,128)S(1)}, u32[]{:S(2)}, u32[]{:S(2)}) collective-permute-start(f32[3,16,1152]{2,1,0:T(8,128)S(1)} %get-tuple-element.74), channel_id=1, source_target_pairs={{0,1},{1,0},{2,3},{3,2},{4,5},{5,4},{6,7},{7,6},{8,9},{9,8},{10,11... | collective-permute-start | bytes 663560 | tf_op jit(solution)/shard_map/ppermute | solution.py:447
  34.6 6.6 %collective-permute-start.8 = (f32[16,1152]{1,0:T(8,128)S(1)}, f32[16,1152]{1,0:T(8,128)S(1)}, u32[]{:S(2)}, u32[]{:S(2)}) collective-permute-start(f32[16,1152]{1,0:T(8,128)S(1)} %get-tuple-element.79), channel_id=1, source_target_pairs={{0,2},{1,9},{2,0},{3,11},{4,6},{5,13},{6,4},{7,15},{8,10},{9,1},{1... | collective-permute-start | bytes 221192 | tf_op jit(solution)/shard_map/ppermute | solution.py:447
  35.3 6.8 %collective-permute-start.9 = (f32[16,1152]{1,0:T(8,128)S(1)}, f32[16,1152]{1,0:T(8,128)S(1)}, u32[]{:S(2)}, u32[]{:S(2)}) collective-permute-start(f32[16,1152]{1,0:T(8,128)S(1)} %get-tuple-element.80), channel_id=1, source_target_pairs={{0,4},{1,17},{2,6},{3,19},{4,0},{5,21},{6,2},{7,23},{8,12},{9,25},... | collective-permute-start | bytes 221192 | tf_op jit(solution)/shard_map/ppermute | solution.py:447
  35.5 6.7 %collective-permute-start.10 = (f32[16,1152]{1,0:T(8,128)S(1)}, f32[16,1152]{1,0:T(8,128)S(1)}, u32[]{:S(2)}, u32[]{:S(2)}) collective-permute-start(f32[16,1152]{1,0:T(8,128)S(1)} %get-tuple-element.81), channel_id=1, source_target_pairs={{0,24},{1,7},{2,26},{3,5},{4,28},{5,3},{6,30},{7,1},{8,16},{9,15},... | collective-permute-start | bytes 221192 | tf_op jit(solution)/shard_map/ppermute | solution.py:447
  42.2 1.3 %collective-permute-start.11 = (f32[16,1152]{1,0:T(8,128)S(1)}, f32[16,1152]{1,0:T(8,128)S(1)}, u32[]{:S(2)}, u32[]{:S(2)}) collective-permute-start(f32[16,1152]{1,0:T(8,128)S(1)} %add_add_fusion.1.mine_ref), channel_id=1, source_target_pairs={{0,1},{1,0},{2,3},{3,2},{4,5},{5,4},{6,7},{7,6},{8,9},{9,8},{10,11... | collective-permute-start | bytes 221192 | tf_op jit(solution)/shard_map/ppermute | solution.py:447
  43.8 8.8 %collective-permute-start.14 = (f32[16,1280]{1,0:T(8,128)S(1)}, f32[16,1280]{1,0:T(8,128)S(1)}, u32[]{:S(2)}, u32[]{:S(2)}) collective-permute-start(f32[16,1280]{1,0:T(8,128)S(1)} %pair.1.refs_3_.refs_9_.refs_0_.pair_ref), channel_id=1, source_target_pairs={{0,24},{1,7},{2,26},{3,5},{4,28},{5,3},{6,30},{7,1},{8,16},{9,15},... | collective-permute-start | bytes 245768 | tf_op jit(solution)/shard_map/ppermute | solution.py:447
  44.7 8.0 %collective-permute-start.13 = (f32[16,1280]{1,0:T(8,128)S(1)}, f32[16,1280]{1,0:T(8,128)S(1)}, u32[]{:S(2)}, u32[]{:S(2)}) collective-permute-start(f32[16,1280]{1,0:T(8,128)S(1)} %pair.1.refs_3_.refs_9_.refs_0_.pair_ref), channel_id=1, source_target_pairs={{0,4},{1,17},{2,6},{3,19},{4,0},{5,21},{6,2},{7,23},{8,12},{9,25},... | collective-permute-start | bytes 245768 | tf_op jit(solution)/shard_map/ppermute | solution.py:447
  47.5 5.2 %collective-permute-start.12 = (f32[16,1280]{1,0:T(8,128)S(1)}, f32[16,1280]{1,0:T(8,128)S(1)}, u32[]{:S(2)}, u32[]{:S(2)}) collective-permute-start(f32[16,1280]{1,0:T(8,128)S(1)} %pair.1.refs_3_.refs_9_.refs_0_.pair_ref), channel_id=1, source_target_pairs={{0,2},{1,9},{2,0},{3,11},{4,6},{5,13},{6,4},{7,15},{8,10},{9,1},{1... | collective-permute-start | bytes 245768 | tf_op jit(solution)/shard_map/ppermute | solution.py:447
  52.7 2.7 %collective-permute-start.15 = (f32[16,1280]{1,0:T(8,128)S(1)}, f32[16,1280]{1,0:T(8,128)S(1)}, u32[]{:S(2)}, u32[]{:S(2)}) collective-permute-start(f32[16,1280]{1,0:T(8,128)S(1)} %collective-permute-done.12.refs_12_.refs_1_), channel_id=1, source_target_pairs={{0,1},{1,0},{2,3},{3,2},{4,5},{5,4},{6,7},{7,6},{8,9},{9,8},{10,11... | collective-permute-start | bytes 245768 | tf_op jit(solution)/shard_map/ppermute | solution.py:447
  52.8 2.6 %collective-permute-start.16 = (f32[16,1280]{1,0:T(8,128)S(1)}, f32[16,1280]{1,0:T(8,128)S(1)}, u32[]{:S(2)}, u32[]{:S(2)}) collective-permute-start(f32[16,1280]{1,0:T(8,128)S(1)} %collective-permute-done.13.refs_13_.refs_2_), channel_id=1, source_target_pairs={{0,1},{1,0},{2,3},{3,2},{4,5},{5,4},{6,7},{7,6},{8,9},{9,8},{10,11... | collective-permute-start | bytes 245768 | tf_op jit(solution)/shard_map/ppermute | solution.py:447
  53.3 2.1 %collective-permute-start.17 = (f32[16,1280]{1,0:T(8,128)S(1)}, f32[16,1280]{1,0:T(8,128)S(1)}, u32[]{:S(2)}, u32[]{:S(2)}) collective-permute-start(f32[16,1280]{1,0:T(8,128)S(1)} %collective-permute-done.14.refs_14_.refs_3_), channel_id=1, source_target_pairs={{0,1},{1,0},{2,3},{3,2},{4,5},{5,4},{6,7},{7,6},{8,9},{9,8},{10,11... | collective-permute-start | bytes 245768 | tf_op jit(solution)/shard_map/ppermute | solution.py:447
  68.5 1.6 %collective-permute-start.18 = (f32[3,16,1152]{2,1,0:T(8,128)S(1)}, f32[3,16,1152]{2,1,0:T(8,128)S(1)}, u32[]{:S(2)}, u32[]{:S(2)}) collective-permute-start(f32[3,16,1152]{2,1,0:T(8,128)S(1)} %get-tuple-element.94), channel_id=1, source_target_pairs={{0,1},{1,0},{2,3},{3,2},{4,5},{5,4},{6,7},{7,6},{8,9},{9,8},{10,11... | collective-permute-start | bytes 663560 | tf_op jit(solution)/shard_map/ppermute | solution.py:447
  70.1 7.9 %collective-permute-start.19 = (f32[16,1280]{1,0:T(8,128)S(1)}, f32[16,1280]{1,0:T(8,128)S(1)}, u32[]{:S(2)}, u32[]{:S(2)}) collective-permute-start(f32[16,1280]{1,0:T(8,128)S(1)} %get-tuple-element.100), channel_id=1, source_target_pairs={{0,2},{1,9},{2,0},{3,11},{4,6},{5,13},{6,4},{7,15},{8,10},{9,1},{1... | collective-permute-start | bytes 245768 | tf_op jit(solution)/shard_map/ppermute | solution.py:447
  70.8 7.2 %collective-permute-start.20 = (f32[16,1280]{1,0:T(8,128)S(1)}, f32[16,1280]{1,0:T(8,128)S(1)}, u32[]{:S(2)}, u32[]{:S(2)}) collective-permute-start(f32[16,1280]{1,0:T(8,128)S(1)} %get-tuple-element.101), channel_id=1, source_target_pairs={{0,4},{1,17},{2,6},{3,19},{4,0},{5,21},{6,2},{7,23},{8,12},{9,25},... | collective-permute-start | bytes 245768 | tf_op jit(solution)/shard_map/ppermute | solution.py:447
  72.5 5.6 %collective-permute-start.21 = (f32[16,1280]{1,0:T(8,128)S(1)}, f32[16,1280]{1,0:T(8,128)S(1)}, u32[]{:S(2)}, u32[]{:S(2)}) collective-permute-start(f32[16,1280]{1,0:T(8,128)S(1)} %get-tuple-element.102), channel_id=1, source_target_pairs={{0,24},{1,7},{2,26},{3,5},{4,28},{5,3},{6,30},{7,1},{8,16},{9,15},... | collective-permute-start | bytes 245768 | tf_op jit(solution)/shard_map/ppermute | solution.py:447
  78.1 1.3 %collective-permute-start.22 = (f32[16,1280]{1,0:T(8,128)S(1)}, f32[16,1280]{1,0:T(8,128)S(1)}, u32[]{:S(2)}, u32[]{:S(2)}) collective-permute-start(f32[16,1280]{1,0:T(8,128)S(1)} %add_add_fusion.mine_ref), channel_id=1, source_target_pairs={{0,1},{1,0},{2,3},{3,2},{4,5},{5,4},{6,7},{7,6},{8,9},{9,8},{10,11... | collective-permute-start | bytes 245768 | tf_op jit(solution)/shard_map/ppermute | solution.py:447
  82.0 4.9 %collective-permute-start.25 = (f32[48,48]{1,0:T(8,128)S(1)}, f32[48,48]{1,0:T(8,128)S(1)}, u32[]{:S(2)}, u32[]{:S(2)}) collective-permute-start(f32[48,48]{1,0:T(8,128)S(1)} %get-tuple-element.107), channel_id=1, source_target_pairs={{0,24},{1,25},{2,26},{3,27},{4,28},{5,29},{6,30},{7,31},{8,16},{9,... | collective-permute-start | bytes 27656 | tf_op jit(solution)/shard_map/ppermute | solution.py:447
  84.1 3.8 %collective-permute-start.24 = (f32[48,48]{1,0:T(8,128)S(1)}, f32[48,48]{1,0:T(8,128)S(1)}, u32[]{:S(2)}, u32[]{:S(2)}) collective-permute-start(f32[48,48]{1,0:T(8,128)S(1)} %get-tuple-element.107), channel_id=1, source_target_pairs={{0,16},{1,17},{2,18},{3,19},{4,20},{5,21},{6,22},{7,23},{8,24},{9,... | collective-permute-start | bytes 27656 | tf_op jit(solution)/shard_map/ppermute | solution.py:447
  84.4 3.8 %collective-permute-start.23 = (f32[48,48]{1,0:T(8,128)S(1)}, f32[48,48]{1,0:T(8,128)S(1)}, u32[]{:S(2)}, u32[]{:S(2)}) collective-permute-start(f32[48,48]{1,0:T(8,128)S(1)} %get-tuple-element.107), channel_id=1, source_target_pairs={{0,8},{1,9},{2,10},{3,11},{4,12},{5,13},{6,14},{7,15},{8,0},{9,1},... | collective-permute-start | bytes 27656 | tf_op jit(solution)/shard_map/ppermute | solution.py:447
  88.3 5.7 %collective-permute-start.28 = (f32[48,48]{1,0:T(8,128)S(1)}, f32[48,48]{1,0:T(8,128)S(1)}, u32[]{:S(2)}, u32[]{:S(2)}) collective-permute-start(f32[48,48]{1,0:T(8,128)S(1)} %add_add_fusion.2.refs_0_), channel_id=1, source_target_pairs={{0,6},{1,7},{2,4},{3,5},{4,2},{5,3},{6,0},{7,1},{8,14},{9,15},{10,... | collective-permute-start | bytes 27656 | tf_op jit(solution)/shard_map/ppermute | solution.py:447
  90.6 4.7 %collective-permute-start.27 = (f32[48,48]{1,0:T(8,128)S(1)}, f32[48,48]{1,0:T(8,128)S(1)}, u32[]{:S(2)}, u32[]{:S(2)}) collective-permute-start(f32[48,48]{1,0:T(8,128)S(1)} %add_add_fusion.2.refs_0_), channel_id=1, source_target_pairs={{0,4},{1,5},{2,6},{3,7},{4,0},{5,1},{6,2},{7,3},{8,12},{9,13},{10,... | collective-permute-start | bytes 27656 | tf_op jit(solution)/shard_map/ppermute | solution.py:447
  90.6 4.7 %collective-permute-start.26 = (f32[48,48]{1,0:T(8,128)S(1)}, f32[48,48]{1,0:T(8,128)S(1)}, u32[]{:S(2)}, u32[]{:S(2)}) collective-permute-start(f32[48,48]{1,0:T(8,128)S(1)} %add_add_fusion.2.refs_0_), channel_id=1, source_target_pairs={{0,2},{1,3},{2,0},{3,1},{4,6},{5,7},{6,4},{7,5},{8,10},{9,11},{10,... | collective-permute-start | bytes 27656 | tf_op jit(solution)/shard_map/ppermute | solution.py:447

commit v9 on v8

--- a/solution.py
+++ b/solution.py
@@ -162,13 +162,21 @@
             self.get(*key)
 
 
-def tiles_of(piece, tile, first, last, step):
+def rows_at(start, tile):
+    return slice(start, start + tile) if isinstance(start, int) else pl.ds(pl.multiple_of(start, tile), tile)
+
+
+def tiles_of(piece, tile, first, last, step, loop=False):
     def body(t, carry):
-        high, low = split(piece[pl.ds(pl.multiple_of(t * tile, tile), tile), :])
+        high, low = split(piece[rows_at(t * tile, tile), :])
         step(t, high, low)
         return carry
 
-    lax.fori_loop(first, last, body, 0)
+    if loop:
+        lax.fori_loop(first, last, body, 0)
+    else:
+        for t in range(first, last):
+            body(t, 0)
 
 
 def across(xg, cols, k, high, low):
@@ -193,10 +201,11 @@
         loader.wait(i)
 
 
-def order_kernel(k, n, own_ref, other_ref, out_ref):
+def order_kernel(k, n, own_ref, other_ref, *outs):
     even = place()[0] == 0
     own, other = own_ref[...], other_ref[...]
-    out_ref[...] = jnp.concatenate([jnp.where(even, own, other), jnp.where(even, other, own)], axis=1)
+    for out in outs:
+        out[...] = jnp.concatenate([jnp.where(even, own, other), jnp.where(even, other, own)], axis=1)
 
 
 def put(slab, at, k, value):
@@ -219,9 +228,9 @@
         rows = piece.shape[0]
 
         def step(t, high, low):
-            u_ref[:, pl.ds(pl.multiple_of(p * rows + t * tile, tile), tile)] = across(xg, slice(None), k, high, low)
-
-        tiles_of(piece, tile, 0, rows // tile, step)
+            u_ref[:, rows_at(p * rows + t * tile, tile)] = across(xg, slice(None), k, high, low)
+
+        tiles_of(piece, tile, 0, rows // tile, step, len(new) > 0)
     pieces.finish()
 
 
@@ -236,9 +245,9 @@
         cols = slice((s - 1) * 2 * n, s * 2 * n)
 
         def step(t, high, low):
-            v_ref[:, cols] += along(xr, pl.ds(pl.multiple_of(t * tile, tile), tile), k, high, low)
-
-        tiles_of(pieces.get(s, 0), tile, 0, n // tile, step)
+            v_ref[:, cols] += along(xr, rows_at(t * tile, tile), k, high, low)
+
+        tiles_of(pieces.get(s, 0), tile, 0, n // tile, step, len(new) > 0)
     pieces.finish()
 
 
@@ -267,11 +276,11 @@
         cols = slice((s - 1) * 2 * n, s * 2 * n)
 
         def step(t, high, low):
-            at = pl.ds(pl.multiple_of(p * rows + t * tile, tile), tile)
+            at = rows_at(p * rows + t * tile, tile)
             v_acc[:, cols] += along(xr, at, k, high, low)
             u_acc[:, at] += across(xg, cols, k, high, low)
 
-        tiles_of(piece, tile, n // tile if p == 0 else 0, rows // tile, step)
+        tiles_of(piece, tile, n // tile if p == 0 else 0, rows // tile, step, len(new) > 0)
 
     own_ref[...] = u_acc[:, :n]
     for s in range(1, group):
@@ -286,7 +295,7 @@
     v_ref[...] = jnp.zeros_like(v_ref)
 
     def step(t, high, low):
-        v_ref[...] += along(xr, pl.ds(pl.multiple_of(t * tile, tile), tile), k, high, low)
+        v_ref[...] += along(xr, rows_at(t * tile, tile), k, high, low)
 
     tiles_of(piece, tile, 0, piece.shape[0] // tile, step)
 
@@ -299,20 +308,19 @@
     even = place()[0] == 0
     v_acc[...] = v_ref[...]
     u_acc[...] = own_ref[...]
-    for p in range(1, parts):
-        rows = near[p - 1].shape[0]
-
-        def step(t, high, low):
-            v_acc[...] += along(xr, pl.ds(pl.multiple_of(p * rows + t * tile, tile), tile), k, high, low)
-
-        tiles_of(near[p - 1], tile, 0, rows // tile, step)
-    for s in range(1, group):
-        cols = slice((s - 1) * 2 * n, s * 2 * n)
-
-        def step(t, high, low):
-            u_acc[:, pl.ds(pl.multiple_of(t * tile, tile), tile)] += across(xg, cols, k, high, low)
-
-        tiles_of(lead[s - 1], tile, 0, n // tile, step)
+    rows = near[0].shape[0]
+    down = [(p, t) for p in range(1, parts) for t in range(rows // tile)]
+    over = [(s, t) for s in range(1, group) for t in range(n // tile)]
+    for i in range(max(len(down), len(over))):
+        if i < len(down):
+            p, t = down[i]
+            high, low = split(near[p - 1][t * tile : (t + 1) * tile, :])
+            v_acc[...] += along(xr, rows_at(p * rows + t * tile, tile), k, high, low)
+        if i < len(over):
+            s, t = over[i]
+            high, low = split(lead[s - 1][t * tile : (t + 1) * tile, :])
+            cols = slice((s - 1) * 2 * n, s * 2 * n)
+            u_acc[:, t * tile : (t + 1) * tile] += across(xg, cols, k, high, low)
     own = energy_ref[...] * own_half(pair_ref, even, n) + u_acc[...]
     out_ref[:, : 2 * n] = v_acc[...] + in_half(own, even)
     if extra:
@@ -337,14 +345,15 @@
             outs[s - 1][:, 2 * n :] = jnp.where(turned(s, group, even), part, jnp.zeros_like(part))
 
 
-def pair_kernel(k, n, first_ref, mine_ref, got_ref, out_ref):
+def pair_kernel(k, n, first_ref, mine_ref, got_ref, *outs):
     value = mine_ref[...] + got_ref[...]
     s = jnp.concatenate([first_ref[...], value], axis=0)
     moments = dot32(s, s, NT)
-    out_ref[:, : 2 * n] = value
-    out_ref[:, 2 * n :] = jnp.zeros((k, 8 * k), F32)
-    out_ref[:, 2 * n : 2 * n + 2 * k] = moments[:k]
-    out_ref[:, 2 * n + 2 * k : 2 * n + 4 * k] = moments[k:]
+    for out in outs:
+        out[:, : 2 * n] = value
+        out[:, 2 * n :] = jnp.zeros((k, 8 * k), F32)
+        out[:, 2 * n : 2 * n + 2 * k] = moments[:k]
+        out[:, 2 * n + 2 * k : 2 * n + 4 * k] = moments[k:]
 
 
 def factor_of(gram):
@@ -376,7 +385,7 @@
     ).astype(F32)
 
 
-def second_kernel(k, n, order, first_ref, pair_ref, mine_ref, got_ref, q_ref, prod_ref, mom_ref, proj_ref, fact_ref):
+def second_kernel(k, n, order, first_ref, pair_ref, mine_ref, got_ref, q_ref, prod_ref, proj_ref, fact_ref, *outs):
     packed = mine_ref[:, 2 * n :] + got_ref[:, 2 * n :]
     moments = jnp.concatenate([packed[:, : 2 * k], packed[:, 2 * k : 4 * k]], axis=0) * (1.0 / order)
     projection = moments[:k, k:]
@@ -391,7 +400,18 @@
     q_ref[...] = q
     prod_ref[...] = prod
     s = jnp.concatenate([q, x, prod], axis=0)
-    mom_ref[...] = dot32(s, s, NT)
+    total = dot32(s, s, NT)
+    for out in outs:
+        out[...] = total
+
+
+def sum_kernel(*refs):
+    count = (len(refs) + 1) // 2
+    total = refs[0][...]
+    for m in refs[1:count]:
+        total = total + m[...]
+    for out in refs[count:]:
+        out[...] = total
 
 
 def last_kernel(k, n, order, first_ref, q_ref, prod_ref, proj0_ref, fact0_ref, *refs):
@@ -479,9 +499,11 @@
         far=2,
         flops=work // 4,
     )(a, block.T)
-    first = call(functools.partial(order_kernel, k, n), shape(k, 2 * n), 2, name="order")(own, other)
-
-    def products(held, pair, name):
+    firsts = call(functools.partial(order_kernel, k, n), (shape(k, 2 * n),) * (group - 1), 2, name="order")(own, other)
+    first = firsts[0]
+
+    def products(held, copies, name):
+        pair = copies[0]
         extra = pair.shape[1] > 2 * n
         sizes = (k, n, group, tile, parts)
         load = len(held) < total_pieces
@@ -502,7 +524,7 @@
             held.extend(outs[len(out_shapes) :])
             return outs[: len(out_shapes)]
 
-        mine = [send(pair, spread(s)) for s in steps]
+        mine = [send(copies[s - 1], spread(s)) for s in steps]
         (u0,) = matrix_call(
             early_kernel,
             range(parts),
@@ -571,17 +593,21 @@
             total = total + v
         return total, swap(total), held
 
-    mine, got, held = products(held, first, "first")
-    pair = call(functools.partial(pair_kernel, k, n), shape(k, 2 * n + 8 * k), 3, name="pair")(first, mine, got)
-    mine, got, held = products(held, pair, "second")
-    q, prod, moments, proj0, fact0 = call(
+    mine, got, held = products(held, firsts, "first")
+    pairs = call(functools.partial(pair_kernel, k, n), (shape(k, 2 * n + 8 * k),) * (group - 1), 3, name="pair")(
+        first, mine, got
+    )
+    pair = pairs[0]
+    mine, got, held = products(held, pairs, "second")
+    q, prod, proj0, fact0, *moments = call(
         functools.partial(second_kernel, k, n, order),
-        (shape(k, 2 * n), shape(k, 2 * n), shape(3 * k, 3 * k), shape(k, k), shape(k, k)),
+        (shape(k, 2 * n), shape(k, 2 * n), shape(k, k), shape(k, k)) + (shape(3 * k, 3 * k),) * (group - 1),
         4,
         name="middle",
     )(first, pair, mine, got)
-    moments = sum([send(moments, lambda r, c, s=s: chip(r, c, s, 0)) for s in steps], moments)
-    sums = [moments] + [send(moments, lambda r, c, s=s: chip(r, c, 0, s)) for s in steps]
+    sums = [moments[0]] + [send(moments[s - 1], lambda r, c, s=s: chip(r, c, s, 0)) for s in steps]
+    moments = call(sum_kernel, (shape(3 * k, 3 * k),) * (group - 1), group, name="sum")(*sums)
+    sums = [moments[0]] + [send(moments[s - 1], lambda r, c, s=s: chip(r, c, 0, s)) for s in steps]
     basis, proj, fact = call(
         functools.partial(last_kernel, k, n, order),
         (shape(k, n), shape(2, k, k), shape(2, k, k)),

time: 98.3 us -> 94.1 us (0.957)
  Pallas kernels: 59.1 us -> 52.7 us
  waiting for transfers between devices: 9.02 us -> 13.2 us
  starting transfers between devices: 29.1 us -> 27.2 us
    pallas_call x17 -> x18, Pallas kernels: 59.1 us -> 52.7 us  [call(): run(*[pltpu.with_memory_space_constraint(v, pltpu.HBM if i < far else plt...]
    ppermute x29, waiting for transfers between devices: 9.02 us -> 13.2 us  [send(): return lax.ppermute(value, axes, [p for p in pairs if p[1] is not None])]
    ppermute x29, starting transfers between devices: 29.1 us -> 27.2 us  [send(): return lax.ppermute(value, axes, [p for p in pairs if p[1] is not None])]
  transfers between devices with their start and end apart: 29 -> 29, of which waited for: 10 -> 12; matrix products, arithmetic and copies ran while one was open for 0% -> 0% of each run, Pallas kernels for 28% -> 24%
where the time goes in v9:
time: 94.1 us; the launch traced here: 94 us
  Pallas kernels  52.7 us (56%)
  starting transfers between devices  27.2 us (29%)
  waiting for transfers between devices  13.2 us (14%)
    pallas_call x18, Pallas kernels, call(): run(*[pltpu.with_memory_space_constraint(v, pltpu.HBM if i < far else plt...  52.7 us
    ppermute x29, starting transfers between devices, send(): return lax.ppermute(value, axes, [p for p in pairs if p[1] is not None])  27.2 us
    ppermute x29, waiting for transfers between devices, send(): return lax.ppermute(value, axes, [p for p in pairs if p[1] is not None])  13.2 us
  transfers between devices with their start and end apart: 29, of which 12 were waited for; matrix products, arithmetic and copies ran while one was open for 0% of the time, Pallas kernels for 24%

profile of v9, /device:TPU:0, one launch (start us, length us, event | category | flops | bytes accessed | tf_op | source)
XLA Modules:
  0.0 94.0 jit_solution(9117562374692053891)
XLA Ops:
  0.6 0.6 collective-permute-start
  1.2 2.0 %begin.1 = (f32[16,576]{1,0:T(8,128)S(1)}, f32[768,1152]{1,0:T(8,128)S(1)}) custom-call(f32[2304,4608]{1,0:T(8,128)} %bitcast.3, f32[16,576]{1,0:T(8,128)} %bitcast.8), custom_call_target="tpu_custom_call" | custom-call | flops 169869312 | bytes 1327104 | tf_op jit(solution)/shard_map/begin/pallas_call | solution.py:447
  3.2 0.1 order.1
  3.3 3.7 %collective-permute-start.2 = (f32[16,1152]{1,0:T(8,128)S(1)}, f32[16,1152]{1,0:T(8,128)S(1)}, u32[]{:S(2)}, u32[]{:S(2)}) collective-permute-start(f32[16,1152]{1,0:T(8,128)S(1)} %get-tuple-element.76), channel_id=1, source_target_pairs={{0,4},{1,17},{2,6},{3,19},{4,0},{5,21},{6,2},{7,23},{8,12},{9,25},... | collective-permute-start | bytes 221192 | tf_op jit(solution)/shard_map/ppermute | solution.py:467
  7.0 2.4 %collective-permute-start.3 = (f32[16,1152]{1,0:T(8,128)S(1)}, f32[16,1152]{1,0:T(8,128)S(1)}, u32[]{:S(2)}, u32[]{:S(2)}) collective-permute-start(f32[16,1152]{1,0:T(8,128)S(1)} %get-tuple-element.77), channel_id=1, source_target_pairs={{0,24},{1,7},{2,26},{3,5},{4,28},{5,3},{6,30},{7,1},{8,16},{9,15},... | collective-permute-start | bytes 221192 | tf_op jit(solution)/shard_map/ppermute | solution.py:467
  9.4 1.6 %collective-permute-start.1 = (f32[16,1152]{1,0:T(8,128)S(1)}, f32[16,1152]{1,0:T(8,128)S(1)}, u32[]{:S(2)}, u32[]{:S(2)}) collective-permute-start(f32[16,1152]{1,0:T(8,128)S(1)} %get-tuple-element.78.refs_2_.refs_3_.refs_5_.refs_9_.first_ref), channel_id=1, source_target_pairs={{0,2},{1,9},{2,0},{3,11},{4,6},{5,13},{6,4},{7,15},{8,10},{9,1},{1... | collective-permute-start | bytes 221192 | tf_op jit(solution)/shard_map/ppermute | solution.py:467
  11.0 5.1 %first_early.1 = (f32[16,2304]{1,0:T(8,128)S(1)}, f32[768,1152]{1,0:T(8,128)S(1)}, f32[768,1152]{1,0:T(8,128)S(1)}, f32[768,1152]{1,0:T(8,128)S(1)}, f32[768,1152]{1,0:T(8,128)S(1)}) custom-call(f32[2304,4608]{1,0:T(8,128)} %bitcast.4, f32[768,1152]{1,0:T(8,128)S(1)} %get-tuple-element.70.refs_1_.piece.refs_0_, ...), custom_call_target="tpu_custom_call" | custom-call | flops 1358954496 | bytes 10616832 | tf_op jit(solution)/shard_map/first_early/pallas_call | solution.py:447
  16.1 0.0 collective-permute-done.3.refs_10_
  16.1 0.0 collective-permute-done.1.refs_8_
  16.1 0.1 collective-permute-start.4
  16.2 0.5 collective-permute-start.5
  16.7 0.1 collective-permute-start.6
  16.8 3.1 %first_own.1 = (f32[16,3456]{1,0:T(8,128)S(1)}, f32[768,1152]{1,0:T(8,128)S(1)}, f32[768,1152]{1,0:T(8,128)S(1)}) custom-call(f32[2304,4608]{1,0:T(8,128)} %bitcast.5, f32[768,1152]{1,0:T(8,128)S(1)} %get-tuple-element.73.refs_1_.refs_2_.refs_0_, f32[768,1152]{1,0:T(8,128)S(1)} %get-tuple-element.74.refs_2_.refs_3_.refs_1_, ...), custom_call_target="tpu_custom_call" | custom-call | flops 679477248 | bytes 5308416 | tf_op jit(solution)/shard_map/first_own/pallas_call | solution.py:447
  19.9 0.0 collective-permute-done.6.refs_13_
  19.9 0.0 copy-start
  20.0 13.1 %first.1 = (f32[3,16,1152]{2,1,0:T(8,128)S(1)}, f32[3,16,1152]{2,1,0:T(8,128)S(1)}, f32[16,576]{1,0:T(8,128)S(1)}, bf16[32,2304]{1,0:T(8,128)(2,1)S(1)}, bf16[32...) custom-call(f32[2304,4608]{1,0:T(8,128)} %bitcast.6, ...), custom_call_target="tpu_custom_call" | custom-call | flops 5435817984 | bytes 42467328 | tf_op jit(solution)/shard_map/first/pallas_call | solution.py:447
  33.1 0.5 collective-permute-start.7
  33.6 0.7 first_near.1.refs_7_
  34.3 0.4 collective-permute-done.7.got_ref
  34.7 0.7 collective-permute-start.8
  35.4 0.1 collective-permute-start.9
  35.6 0.8 collective-permute-start.10
  36.3 3.2 %first_late.1 = f32[16,1152]{1,0:T(8,128)S(1)} custom-call(f32[768,1152]{1,0:T(8,128)S(1)} %get-tuple-element.71.refs_0_.refs_1_, f32[768,1152]{1,0:T(8,128)S(1)} %get-tuple-element.72.refs_1_.refs_2_, f32[768,1152]{1,0:T(8,128)S(1)} %get-tuple-element.73.refs_1_.refs_2_.refs_0_, f32[768,1152]{1,0:T(8,128)S(1)} %get-tuple-element.74.refs_2_.refs_3_.refs_1_, ...), custom_call_target="tpu_custom_call" | custom-call | flops 2038431744 | bytes 15925248 | tf_op jit(solution)/shard_map/first_late/pallas_call | solution.py:447
  39.6 0.0 collective-permute-done.8
  39.6 2.6 %collective-permute-done.9 = f32[16,1152]{1,0:T(8,128)S(1)} collective-permute-done((f32[16,1152]{1,0:T(8,128)S(1)}, f32[16,1152]{1,0:T(8,128)S(1)}, u32[]{:S(2)}, u32[]{:S(2)}) %collective-permute-start.9) | collective-permute-done | bytes 73760 | tf_op jit(solution)/shard_map/ppermute | solution.py:467
  42.3 0.1 collective-permute-start.11
  42.4 1.3 %collective-permute-done.11.got_ref = f32[16,1152]{1,0:T(8,128)S(1)} collective-permute-done((f32[16,1152]{1,0:T(8,128)S(1)}, f32[16,1152]{1,0:T(8,128)S(1)}, u32[]{:S(2)}, u32[]{:S(2)}) %collective-permute-start.11) | collective-permute-done | bytes 73760 | tf_op jit(solution)/shard_map/ppermute | solution.py:467
  43.6 0.4 pair.1
  44.0 1.4 %collective-permute-start.13 = (f32[16,1280]{1,0:T(8,128)S(1)}, f32[16,1280]{1,0:T(8,128)S(1)}, u32[]{:S(2)}, u32[]{:S(2)}) collective-permute-start(f32[16,1280]{1,0:T(8,128)S(1)} %get-tuple-element.102), channel_id=1, source_target_pairs={{0,4},{1,17},{2,6},{3,19},{4,0},{5,21},{6,2},{7,23},{8,12},{9,25},... | collective-permute-start | bytes 245768 | tf_op jit(solution)/shard_map/ppermute | solution.py:467
  45.3 1.0 %collective-permute-start.14 = (f32[16,1280]{1,0:T(8,128)S(1)}, f32[16,1280]{1,0:T(8,128)S(1)}, u32[]{:S(2)}, u32[]{:S(2)}) collective-permute-start(f32[16,1280]{1,0:T(8,128)S(1)} %get-tuple-element.103), channel_id=1, source_target_pairs={{0,24},{1,7},{2,26},{3,5},{4,28},{5,3},{6,30},{7,1},{8,16},{9,15},... | collective-permute-start | bytes 245768 | tf_op jit(solution)/shard_map/ppermute | solution.py:467
  46.3 1.4 %collective-permute-start.12 = (f32[16,1280]{1,0:T(8,128)S(1)}, f32[16,1280]{1,0:T(8,128)S(1)}, u32[]{:S(2)}, u32[]{:S(2)}) collective-permute-start(f32[16,1280]{1,0:T(8,128)S(1)} %get-tuple-element.105.refs_3_.refs_9_.refs_0_.pair_ref), channel_id=1, source_target_pairs={{0,2},{1,9},{2,0},{3,11},{4,6},{5,13},{6,4},{7,15},{8,10},{9,1},{1... | collective-permute-start | bytes 245768 | tf_op jit(solution)/shard_map/ppermute | solution.py:467
  47.7 3.0 %second_early.1.refs_10_ = f32[16,2304]{1,0:T(8,128)S(1)} custom-call(f32[768,1152]{1,0:T(8,128)S(1)} %get-tuple-element.70.refs_1_.piece.refs_0_, f32[768,1152]{1,0:T(8,128)S(1)} %get-tuple-element.71.refs_0_.refs_1_, f32[768,1152]{1,0:T(8,128)S(1)} %get-tuple-element.72.refs_1_.refs_2_, f32[16,1280]{1,0:T(8,128)S(1)} %get-tuple-element.105.refs_3_.refs_9_.refs_0_.pair_ref), custom_call_target="tpu_custom_call" | custom-call | flops 1358954496 | bytes 10616832 | tf_op jit(solution)/shard_map/second_early/pallas_call | solution.py:447
  50.7 0.0 collective-permute-done.13.refs_13_.refs_2_
  50.7 0.8 collective-permute-done.14.refs_14_.refs_3_
  51.5 0.0 collective-permute-done.12.refs_12_.refs_1_
  51.5 0.0 collective-permute-start.15
  51.5 0.5 collective-permute-start.16
  52.0 0.0 collective-permute-start.17
  52.0 1.5 %second_own.1.refs_11_ = f32[16,3456]{1,0:T(8,128)S(1)} custom-call(f32[768,1152]{1,0:T(8,128)S(1)} %get-tuple-element.73.refs_1_.refs_2_.refs_0_, f32[768,1152]{1,0:T(8,128)S(1)} %get-tuple-element.74.refs_2_.refs_3_.refs_1_, f32[768,1152]{1,0:T(8,128)S(1)} %get-tuple-element.79.refs_3_.refs_4_.refs_2_, ...), custom_call_target="tpu_custom_call" | custom-call | flops 679477248 | bytes 5308416 | tf_op jit(solution)/shard_map/second_own/pallas_call | solution.py:447
  53.5 0.0 collective-permute-done.16.refs_16_.refs_5_
  53.5 10.9 %second.1 = (f32[3,16,1152]{2,1,0:T(8,128)S(1)}, f32[3,16,1152]{2,1,0:T(8,128)S(1)}, f32[16,576]{1,0:T(8,128)S(1)}, bf16[32,2304]{1,0:T(8,128)(2,1)S(1)}, bf16[32,3456]{1,0:T(8,128)(2,1)S(1)}) custom-call(f32[768,1152]{1,0:T(8,128)S(1)} %get-tuple-element.73.refs_1_.refs_2_.refs_0_, f32[768,1152]{1,0:T(8,128)S(1)} %get-tuple-element.74.refs_2_.refs_3_.refs_1_, ...), custom_call_target="tpu_custom_call" | custom-call | flops 5435817984 | bytes 42467328 | tf_op jit(solution)/shard_map/second/pallas_call | solution.py:447
  64.4 0.6 collective-permute-start.18
  65.0 0.7 second_near.1.refs_7_
  65.8 0.4 collective-permute-done.18.got_ref
  66.1 0.6 collective-permute-start.19
  66.8 2.0 %collective-permute-start.20 = (f32[16,1280]{1,0:T(8,128)S(1)}, f32[16,1280]{1,0:T(8,128)S(1)}, u32[]{:S(2)}, u32[]{:S(2)}) collective-permute-start(f32[16,1280]{1,0:T(8,128)S(1)} %get-tuple-element.118), channel_id=1, source_target_pairs={{0,4},{1,17},{2,6},{3,19},{4,0},{5,21},{6,2},{7,23},{8,12},{9,25},... | collective-permute-start | bytes 245768 | tf_op jit(solution)/shard_map/ppermute | solution.py:467
  68.7 1.6 %collective-permute-start.21 = (f32[16,1280]{1,0:T(8,128)S(1)}, f32[16,1280]{1,0:T(8,128)S(1)}, u32[]{:S(2)}, u32[]{:S(2)}) collective-permute-start(f32[16,1280]{1,0:T(8,128)S(1)} %get-tuple-element.119), channel_id=1, source_target_pairs={{0,24},{1,7},{2,26},{3,5},{4,28},{5,3},{6,30},{7,1},{8,16},{9,15},... | collective-permute-start | bytes 245768 | tf_op jit(solution)/shard_map/ppermute | solution.py:467
  70.3 3.3 %second_late.1 = f32[16,1280]{1,0:T(8,128)S(1)} custom-call(f32[768,1152]{1,0:T(8,128)S(1)} %get-tuple-element.71.refs_0_.refs_1_, f32[768,1152]{1,0:T(8,128)S(1)} %get-tuple-element.72.refs_1_.refs_2_, f32[768,1152]{1,0:T(8,128)S(1)} %get-tuple-element.73.refs_1_.refs_2_.refs_0_, f32[768,1152]{1,0:T(8,128)S(1)} %get-tuple-element.74.refs_2_.refs_3_.refs_1_, ...), custom_call_target="tpu_custom_call" | custom-call | flops 2038431744 | bytes 15925248 | tf_op jit(solution)/shard_map/second_late/pallas_call | solution.py:447
  73.6 1.0 %collective-permute-done.20 = f32[16,1280]{1,0:T(8,128)S(1)} collective-permute-done((f32[16,1280]{1,0:T(8,128)S(1)}, f32[16,1280]{1,0:T(8,128)S(1)}, u32[]{:S(2)}, u32[]{:S(2)}) %collective-permute-start.20) | collective-permute-done | bytes 81952 | tf_op jit(solution)/shard_map/ppermute | solution.py:467
  74.7 0.1 collective-permute-start.22
  74.8 1.3 %collective-permute-done.22.got_ref = f32[16,1280]{1,0:T(8,128)S(1)} collective-permute-done((f32[16,1280]{1,0:T(8,128)S(1)}, f32[16,1280]{1,0:T(8,128)S(1)}, u32[]{:S(2)}, u32[]{:S(2)}) %collective-permute-start.22) | collective-permute-done | bytes 81952 | tf_op jit(solution)/shard_map/ppermute | solution.py:467
  76.0 2.6 %middle.1 = (f32[16,1152]{1,0:T(8,128)S(1)}, f32[16,1152]{1,0:T(8,128)S(1)}, f32[16,16]{1,0:T(8,128)S(1)}, f32[16,16]{1,0:T(8,128)S(1)}, f32[48,48]{1,0:T(8,128)...) custom-call(f32[16,1152]{1,0:T(8,128)S(1)} %get-tuple-element.78.refs_2_.refs_3_.refs_5_.refs_9_.first_ref, ...), custom_call_target="tpu_custom_call" | custom-call | tf_op jit(solution)/shard_map/middle/pallas_call | solution.py:447
  78.7 0.7 collective-permute-start.24
  79.4 1.4 %collective-permute-start.25 = (f32[48,48]{1,0:T(8,128)S(1)}, f32[48,48]{1,0:T(8,128)S(1)}, u32[]{:S(2)}, u32[]{:S(2)}) collective-permute-start(f32[48,48]{1,0:T(8,128)S(1)} %get-tuple-element.126), channel_id=1, source_target_pairs={{0,24},{1,25},{2,26},{3,27},{4,28},{5,29},{6,30},{7,31},{8,16},{9,... | collective-permute-start | bytes 27656 | tf_op jit(solution)/shard_map/ppermute | solution.py:467
  80.7 1.5 %collective-permute-start.23 = (f32[48,48]{1,0:T(8,128)S(1)}, f32[48,48]{1,0:T(8,128)S(1)}, u32[]{:S(2)}, u32[]{:S(2)}) collective-permute-start(f32[48,48]{1,0:T(8,128)S(1)} %get-tuple-element.124.refs_0_), channel_id=1, source_target_pairs={{0,8},{1,9},{2,10},{3,11},{4,12},{5,13},{6,14},{7,15},{8,0},{9,1},... | collective-permute-start | bytes 27656 | tf_op jit(solution)/shard_map/ppermute | solution.py:467
  82.2 0.3 collective-permute-done.24.refs_2_
  82.6 1.5 %collective-permute-done.25.refs_3_ = f32[48,48]{1,0:T(8,128)S(1)} collective-permute-done((f32[48,48]{1,0:T(8,128)S(1)}, f32[48,48]{1,0:T(8,128)S(1)}, u32[]{:S(2)}, u32[]{:S(2)}) %collective-permute-start.25) | collective-permute-done | bytes 9248 | tf_op jit(solution)/shard_map/ppermute | solution.py:467
  84.1 0.5 collective-permute-done.23.refs_1_
  84.6 0.9 collective-permute-start.27
  85.5 1.6 %collective-permute-start.28 = (f32[48,48]{1,0:T(8,128)S(1)}, f32[48,48]{1,0:T(8,128)S(1)}, u32[]{:S(2)}, u32[]{:S(2)}) collective-permute-start(f32[48,48]{1,0:T(8,128)S(1)} %get-tuple-element.129), channel_id=1, source_target_pairs={{0,6},{1,7},{2,4},{3,5},{4,2},{5,3},{6,0},{7,1},{8,14},{9,15},{10,... | collective-permute-start | bytes 27656 | tf_op jit(solution)/shard_map/ppermute | solution.py:467
  87.1 1.1 %collective-permute-start.26 = (f32[48,48]{1,0:T(8,128)S(1)}, f32[48,48]{1,0:T(8,128)S(1)}, u32[]{:S(2)}, u32[]{:S(2)}) collective-permute-start(f32[48,48]{1,0:T(8,128)S(1)} %get-tuple-element.127.refs_0_), channel_id=1, source_target_pairs={{0,2},{1,3},{2,0},{3,1},{4,6},{5,7},{6,4},{7,5},{8,10},{9,11},{10,... | collective-permute-start | bytes 27656 | tf_op jit(solution)/shard_map/ppermute | solution.py:467
  88.1 1.2 %collective-permute-done.27.refs_2_ = f32[48,48]{1,0:T(8,128)S(1)} collective-permute-done((f32[48,48]{1,0:T(8,128)S(1)}, f32[48,48]{1,0:T(8,128)S(1)}, u32[]{:S(2)}, u32[]{:S(2)}) %collective-permute-start.27) | collective-permute-done | bytes 9248 | tf_op jit(solution)/shard_map/ppermute | solution.py:467
  89.4 1.8 %collective-permute-done.28.refs_3_ = f32[48,48]{1,0:T(8,128)S(1)} collective-permute-done((f32[48,48]{1,0:T(8,128)S(1)}, f32[48,48]{1,0:T(8,128)S(1)}, u32[]{:S(2)}, u32[]{:S(2)}) %collective-permute-start.28) | collective-permute-done | bytes 9248 | tf_op jit(solution)/shard_map/ppermute | solution.py:467
  91.2 2.8 %last.1 = (f32[16,576]{1,0:T(8,128)}, f32[2,16,16]{2,1,0:T(8,128)}, f32[2,16,16]{2,1,0:T(8,128)}) custom-call(f32[16,1152]{1,0:T(8,128)S(1)} %get-tuple-element.78.refs_2_.refs_3_.refs_5_.refs_9_.first_ref, f32[16,1152]{1,0:T(8,128)S(1)} %get-tuple-element.120.q_ref, f32[16,1152]{1,0:T(8,128)S(1)} %get-tuple-element.121.prod_ref, ...), custom_call_target="tpu_custom_call" | custom-call | tf_op jit(solution)/shard_map/last/pallas_call | solution.py:447
  (17 shorter events, 0.1 us)
Async XLA Ops:
  0.6 2.6 %collective-permute-start = (f32[16,576]{1,0:T(8,128)}, f32[16,576]{1,0:T(8,128)S(1)}, u32[]{:S(2)}, u32[]{:S(2)}) collective-permute-start(f32[16,576]{1,0:T(8,128)} %bitcast.7), channel_id=1, source_target_pairs={{0,1},{1,0},{2,3},{3,2},{4,5},{5,4},{6,7},{7,6},{8,9},{9,8},{10,11... | collective-permute-start | bytes 110600 | tf_op jit(solution)/shard_map/ppermute | solution.py:467
  3.3 12.8 %collective-permute-start.2 = (f32[16,1152]{1,0:T(8,128)S(1)}, f32[16,1152]{1,0:T(8,128)S(1)}, u32[]{:S(2)}, u32[]{:S(2)}) collective-permute-start(f32[16,1152]{1,0:T(8,128)S(1)} %get-tuple-element.76), channel_id=1, source_target_pairs={{0,4},{1,17},{2,6},{3,19},{4,0},{5,21},{6,2},{7,23},{8,12},{9,25},... | collective-permute-start | bytes 221192 | tf_op jit(solution)/shard_map/ppermute | solution.py:467
  7.0 9.1 %collective-permute-start.3 = (f32[16,1152]{1,0:T(8,128)S(1)}, f32[16,1152]{1,0:T(8,128)S(1)}, u32[]{:S(2)}, u32[]{:S(2)}) collective-permute-start(f32[16,1152]{1,0:T(8,128)S(1)} %get-tuple-element.77), channel_id=1, source_target_pairs={{0,24},{1,7},{2,26},{3,5},{4,28},{5,3},{6,30},{7,1},{8,16},{9,15},... | collective-permute-start | bytes 221192 | tf_op jit(solution)/shard_map/ppermute | solution.py:467
  9.4 6.7 %collective-permute-start.1 = (f32[16,1152]{1,0:T(8,128)S(1)}, f32[16,1152]{1,0:T(8,128)S(1)}, u32[]{:S(2)}, u32[]{:S(2)}) collective-permute-start(f32[16,1152]{1,0:T(8,128)S(1)} %get-tuple-element.78.refs_2_.refs_3_.refs_5_.refs_9_.first_ref), channel_id=1, source_target_pairs={{0,2},{1,9},{2,0},{3,11},{4,6},{5,13},{6,4},{7,15},{8,10},{9,1},{1... | collective-permute-start | bytes 221192 | tf_op jit(solution)/shard_map/ppermute | solution.py:467
  16.1 3.8 %collective-permute-start.4 = (f32[16,1152]{1,0:T(8,128)S(1)}, f32[16,1152]{1,0:T(8,128)S(1)}, u32[]{:S(2)}, u32[]{:S(2)}) collective-permute-start(f32[16,1152]{1,0:T(8,128)S(1)} %collective-permute-done.1.refs_8_), channel_id=1, source_target_pairs={{0,1},{1,0},{2,3},{3,2},{4,5},{5,4},{6,7},{7,6},{8,9},{9,8},{10,11... | collective-permute-start | bytes 221192 | tf_op jit(solution)/shard_map/ppermute | solution.py:467
  16.2 3.7 %collective-permute-start.5 = (f32[16,1152]{1,0:T(8,128)S(1)}, f32[16,1152]{1,0:T(8,128)S(1)}, u32[]{:S(2)}, u32[]{:S(2)}) collective-permute-start(f32[16,1152]{1,0:T(8,128)S(1)} %collective-permute-done.2.refs_9_), channel_id=1, source_target_pairs={{0,1},{1,0},{2,3},{3,2},{4,5},{5,4},{6,7},{7,6},{8,9},{9,8},{10,11... | collective-permute-start | bytes 221192 | tf_op jit(solution)/shard_map/ppermute | solution.py:467
  16.7 3.2 %collective-permute-start.6 = (f32[16,1152]{1,0:T(8,128)S(1)}, f32[16,1152]{1,0:T(8,128)S(1)}, u32[]{:S(2)}, u32[]{:S(2)}) collective-permute-start(f32[16,1152]{1,0:T(8,128)S(1)} %collective-permute-done.3.refs_10_), channel_id=1, source_target_pairs={{0,1},{1,0},{2,3},{3,2},{4,5},{5,4},{6,7},{7,6},{8,9},{9,8},{10,11... | collective-permute-start | bytes 221192 | tf_op jit(solution)/shard_map/ppermute | solution.py:467
  19.9 13.6 %copy-start = (f32[576]{0:T(1024)S(1)}, f32[576]{0:T(1024)}, u32[]{:S(2)}) copy-start(f32[576]{0:T(1024)} %param.4) | copy-start | bytes 6916
  33.1 1.6 %collective-permute-start.7 = (f32[3,16,1152]{2,1,0:T(8,128)S(1)}, f32[3,16,1152]{2,1,0:T(8,128)S(1)}, u32[]{:S(2)}, u32[]{:S(2)}) collective-permute-start(f32[3,16,1152]{2,1,0:T(8,128)S(1)} %get-tuple-element.88), channel_id=1, source_target_pairs={{0,1},{1,0},{2,3},{3,2},{4,5},{5,4},{6,7},{7,6},{8,9},{9,8},{10,11... | collective-permute-start | bytes 663560 | tf_op jit(solution)/shard_map/ppermute | solution.py:467
  34.7 4.9 %collective-permute-start.8 = (f32[16,1152]{1,0:T(8,128)S(1)}, f32[16,1152]{1,0:T(8,128)S(1)}, u32[]{:S(2)}, u32[]{:S(2)}) collective-permute-start(f32[16,1152]{1,0:T(8,128)S(1)} %get-tuple-element.93), channel_id=1, source_target_pairs={{0,2},{1,9},{2,0},{3,11},{4,6},{5,13},{6,4},{7,15},{8,10},{9,1},{1... | collective-permute-start | bytes 221192 | tf_op jit(solution)/shard_map/ppermute | solution.py:467
  35.4 6.8 %collective-permute-start.9 = (f32[16,1152]{1,0:T(8,128)S(1)}, f32[16,1152]{1,0:T(8,128)S(1)}, u32[]{:S(2)}, u32[]{:S(2)}) collective-permute-start(f32[16,1152]{1,0:T(8,128)S(1)} %get-tuple-element.94), channel_id=1, source_target_pairs={{0,4},{1,17},{2,6},{3,19},{4,0},{5,21},{6,2},{7,23},{8,12},{9,25},... | collective-permute-start | bytes 221192 | tf_op jit(solution)/shard_map/ppermute | solution.py:467
  35.6 6.7 %collective-permute-start.10 = (f32[16,1152]{1,0:T(8,128)S(1)}, f32[16,1152]{1,0:T(8,128)S(1)}, u32[]{:S(2)}, u32[]{:S(2)}) collective-permute-start(f32[16,1152]{1,0:T(8,128)S(1)} %get-tuple-element.95), channel_id=1, source_target_pairs={{0,24},{1,7},{2,26},{3,5},{4,28},{5,3},{6,30},{7,1},{8,16},{9,15},... | collective-permute-start | bytes 221192 | tf_op jit(solution)/shard_map/ppermute | solution.py:467
  42.3 1.3 %collective-permute-start.11 = (f32[16,1152]{1,0:T(8,128)S(1)}, f32[16,1152]{1,0:T(8,128)S(1)}, u32[]{:S(2)}, u32[]{:S(2)}) collective-permute-start(f32[16,1152]{1,0:T(8,128)S(1)} %add_add_fusion.1.mine_ref), channel_id=1, source_target_pairs={{0,1},{1,0},{2,3},{3,2},{4,5},{5,4},{6,7},{7,6},{8,9},{9,8},{10,11... | collective-permute-start | bytes 221192 | tf_op jit(solution)/shard_map/ppermute | solution.py:467
  44.0 6.8 %collective-permute-start.13 = (f32[16,1280]{1,0:T(8,128)S(1)}, f32[16,1280]{1,0:T(8,128)S(1)}, u32[]{:S(2)}, u32[]{:S(2)}) collective-permute-start(f32[16,1280]{1,0:T(8,128)S(1)} %get-tuple-element.102), channel_id=1, source_target_pairs={{0,4},{1,17},{2,6},{3,19},{4,0},{5,21},{6,2},{7,23},{8,12},{9,25},... | collective-permute-start | bytes 245768 | tf_op jit(solution)/shard_map/ppermute | solution.py:467
  45.3 6.2 %collective-permute-start.14 = (f32[16,1280]{1,0:T(8,128)S(1)}, f32[16,1280]{1,0:T(8,128)S(1)}, u32[]{:S(2)}, u32[]{:S(2)}) collective-permute-start(f32[16,1280]{1,0:T(8,128)S(1)} %get-tuple-element.103), channel_id=1, source_target_pairs={{0,24},{1,7},{2,26},{3,5},{4,28},{5,3},{6,30},{7,1},{8,16},{9,15},... | collective-permute-start | bytes 245768 | tf_op jit(solution)/shard_map/ppermute | solution.py:467
  46.3 5.2 %collective-permute-start.12 = (f32[16,1280]{1,0:T(8,128)S(1)}, f32[16,1280]{1,0:T(8,128)S(1)}, u32[]{:S(2)}, u32[]{:S(2)}) collective-permute-start(f32[16,1280]{1,0:T(8,128)S(1)} %get-tuple-element.105.refs_3_.refs_9_.refs_0_.pair_ref), channel_id=1, source_target_pairs={{0,2},{1,9},{2,0},{3,11},{4,6},{5,13},{6,4},{7,15},{8,10},{9,1},{1... | collective-permute-start | bytes 245768 | tf_op jit(solution)/shard_map/ppermute | solution.py:467
  51.5 2.0 %collective-permute-start.15 = (f32[16,1280]{1,0:T(8,128)S(1)}, f32[16,1280]{1,0:T(8,128)S(1)}, u32[]{:S(2)}, u32[]{:S(2)}) collective-permute-start(f32[16,1280]{1,0:T(8,128)S(1)} %collective-permute-done.12.refs_12_.refs_1_), channel_id=1, source_target_pairs={{0,1},{1,0},{2,3},{3,2},{4,5},{5,4},{6,7},{7,6},{8,9},{9,8},{10,11... | collective-permute-start | bytes 245768 | tf_op jit(solution)/shard_map/ppermute | solution.py:467
  51.5 2.0 %collective-permute-start.16 = (f32[16,1280]{1,0:T(8,128)S(1)}, f32[16,1280]{1,0:T(8,128)S(1)}, u32[]{:S(2)}, u32[]{:S(2)}) collective-permute-start(f32[16,1280]{1,0:T(8,128)S(1)} %collective-permute-done.13.refs_13_.refs_2_), channel_id=1, source_target_pairs={{0,1},{1,0},{2,3},{3,2},{4,5},{5,4},{6,7},{7,6},{8,9},{9,8},{10,11... | collective-permute-start | bytes 245768 | tf_op jit(solution)/shard_map/ppermute | solution.py:467
  52.0 1.5 %collective-permute-start.17 = (f32[16,1280]{1,0:T(8,128)S(1)}, f32[16,1280]{1,0:T(8,128)S(1)}, u32[]{:S(2)}, u32[]{:S(2)}) collective-permute-start(f32[16,1280]{1,0:T(8,128)S(1)} %collective-permute-done.14.refs_14_.refs_3_), channel_id=1, source_target_pairs={{0,1},{1,0},{2,3},{3,2},{4,5},{5,4},{6,7},{7,6},{8,9},{9,8},{10,11... | collective-permute-start | bytes 245768 | tf_op jit(solution)/shard_map/ppermute | solution.py:467
  64.4 1.7 %collective-permute-start.18 = (f32[3,16,1152]{2,1,0:T(8,128)S(1)}, f32[3,16,1152]{2,1,0:T(8,128)S(1)}, u32[]{:S(2)}, u32[]{:S(2)}) collective-permute-start(f32[3,16,1152]{2,1,0:T(8,128)S(1)} %get-tuple-element.111), channel_id=1, source_target_pairs={{0,1},{1,0},{2,3},{3,2},{4,5},{5,4},{6,7},{7,6},{8,9},{9,8},{10,11... | collective-permute-start | bytes 663560 | tf_op jit(solution)/shard_map/ppermute | solution.py:467
  66.1 7.4 %collective-permute-start.19 = (f32[16,1280]{1,0:T(8,128)S(1)}, f32[16,1280]{1,0:T(8,128)S(1)}, u32[]{:S(2)}, u32[]{:S(2)}) collective-permute-start(f32[16,1280]{1,0:T(8,128)S(1)} %get-tuple-element.117), channel_id=1, source_target_pairs={{0,2},{1,9},{2,0},{3,11},{4,6},{5,13},{6,4},{7,15},{8,10},{9,1},{1... | collective-permute-start | bytes 245768 | tf_op jit(solution)/shard_map/ppermute | solution.py:467
  66.8 7.9 %collective-permute-start.20 = (f32[16,1280]{1,0:T(8,128)S(1)}, f32[16,1280]{1,0:T(8,128)S(1)}, u32[]{:S(2)}, u32[]{:S(2)}) collective-permute-start(f32[16,1280]{1,0:T(8,128)S(1)} %get-tuple-element.118), channel_id=1, source_target_pairs={{0,4},{1,17},{2,6},{3,19},{4,0},{5,21},{6,2},{7,23},{8,12},{9,25},... | collective-permute-start | bytes 245768 | tf_op jit(solution)/shard_map/ppermute | solution.py:467
  68.7 5.9 %collective-permute-start.21 = (f32[16,1280]{1,0:T(8,128)S(1)}, f32[16,1280]{1,0:T(8,128)S(1)}, u32[]{:S(2)}, u32[]{:S(2)}) collective-permute-start(f32[16,1280]{1,0:T(8,128)S(1)} %get-tuple-element.119), channel_id=1, source_target_pairs={{0,24},{1,7},{2,26},{3,5},{4,28},{5,3},{6,30},{7,1},{8,16},{9,15},... | collective-permute-start | bytes 245768 | tf_op jit(solution)/shard_map/ppermute | solution.py:467
  74.7 1.3 %collective-permute-start.22 = (f32[16,1280]{1,0:T(8,128)S(1)}, f32[16,1280]{1,0:T(8,128)S(1)}, u32[]{:S(2)}, u32[]{:S(2)}) collective-permute-start(f32[16,1280]{1,0:T(8,128)S(1)} %add_add_fusion.mine_ref), channel_id=1, source_target_pairs={{0,1},{1,0},{2,3},{3,2},{4,5},{5,4},{6,7},{7,6},{8,9},{9,8},{10,11... | collective-permute-start | bytes 245768 | tf_op jit(solution)/shard_map/ppermute | solution.py:467
  78.7 3.9 %collective-permute-start.24 = (f32[48,48]{1,0:T(8,128)S(1)}, f32[48,48]{1,0:T(8,128)S(1)}, u32[]{:S(2)}, u32[]{:S(2)}) collective-permute-start(f32[48,48]{1,0:T(8,128)S(1)} %get-tuple-element.125), channel_id=1, source_target_pairs={{0,16},{1,17},{2,18},{3,19},{4,20},{5,21},{6,22},{7,23},{8,24},{9,... | collective-permute-start | bytes 27656 | tf_op jit(solution)/shard_map/ppermute | solution.py:467
  79.4 4.7 %collective-permute-start.25 = (f32[48,48]{1,0:T(8,128)S(1)}, f32[48,48]{1,0:T(8,128)S(1)}, u32[]{:S(2)}, u32[]{:S(2)}) collective-permute-start(f32[48,48]{1,0:T(8,128)S(1)} %get-tuple-element.126), channel_id=1, source_target_pairs={{0,24},{1,25},{2,26},{3,27},{4,28},{5,29},{6,30},{7,31},{8,16},{9,... | collective-permute-start | bytes 27656 | tf_op jit(solution)/shard_map/ppermute | solution.py:467
  80.7 3.8 %collective-permute-start.23 = (f32[48,48]{1,0:T(8,128)S(1)}, f32[48,48]{1,0:T(8,128)S(1)}, u32[]{:S(2)}, u32[]{:S(2)}) collective-permute-start(f32[48,48]{1,0:T(8,128)S(1)} %get-tuple-element.124.refs_0_), channel_id=1, source_target_pairs={{0,8},{1,9},{2,10},{3,11},{4,12},{5,13},{6,14},{7,15},{8,0},{9,1},... | collective-permute-start | bytes 27656 | tf_op jit(solution)/shard_map/ppermute | solution.py:467
  84.6 4.8 %collective-permute-start.27 = (f32[48,48]{1,0:T(8,128)S(1)}, f32[48,48]{1,0:T(8,128)S(1)}, u32[]{:S(2)}, u32[]{:S(2)}) collective-permute-start(f32[48,48]{1,0:T(8,128)S(1)} %get-tuple-element.128), channel_id=1, source_target_pairs={{0,4},{1,5},{2,6},{3,7},{4,0},{5,1},{6,2},{7,3},{8,12},{9,13},{10,... | collective-permute-start | bytes 27656 | tf_op jit(solution)/shard_map/ppermute | solution.py:467
  85.5 5.7 %collective-permute-start.28 = (f32[48,48]{1,0:T(8,128)S(1)}, f32[48,48]{1,0:T(8,128)S(1)}, u32[]{:S(2)}, u32[]{:S(2)}) collective-permute-start(f32[48,48]{1,0:T(8,128)S(1)} %get-tuple-element.129), channel_id=1, source_target_pairs={{0,6},{1,7},{2,4},{3,5},{4,2},{5,3},{6,0},{7,1},{8,14},{9,15},{10,... | collective-permute-start | bytes 27656 | tf_op jit(solution)/shard_map/ppermute | solution.py:467
  87.1 4.1 %collective-permute-start.26 = (f32[48,48]{1,0:T(8,128)S(1)}, f32[48,48]{1,0:T(8,128)S(1)}, u32[]{:S(2)}, u32[]{:S(2)}) collective-permute-start(f32[48,48]{1,0:T(8,128)S(1)} %get-tuple-element.127.refs_0_), channel_id=1, source_target_pairs={{0,2},{1,3},{2,0},{3,1},{4,6},{5,7},{6,4},{7,5},{8,10},{9,11},{10,... | collective-permute-start | bytes 27656 | tf_op jit(solution)/shard_map/ppermute | solution.py:467

commit v10 on v9

--- a/solution.py
+++ b/solution.py
@@ -215,7 +215,7 @@
 
 
 def turned(s, group, even):
-    return jnp.logical_not(even) if s == group - 1 else even
+    return jnp.logical_not(even) if s >= group // 2 else even
 
 
 def early_kernel(k, n, group, tile, parts, given, new, *refs):
@@ -474,7 +474,7 @@
 
     def spread(s):
         def to(r, c):
-            along_z = (c % 2 == 0) != (s == group - 1)
+            along_z = (c % 2 == 0) != (s >= group // 2)
             return chip(r, c, 0, s) if along_z else chip(r, c, s, 0)
 
         return to

time: 94.1 us -> 93.1 us (0.989)
  starting transfers between devices: 27.2 us -> 26.2 us
    ppermute x29, starting transfers between devices: 27.2 us -> 26.2 us  [send(): return lax.ppermute(value, axes, [p for p in pairs if p[1] is not None])]
  transfers between devices with their start and end apart: 29 -> 29, of which waited for: 12 -> 14; matrix products, arithmetic and copies ran while one was open for 0% -> 0% of each run, Pallas kernels for 24% -> 24%
where the time goes in v10:
time: 93.1 us; the launch traced here: 92.9 us
  Pallas kernels  52.7 us (57%)
  starting transfers between devices  26.2 us (28%)
  waiting for transfers between devices  13.1 us (14%)
    pallas_call x18, Pallas kernels, call(): run(*[pltpu.with_memory_space_constraint(v, pltpu.HBM if i < far else plt...  52.7 us
    ppermute x29, starting transfers between devices, send(): return lax.ppermute(value, axes, [p for p in pairs if p[1] is not None])  26.2 us
    ppermute x29, waiting for transfers between devices, send(): return lax.ppermute(value, axes, [p for p in pairs if p[1] is not None])  13.1 us
  transfers between devices with their start and end apart: 29, of which 14 were waited for; matrix products, arithmetic and copies ran while one was open for 0% of the time, Pallas kernels for 24%

profile of v10, /device:TPU:0, one launch (start us, length us, event | category | flops | bytes accessed | tf_op | source)
XLA Modules:
  0.0 92.9 jit_solution(1543080557757443482)
XLA Ops:
  0.6 0.6 collective-permute-start
  1.2 2.0 %begin.1 = (f32[16,576]{1,0:T(8,128)S(1)}, f32[768,1152]{1,0:T(8,128)S(1)}) custom-call(f32[2304,4608]{1,0:T(8,128)} %bitcast.3, f32[16,576]{1,0:T(8,128)} %bitcast.8), custom_call_target="tpu_custom_call" | custom-call | flops 169869312 | bytes 1327104 | tf_op jit(solution)/shard_map/begin/pallas_call | solution.py:447
  3.2 0.0 collective-permute-done.other_ref
  3.2 0.1 order.1
  3.3 2.6 %collective-permute-start.2 = (f32[16,1152]{1,0:T(8,128)S(1)}, f32[16,1152]{1,0:T(8,128)S(1)}, u32[]{:S(2)}, u32[]{:S(2)}) collective-permute-start(f32[16,1152]{1,0:T(8,128)S(1)} %get-tuple-element.76), channel_id=1, source_target_pairs={{0,16},{1,5},{2,18},{3,7},{4,20},{5,1},{6,22},{7,3},{8,24},{9,13},... | collective-permute-start | bytes 221192 | tf_op jit(solution)/shard_map/ppermute | solution.py:467
  5.9 1.4 %collective-permute-start.3 = (f32[16,1152]{1,0:T(8,128)S(1)}, f32[16,1152]{1,0:T(8,128)S(1)}, u32[]{:S(2)}, u32[]{:S(2)}) collective-permute-start(f32[16,1152]{1,0:T(8,128)S(1)} %get-tuple-element.77), channel_id=1, source_target_pairs={{0,24},{1,7},{2,26},{3,5},{4,28},{5,3},{6,30},{7,1},{8,16},{9,15},... | collective-permute-start | bytes 221192 | tf_op jit(solution)/shard_map/ppermute | solution.py:467
  7.3 1.6 %collective-permute-start.1 = (f32[16,1152]{1,0:T(8,128)S(1)}, f32[16,1152]{1,0:T(8,128)S(1)}, u32[]{:S(2)}, u32[]{:S(2)}) collective-permute-start(f32[16,1152]{1,0:T(8,128)S(1)} %get-tuple-element.78.refs_2_.refs_3_.refs_5_.refs_9_.first_ref), channel_id=1, source_target_pairs={{0,2},{1,9},{2,0},{3,11},{4,6},{5,13},{6,4},{7,15},{8,10},{9,1},{1... | collective-permute-start | bytes 221192 | tf_op jit(solution)/shard_map/ppermute | solution.py:467
  8.9 5.1 %first_early.1 = (f32[16,2304]{1,0:T(8,128)S(1)}, f32[768,1152]{1,0:T(8,128)S(1)}, f32[768,1152]{1,0:T(8,128)S(1)}, f32[768,1152]{1,0:T(8,128)S(1)}, f32[768,1152]{1,0:T(8,128)S(1)}) custom-call(f32[2304,4608]{1,0:T(8,128)} %bitcast.4, f32[768,1152]{1,0:T(8,128)S(1)} %get-tuple-element.70.refs_1_.piece.refs_0_, ...), custom_call_target="tpu_custom_call" | custom-call | flops 1358954496 | bytes 10616832 | tf_op jit(solution)/shard_map/first_early/pallas_call | solution.py:447
  14.0 0.0 collective-permute-done.3.refs_10_
  14.0 0.0 collective-permute-done.1.refs_8_
  14.1 0.6 collective-permute-start.4
  14.7 0.1 collective-permute-start.5
  14.8 0.4 collective-permute-start.6
  15.2 3.1 %first_own.1 = (f32[16,3456]{1,0:T(8,128)S(1)}, f32[768,1152]{1,0:T(8,128)S(1)}, f32[768,1152]{1,0:T(8,128)S(1)}) custom-call(f32[2304,4608]{1,0:T(8,128)} %bitcast.5, f32[768,1152]{1,0:T(8,128)S(1)} %get-tuple-element.73.refs_1_.refs_2_.refs_0_, f32[768,1152]{1,0:T(8,128)S(1)} %get-tuple-element.74.refs_2_.refs_3_.refs_1_, ...), custom_call_target="tpu_custom_call" | custom-call | flops 679477248 | bytes 5308416 | tf_op jit(solution)/shard_map/first_own/pallas_call | solution.py:447
  18.3 0.0 collective-permute-done.4.refs_11_
  18.3 0.0 collective-permute-done.5.refs_12_
  18.4 0.0 copy-start
  18.4 13.1 %first.1 = (f32[3,16,1152]{2,1,0:T(8,128)S(1)}, f32[3,16,1152]{2,1,0:T(8,128)S(1)}, f32[16,576]{1,0:T(8,128)S(1)}, bf16[32,2304]{1,0:T(8,128)(2,1)S(1)}, bf16[32...) custom-call(f32[2304,4608]{1,0:T(8,128)} %bitcast.6, ...), custom_call_target="tpu_custom_call" | custom-call | flops 5435817984 | bytes 42467328 | tf_op jit(solution)/shard_map/first/pallas_call | solution.py:447
  31.5 0.1 collective-permute-start.7
  31.6 0.7 first_near.1.refs_7_
  32.4 0.7 collective-permute-done.7.got_ref
  33.1 0.7 collective-permute-start.8
  33.8 1.3 %collective-permute-start.9 = (f32[16,1152]{1,0:T(8,128)S(1)}, f32[16,1152]{1,0:T(8,128)S(1)}, u32[]{:S(2)}, u32[]{:S(2)}) collective-permute-start(f32[16,1152]{1,0:T(8,128)S(1)} %get-tuple-element.94), channel_id=1, source_target_pairs={{0,16},{1,5},{2,18},{3,7},{4,20},{5,1},{6,22},{7,3},{8,24},{9,13},... | collective-permute-start | bytes 221192 | tf_op jit(solution)/shard_map/ppermute | solution.py:467
  35.1 0.6 collective-permute-start.10
  35.7 3.2 %first_late.1 = f32[16,1152]{1,0:T(8,128)S(1)} custom-call(f32[768,1152]{1,0:T(8,128)S(1)} %get-tuple-element.71.refs_0_.refs_1_, f32[768,1152]{1,0:T(8,128)S(1)} %get-tuple-element.72.refs_1_.refs_2_, f32[768,1152]{1,0:T(8,128)S(1)} %get-tuple-element.73.refs_1_.refs_2_.refs_0_, f32[768,1152]{1,0:T(8,128)S(1)} %get-tuple-element.74.refs_2_.refs_3_.refs_1_, ...), custom_call_target="tpu_custom_call" | custom-call | flops 2038431744 | bytes 15925248 | tf_op jit(solution)/shard_map/first_late/pallas_call | solution.py:447
  38.9 0.0 collective-permute-done.8
  39.0 1.4 %collective-permute-done.10 = f32[16,1152]{1,0:T(8,128)S(1)} collective-permute-done((f32[16,1152]{1,0:T(8,128)S(1)}, f32[16,1152]{1,0:T(8,128)S(1)}, u32[]{:S(2)}, u32[]{:S(2)}) %collective-permute-start.10) | collective-permute-done | bytes 73760 | tf_op jit(solution)/shard_map/ppermute | solution.py:467
  40.4 0.3 collective-permute-start.11
  40.7 1.0 %collective-permute-done.11.got_ref = f32[16,1152]{1,0:T(8,128)S(1)} collective-permute-done((f32[16,1152]{1,0:T(8,128)S(1)}, f32[16,1152]{1,0:T(8,128)S(1)}, u32[]{:S(2)}, u32[]{:S(2)}) %collective-permute-start.11) | collective-permute-done | bytes 73760 | tf_op jit(solution)/shard_map/ppermute | solution.py:467
  41.7 0.4 pair.1
  42.1 1.4 %collective-permute-start.13 = (f32[16,1280]{1,0:T(8,128)S(1)}, f32[16,1280]{1,0:T(8,128)S(1)}, u32[]{:S(2)}, u32[]{:S(2)}) collective-permute-start(f32[16,1280]{1,0:T(8,128)S(1)} %get-tuple-element.102), channel_id=1, source_target_pairs={{0,16},{1,5},{2,18},{3,7},{4,20},{5,1},{6,22},{7,3},{8,24},{9,13},... | collective-permute-start | bytes 245768 | tf_op jit(solution)/shard_map/ppermute | solution.py:467
  43.5 1.4 %collective-permute-start.14 = (f32[16,1280]{1,0:T(8,128)S(1)}, f32[16,1280]{1,0:T(8,128)S(1)}, u32[]{:S(2)}, u32[]{:S(2)}) collective-permute-start(f32[16,1280]{1,0:T(8,128)S(1)} %get-tuple-element.103), channel_id=1, source_target_pairs={{0,24},{1,7},{2,26},{3,5},{4,28},{5,3},{6,30},{7,1},{8,16},{9,15},... | collective-permute-start | bytes 245768 | tf_op jit(solution)/shard_map/ppermute | solution.py:467
  45.0 0.7 collective-permute-start.12
  45.7 3.0 %second_early.1.refs_10_ = f32[16,2304]{1,0:T(8,128)S(1)} custom-call(f32[768,1152]{1,0:T(8,128)S(1)} %get-tuple-element.70.refs_1_.piece.refs_0_, f32[768,1152]{1,0:T(8,128)S(1)} %get-tuple-element.71.refs_0_.refs_1_, f32[768,1152]{1,0:T(8,128)S(1)} %get-tuple-element.72.refs_1_.refs_2_, f32[16,1280]{1,0:T(8,128)S(1)} %get-tuple-element.105.refs_3_.refs_9_.refs_0_.pair_ref), custom_call_target="tpu_custom_call" | custom-call | flops 1358954496 | bytes 10616832 | tf_op jit(solution)/shard_map/second_early/pallas_call | solution.py:447
  48.7 0.9 collective-permute-done.14.refs_14_.refs_3_
  49.6 0.7 collective-permute-done.12.refs_12_.refs_1_
  50.3 0.5 collective-permute-start.16
  50.8 0.0 collective-permute-start.17
  50.8 1.5 %second_own.1.refs_11_ = f32[16,3456]{1,0:T(8,128)S(1)} custom-call(f32[768,1152]{1,0:T(8,128)S(1)} %get-tuple-element.73.refs_1_.refs_2_.refs_0_, f32[768,1152]{1,0:T(8,128)S(1)} %get-tuple-element.74.refs_2_.refs_3_.refs_1_, f32[768,1152]{1,0:T(8,128)S(1)} %get-tuple-element.79.refs_3_.refs_4_.refs_2_, ...), custom_call_target="tpu_custom_call" | custom-call | flops 679477248 | bytes 5308416 | tf_op jit(solution)/shard_map/second_own/pallas_call | solution.py:447
  52.2 0.0 collective-permute-done.16.refs_16_.refs_5_
  52.3 10.9 %second.1 = (f32[3,16,1152]{2,1,0:T(8,128)S(1)}, f32[3,16,1152]{2,1,0:T(8,128)S(1)}, f32[16,576]{1,0:T(8,128)S(1)}, bf16[32,2304]{1,0:T(8,128)(2,1)S(1)}, bf16[32,3456]{1,0:T(8,128)(2,1)S(1)}) custom-call(f32[768,1152]{1,0:T(8,128)S(1)} %get-tuple-element.73.refs_1_.refs_2_.refs_0_, f32[768,1152]{1,0:T(8,128)S(1)} %get-tuple-element.74.refs_2_.refs_3_.refs_1_, ...), custom_call_target="tpu_custom_call" | custom-call | flops 5435817984 | bytes 42467328 | tf_op jit(solution)/shard_map/second/pallas_call | solution.py:447
  63.2 0.6 collective-permute-start.18
  63.8 0.7 second_near.1.refs_7_
  64.5 0.4 collective-permute-done.18.got_ref
  64.9 0.1 collective-permute-start.19
  65.0 1.5 %collective-permute-start.20 = (f32[16,1280]{1,0:T(8,128)S(1)}, f32[16,1280]{1,0:T(8,128)S(1)}, u32[]{:S(2)}, u32[]{:S(2)}) collective-permute-start(f32[16,1280]{1,0:T(8,128)S(1)} %get-tuple-element.118), channel_id=1, source_target_pairs={{0,16},{1,5},{2,18},{3,7},{4,20},{5,1},{6,22},{7,3},{8,24},{9,13},... | collective-permute-start | bytes 245768 | tf_op jit(solution)/shard_map/ppermute | solution.py:467
  66.4 1.3 %collective-permute-start.21 = (f32[16,1280]{1,0:T(8,128)S(1)}, f32[16,1280]{1,0:T(8,128)S(1)}, u32[]{:S(2)}, u32[]{:S(2)}) collective-permute-start(f32[16,1280]{1,0:T(8,128)S(1)} %get-tuple-element.119), channel_id=1, source_target_pairs={{0,24},{1,7},{2,26},{3,5},{4,28},{5,3},{6,30},{7,1},{8,16},{9,15},... | collective-permute-start | bytes 245768 | tf_op jit(solution)/shard_map/ppermute | solution.py:467
  67.7 3.3 %second_late.1 = f32[16,1280]{1,0:T(8,128)S(1)} custom-call(f32[768,1152]{1,0:T(8,128)S(1)} %get-tuple-element.71.refs_0_.refs_1_, f32[768,1152]{1,0:T(8,128)S(1)} %get-tuple-element.72.refs_1_.refs_2_, f32[768,1152]{1,0:T(8,128)S(1)} %get-tuple-element.73.refs_1_.refs_2_.refs_0_, f32[768,1152]{1,0:T(8,128)S(1)} %get-tuple-element.74.refs_2_.refs_3_.refs_1_, ...), custom_call_target="tpu_custom_call" | custom-call | flops 2038431744 | bytes 15925248 | tf_op jit(solution)/shard_map/second_late/pallas_call | solution.py:447
  71.0 0.7 collective-permute-done.21
  71.8 0.5 collective-permute-start.22
  72.3 0.9 collective-permute-done.22.got_ref
  73.3 2.6 %middle.1 = (f32[16,1152]{1,0:T(8,128)S(1)}, f32[16,1152]{1,0:T(8,128)S(1)}, f32[16,16]{1,0:T(8,128)S(1)}, f32[16,16]{1,0:T(8,128)S(1)}, f32[48,48]{1,0:T(8,128)...) custom-call(f32[16,1152]{1,0:T(8,128)S(1)} %get-tuple-element.78.refs_2_.refs_3_.refs_5_.refs_9_.first_ref, ...), custom_call_target="tpu_custom_call" | custom-call | tf_op jit(solution)/shard_map/middle/pallas_call | solution.py:447
  75.9 0.7 collective-permute-start.24
  76.6 1.5 %collective-permute-start.25 = (f32[48,48]{1,0:T(8,128)S(1)}, f32[48,48]{1,0:T(8,128)S(1)}, u32[]{:S(2)}, u32[]{:S(2)}) collective-permute-start(f32[48,48]{1,0:T(8,128)S(1)} %get-tuple-element.126), channel_id=1, source_target_pairs={{0,24},{1,25},{2,26},{3,27},{4,28},{5,29},{6,30},{7,31},{8,16},{9,... | collective-permute-start | bytes 27656 | tf_op jit(solution)/shard_map/ppermute | solution.py:467
  78.1 1.4 %collective-permute-start.23 = (f32[48,48]{1,0:T(8,128)S(1)}, f32[48,48]{1,0:T(8,128)S(1)}, u32[]{:S(2)}, u32[]{:S(2)}) collective-permute-start(f32[48,48]{1,0:T(8,128)S(1)} %get-tuple-element.124.refs_0_), channel_id=1, source_target_pairs={{0,8},{1,9},{2,10},{3,11},{4,12},{5,13},{6,14},{7,15},{8,0},{9,1},... | collective-permute-start | bytes 27656 | tf_op jit(solution)/shard_map/ppermute | solution.py:467
  79.5 0.3 collective-permute-done.24.refs_2_
  79.8 1.5 %collective-permute-done.25.refs_3_ = f32[48,48]{1,0:T(8,128)S(1)} collective-permute-done((f32[48,48]{1,0:T(8,128)S(1)}, f32[48,48]{1,0:T(8,128)S(1)}, u32[]{:S(2)}, u32[]{:S(2)}) %collective-permute-start.25) | collective-permute-done | bytes 9248 | tf_op jit(solution)/shard_map/ppermute | solution.py:467
  81.3 0.6 collective-permute-done.23.refs_1_
  81.9 2.3 %collective-permute-start.27 = (f32[48,48]{1,0:T(8,128)S(1)}, f32[48,48]{1,0:T(8,128)S(1)}, u32[]{:S(2)}, u32[]{:S(2)}) collective-permute-start(f32[48,48]{1,0:T(8,128)S(1)} %get-tuple-element.128), channel_id=1, source_target_pairs={{0,4},{1,5},{2,6},{3,7},{4,0},{5,1},{6,2},{7,3},{8,12},{9,13},{10,... | collective-permute-start | bytes 27656 | tf_op jit(solution)/shard_map/ppermute | solution.py:467
  84.2 1.9 %collective-permute-start.28 = (f32[48,48]{1,0:T(8,128)S(1)}, f32[48,48]{1,0:T(8,128)S(1)}, u32[]{:S(2)}, u32[]{:S(2)}) collective-permute-start(f32[48,48]{1,0:T(8,128)S(1)} %get-tuple-element.129), channel_id=1, source_target_pairs={{0,6},{1,7},{2,4},{3,5},{4,2},{5,3},{6,0},{7,1},{8,14},{9,15},{10,... | collective-permute-start | bytes 27656 | tf_op jit(solution)/shard_map/ppermute | solution.py:467
  86.1 0.6 collective-permute-done.27.refs_2_
  86.7 3.1 %collective-permute-done.28.refs_3_ = f32[48,48]{1,0:T(8,128)S(1)} collective-permute-done((f32[48,48]{1,0:T(8,128)S(1)}, f32[48,48]{1,0:T(8,128)S(1)}, u32[]{:S(2)}, u32[]{:S(2)}) %collective-permute-start.28) | collective-permute-done | bytes 9248 | tf_op jit(solution)/shard_map/ppermute | solution.py:467
  89.9 0.2 collective-permute-done.26.refs_1_
  90.1 2.8 %last.1 = (f32[16,576]{1,0:T(8,128)}, f32[2,16,16]{2,1,0:T(8,128)}, f32[2,16,16]{2,1,0:T(8,128)}) custom-call(f32[16,1152]{1,0:T(8,128)S(1)} %get-tuple-element.78.refs_2_.refs_3_.refs_5_.refs_9_.first_ref, f32[16,1152]{1,0:T(8,128)S(1)} %get-tuple-element.120.q_ref, f32[16,1152]{1,0:T(8,128)S(1)} %get-tuple-element.121.prod_ref, ...), custom_call_target="tpu_custom_call" | custom-call | tf_op jit(solution)/shard_map/last/pallas_call | solution.py:447
  (17 shorter events, 0.1 us)
Async XLA Ops:
  0.6 2.6 %collective-permute-start = (f32[16,576]{1,0:T(8,128)}, f32[16,576]{1,0:T(8,128)S(1)}, u32[]{:S(2)}, u32[]{:S(2)}) collective-permute-start(f32[16,576]{1,0:T(8,128)} %bitcast.7), channel_id=1, source_target_pairs={{0,1},{1,0},{2,3},{3,2},{4,5},{5,4},{6,7},{7,6},{8,9},{9,8},{10,11... | collective-permute-start | bytes 110600 | tf_op jit(solution)/shard_map/ppermute | solution.py:467
  3.3 10.7 %collective-permute-start.2 = (f32[16,1152]{1,0:T(8,128)S(1)}, f32[16,1152]{1,0:T(8,128)S(1)}, u32[]{:S(2)}, u32[]{:S(2)}) collective-permute-start(f32[16,1152]{1,0:T(8,128)S(1)} %get-tuple-element.76), channel_id=1, source_target_pairs={{0,16},{1,5},{2,18},{3,7},{4,20},{5,1},{6,22},{7,3},{8,24},{9,13},... | collective-permute-start | bytes 221192 | tf_op jit(solution)/shard_map/ppermute | solution.py:467
  5.9 8.1 %collective-permute-start.3 = (f32[16,1152]{1,0:T(8,128)S(1)}, f32[16,1152]{1,0:T(8,128)S(1)}, u32[]{:S(2)}, u32[]{:S(2)}) collective-permute-start(f32[16,1152]{1,0:T(8,128)S(1)} %get-tuple-element.77), channel_id=1, source_target_pairs={{0,24},{1,7},{2,26},{3,5},{4,28},{5,3},{6,30},{7,1},{8,16},{9,15},... | collective-permute-start | bytes 221192 | tf_op jit(solution)/shard_map/ppermute | solution.py:467
  7.3 6.7 %collective-permute-start.1 = (f32[16,1152]{1,0:T(8,128)S(1)}, f32[16,1152]{1,0:T(8,128)S(1)}, u32[]{:S(2)}, u32[]{:S(2)}) collective-permute-start(f32[16,1152]{1,0:T(8,128)S(1)} %get-tuple-element.78.refs_2_.refs_3_.refs_5_.refs_9_.first_ref), channel_id=1, source_target_pairs={{0,2},{1,9},{2,0},{3,11},{4,6},{5,13},{6,4},{7,15},{8,10},{9,1},{1... | collective-permute-start | bytes 221192 | tf_op jit(solution)/shard_map/ppermute | solution.py:467
  14.1 4.3 %collective-permute-start.4 = (f32[16,1152]{1,0:T(8,128)S(1)}, f32[16,1152]{1,0:T(8,128)S(1)}, u32[]{:S(2)}, u32[]{:S(2)}) collective-permute-start(f32[16,1152]{1,0:T(8,128)S(1)} %collective-permute-done.1.refs_8_), channel_id=1, source_target_pairs={{0,1},{1,0},{2,3},{3,2},{4,5},{5,4},{6,7},{7,6},{8,9},{9,8},{10,11... | collective-permute-start | bytes 221192 | tf_op jit(solution)/shard_map/ppermute | solution.py:467
  14.7 3.7 %collective-permute-start.5 = (f32[16,1152]{1,0:T(8,128)S(1)}, f32[16,1152]{1,0:T(8,128)S(1)}, u32[]{:S(2)}, u32[]{:S(2)}) collective-permute-start(f32[16,1152]{1,0:T(8,128)S(1)} %collective-permute-done.2.refs_9_), channel_id=1, source_target_pairs={{0,1},{1,0},{2,3},{3,2},{4,5},{5,4},{6,7},{7,6},{8,9},{9,8},{10,11... | collective-permute-start | bytes 221192 | tf_op jit(solution)/shard_map/ppermute | solution.py:467
  14.8 3.6 %collective-permute-start.6 = (f32[16,1152]{1,0:T(8,128)S(1)}, f32[16,1152]{1,0:T(8,128)S(1)}, u32[]{:S(2)}, u32[]{:S(2)}) collective-permute-start(f32[16,1152]{1,0:T(8,128)S(1)} %collective-permute-done.3.refs_10_), channel_id=1, source_target_pairs={{0,1},{1,0},{2,3},{3,2},{4,5},{5,4},{6,7},{7,6},{8,9},{9,8},{10,11... | collective-permute-start | bytes 221192 | tf_op jit(solution)/shard_map/ppermute | solution.py:467
  18.4 13.3 %copy-start = (f32[576]{0:T(1024)S(1)}, f32[576]{0:T(1024)}, u32[]{:S(2)}) copy-start(f32[576]{0:T(1024)} %param.4) | copy-start | bytes 6916
  31.5 1.5 %collective-permute-start.7 = (f32[3,16,1152]{2,1,0:T(8,128)S(1)}, f32[3,16,1152]{2,1,0:T(8,128)S(1)}, u32[]{:S(2)}, u32[]{:S(2)}) collective-permute-start(f32[3,16,1152]{2,1,0:T(8,128)S(1)} %get-tuple-element.88), channel_id=1, source_target_pairs={{0,1},{1,0},{2,3},{3,2},{4,5},{5,4},{6,7},{7,6},{8,9},{9,8},{10,11... | collective-permute-start | bytes 663560 | tf_op jit(solution)/shard_map/ppermute | solution.py:467
  33.1 5.9 %collective-permute-start.8 = (f32[16,1152]{1,0:T(8,128)S(1)}, f32[16,1152]{1,0:T(8,128)S(1)}, u32[]{:S(2)}, u32[]{:S(2)}) collective-permute-start(f32[16,1152]{1,0:T(8,128)S(1)} %get-tuple-element.93), channel_id=1, source_target_pairs={{0,2},{1,9},{2,0},{3,11},{4,6},{5,13},{6,4},{7,15},{8,10},{9,1},{1... | collective-permute-start | bytes 221192 | tf_op jit(solution)/shard_map/ppermute | solution.py:467
  33.8 5.2 %collective-permute-start.9 = (f32[16,1152]{1,0:T(8,128)S(1)}, f32[16,1152]{1,0:T(8,128)S(1)}, u32[]{:S(2)}, u32[]{:S(2)}) collective-permute-start(f32[16,1152]{1,0:T(8,128)S(1)} %get-tuple-element.94), channel_id=1, source_target_pairs={{0,16},{1,5},{2,18},{3,7},{4,20},{5,1},{6,22},{7,3},{8,24},{9,13},... | collective-permute-start | bytes 221192 | tf_op jit(solution)/shard_map/ppermute | solution.py:467
  35.1 5.3 %collective-permute-start.10 = (f32[16,1152]{1,0:T(8,128)S(1)}, f32[16,1152]{1,0:T(8,128)S(1)}, u32[]{:S(2)}, u32[]{:S(2)}) collective-permute-start(f32[16,1152]{1,0:T(8,128)S(1)} %get-tuple-element.95), channel_id=1, source_target_pairs={{0,24},{1,7},{2,26},{3,5},{4,28},{5,3},{6,30},{7,1},{8,16},{9,15},... | collective-permute-start | bytes 221192 | tf_op jit(solution)/shard_map/ppermute | solution.py:467
  40.4 1.3 %collective-permute-start.11 = (f32[16,1152]{1,0:T(8,128)S(1)}, f32[16,1152]{1,0:T(8,128)S(1)}, u32[]{:S(2)}, u32[]{:S(2)}) collective-permute-start(f32[16,1152]{1,0:T(8,128)S(1)} %add_add_fusion.1.mine_ref), channel_id=1, source_target_pairs={{0,1},{1,0},{2,3},{3,2},{4,5},{5,4},{6,7},{7,6},{8,9},{9,8},{10,11... | collective-permute-start | bytes 221192 | tf_op jit(solution)/shard_map/ppermute | solution.py:467
  42.1 6.6 %collective-permute-start.13 = (f32[16,1280]{1,0:T(8,128)S(1)}, f32[16,1280]{1,0:T(8,128)S(1)}, u32[]{:S(2)}, u32[]{:S(2)}) collective-permute-start(f32[16,1280]{1,0:T(8,128)S(1)} %get-tuple-element.102), channel_id=1, source_target_pairs={{0,16},{1,5},{2,18},{3,7},{4,20},{5,1},{6,22},{7,3},{8,24},{9,13},... | collective-permute-start | bytes 245768 | tf_op jit(solution)/shard_map/ppermute | solution.py:467
  43.5 6.1 %collective-permute-start.14 = (f32[16,1280]{1,0:T(8,128)S(1)}, f32[16,1280]{1,0:T(8,128)S(1)}, u32[]{:S(2)}, u32[]{:S(2)}) collective-permute-start(f32[16,1280]{1,0:T(8,128)S(1)} %get-tuple-element.103), channel_id=1, source_target_pairs={{0,24},{1,7},{2,26},{3,5},{4,28},{5,3},{6,30},{7,1},{8,16},{9,15},... | collective-permute-start | bytes 245768 | tf_op jit(solution)/shard_map/ppermute | solution.py:467
  45.0 5.3 %collective-permute-start.12 = (f32[16,1280]{1,0:T(8,128)S(1)}, f32[16,1280]{1,0:T(8,128)S(1)}, u32[]{:S(2)}, u32[]{:S(2)}) collective-permute-start(f32[16,1280]{1,0:T(8,128)S(1)} %get-tuple-element.105.refs_3_.refs_9_.refs_0_.pair_ref), channel_id=1, source_target_pairs={{0,2},{1,9},{2,0},{3,11},{4,6},{5,13},{6,4},{7,15},{8,10},{9,1},{1... | collective-permute-start | bytes 245768 | tf_op jit(solution)/shard_map/ppermute | solution.py:467
  50.3 2.0 %collective-permute-start.15 = (f32[16,1280]{1,0:T(8,128)S(1)}, f32[16,1280]{1,0:T(8,128)S(1)}, u32[]{:S(2)}, u32[]{:S(2)}) collective-permute-start(f32[16,1280]{1,0:T(8,128)S(1)} %collective-permute-done.12.refs_12_.refs_1_), channel_id=1, source_target_pairs={{0,1},{1,0},{2,3},{3,2},{4,5},{5,4},{6,7},{7,6},{8,9},{9,8},{10,11... | collective-permute-start | bytes 245768 | tf_op jit(solution)/shard_map/ppermute | solution.py:467
  50.3 2.0 %collective-permute-start.16 = (f32[16,1280]{1,0:T(8,128)S(1)}, f32[16,1280]{1,0:T(8,128)S(1)}, u32[]{:S(2)}, u32[]{:S(2)}) collective-permute-start(f32[16,1280]{1,0:T(8,128)S(1)} %collective-permute-done.13.refs_13_.refs_2_), channel_id=1, source_target_pairs={{0,1},{1,0},{2,3},{3,2},{4,5},{5,4},{6,7},{7,6},{8,9},{9,8},{10,11... | collective-permute-start | bytes 245768 | tf_op jit(solution)/shard_map/ppermute | solution.py:467
  50.8 1.5 %collective-permute-start.17 = (f32[16,1280]{1,0:T(8,128)S(1)}, f32[16,1280]{1,0:T(8,128)S(1)}, u32[]{:S(2)}, u32[]{:S(2)}) collective-permute-start(f32[16,1280]{1,0:T(8,128)S(1)} %collective-permute-done.14.refs_14_.refs_3_), channel_id=1, source_target_pairs={{0,1},{1,0},{2,3},{3,2},{4,5},{5,4},{6,7},{7,6},{8,9},{9,8},{10,11... | collective-permute-start | bytes 245768 | tf_op jit(solution)/shard_map/ppermute | solution.py:467
  63.2 1.7 %collective-permute-start.18 = (f32[3,16,1152]{2,1,0:T(8,128)S(1)}, f32[3,16,1152]{2,1,0:T(8,128)S(1)}, u32[]{:S(2)}, u32[]{:S(2)}) collective-permute-start(f32[3,16,1152]{2,1,0:T(8,128)S(1)} %get-tuple-element.111), channel_id=1, source_target_pairs={{0,1},{1,0},{2,3},{3,2},{4,5},{5,4},{6,7},{7,6},{8,9},{9,8},{10,11... | collective-permute-start | bytes 663560 | tf_op jit(solution)/shard_map/ppermute | solution.py:467
  64.9 6.1 %collective-permute-start.19 = (f32[16,1280]{1,0:T(8,128)S(1)}, f32[16,1280]{1,0:T(8,128)S(1)}, u32[]{:S(2)}, u32[]{:S(2)}) collective-permute-start(f32[16,1280]{1,0:T(8,128)S(1)} %get-tuple-element.117), channel_id=1, source_target_pairs={{0,2},{1,9},{2,0},{3,11},{4,6},{5,13},{6,4},{7,15},{8,10},{9,1},{1... | collective-permute-start | bytes 245768 | tf_op jit(solution)/shard_map/ppermute | solution.py:467
  65.0 6.1 %collective-permute-start.20 = (f32[16,1280]{1,0:T(8,128)S(1)}, f32[16,1280]{1,0:T(8,128)S(1)}, u32[]{:S(2)}, u32[]{:S(2)}) collective-permute-start(f32[16,1280]{1,0:T(8,128)S(1)} %get-tuple-element.118), channel_id=1, source_target_pairs={{0,16},{1,5},{2,18},{3,7},{4,20},{5,1},{6,22},{7,3},{8,24},{9,13},... | collective-permute-start | bytes 245768 | tf_op jit(solution)/shard_map/ppermute | solution.py:467
  66.4 5.3 %collective-permute-start.21 = (f32[16,1280]{1,0:T(8,128)S(1)}, f32[16,1280]{1,0:T(8,128)S(1)}, u32[]{:S(2)}, u32[]{:S(2)}) collective-permute-start(f32[16,1280]{1,0:T(8,128)S(1)} %get-tuple-element.119), channel_id=1, source_target_pairs={{0,24},{1,7},{2,26},{3,5},{4,28},{5,3},{6,30},{7,1},{8,16},{9,15},... | collective-permute-start | bytes 245768 | tf_op jit(solution)/shard_map/ppermute | solution.py:467
  71.8 1.5 %collective-permute-start.22 = (f32[16,1280]{1,0:T(8,128)S(1)}, f32[16,1280]{1,0:T(8,128)S(1)}, u32[]{:S(2)}, u32[]{:S(2)}) collective-permute-start(f32[16,1280]{1,0:T(8,128)S(1)} %add_add_fusion.mine_ref), channel_id=1, source_target_pairs={{0,1},{1,0},{2,3},{3,2},{4,5},{5,4},{6,7},{7,6},{8,9},{9,8},{10,11... | collective-permute-start | bytes 245768 | tf_op jit(solution)/shard_map/ppermute | solution.py:467
  75.9 3.9 %collective-permute-start.24 = (f32[48,48]{1,0:T(8,128)S(1)}, f32[48,48]{1,0:T(8,128)S(1)}, u32[]{:S(2)}, u32[]{:S(2)}) collective-permute-start(f32[48,48]{1,0:T(8,128)S(1)} %get-tuple-element.125), channel_id=1, source_target_pairs={{0,16},{1,17},{2,18},{3,19},{4,20},{5,21},{6,22},{7,23},{8,24},{9,... | collective-permute-start | bytes 27656 | tf_op jit(solution)/shard_map/ppermute | solution.py:467
  76.6 4.7 %collective-permute-start.25 = (f32[48,48]{1,0:T(8,128)S(1)}, f32[48,48]{1,0:T(8,128)S(1)}, u32[]{:S(2)}, u32[]{:S(2)}) collective-permute-start(f32[48,48]{1,0:T(8,128)S(1)} %get-tuple-element.126), channel_id=1, source_target_pairs={{0,24},{1,25},{2,26},{3,27},{4,28},{5,29},{6,30},{7,31},{8,16},{9,... | collective-permute-start | bytes 27656 | tf_op jit(solution)/shard_map/ppermute | solution.py:467
  78.1 3.8 %collective-permute-start.23 = (f32[48,48]{1,0:T(8,128)S(1)}, f32[48,48]{1,0:T(8,128)S(1)}, u32[]{:S(2)}, u32[]{:S(2)}) collective-permute-start(f32[48,48]{1,0:T(8,128)S(1)} %get-tuple-element.124.refs_0_), channel_id=1, source_target_pairs={{0,8},{1,9},{2,10},{3,11},{4,12},{5,13},{6,14},{7,15},{8,0},{9,1},... | collective-permute-start | bytes 27656 | tf_op jit(solution)/shard_map/ppermute | solution.py:467
  81.9 4.8 %collective-permute-start.27 = (f32[48,48]{1,0:T(8,128)S(1)}, f32[48,48]{1,0:T(8,128)S(1)}, u32[]{:S(2)}, u32[]{:S(2)}) collective-permute-start(f32[48,48]{1,0:T(8,128)S(1)} %get-tuple-element.128), channel_id=1, source_target_pairs={{0,4},{1,5},{2,6},{3,7},{4,0},{5,1},{6,2},{7,3},{8,12},{9,13},{10,... | collective-permute-start | bytes 27656 | tf_op jit(solution)/shard_map/ppermute | solution.py:467
  84.2 5.6 %collective-permute-start.28 = (f32[48,48]{1,0:T(8,128)S(1)}, f32[48,48]{1,0:T(8,128)S(1)}, u32[]{:S(2)}, u32[]{:S(2)}) collective-permute-start(f32[48,48]{1,0:T(8,128)S(1)} %get-tuple-element.129), channel_id=1, source_target_pairs={{0,6},{1,7},{2,4},{3,5},{4,2},{5,3},{6,0},{7,1},{8,14},{9,15},{10,... | collective-permute-start | bytes 27656 | tf_op jit(solution)/shard_map/ppermute | solution.py:467
  86.1 4.0 %collective-permute-start.26 = (f32[48,48]{1,0:T(8,128)S(1)}, f32[48,48]{1,0:T(8,128)S(1)}, u32[]{:S(2)}, u32[]{:S(2)}) collective-permute-start(f32[48,48]{1,0:T(8,128)S(1)} %get-tuple-element.127.refs_0_), channel_id=1, source_target_pairs={{0,2},{1,3},{2,0},{3,1},{4,6},{5,7},{6,4},{7,5},{8,10},{9,11},{10,... | collective-permute-start | bytes 27656 | tf_op jit(solution)/shard_map/ppermute | solution.py:467

commit v11 on v10

--- a/solution.py
+++ b/solution.py
@@ -528,7 +528,7 @@
         (u0,) = matrix_call(
             early_kernel,
             range(parts),
-            parts + 2,
+            parts + 3,
             [shape(k, rows)],
             [pair],
             [pltpu.VMEM((2 * k, 2 * n), BF16)],

time: 93.1 us -> 92.9 us (level)
  no operation moved by 1% of the time
where the time goes in v11:
time: 92.9 us; the launch traced here: 92.8 us
  Pallas kernels  52.5 us (57%)
  starting transfers between devices  26.4 us (28%)
  waiting for transfers between devices  12.9 us (14%)
    pallas_call x18, Pallas kernels, call(): run(*[pltpu.with_memory_space_constraint(v, pltpu.HBM if i < far else plt...  52.5 us
    ppermute x29, starting transfers between devices, send(): return lax.ppermute(value, axes, [p for p in pairs if p[1] is not None])  26.4 us
    ppermute x29, waiting for transfers between devices, send(): return lax.ppermute(value, axes, [p for p in pairs if p[1] is not None])  12.9 us
  transfers between devices with their start and end apart: 29, of which 14 were waited for; matrix products, arithmetic and copies ran while one was open for 0% of the time, Pallas kernels for 24%

profile of v11, /device:TPU:0, one launch (start us, length us, event | category | flops | bytes accessed | tf_op | source)
XLA Modules:
  0.0 92.8 jit_solution(17680113168197419642)
XLA Ops:
  0.6 0.6 collective-permute-start
  1.2 2.0 %begin.1 = (f32[16,576]{1,0:T(8,128)S(1)}, f32[768,1152]{1,0:T(8,128)S(1)}) custom-call(f32[2304,4608]{1,0:T(8,128)} %bitcast.3, f32[16,576]{1,0:T(8,128)} %bitcast.8), custom_call_target="tpu_custom_call" | custom-call | flops 169869312 | bytes 1327104 | tf_op jit(solution)/shard_map/begin/pallas_call | solution.py:447
  3.2 0.0 collective-permute-done.other_ref
  3.2 0.1 order.1
  3.3 2.6 %collective-permute-start.2 = (f32[16,1152]{1,0:T(8,128)S(1)}, f32[16,1152]{1,0:T(8,128)S(1)}, u32[]{:S(2)}, u32[]{:S(2)}) collective-permute-start(f32[16,1152]{1,0:T(8,128)S(1)} %get-tuple-element.77), channel_id=1, source_target_pairs={{0,16},{1,5},{2,18},{3,7},{4,20},{5,1},{6,22},{7,3},{8,24},{9,13},... | collective-permute-start | bytes 221192 | tf_op jit(solution)/shard_map/ppermute | solution.py:467
  5.9 1.4 %collective-permute-start.3 = (f32[16,1152]{1,0:T(8,128)S(1)}, f32[16,1152]{1,0:T(8,128)S(1)}, u32[]{:S(2)}, u32[]{:S(2)}) collective-permute-start(f32[16,1152]{1,0:T(8,128)S(1)} %get-tuple-element.78), channel_id=1, source_target_pairs={{0,24},{1,7},{2,26},{3,5},{4,28},{5,3},{6,30},{7,1},{8,16},{9,15},... | collective-permute-start | bytes 221192 | tf_op jit(solution)/shard_map/ppermute | solution.py:467
  7.3 1.6 %collective-permute-start.1 = (f32[16,1152]{1,0:T(8,128)S(1)}, f32[16,1152]{1,0:T(8,128)S(1)}, u32[]{:S(2)}, u32[]{:S(2)}) collective-permute-start(f32[16,1152]{1,0:T(8,128)S(1)} %get-tuple-element.79.refs_2_.refs_4_.refs_5_.refs_9_.first_ref), channel_id=1, source_target_pairs={{0,2},{1,9},{2,0},{3,11},{4,6},{5,13},{6,4},{7,15},{8,10},{9,1},{1... | collective-permute-start | bytes 221192 | tf_op jit(solution)/shard_map/ppermute | solution.py:467
  8.9 6.1 %first_early.1 = (f32[16,2304]{1,0:T(8,128)S(1)}, f32[768,1152]{1,0:T(8,128)S(1)}, f32[768,1152]{1,0:T(8,128)S(1)}, f32[768,1152]{1,0:T(8,128)S(1)}, f32[768,1152]{1,0:T(8,128)S(1)}, /*index=5*/f32[768,1152]{1,0:T(8,128)S(1)}) custom-call(f32[2304,4608]{1,0:T(8,128)} %bitcast.4, f32[768,1152]{1,0:T(8,128)S(1)} %get-tuple-element.70.refs_1_.piece.refs_0_, ...), custom_call_target="tpu_custom_call" | custom-call | flops 1358954496 | bytes 10616832 | tf_op jit(solution)/shard_map/first_early/pallas_call | solution.py:447
  15.1 0.0 collective-permute-done.2.refs_9_
  15.1 0.6 collective-permute-start.4
  15.7 0.1 collective-permute-start.5
  15.8 0.4 collective-permute-start.6
  16.2 2.1 %first_own.1 = (f32[16,3456]{1,0:T(8,128)S(1)}, f32[768,1152]{1,0:T(8,128)S(1)}) custom-call(f32[2304,4608]{1,0:T(8,128)} %bitcast.5, f32[768,1152]{1,0:T(8,128)S(1)} %get-tuple-element.73.refs_1_.refs_2_.refs_0_, f32[768,1152]{1,0:T(8,128)S(1)} %get-tuple-element.74.refs_2_.refs_3_.refs_1_, f32[768,1152]{1,0:T(8,128)S(1)} %get-tuple-element.75.refs_3_.refs_4_.refs_2_, ...), custom_call_target="tpu_custom_call" | custom-call | flops 679477248 | bytes 5308416 | tf_op jit(solution)/shard_map/first_own/pallas_call | solution.py:447
  18.3 0.0 collective-permute-done.5.refs_12_
  18.3 0.0 collective-permute-done.6.refs_13_
  18.3 0.0 copy-start
  18.3 13.1 %first.1 = (f32[3,16,1152]{2,1,0:T(8,128)S(1)}, f32[3,16,1152]{2,1,0:T(8,128)S(1)}, f32[16,576]{1,0:T(8,128)S(1)}, bf16[32,2304]{1,0:T(8,128)(2,1)S(1)}, bf16[32...) custom-call(f32[2304,4608]{1,0:T(8,128)} %bitcast.6, ...), custom_call_target="tpu_custom_call" | custom-call | flops 5435817984 | bytes 42467328 | tf_op jit(solution)/shard_map/first/pallas_call | solution.py:447
  31.4 0.1 collective-permute-start.7
  31.5 0.7 first_near.1.refs_7_
  32.3 0.7 collective-permute-done.7.got_ref
  33.0 0.9 collective-permute-start.8
  33.8 1.2 %collective-permute-start.9 = (f32[16,1152]{1,0:T(8,128)S(1)}, f32[16,1152]{1,0:T(8,128)S(1)}, u32[]{:S(2)}, u32[]{:S(2)}) collective-permute-start(f32[16,1152]{1,0:T(8,128)S(1)} %get-tuple-element.94), channel_id=1, source_target_pairs={{0,16},{1,5},{2,18},{3,7},{4,20},{5,1},{6,22},{7,3},{8,24},{9,13},... | collective-permute-start | bytes 221192 | tf_op jit(solution)/shard_map/ppermute | solution.py:467
  35.0 0.5 collective-permute-start.10
  35.6 3.2 %first_late.1 = f32[16,1152]{1,0:T(8,128)S(1)} custom-call(f32[768,1152]{1,0:T(8,128)S(1)} %get-tuple-element.71.refs_0_.refs_1_, f32[768,1152]{1,0:T(8,128)S(1)} %get-tuple-element.72.refs_1_.refs_2_, f32[768,1152]{1,0:T(8,128)S(1)} %get-tuple-element.73.refs_1_.refs_2_.refs_0_, f32[768,1152]{1,0:T(8,128)S(1)} %get-tuple-element.74.refs_2_.refs_3_.refs_1_, ...), custom_call_target="tpu_custom_call" | custom-call | flops 2038431744 | bytes 15925248 | tf_op jit(solution)/shard_map/first_late/pallas_call | solution.py:447
  38.9 1.4 %collective-permute-done.10 = f32[16,1152]{1,0:T(8,128)S(1)} collective-permute-done((f32[16,1152]{1,0:T(8,128)S(1)}, f32[16,1152]{1,0:T(8,128)S(1)}, u32[]{:S(2)}, u32[]{:S(2)}) %collective-permute-start.10) | collective-permute-done | bytes 73760 | tf_op jit(solution)/shard_map/ppermute | solution.py:467
  40.3 0.3 collective-permute-start.11
  40.6 1.0 %collective-permute-done.11.got_ref = f32[16,1152]{1,0:T(8,128)S(1)} collective-permute-done((f32[16,1152]{1,0:T(8,128)S(1)}, f32[16,1152]{1,0:T(8,128)S(1)}, u32[]{:S(2)}, u32[]{:S(2)}) %collective-permute-start.11) | collective-permute-done | bytes 73760 | tf_op jit(solution)/shard_map/ppermute | solution.py:467
  41.6 0.4 pair.1
  42.0 1.4 %collective-permute-start.13 = (f32[16,1280]{1,0:T(8,128)S(1)}, f32[16,1280]{1,0:T(8,128)S(1)}, u32[]{:S(2)}, u32[]{:S(2)}) collective-permute-start(f32[16,1280]{1,0:T(8,128)S(1)} %get-tuple-element.102), channel_id=1, source_target_pairs={{0,16},{1,5},{2,18},{3,7},{4,20},{5,1},{6,22},{7,3},{8,24},{9,13},... | collective-permute-start | bytes 245768 | tf_op jit(solution)/shard_map/ppermute | solution.py:467
  43.5 1.4 %collective-permute-start.14 = (f32[16,1280]{1,0:T(8,128)S(1)}, f32[16,1280]{1,0:T(8,128)S(1)}, u32[]{:S(2)}, u32[]{:S(2)}) collective-permute-start(f32[16,1280]{1,0:T(8,128)S(1)} %get-tuple-element.103), channel_id=1, source_target_pairs={{0,24},{1,7},{2,26},{3,5},{4,28},{5,3},{6,30},{7,1},{8,16},{9,15},... | collective-permute-start | bytes 245768 | tf_op jit(solution)/shard_map/ppermute | solution.py:467
  44.9 0.8 collective-permute-start.12
  45.7 3.0 %second_early.1.refs_10_ = f32[16,2304]{1,0:T(8,128)S(1)} custom-call(f32[768,1152]{1,0:T(8,128)S(1)} %get-tuple-element.70.refs_1_.piece.refs_0_, f32[768,1152]{1,0:T(8,128)S(1)} %get-tuple-element.71.refs_0_.refs_1_, f32[768,1152]{1,0:T(8,128)S(1)} %get-tuple-element.72.refs_1_.refs_2_, f32[16,1280]{1,0:T(8,128)S(1)} %get-tuple-element.105.refs_3_.refs_9_.refs_0_.pair_ref), custom_call_target="tpu_custom_call" | custom-call | flops 1358954496 | bytes 10616832 | tf_op jit(solution)/shard_map/second_early/pallas_call | solution.py:447
  48.7 0.0 collective-permute-done.13.refs_13_.refs_2_
  48.7 0.8 collective-permute-done.14.refs_14_.refs_3_
  49.5 0.6 collective-permute-done.12.refs_12_.refs_1_
  50.2 0.0 collective-permute-start.15
  50.2 0.5 collective-permute-start.16
  50.7 0.0 collective-permute-start.17
  50.7 1.5 %second_own.1.refs_11_ = f32[16,3456]{1,0:T(8,128)S(1)} custom-call(f32[768,1152]{1,0:T(8,128)S(1)} %get-tuple-element.73.refs_1_.refs_2_.refs_0_, f32[768,1152]{1,0:T(8,128)S(1)} %get-tuple-element.74.refs_2_.refs_3_.refs_1_, f32[768,1152]{1,0:T(8,128)S(1)} %get-tuple-element.75.refs_3_.refs_4_.refs_2_, ...), custom_call_target="tpu_custom_call" | custom-call | flops 679477248 | bytes 5308416 | tf_op jit(solution)/shard_map/second_own/pallas_call | solution.py:447
  52.1 0.0 collective-permute-done.16.refs_16_.refs_5_
  52.2 10.9 %second.1 = (f32[3,16,1152]{2,1,0:T(8,128)S(1)}, f32[3,16,1152]{2,1,0:T(8,128)S(1)}, f32[16,576]{1,0:T(8,128)S(1)}, bf16[32,2304]{1,0:T(8,128)(2,1)S(1)}, bf16[32,3456]{1,0:T(8,128)(2,1)S(1)}) custom-call(f32[768,1152]{1,0:T(8,128)S(1)} %get-tuple-element.73.refs_1_.refs_2_.refs_0_, f32[768,1152]{1,0:T(8,128)S(1)} %get-tuple-element.74.refs_2_.refs_3_.refs_1_, ...), custom_call_target="tpu_custom_call" | custom-call | flops 5435817984 | bytes 42467328 | tf_op jit(solution)/shard_map/second/pallas_call | solution.py:447
  63.1 0.6 collective-permute-start.18
  63.6 0.7 second_near.1.refs_7_
  64.4 0.4 collective-permute-done.18.got_ref
  64.8 0.1 collective-permute-start.19
  64.8 1.3 %collective-permute-start.20 = (f32[16,1280]{1,0:T(8,128)S(1)}, f32[16,1280]{1,0:T(8,128)S(1)}, u32[]{:S(2)}, u32[]{:S(2)}) collective-permute-start(f32[16,1280]{1,0:T(8,128)S(1)} %get-tuple-element.118), channel_id=1, source_target_pairs={{0,16},{1,5},{2,18},{3,7},{4,20},{5,1},{6,22},{7,3},{8,24},{9,13},... | collective-permute-start | bytes 245768 | tf_op jit(solution)/shard_map/ppermute | solution.py:467
  66.2 1.5 %collective-permute-start.21 = (f32[16,1280]{1,0:T(8,128)S(1)}, f32[16,1280]{1,0:T(8,128)S(1)}, u32[]{:S(2)}, u32[]{:S(2)}) collective-permute-start(f32[16,1280]{1,0:T(8,128)S(1)} %get-tuple-element.119), channel_id=1, source_target_pairs={{0,24},{1,7},{2,26},{3,5},{4,28},{5,3},{6,30},{7,1},{8,16},{9,15},... | collective-permute-start | bytes 245768 | tf_op jit(solution)/shard_map/ppermute | solution.py:467
  67.6 3.3 %second_late.1 = f32[16,1280]{1,0:T(8,128)S(1)} custom-call(f32[768,1152]{1,0:T(8,128)S(1)} %get-tuple-element.71.refs_0_.refs_1_, f32[768,1152]{1,0:T(8,128)S(1)} %get-tuple-element.72.refs_1_.refs_2_, f32[768,1152]{1,0:T(8,128)S(1)} %get-tuple-element.73.refs_1_.refs_2_.refs_0_, f32[768,1152]{1,0:T(8,128)S(1)} %get-tuple-element.74.refs_2_.refs_3_.refs_1_, ...), custom_call_target="tpu_custom_call" | custom-call | flops 2038431744 | bytes 15925248 | tf_op jit(solution)/shard_map/second_late/pallas_call | solution.py:447
  71.0 0.6 collective-permute-done.21
  71.5 0.7 collective-permute-start.22
  72.3 0.9 collective-permute-done.22.got_ref
  73.2 2.6 %middle.1 = (f32[16,1152]{1,0:T(8,128)S(1)}, f32[16,1152]{1,0:T(8,128)S(1)}, f32[16,16]{1,0:T(8,128)S(1)}, f32[16,16]{1,0:T(8,128)S(1)}, f32[48,48]{1,0:T(8,128)...) custom-call(f32[16,1152]{1,0:T(8,128)S(1)} %get-tuple-element.79.refs_2_.refs_4_.refs_5_.refs_9_.first_ref, ...), custom_call_target="tpu_custom_call" | custom-call | tf_op jit(solution)/shard_map/middle/pallas_call | solution.py:447
  75.8 0.7 collective-permute-start.24
  76.5 1.5 %collective-permute-start.25 = (f32[48,48]{1,0:T(8,128)S(1)}, f32[48,48]{1,0:T(8,128)S(1)}, u32[]{:S(2)}, u32[]{:S(2)}) collective-permute-start(f32[48,48]{1,0:T(8,128)S(1)} %get-tuple-element.126), channel_id=1, source_target_pairs={{0,24},{1,25},{2,26},{3,27},{4,28},{5,29},{6,30},{7,31},{8,16},{9,... | collective-permute-start | bytes 27656 | tf_op jit(solution)/shard_map/ppermute | solution.py:467
  78.0 1.3 %collective-permute-start.23 = (f32[48,48]{1,0:T(8,128)S(1)}, f32[48,48]{1,0:T(8,128)S(1)}, u32[]{:S(2)}, u32[]{:S(2)}) collective-permute-start(f32[48,48]{1,0:T(8,128)S(1)} %get-tuple-element.124.refs_0_), channel_id=1, source_target_pairs={{0,8},{1,9},{2,10},{3,11},{4,12},{5,13},{6,14},{7,15},{8,0},{9,1},... | collective-permute-start | bytes 27656 | tf_op jit(solution)/shard_map/ppermute | solution.py:467
  79.4 0.3 collective-permute-done.24.refs_2_
  79.7 1.5 %collective-permute-done.25.refs_3_ = f32[48,48]{1,0:T(8,128)S(1)} collective-permute-done((f32[48,48]{1,0:T(8,128)S(1)}, f32[48,48]{1,0:T(8,128)S(1)}, u32[]{:S(2)}, u32[]{:S(2)}) %collective-permute-start.25) | collective-permute-done | bytes 9248 | tf_op jit(solution)/shard_map/ppermute | solution.py:467
  81.2 0.6 collective-permute-done.23.refs_1_
  81.9 2.2 %collective-permute-start.27 = (f32[48,48]{1,0:T(8,128)S(1)}, f32[48,48]{1,0:T(8,128)S(1)}, u32[]{:S(2)}, u32[]{:S(2)}) collective-permute-start(f32[48,48]{1,0:T(8,128)S(1)} %get-tuple-element.128), channel_id=1, source_target_pairs={{0,4},{1,5},{2,6},{3,7},{4,0},{5,1},{6,2},{7,3},{8,12},{9,13},{10,... | collective-permute-start | bytes 27656 | tf_op jit(solution)/shard_map/ppermute | solution.py:467
  84.1 2.0 %collective-permute-start.28 = (f32[48,48]{1,0:T(8,128)S(1)}, f32[48,48]{1,0:T(8,128)S(1)}, u32[]{:S(2)}, u32[]{:S(2)}) collective-permute-start(f32[48,48]{1,0:T(8,128)S(1)} %get-tuple-element.129), channel_id=1, source_target_pairs={{0,6},{1,7},{2,4},{3,5},{4,2},{5,3},{6,0},{7,1},{8,14},{9,15},{10,... | collective-permute-start | bytes 27656 | tf_op jit(solution)/shard_map/ppermute | solution.py:467
  86.1 0.6 collective-permute-done.27.refs_2_
  86.7 3.0 %collective-permute-done.28.refs_3_ = f32[48,48]{1,0:T(8,128)S(1)} collective-permute-done((f32[48,48]{1,0:T(8,128)S(1)}, f32[48,48]{1,0:T(8,128)S(1)}, u32[]{:S(2)}, u32[]{:S(2)}) %collective-permute-start.28) | collective-permute-done | bytes 9248 | tf_op jit(solution)/shard_map/ppermute | solution.py:467
  89.7 0.3 collective-permute-done.26.refs_1_
  90.0 2.8 %last.1 = (f32[16,576]{1,0:T(8,128)}, f32[2,16,16]{2,1,0:T(8,128)}, f32[2,16,16]{2,1,0:T(8,128)}) custom-call(f32[16,1152]{1,0:T(8,128)S(1)} %get-tuple-element.79.refs_2_.refs_4_.refs_5_.refs_9_.first_ref, f32[16,1152]{1,0:T(8,128)S(1)} %get-tuple-element.120.q_ref, f32[16,1152]{1,0:T(8,128)S(1)} %get-tuple-element.121.prod_ref, ...), custom_call_target="tpu_custom_call" | custom-call | tf_op jit(solution)/shard_map/last/pallas_call | solution.py:447
  (17 shorter events, 0.1 us)
Async XLA Ops:
  0.6 2.6 %collective-permute-start = (f32[16,576]{1,0:T(8,128)}, f32[16,576]{1,0:T(8,128)S(1)}, u32[]{:S(2)}, u32[]{:S(2)}) collective-permute-start(f32[16,576]{1,0:T(8,128)} %bitcast.7), channel_id=1, source_target_pairs={{0,1},{1,0},{2,3},{3,2},{4,5},{5,4},{6,7},{7,6},{8,9},{9,8},{10,11... | collective-permute-start | bytes 110600 | tf_op jit(solution)/shard_map/ppermute | solution.py:467
  3.3 11.7 %collective-permute-start.2 = (f32[16,1152]{1,0:T(8,128)S(1)}, f32[16,1152]{1,0:T(8,128)S(1)}, u32[]{:S(2)}, u32[]{:S(2)}) collective-permute-start(f32[16,1152]{1,0:T(8,128)S(1)} %get-tuple-element.77), channel_id=1, source_target_pairs={{0,16},{1,5},{2,18},{3,7},{4,20},{5,1},{6,22},{7,3},{8,24},{9,13},... | collective-permute-start | bytes 221192 | tf_op jit(solution)/shard_map/ppermute | solution.py:467
  5.9 9.2 %collective-permute-start.3 = (f32[16,1152]{1,0:T(8,128)S(1)}, f32[16,1152]{1,0:T(8,128)S(1)}, u32[]{:S(2)}, u32[]{:S(2)}) collective-permute-start(f32[16,1152]{1,0:T(8,128)S(1)} %get-tuple-element.78), channel_id=1, source_target_pairs={{0,24},{1,7},{2,26},{3,5},{4,28},{5,3},{6,30},{7,1},{8,16},{9,15},... | collective-permute-start | bytes 221192 | tf_op jit(solution)/shard_map/ppermute | solution.py:467
  7.3 7.7 %collective-permute-start.1 = (f32[16,1152]{1,0:T(8,128)S(1)}, f32[16,1152]{1,0:T(8,128)S(1)}, u32[]{:S(2)}, u32[]{:S(2)}) collective-permute-start(f32[16,1152]{1,0:T(8,128)S(1)} %get-tuple-element.79.refs_2_.refs_4_.refs_5_.refs_9_.first_ref), channel_id=1, source_target_pairs={{0,2},{1,9},{2,0},{3,11},{4,6},{5,13},{6,4},{7,15},{8,10},{9,1},{1... | collective-permute-start | bytes 221192 | tf_op jit(solution)/shard_map/ppermute | solution.py:467
  15.1 3.2 %collective-permute-start.4 = (f32[16,1152]{1,0:T(8,128)S(1)}, f32[16,1152]{1,0:T(8,128)S(1)}, u32[]{:S(2)}, u32[]{:S(2)}) collective-permute-start(f32[16,1152]{1,0:T(8,128)S(1)} %collective-permute-done.1.refs_8_), channel_id=1, source_target_pairs={{0,1},{1,0},{2,3},{3,2},{4,5},{5,4},{6,7},{7,6},{8,9},{9,8},{10,11... | collective-permute-start | bytes 221192 | tf_op jit(solution)/shard_map/ppermute | solution.py:467
  15.7 2.6 %collective-permute-start.5 = (f32[16,1152]{1,0:T(8,128)S(1)}, f32[16,1152]{1,0:T(8,128)S(1)}, u32[]{:S(2)}, u32[]{:S(2)}) collective-permute-start(f32[16,1152]{1,0:T(8,128)S(1)} %collective-permute-done.2.refs_9_), channel_id=1, source_target_pairs={{0,1},{1,0},{2,3},{3,2},{4,5},{5,4},{6,7},{7,6},{8,9},{9,8},{10,11... | collective-permute-start | bytes 221192 | tf_op jit(solution)/shard_map/ppermute | solution.py:467
  15.8 2.5 %collective-permute-start.6 = (f32[16,1152]{1,0:T(8,128)S(1)}, f32[16,1152]{1,0:T(8,128)S(1)}, u32[]{:S(2)}, u32[]{:S(2)}) collective-permute-start(f32[16,1152]{1,0:T(8,128)S(1)} %collective-permute-done.3.refs_10_), channel_id=1, source_target_pairs={{0,1},{1,0},{2,3},{3,2},{4,5},{5,4},{6,7},{7,6},{8,9},{9,8},{10,11... | collective-permute-start | bytes 221192 | tf_op jit(solution)/shard_map/ppermute | solution.py:467
  18.3 13.2 %copy-start = (f32[576]{0:T(1024)S(1)}, f32[576]{0:T(1024)}, u32[]{:S(2)}) copy-start(f32[576]{0:T(1024)} %param.4) | copy-start | bytes 6916
  31.4 1.5 %collective-permute-start.7 = (f32[3,16,1152]{2,1,0:T(8,128)S(1)}, f32[3,16,1152]{2,1,0:T(8,128)S(1)}, u32[]{:S(2)}, u32[]{:S(2)}) collective-permute-start(f32[3,16,1152]{2,1,0:T(8,128)S(1)} %get-tuple-element.88), channel_id=1, source_target_pairs={{0,1},{1,0},{2,3},{3,2},{4,5},{5,4},{6,7},{7,6},{8,9},{9,8},{10,11... | collective-permute-start | bytes 663560 | tf_op jit(solution)/shard_map/ppermute | solution.py:467
  33.0 5.9 %collective-permute-start.8 = (f32[16,1152]{1,0:T(8,128)S(1)}, f32[16,1152]{1,0:T(8,128)S(1)}, u32[]{:S(2)}, u32[]{:S(2)}) collective-permute-start(f32[16,1152]{1,0:T(8,128)S(1)} %get-tuple-element.93), channel_id=1, source_target_pairs={{0,2},{1,9},{2,0},{3,11},{4,6},{5,13},{6,4},{7,15},{8,10},{9,1},{1... | collective-permute-start | bytes 221192 | tf_op jit(solution)/shard_map/ppermute | solution.py:467
  33.8 5.0 %collective-permute-start.9 = (f32[16,1152]{1,0:T(8,128)S(1)}, f32[16,1152]{1,0:T(8,128)S(1)}, u32[]{:S(2)}, u32[]{:S(2)}) collective-permute-start(f32[16,1152]{1,0:T(8,128)S(1)} %get-tuple-element.94), channel_id=1, source_target_pairs={{0,16},{1,5},{2,18},{3,7},{4,20},{5,1},{6,22},{7,3},{8,24},{9,13},... | collective-permute-start | bytes 221192 | tf_op jit(solution)/shard_map/ppermute | solution.py:467
  35.0 5.3 %collective-permute-start.10 = (f32[16,1152]{1,0:T(8,128)S(1)}, f32[16,1152]{1,0:T(8,128)S(1)}, u32[]{:S(2)}, u32[]{:S(2)}) collective-permute-start(f32[16,1152]{1,0:T(8,128)S(1)} %get-tuple-element.95), channel_id=1, source_target_pairs={{0,24},{1,7},{2,26},{3,5},{4,28},{5,3},{6,30},{7,1},{8,16},{9,15},... | collective-permute-start | bytes 221192 | tf_op jit(solution)/shard_map/ppermute | solution.py:467
  40.3 1.3 %collective-permute-start.11 = (f32[16,1152]{1,0:T(8,128)S(1)}, f32[16,1152]{1,0:T(8,128)S(1)}, u32[]{:S(2)}, u32[]{:S(2)}) collective-permute-start(f32[16,1152]{1,0:T(8,128)S(1)} %add_add_fusion.1.mine_ref), channel_id=1, source_target_pairs={{0,1},{1,0},{2,3},{3,2},{4,5},{5,4},{6,7},{7,6},{8,9},{9,8},{10,11... | collective-permute-start | bytes 221192 | tf_op jit(solution)/shard_map/ppermute | solution.py:467
  42.0 6.7 %collective-permute-start.13 = (f32[16,1280]{1,0:T(8,128)S(1)}, f32[16,1280]{1,0:T(8,128)S(1)}, u32[]{:S(2)}, u32[]{:S(2)}) collective-permute-start(f32[16,1280]{1,0:T(8,128)S(1)} %get-tuple-element.102), channel_id=1, source_target_pairs={{0,16},{1,5},{2,18},{3,7},{4,20},{5,1},{6,22},{7,3},{8,24},{9,13},... | collective-permute-start | bytes 245768 | tf_op jit(solution)/shard_map/ppermute | solution.py:467
  43.5 6.1 %collective-permute-start.14 = (f32[16,1280]{1,0:T(8,128)S(1)}, f32[16,1280]{1,0:T(8,128)S(1)}, u32[]{:S(2)}, u32[]{:S(2)}) collective-permute-start(f32[16,1280]{1,0:T(8,128)S(1)} %get-tuple-element.103), channel_id=1, source_target_pairs={{0,24},{1,7},{2,26},{3,5},{4,28},{5,3},{6,30},{7,1},{8,16},{9,15},... | collective-permute-start | bytes 245768 | tf_op jit(solution)/shard_map/ppermute | solution.py:467
  44.9 5.3 %collective-permute-start.12 = (f32[16,1280]{1,0:T(8,128)S(1)}, f32[16,1280]{1,0:T(8,128)S(1)}, u32[]{:S(2)}, u32[]{:S(2)}) collective-permute-start(f32[16,1280]{1,0:T(8,128)S(1)} %get-tuple-element.105.refs_3_.refs_9_.refs_0_.pair_ref), channel_id=1, source_target_pairs={{0,2},{1,9},{2,0},{3,11},{4,6},{5,13},{6,4},{7,15},{8,10},{9,1},{1... | collective-permute-start | bytes 245768 | tf_op jit(solution)/shard_map/ppermute | solution.py:467
  50.2 2.0 %collective-permute-start.15 = (f32[16,1280]{1,0:T(8,128)S(1)}, f32[16,1280]{1,0:T(8,128)S(1)}, u32[]{:S(2)}, u32[]{:S(2)}) collective-permute-start(f32[16,1280]{1,0:T(8,128)S(1)} %collective-permute-done.12.refs_12_.refs_1_), channel_id=1, source_target_pairs={{0,1},{1,0},{2,3},{3,2},{4,5},{5,4},{6,7},{7,6},{8,9},{9,8},{10,11... | collective-permute-start | bytes 245768 | tf_op jit(solution)/shard_map/ppermute | solution.py:467
  50.2 2.0 %collective-permute-start.16 = (f32[16,1280]{1,0:T(8,128)S(1)}, f32[16,1280]{1,0:T(8,128)S(1)}, u32[]{:S(2)}, u32[]{:S(2)}) collective-permute-start(f32[16,1280]{1,0:T(8,128)S(1)} %collective-permute-done.13.refs_13_.refs_2_), channel_id=1, source_target_pairs={{0,1},{1,0},{2,3},{3,2},{4,5},{5,4},{6,7},{7,6},{8,9},{9,8},{10,11... | collective-permute-start | bytes 245768 | tf_op jit(solution)/shard_map/ppermute | solution.py:467
  50.7 1.5 %collective-permute-start.17 = (f32[16,1280]{1,0:T(8,128)S(1)}, f32[16,1280]{1,0:T(8,128)S(1)}, u32[]{:S(2)}, u32[]{:S(2)}) collective-permute-start(f32[16,1280]{1,0:T(8,128)S(1)} %collective-permute-done.14.refs_14_.refs_3_), channel_id=1, source_target_pairs={{0,1},{1,0},{2,3},{3,2},{4,5},{5,4},{6,7},{7,6},{8,9},{9,8},{10,11... | collective-permute-start | bytes 245768 | tf_op jit(solution)/shard_map/ppermute | solution.py:467
  63.1 1.7 %collective-permute-start.18 = (f32[3,16,1152]{2,1,0:T(8,128)S(1)}, f32[3,16,1152]{2,1,0:T(8,128)S(1)}, u32[]{:S(2)}, u32[]{:S(2)}) collective-permute-start(f32[3,16,1152]{2,1,0:T(8,128)S(1)} %get-tuple-element.111), channel_id=1, source_target_pairs={{0,1},{1,0},{2,3},{3,2},{4,5},{5,4},{6,7},{7,6},{8,9},{9,8},{10,11... | collective-permute-start | bytes 663560 | tf_op jit(solution)/shard_map/ppermute | solution.py:467
  64.8 6.2 %collective-permute-start.19 = (f32[16,1280]{1,0:T(8,128)S(1)}, f32[16,1280]{1,0:T(8,128)S(1)}, u32[]{:S(2)}, u32[]{:S(2)}) collective-permute-start(f32[16,1280]{1,0:T(8,128)S(1)} %get-tuple-element.117), channel_id=1, source_target_pairs={{0,2},{1,9},{2,0},{3,11},{4,6},{5,13},{6,4},{7,15},{8,10},{9,1},{1... | collective-permute-start | bytes 245768 | tf_op jit(solution)/shard_map/ppermute | solution.py:467
  64.8 6.1 %collective-permute-start.20 = (f32[16,1280]{1,0:T(8,128)S(1)}, f32[16,1280]{1,0:T(8,128)S(1)}, u32[]{:S(2)}, u32[]{:S(2)}) collective-permute-start(f32[16,1280]{1,0:T(8,128)S(1)} %get-tuple-element.118), channel_id=1, source_target_pairs={{0,16},{1,5},{2,18},{3,7},{4,20},{5,1},{6,22},{7,3},{8,24},{9,13},... | collective-permute-start | bytes 245768 | tf_op jit(solution)/shard_map/ppermute | solution.py:467
  66.2 5.3 %collective-permute-start.21 = (f32[16,1280]{1,0:T(8,128)S(1)}, f32[16,1280]{1,0:T(8,128)S(1)}, u32[]{:S(2)}, u32[]{:S(2)}) collective-permute-start(f32[16,1280]{1,0:T(8,128)S(1)} %get-tuple-element.119), channel_id=1, source_target_pairs={{0,24},{1,7},{2,26},{3,5},{4,28},{5,3},{6,30},{7,1},{8,16},{9,15},... | collective-permute-start | bytes 245768 | tf_op jit(solution)/shard_map/ppermute | solution.py:467
  71.5 1.6 %collective-permute-start.22 = (f32[16,1280]{1,0:T(8,128)S(1)}, f32[16,1280]{1,0:T(8,128)S(1)}, u32[]{:S(2)}, u32[]{:S(2)}) collective-permute-start(f32[16,1280]{1,0:T(8,128)S(1)} %add_add_fusion.mine_ref), channel_id=1, source_target_pairs={{0,1},{1,0},{2,3},{3,2},{4,5},{5,4},{6,7},{7,6},{8,9},{9,8},{10,11... | collective-permute-start | bytes 245768 | tf_op jit(solution)/shard_map/ppermute | solution.py:467
  75.8 3.9 %collective-permute-start.24 = (f32[48,48]{1,0:T(8,128)S(1)}, f32[48,48]{1,0:T(8,128)S(1)}, u32[]{:S(2)}, u32[]{:S(2)}) collective-permute-start(f32[48,48]{1,0:T(8,128)S(1)} %get-tuple-element.125), channel_id=1, source_target_pairs={{0,16},{1,17},{2,18},{3,19},{4,20},{5,21},{6,22},{7,23},{8,24},{9,... | collective-permute-start | bytes 27656 | tf_op jit(solution)/shard_map/ppermute | solution.py:467
  76.5 4.7 %collective-permute-start.25 = (f32[48,48]{1,0:T(8,128)S(1)}, f32[48,48]{1,0:T(8,128)S(1)}, u32[]{:S(2)}, u32[]{:S(2)}) collective-permute-start(f32[48,48]{1,0:T(8,128)S(1)} %get-tuple-element.126), channel_id=1, source_target_pairs={{0,24},{1,25},{2,26},{3,27},{4,28},{5,29},{6,30},{7,31},{8,16},{9,... | collective-permute-start | bytes 27656 | tf_op jit(solution)/shard_map/ppermute | solution.py:467
  78.0 3.8 %collective-permute-start.23 = (f32[48,48]{1,0:T(8,128)S(1)}, f32[48,48]{1,0:T(8,128)S(1)}, u32[]{:S(2)}, u32[]{:S(2)}) collective-permute-start(f32[48,48]{1,0:T(8,128)S(1)} %get-tuple-element.124.refs_0_), channel_id=1, source_target_pairs={{0,8},{1,9},{2,10},{3,11},{4,12},{5,13},{6,14},{7,15},{8,0},{9,1},... | collective-permute-start | bytes 27656 | tf_op jit(solution)/shard_map/ppermute | solution.py:467
  81.9 4.8 %collective-permute-start.27 = (f32[48,48]{1,0:T(8,128)S(1)}, f32[48,48]{1,0:T(8,128)S(1)}, u32[]{:S(2)}, u32[]{:S(2)}) collective-permute-start(f32[48,48]{1,0:T(8,128)S(1)} %get-tuple-element.128), channel_id=1, source_target_pairs={{0,4},{1,5},{2,6},{3,7},{4,0},{5,1},{6,2},{7,3},{8,12},{9,13},{10,... | collective-permute-start | bytes 27656 | tf_op jit(solution)/shard_map/ppermute | solution.py:467
  84.1 5.6 %collective-permute-start.28 = (f32[48,48]{1,0:T(8,128)S(1)}, f32[48,48]{1,0:T(8,128)S(1)}, u32[]{:S(2)}, u32[]{:S(2)}) collective-permute-start(f32[48,48]{1,0:T(8,128)S(1)} %get-tuple-element.129), channel_id=1, source_target_pairs={{0,6},{1,7},{2,4},{3,5},{4,2},{5,3},{6,0},{7,1},{8,14},{9,15},{10,... | collective-permute-start | bytes 27656 | tf_op jit(solution)/shard_map/ppermute | solution.py:467
  86.0 3.9 %collective-permute-start.26 = (f32[48,48]{1,0:T(8,128)S(1)}, f32[48,48]{1,0:T(8,128)S(1)}, u32[]{:S(2)}, u32[]{:S(2)}) collective-permute-start(f32[48,48]{1,0:T(8,128)S(1)} %get-tuple-element.127.refs_0_), channel_id=1, source_target_pairs={{0,2},{1,3},{2,0},{3,1},{4,6},{5,7},{6,4},{7,5},{8,10},{9,11},{10,... | collective-permute-start | bytes 27656 | tf_op jit(solution)/shard_map/ppermute | solution.py:467
